TPU v7x, 32 devices: a whole 2x2x4 slice. The times are simulated.
32 devices in a mesh: fsdp: 4 (over y, x), dp: 8 (over z, core).
Axes of the slice: x: 2, y: 2, z: 4, core: 2. Of those that a mesh axis runs over, the one named last changes fastest.
Arguments:
- tokens: bfloat16 [16384, 1152], P(('fsdp', 'dp')), may hold values from -6 to 6
- conditions: bfloat16 [64, 1152], P(('fsdp', 'dp')), may hold values from -6 to 6
- cotangent: bfloat16 [16384, 1152], P(('fsdp', 'dp')), may hold values from -6 to 6
- slot_mask: int32 [64], P(('fsdp', 'dp')), may hold values from 0 to 1, as said below
- weight_flat: bfloat16 [186624, 128], P(('fsdp', 'dp')), may hold values from -3 to 3
- bias_flat: bfloat16 [17664], P(('fsdp', 'dp')), may hold values from -2 to 2
Outputs:
- out: bfloat16 [16384, 1152], P(('fsdp', 'dp'))
- grad_tokens: float32 [16384, 1152], P(('fsdp', 'dp'))
- grad_conditions: float32 [64, 1152], P(('fsdp', 'dp'))
- grad_weights: float32 [186624, 128], P(('fsdp', 'dp'))
- grad_biases: float32 [17664], P(('fsdp', 'dp'))
Inputs may be any that keep to these rules, and one draw needn't show every extreme that they name: `slot_mask`: on each device's 2 image slots the live ones come first; a device has one live image or all 2, and some device has all 2 live in every draw.
All inputs are finite; a program needn't handle non-finite values.
Results may differ from a plain program's by a relative error of at most 0.0095.
Values may be sent and summed in bfloat16 or wider, within the bound.
No kernel may reach another device: no remote copies, remote signals or barrier semaphores. Data moves between devices by JAX's collectives and lax.ppermute only.
A program may use at most 576 MiB of HBM per device.

v0:
```python
import math

import jax
import jax.numpy as jnp
from jax import lax
from jax.sharding import PartitionSpec as P

D = 1152
HEADS = 16
HEAD_DIM = 72
FF = 3072
GRID = 16


eps_norm = 1e-06


def unpack_weights(weight_all, bias_all):
    flat = weight_all.reshape(-1)
    layouts = ((D, 3 * D), (D, D), (D, 2 * FF), (D, 6 * D), (FF, D))
    pieces = []
    offset = 0
    for layout in layouts:
        amount = layout[0] * layout[1]
        pieces.append(flat[offset : offset + amount].reshape(layout))
        offset = offset + amount
    offset = 0
    for amount in (3 * D, D, 2 * FF, 6 * D):
        pieces.append(bias_all[offset : offset + amount])
        offset = offset + amount
    return tuple(pieces)


def rope_tables():
    quarter = HEAD_DIM // 4
    places = jnp.arange(GRID * GRID, dtype=jnp.int32)
    rows_at = (places // GRID).astype(jnp.float32)
    cols_at = (places % GRID).astype(jnp.float32)
    freqs = 10000.0 ** (-jnp.arange(quarter, dtype=jnp.float32) / quarter)
    along_rows = rows_at[:, None] * freqs[None, :]
    along_cols = cols_at[:, None] * freqs[None, :]
    angles = jnp.concatenate([along_rows, along_rows, along_cols, along_cols], axis=1)
    return (jnp.cos(angles)[:, None, :], jnp.sin(angles)[:, None, :])


def turn_half(values):
    quarter = values.shape[-1] // 4
    first = values[..., :quarter]
    second = values[..., quarter : 2 * quarter]
    third = values[..., 2 * quarter : 3 * quarter]
    fourth = values[..., 3 * quarter :]
    return jnp.concatenate([-second, first, -fourth, third], axis=-1)


def norm_parts(values):
    centred = values - jnp.mean(values, -1, keepdims=True)
    inverse = lax.rsqrt(jnp.mean(centred * centred, -1, keepdims=True) + eps_norm)
    return (centred * inverse, inverse)


def norm_back(grad_normed, normed, inverse):
    return inverse * (
        grad_normed
        - jnp.mean(grad_normed, -1, keepdims=True)
        - normed * jnp.mean(grad_normed * normed, -1, keepdims=True)
    )


def rms_parts(values):
    inverse = lax.rsqrt(jnp.mean(values * values, -1, keepdims=True) + eps_norm)
    return (values * inverse, inverse)


def rms_back(grad_normed, normed, inverse):
    return inverse * (grad_normed - normed * jnp.mean(grad_normed * normed, -1, keepdims=True))


def on_device(tokens, conditions, cotangent, slot_mask, weight_flat, bias_flat):
    f32 = jnp.float32
    bf16 = jnp.bfloat16
    slots = conditions.shape[0]
    length = GRID * GRID
    rows_all = slots * length
    scale = 1.0 / math.sqrt(HEAD_DIM)
    heads_shape = (slots, length, HEADS, HEAD_DIM)
    weight_all, bias_all = (
        lax.all_gather(weight_flat, ("fsdp", "dp"), axis=0, tiled=True),
        lax.all_gather(bias_flat, ("fsdp", "dp"), axis=0, tiled=True),
    )
    (
        query_key_value_weight,
        projection_weight,
        feedforward_weight,
        w_ada,
        down_weight,
        query_key_value_bias,
        projection_bias,
        feedforward_bias,
        b_ada,
    ) = unpack_weights(weight_all, bias_all)
    cosines, sines = rope_tables()
    mask_f = slot_mask.astype(f32)[:, None, None]
    x_f = tokens.astype(f32).reshape(slots, length, D)
    cond_f = conditions.astype(f32)
    cond_act = jax.nn.silu(cond_f).astype(bf16)
    modulation = jnp.dot(cond_act, w_ada, preferred_element_type=f32) + b_ada.astype(f32)
    shift_a, scale_a, gate_a, shift_b, scale_b, gate_b = [
        modulation[:, None, place * D : (place + 1) * D] for place in range(6)
    ]
    normed_a, inv_a = norm_parts(x_f)
    attention_input = (normed_a * (1.0 + scale_a) + shift_a).astype(bf16).reshape(rows_all, D)
    projected_output = (
        jnp.dot(attention_input, query_key_value_weight, preferred_element_type=f32)
        + query_key_value_bias.astype(f32)
    ).reshape(slots, length, 3 * D)
    q_norm, inv_q = rms_parts(projected_output[..., :D].reshape(heads_shape))
    k_norm, inv_k = rms_parts(projected_output[..., D : 2 * D].reshape(heads_shape))
    queries = (q_norm * cosines + turn_half(q_norm) * sines).astype(bf16)
    keys = (k_norm * cosines + turn_half(k_norm) * sines).astype(bf16)
    values = projected_output[..., 2 * D :].reshape(heads_shape).astype(bf16)
    scores = jnp.einsum("slhe,smhe->shlm", queries, keys, preferred_element_type=f32) * scale
    row_max = jnp.max(scores, -1, keepdims=True)
    log_total = row_max + jnp.log(jnp.sum(jnp.exp(scores - row_max), -1, keepdims=True))
    probs_low = jnp.exp(scores - log_total).astype(bf16)
    attention_output = (
        jnp.einsum("shlm,smhe->slhe", probs_low, values, preferred_element_type=f32)
        .astype(bf16)
        .reshape(rows_all, D)
    )
    attention_branch = (
        jnp.dot(attention_output, projection_weight, preferred_element_type=f32)
        + projection_bias.astype(f32)
    ).reshape(slots, length, D)
    middle = x_f + gate_a * attention_branch
    normed_b, inv_b = norm_parts(middle)
    feedforward_input = (normed_b * (1.0 + scale_b) + shift_b).astype(bf16).reshape(rows_all, D)
    mixed_tokens = jnp.dot(
        feedforward_input, feedforward_weight, preferred_element_type=f32
    ) + feedforward_bias.astype(f32)
    gate_part = mixed_tokens[:, :FF]
    up_part = mixed_tokens[:, FF:]
    hidden_state = (jax.nn.silu(gate_part) * up_part).astype(bf16)
    feedforward_branch = jnp.dot(hidden_state, down_weight, preferred_element_type=f32).reshape(
        slots, length, D
    )
    out = ((middle + gate_b * feedforward_branch) * mask_f).astype(bf16).reshape(rows_all, D)
    weight_all, bias_all = (
        lax.all_gather(weight_flat, ("fsdp", "dp"), axis=0, tiled=True),
        lax.all_gather(bias_flat, ("fsdp", "dp"), axis=0, tiled=True),
    )
    (
        query_key_value_weight,
        projection_weight,
        feedforward_weight,
        w_ada,
        down_weight,
        query_key_value_bias,
        projection_bias,
        feedforward_bias,
        b_ada,
    ) = unpack_weights(weight_all, bias_all)
    g_out = cotangent.astype(f32).reshape(slots, length, D) * mask_f
    g_branch_b = (gate_b * g_out).astype(bf16).reshape(rows_all, D)
    g_gate_b = jnp.sum(g_out * feedforward_branch, axis=1)
    grad_down = jnp.einsum("rf,rd->fd", hidden_state, g_branch_b, preferred_element_type=f32)
    g_hidden = jnp.einsum("rd,fd->rf", g_branch_b, down_weight, preferred_element_type=f32)
    sigma_gate = jax.nn.sigmoid(gate_part)
    g_mixed = jnp.concatenate(
        [
            g_hidden * up_part * sigma_gate * (1.0 + gate_part * (1.0 - sigma_gate)),
            g_hidden * (gate_part * sigma_gate),
        ],
        axis=1,
    ).astype(bf16)
    grad_mlp = jnp.einsum("rd,rf->df", feedforward_input, g_mixed, preferred_element_type=f32)
    grad_b_mlp = jnp.sum(g_mixed.astype(f32), axis=0)
    g_input_b = jnp.einsum(
        "rf,df->rd", g_mixed, feedforward_weight, preferred_element_type=f32
    ).reshape(slots, length, D)
    g_shift_b = jnp.sum(g_input_b, axis=1)
    g_scale_b = jnp.sum(g_input_b * normed_b, axis=1)
    g_middle = g_out + norm_back(g_input_b * (1.0 + scale_b), normed_b, inv_b)
    g_branch_a = (gate_a * g_middle).astype(bf16).reshape(rows_all, D)
    g_gate_a = jnp.sum(g_middle * attention_branch, axis=1)
    grad_w_out = jnp.einsum("rd,re->de", attention_output, g_branch_a, preferred_element_type=f32)
    grad_b_out = jnp.sum(g_branch_a.astype(f32), axis=0)
    g_attended = (
        jnp.einsum("re,de->rd", g_branch_a, projection_weight, preferred_element_type=f32)
        .astype(bf16)
        .reshape(heads_shape)
    )
    scores = jnp.einsum("slhe,smhe->shlm", queries, keys, preferred_element_type=f32) * scale
    probs = jnp.exp(scores - log_total)
    probs_low = probs.astype(bf16)
    g_probs = jnp.einsum("slhe,smhe->shlm", g_attended, values, preferred_element_type=f32)
    g_values = jnp.einsum("shlm,slhe->smhe", probs_low, g_attended, preferred_element_type=f32)
    g_scores = (probs * (g_probs - jnp.sum(probs * g_probs, -1, keepdims=True))).astype(bf16)
    g_queries = jnp.einsum("shlm,smhe->slhe", g_scores, keys, preferred_element_type=f32) * scale
    g_keys = jnp.einsum("shlm,slhe->smhe", g_scores, queries, preferred_element_type=f32) * scale
    g_q = rms_back(g_queries * cosines - turn_half(g_queries) * sines, q_norm, inv_q)
    g_k = rms_back(g_keys * cosines - turn_half(g_keys) * sines, k_norm, inv_k)
    g_projected = jnp.concatenate(
        [g_q.reshape(rows_all, D), g_k.reshape(rows_all, D), g_values.reshape(rows_all, D)], axis=1
    ).astype(bf16)
    grad_qkv = jnp.einsum("rd,re->de", attention_input, g_projected, preferred_element_type=f32)
    grad_b_qkv = jnp.sum(g_projected.astype(f32), axis=0)
    g_input_a = jnp.einsum(
        "re,de->rd", g_projected, query_key_value_weight, preferred_element_type=f32
    ).reshape(slots, length, D)
    g_shift_a = jnp.sum(g_input_a, axis=1)
    g_scale_a = jnp.sum(g_input_a * normed_a, axis=1)
    grad_tokens = g_middle + norm_back(g_input_a * (1.0 + scale_a), normed_a, inv_a)
    g_modulation = jnp.concatenate(
        [g_shift_a, g_scale_a, g_gate_a, g_shift_b, g_scale_b, g_gate_b], axis=1
    ).astype(bf16)
    grad_ada = jnp.einsum("sd,se->de", cond_act, g_modulation, preferred_element_type=f32)
    grad_b_ada = jnp.sum(g_modulation.astype(f32), axis=0)
    g_cond = jnp.einsum("se,de->sd", g_modulation, w_ada, preferred_element_type=f32)
    sigma_cond = jax.nn.sigmoid(cond_f)
    grad_conditions = g_cond * sigma_cond * (1.0 + cond_f * (1.0 - sigma_cond))
    narrow_count = lax.axis_size("fsdp")
    wide_count = lax.axis_size("dp")
    grads_big = jnp.concatenate(
        [
            grad_qkv.reshape(-1),
            grad_w_out.reshape(-1),
            grad_mlp.reshape(-1),
            grad_ada.reshape(-1),
            grad_down.reshape(-1),
        ]
    ).reshape(narrow_count, wide_count, -1, 128)
    grads_small = jnp.concatenate([grad_b_qkv, grad_b_out, grad_b_mlp, grad_b_ada]).reshape(
        narrow_count, wide_count, -1
    )
    spread_big, spread_small = (
        lax.all_to_all(
            lax.all_to_all(
                grads_big.astype(jnp.bfloat16), "fsdp", split_axis=0, concat_axis=0, tiled=True
            ),
            "dp",
            split_axis=1,
            concat_axis=1,
            tiled=True,
        ).astype(grads_big.dtype),
        lax.all_to_all(
            lax.all_to_all(
                grads_small.astype(jnp.bfloat16), "fsdp", split_axis=0, concat_axis=0, tiled=True
            ),
            "dp",
            split_axis=1,
            concat_axis=1,
            tiled=True,
        ).astype(grads_small.dtype),
    )
    part_weights = jnp.sum(spread_big, axis=(0, 1))
    part_biases = jnp.sum(spread_small, axis=(0, 1))
    return (out, grad_tokens.reshape(rows_all, D), grad_conditions, part_weights, part_biases)


def solution(mesh):
    return jax.shard_map(
        on_device,
        mesh=mesh,
        in_specs=(
            P(("fsdp", "dp"), None),
            P(("fsdp", "dp"), None),
            P(("fsdp", "dp"), None),
            P(("fsdp", "dp")),
            P(("fsdp", "dp"), None),
            P(("fsdp", "dp")),
        ),
        out_specs=(
            P(("fsdp", "dp"), None),
            P(("fsdp", "dp"), None),
            P(("fsdp", "dp"), None),
            P(("fsdp", "dp"), None),
            P(("fsdp", "dp")),
        ),
        check_vma=False,
    )
```

profile of v0, /device:TPU:9, one launch (start us, length us, event | category | flops | bytes accessed | tf_op | source)
XLA Modules:
  0.0 2408.7 jit_solution(1016306333423830473)
XLA Ops:
  13.1 42.9 %all-reduce = bf16[17664]{0:T(1024)(128)(2,1)S(1)} all-reduce(bf16[17664]{0:T(1024)(128)(2,1)S(1)} %dynamic-update-slice), channel_id=1, replica_groups=mesh['fsdp'=4,'dp'=8] {'fsdp','dp'}, use_global_device_ids=true, to_apply=%add | all-reduce | flops 17664 | bytes 70656
  58.4 216.6 %all-gather.2.cloned.1.call-done = bf16[186624,128]{1,0:T(8,128)(2,1)} async-done(((bf16[5832,128]{1,0:T(8,128)(2,1)}), bf16[186624,128]{1,0:T(8,128)(2,1)}) %all-gather.2.cloned.1.call-update) | async-done | bytes 47775760 | tf_op jit(solution)/shard_map/all_gather | solution.py:87
  275.0 6.4 slice.182
  281.4 14.0 reshape.431
  295.3 14.0 reshape.415
  309.3 6.8 slice.160
  316.1 15.2 reshape.433
  331.3 15.2 reshape.407
  346.5 13.4 slice.155
  359.9 29.2 %reshape.406 = bf16[1152,6912]{1,0:T(8,128)(2,1)} reshape(bf16[62208,128]{1,0:T(8,128)(2,1)} %slice.155) | data formatting | bytes 31850496 | tf_op jit(solution)/shard_map/reshape | solution.py:25
  389.1 7.8 convolution_add_fusion.1
  398.3 4.9 convolution_add_fusion.2
  404.4 2.5 fusion.50
  406.9 12.8 slice.178
  419.7 20.3 reshape.432
  440.0 20.3 reshape.414
  460.3 2.9 slice.173
  463.2 6.2 reshape.412
  471.4 2.4 copy.76
  476.6 3.0 copy.77
  494.3 3.5 fusion.26
  498.3 2.2 multiply_reduce_fusion.10
  502.4 3.0 fusion.20
  505.5 15.8 convolution_add_fusion
  521.3 13.0 multiply_convert_fusion.2
  534.3 5.2 fusion.7
  539.6 8.8 multiply_convert_fusion.7
  548.5 17.1 multiply_reduce_fusion.3
  567.0 4.5 fusion.49
  571.5 2.9 convolution_convert_fusion.5
  574.4 3.2 convolution_convert_fusion.4
  577.6 6.3 convolution_convert_fusion.3
  583.9 5.7 reshape.437
  589.6 4.3 copy.82
  593.9 5.4 convolution_convert_fusion.6
  599.4 5.1 multiply_reduce_fusion
  612.5 2.5 multiply_reduce_fusion.8
  615.1 3.2 multiply_convert_fusion.5
  624.6 3.3 reduce.5
  627.9 8.7 convolution_convert_fusion.2
  636.6 10.5 fusion
  648.5 2.5 copy.88
  652.7 9.3 multiply_reduce_fusion.14
  662.2 2.5 multiply_reduce_fusion.4
  665.4 7.8 convolution_convert_fusion
  673.2 4.9 reshape.425
  678.1 13.6 reshape.428
  692.4 3.5 all-to-all-start.2
  695.9 15.9 reshape.424
  711.8 13.9 copy.106
  725.7 30.9 %reshape.427 = bf16[7962624]{0:T(1024)(128)(2,1)} reshape(bf16[1152,6912]{1,0:T(8,128)(2,1)} %convolution_convert_fusion) | data formatting | bytes 31850496 | tf_op jit(solution)/shard_map/reshape | solution.py:228
  756.7 7.2 constant_dynamic-update-slice_fusion.9
  765.5 2.4 copy-done.4
  767.9 7.1 constant_dynamic-update-slice_fusion.12
  777.5 6.8 constant_dynamic-update-slice_fusion.11
  784.3 3.4 constant_dynamic-update-slice_fusion.10
  787.7 11.6 all-to-all-start
  799.9 513.6 %all-to-all-done = bf16[4,8,5832,128]{3,2,1,0:T(8,128)(2,1)} async-done(((bf16[4,8,5832,128]{3,2,1,0:T(8,128)(2,1)}), bf16[4,8,5832,128]{3,2,1,0:T(8,128)(2,1)}, u32[]{:S(2)}, u32[]{:S(2)}) %all-to-all-start) | async-done | bytes 47775776 | tf_op jit(solution)/shard_map/all_to_all | solution.py:237
  1313.6 6.3 all-to-all-start.3
  1319.9 31.9 %copy.93 = bf16[4,8,5832,128]{3,2,0,1:T(8,128)(2,1)} copy(bf16[4,8,5832,128]{3,2,1,0:T(8,128)(2,1)} %all-to-all-done) | data formatting | bytes 95551488 | tf_op jit(solution)/shard_map/all_to_all | solution.py:237
  1351.9 8.3 all-to-all-start.1
  1360.2 10.4 fusion.24
  1371.2 1013.4 %all-to-all-done.1 = bf16[4,8,5832,128]{3,2,0,1:T(8,128)(2,1)} async-done(((bf16[4,8,5832,128]{3,2,0,1:T(8,128)(2,1)}), bf16[4,8,5832,128]{3,2,0,1:T(8,128)(2,1)}, u32[]{:S(2)}, u32[]{:S(2)}) %all-to-all-start.1) | async-done | bytes 47775776 | tf_op jit(solution)/shard_map/all_to_all | solution.py:236
  2384.6 17.1 convert_reduce_fusion
  (250 shorter events, 57.9 us)
Async XLA Ops:
  7.2 4.7 copy-start.3
  7.2 5.7 copy-start.71
  7.2 267.8 %all-gather.2.cloned.1.call-start = ((), (), s32[]{:S(2)}) async-start(), calls=%async_computation.4 | async-start | bytes 49268736 | tf_op jit(solution)/shard_map/all_gather | solution.py:87
  359.9 29.2 %copy-start.55 = (bf16[2,1152]{1,0:T(2,128)(2,1)S(1)}, bf16[2,1152]{1,0:T(2,128)(2,1)}, u32[]{:S(2)}) copy-start(bf16[2,1152]{1,0:T(2,128)(2,1)} %param.7) | copy-start | bytes 13828
  389.1 9.2 copy-start.22
  397.6 5.6 copy-start.53
  398.3 4.9 copy-start.40
  479.7 2.4 copy-start.1
  487.7 3.3 copy-start
  487.7 3.3 copy-start.12
  489.3 3.3 copy-start.47
  494.1 3.7 copy-start.24
  502.4 3.1 copy-start.62
  505.5 15.8 copy-start.35
  505.5 15.8 copy-start.37
  505.5 34.1 %slice-start.8 = ((s8[7077888]{0:T(1024)(128)(4,1)}), s8[4194304]{0:T(1024)(128)(4,1)S(1)}, s32[]{:S(2)}) async-start(s8[7077888]{0:T(1024)(128)(4,1)} %bitcast.165), calls=%async_computation.13 | async-start | bytes 8388608
  521.3 18.3 slice-start.9
  534.3 5.3 copy-start.30
  534.3 5.3 copy-start.5
  534.3 5.3 copy-start.23
  534.3 5.3 copy-start.59
  534.3 5.3 copy-start.70
  539.6 8.8 copy-start.65
  567.0 4.5 copy-start.17
  571.5 2.9 copy-start.25
  574.4 3.2 copy-start.38
  574.4 3.2 copy-start.72
  593.9 5.4 copy-start.11
  593.9 5.4 copy-start.13
  593.9 5.4 copy-start.48
  593.9 10.6 slice-start
  599.3 9.7 copy-start.14
  599.4 5.2 slice-start.1
  624.6 3.3 copy-start.41
  627.9 8.7 copy-start.31
  627.9 8.7 copy-start.32
  627.9 8.7 copy-start.36
  636.6 10.5 copy-start.15
  647.1 3.9 copy-start.19
  648.5 4.1 copy-start.39
  648.5 4.1 copy-start.54
  652.7 9.4 copy-start.6
  652.7 9.4 copy-start.21
  652.7 9.4 copy-start.63
  652.7 9.4 copy-start.64
  662.1 2.6 copy-start.68
  662.1 2.6 copy-start.67
  662.2 2.6 copy-start.66
  662.2 3.2 copy-start.56
  678.0 13.6 copy-start.58
  678.0 13.6 copy-start.60
  692.4 95.3 %all-to-all-start.2 = ((bf16[4,8,552]{2,1,0:T(8,128)(2,1)}), bf16[4,8,552]{2,1,0:T(8,128)(2,1)S(1)}, u32[]{:S(2)}, u32[]{:S(2)}) async-start(bf16[4,8,552]{2,1,0:T(8,128)(2,1)} %convert_element_type.155), calls=%async_computation.2 | async-start | bytes 81920 | tf_op jit(solution)/shard_map/all_to_all | solution.py:246
  756.7 11.3 copy-start.4
  763.8 11.2 slice-start.2
  767.9 7.1 slice-start.3
  767.9 8.6 slice-start.4
  767.9 9.6 slice-start.5
  767.9 16.4 slice-start.6
  777.5 6.8 slice-start.7
  787.7 525.9 %all-to-all-start = ((bf16[4,8,5832,128]{3,2,1,0:T(8,128)(2,1)}), bf16[4,8,5832,128]{3,2,1,0:T(8,128)(2,1)}, u32[]{:S(2)}, u32[]{:S(2)}) async-start(bf16[4,8,5832,128]{3,2,1,0:T(8,128)(2,1)} %bitcast.151), calls=%async_computation | async-start | bytes 95551488 | tf_op jit(solution)/shard_map/all_to_all | solution.py:237
  1313.6 38.3 %all-to-all-start.3 = ((bf16[4,8,552]{2,0,1:T(4,128)(2,1)}), bf16[4,8,552]{2,0,1:T(4,128)(2,1)S(1)}, u32[]{:S(2)}, u32[]{:S(2)}) async-start(bf16[4,8,552]{2,0,1:T(4,128)(2,1)} %copy.94), calls=%async_computation.3 | async-start | bytes 81920 | tf_op jit(solution)/shard_map/all_to_all | solution.py:245
  1351.9 8.3 copy-start.52
  1351.9 8.3 copy-start.57
  1351.9 1032.7 %all-to-all-start.1 = ((bf16[4,8,5832,128]{3,2,0,1:T(8,128)(2,1)}), bf16[4,8,5832,128]{3,2,0,1:T(8,128)(2,1)}, u32[]{:S(2)}, u32[]{:S(2)}) async-start(bf16[4,8,5832,128]{3,2,0,1:T(8,128)(2,1)} %copy.93), calls=%async_computation.1 | async-start | bytes 95551488 | tf_op jit(solution)/shard_map/all_to_all | solution.py:236
  (24 other events, 34.9 us)
Sparse Core Ops, SparseCore 0:
  10.9 264.0 all-gather.1
where the time goes:
time: 2420 us; the launch traced here: 2410 us
  waiting for transfers between devices  1740 us (72%)
  local copies, waits for them, and re-layouts  367 us (15%)
  matrix products  146 us (6%)
  other arithmetic  63.7 us (3%)
  blocking collectives  42.9 us (2%)
  starting transfers between devices  29.8 us (1%)
    all_to_all x1, waiting for transfers between devices, on_device(): lax.all_to_all(lax.all_to_all(grads_big.astype(jnp.bfloat16), 'fsdp', spl...  1010 us
    all_to_all x1, waiting for transfers between devices, on_device(): lax.all_to_all(grads_big.astype(jnp.bfloat16), 'fsdp', split_axis=0, conc...  514 us
    all_gather x1, waiting for transfers between devices, on_device(): lax.all_gather(weight_flat, ('fsdp', 'dp'), axis=0, tiled=True)  217 us
    reshape x8, local copies, waits for them, and re-layouts, unpack_weights(): pieces.append(flat[offset:offset + amount].reshape(layout))  134 us
    unnamed x186, local copies, waits for them, and re-layouts  52.7 us
  transfers between devices with their start and end apart: 5, of which 3 were waited for; matrix products, arithmetic and copies ran while one was open for 6% of the time, Pallas kernels for 0%

commit v1 on v0

--- a/solution.py
+++ b/solution.py
@@ -218,42 +218,22 @@
     g_cond = jnp.einsum("se,de->sd", g_modulation, w_ada, preferred_element_type=f32)
     sigma_cond = jax.nn.sigmoid(cond_f)
     grad_conditions = g_cond * sigma_cond * (1.0 + cond_f * (1.0 - sigma_cond))
-    narrow_count = lax.axis_size("fsdp")
-    wide_count = lax.axis_size("dp")
     grads_big = jnp.concatenate(
         [
-            grad_qkv.reshape(-1),
-            grad_w_out.reshape(-1),
-            grad_mlp.reshape(-1),
-            grad_ada.reshape(-1),
-            grad_down.reshape(-1),
+            grad_qkv.astype(bf16).reshape(-1),
+            grad_w_out.astype(bf16).reshape(-1),
+            grad_mlp.astype(bf16).reshape(-1),
+            grad_ada.astype(bf16).reshape(-1),
+            grad_down.astype(bf16).reshape(-1),
         ]
-    ).reshape(narrow_count, wide_count, -1, 128)
-    grads_small = jnp.concatenate([grad_b_qkv, grad_b_out, grad_b_mlp, grad_b_ada]).reshape(
-        narrow_count, wide_count, -1
-    )
-    spread_big, spread_small = (
-        lax.all_to_all(
-            lax.all_to_all(
-                grads_big.astype(jnp.bfloat16), "fsdp", split_axis=0, concat_axis=0, tiled=True
-            ),
-            "dp",
-            split_axis=1,
-            concat_axis=1,
-            tiled=True,
-        ).astype(grads_big.dtype),
-        lax.all_to_all(
-            lax.all_to_all(
-                grads_small.astype(jnp.bfloat16), "fsdp", split_axis=0, concat_axis=0, tiled=True
-            ),
-            "dp",
-            split_axis=1,
-            concat_axis=1,
-            tiled=True,
-        ).astype(grads_small.dtype),
-    )
-    part_weights = jnp.sum(spread_big, axis=(0, 1))
-    part_biases = jnp.sum(spread_small, axis=(0, 1))
+    ).reshape(-1, 128)
+    grads_small = jnp.concatenate([grad_b_qkv, grad_b_out, grad_b_mlp, grad_b_ada])
+    part_weights = lax.psum_scatter(
+        grads_big, ("fsdp", "dp"), scatter_dimension=0, tiled=True
+    ).astype(f32)
+    part_biases = lax.psum_scatter(
+        grads_small, ("fsdp", "dp"), scatter_dimension=0, tiled=True
+    )
     return (out, grad_tokens.reshape(rows_all, D), grad_conditions, part_weights, part_biases)
 
 

time: 2420 us -> 1240 us (0.51)
  waiting for transfers between devices: 1740 us -> 645 us
  local copies, waits for them, and re-layouts: 367 us -> 333 us
  starting transfers between devices: 29.8 us -> 0.12 us
    all_to_all x4 -> x0, waiting for transfers between devices: 1530 us -> none  [the longest x1 1010 us: on_device(): lax.all_to_all(lax.all_to_all(grads_big.astype(jnp.bfloat16), 'fsdp', spl...]
    unnamed x1 -> x5, waiting for transfers between devices: 0.68 us -> 428 us
    all_to_all x2 -> x0, local copies, waits for them, and re-layouts: 32.6 us -> none  [the longest x1 31.9 us: on_device(): lax.all_to_all(grads_big.astype(jnp.bfloat16), 'fsdp', split_axis=0, conc...]
    all_to_all x4 -> x0, starting transfers between devices: 29.8 us -> none  [the longest x1 11.6 us: on_device(): lax.all_to_all(grads_big.astype(jnp.bfloat16), 'fsdp', split_axis=0, conc...]
    unnamed x186 -> x189, local copies, waits for them, and re-layouts: 52.7 us -> 52.8 us
  transfers between devices with their start and end apart: 5 -> 3, of which waited for: 3 -> 3; matrix products, arithmetic and copies ran while one was open for 6% -> 9% of each run, Pallas kernels for 0% -> 0%
where the time goes in v1:
time: 1240 us; the launch traced here: 1230 us
  waiting for transfers between devices  645 us (52%)
  local copies, waits for them, and re-layouts  333 us (27%)
  matrix products  144 us (12%)
  other arithmetic  48.1 us (4%)
  blocking collectives  42.9 us (3%)
  between operations  15.4 us (1%)
    unnamed x5, waiting for transfers between devices  428 us
    all_gather x1, waiting for transfers between devices, on_device(): lax.all_gather(weight_flat, ('fsdp', 'dp'), axis=0, tiled=True)  217 us
    reshape x8, local copies, waits for them, and re-layouts, unpack_weights(): pieces.append(flat[offset:offset + amount].reshape(layout))  135 us
    unnamed x189, local copies, waits for them, and re-layouts  52.8 us
    unnamed x1, blocking collectives  42.9 us
    slice x5, local copies, waits for them, and re-layouts, unpack_weights(): pieces.append(flat[offset:offset + amount].reshape(layout))  42.2 us
    reshape x1, local copies, waits for them, and re-layouts, on_device(): grad_ada.astype(bf16).reshape(-1)  31 us
  transfers between devices with their start and end apart: 3, of which 3 were waited for; matrix products, arithmetic and copies ran while one was open for 9% of the time, Pallas kernels for 0%

profile of v1, /device:TPU:9, one launch (start us, length us, event | category | flops | bytes accessed | tf_op | source)
XLA Modules:
  0.0 1228.7 jit_solution(11173113660705888044)
XLA Ops:
  13.2 42.9 %all-reduce = bf16[17664]{0:T(1024)(128)(2,1)S(1)} all-reduce(bf16[17664]{0:T(1024)(128)(2,1)S(1)} %dynamic-update-slice), channel_id=1, replica_groups=mesh['fsdp'=4,'dp'=8] {'fsdp','dp'}, use_global_device_ids=true, to_apply=%add | all-reduce | flops 17664 | bytes 70656
  58.4 216.6 %all-gather.2.cloned.1.call-done = bf16[186624,128]{1,0:T(8,128)(2,1)} async-done(((bf16[5832,128]{1,0:T(8,128)(2,1)}), bf16[186624,128]{1,0:T(8,128)(2,1)}) %all-gather.2.cloned.1.call-update) | async-done | bytes 47775760 | tf_op jit(solution)/shard_map/all_gather | solution.py:87
  275.0 6.4 slice.182
  281.4 14.0 %reshape.426 = bf16[3072,1152,1]{1,0,2:T(8,128)(2,1)} reshape(bf16[27648,128]{1,0:T(8,128)(2,1)} %slice.182) | data formatting | bytes 14155776 | tf_op jit(solution)/shard_map/reshape | solution.py:25
  295.4 14.0 %reshape.409 = bf16[3072,1152]{1,0:T(8,128)(2,1)} reshape(bf16[27648,128]{1,0:T(8,128)(2,1)} %slice.182) | data formatting | bytes 14155776 | tf_op jit(solution)/shard_map/reshape | solution.py:25
  309.3 6.8 slice.160
  316.1 15.2 %reshape.428 = bf16[1152,3456,1]{1,0,2:T(8,128)(2,1)} reshape(bf16[31104,128]{1,0:T(8,128)(2,1)} %slice.160) | data formatting | bytes 15925248 | tf_op jit(solution)/shard_map/reshape | solution.py:25
  331.3 15.2 %reshape.401 = bf16[1152,3456]{1,0:T(8,128)(2,1)} reshape(bf16[31104,128]{1,0:T(8,128)(2,1)} %slice.160) | data formatting | bytes 15925248 | tf_op jit(solution)/shard_map/reshape | solution.py:25
  346.5 13.3 %slice.155 = bf16[62208,128]{1,0:T(8,128)(2,1)} slice(bf16[186624,128]{1,0:T(8,128)(2,1)} %all-gather.2.cloned.1.call-done), slice={[96768:158976], [0:128]} | slice | bytes 31850496 | tf_op jit(solution)/shard_map/slice | solution.py:25
  359.9 29.5 %reshape.400 = bf16[1152,6912]{1,0:T(8,128)(2,1)} reshape(bf16[62208,128]{1,0:T(8,128)(2,1)} %slice.155) | data formatting | bytes 31850496 | tf_op jit(solution)/shard_map/reshape | solution.py:25
  389.4 7.8 convolution_add_fusion.1
  398.6 4.9 convolution_add_fusion.2
  404.6 2.5 fusion.48
  407.2 12.8 %slice.178 = bf16[55296,128]{1,0:T(8,128)(2,1)} slice(bf16[186624,128]{1,0:T(8,128)(2,1)} %all-gather.2.cloned.1.call-done), slice={[41472:96768], [0:128]} | slice | bytes 28311552 | tf_op jit(solution)/shard_map/slice | solution.py:25
  419.9 20.3 %reshape.427 = bf16[1152,6144,1]{1,0,2:T(8,128)(2,1)} reshape(bf16[55296,128]{1,0:T(8,128)(2,1)} %slice.178) | data formatting | bytes 28311552 | tf_op jit(solution)/shard_map/reshape | solution.py:25
  440.2 20.3 %reshape.408 = bf16[1152,6144]{1,0:T(8,128)(2,1)} reshape(bf16[55296,128]{1,0:T(8,128)(2,1)} %slice.178) | data formatting | bytes 28311552 | tf_op jit(solution)/shard_map/reshape | solution.py:25
  460.6 2.9 slice.173
  463.5 6.2 reshape.406
  469.7 2.0 copy.59
  471.8 2.4 copy.57
  475.2 1.7 slice_negate_fusion.5
  477.0 3.0 copy.58
  480.0 2.0 multiply_reduce_fusion.12
  484.5 2.0 fusion.16
  494.5 3.5 fusion.25
  498.6 2.2 multiply_reduce_fusion.10
  502.7 3.0 fusion.19
  505.7 15.5 %convolution_add_fusion = f32[512,6144]{1,0:T(8,128)} fusion(bf16[512,1152]{1,0:T(8,128)(2,1)S(1)} %get-tuple-element.72, bf16[1152,6144]{1,0:T(8,128)(2,1)} %reshape.408, f32[6144]{0:T(1024)S(1)} %copy-done.63), kind=kOutput, calls=%fused_computation.5 | convolution fusion | flops 7250903040 | bytes 27942912 | tf_op jit(solution)/shard_map/dot_general | solution.py:137
  521.2 13.0 %multiply_convert_fusion.2 = (bf16[512,3072]{1,0:T(8,128)(2,1)S(1)}, bf16[512,3072]{1,0:T(8,128)(2,1)}, bf16[512,3072]{1,0:T(8,128)(2,1)}) fusion(f32[512,6144]{1,0:T(8,128)} %convolution_add_fusion, bf16[512,1152]{1,0:T(8,128)(2,1)S(1)} %get-tuple-element.71, bf16[3072,1152]{1,0:T(8,128)(2,1)} %reshape.409), kind=kOutput, calls=%fused_computation.21 | convolution fusion | flops 3647471616 | bytes 30277632 | tf_op jit(solution)/shard_map/rd,fd->rf/dot_general | solution.py:166
  534.3 5.2 convert_reduce_fusion
  539.6 8.8 multiply_convert_fusion.7
  548.4 17.4 %multiply_reduce_fusion.3 = (bf16[2,1152]{1,0:T(2,128)(2,1)}, f32[2,256]{1,0:T(2,128)}, f32[2,256]{1,0:T(2,128)}, bf16[2,1152]{1,0:T(2,128)(2,1)}, f32[2,256,1152]{2,1,0:T(8,128)}) fusion(f32[2,256,1152]{2,1,0:T(8,128)} %get-tuple-element.19, f32[2,256]{1,0:T(2,128)S(1)} %copy-done.66, f32[2,256]{1,0:T(2,128)} %rsqrt.44, f32[2,1152]{1,0:T(2,128)} %get-tuple-element.50, ...), kind=kOutput, calls=%fused_computation.62 | convolution fusion | flops 7265643520 | bytes 25192448 | tf_op jit(solution)/shard_map/rf,df->rd/dot_general | solution.py:177
  567.2 5.1 convert_reduce_fusion.2
  572.3 2.9 convolution_convert_fusion.5
  575.2 3.2 convolution_convert_fusion.4
  578.4 6.3 convolution_convert_fusion.3
  584.7 5.7 reshape.432
  590.4 4.3 copy.63
  594.7 5.4 convolution_convert_fusion.6
  600.1 5.1 multiply_reduce_fusion
  605.3 2.2 multiply_convert_fusion
  613.3 2.5 multiply_reduce_fusion.8
  615.9 3.0 multiply_convert_fusion.5
  623.4 6.7 convolution_convert_fusion.2
  630.1 10.6 fusion
  642.2 2.5 copy.69
  646.4 9.4 multiply_reduce_fusion.14
  655.9 2.5 multiply_reduce_fusion.4
  659.1 7.8 convolution_convert_fusion
  666.9 4.9 reshape.419
  671.8 13.6 %reshape.422 = bf16[3538944]{0:T(1024)(128)(2,1)} reshape(bf16[3072,1152]{1,0:T(8,128)(2,1)} %convolution_convert_fusion.3) | data formatting | bytes 14155776 | tf_op jit(solution)/shard_map/reshape | solution.py:227
  686.1 16.2 %reshape.418 = bf16[3981312]{0:T(1024)(128)(2,1)} reshape(bf16[1152,3456]{1,0:T(8,128)(2,1)} %convolution_convert_fusion.2) | data formatting | bytes 15925248 | tf_op jit(solution)/shard_map/reshape | solution.py:223
  702.3 14.0 %copy.85 = bf16[144,48,8,128]{3,1,2,0:T(8,128)(2,1)} copy(bf16[144,48,8,128]{3,2,1,0:T(8,128)(2,1)} %fusion) | data formatting | bytes 28311552
  716.3 31.0 %reshape.421 = bf16[7962624]{0:T(1024)(128)(2,1)} reshape(bf16[1152,6912]{1,0:T(8,128)(2,1)} %convolution_convert_fusion) | data formatting | bytes 31850496 | tf_op jit(solution)/shard_map/reshape | solution.py:226
  747.2 7.2 constant_dynamic-update-slice_fusion.9
  754.4 1.7 constant_dynamic-update-slice_fusion.13
  756.1 2.4 copy-done.4
  758.5 7.1 constant_dynamic-update-slice_fusion.12
  768.1 6.8 constant_dynamic-update-slice_fusion.11
  774.9 3.4 constant_dynamic-update-slice_fusion.10
  779.1 10.4 fusion.23
  789.4 14.2 %all-reduce.5.cloned.1.call-done = f32[17664]{0:T(1024)} async-done(((f32[17664]{0:T(1024)}), f32[17664]{0:T(1024)}) %all-reduce.5.cloned.1.call-update) | async-done | bytes 70672
  805.0 413.5 %reduce-scatter.4.cloned.1.call-done = bf16[5832,128]{1,0:T(8,128)(2,1)} async-done(((bf16[186624,128]{1,0:T(8,128)(2,1)}), bf16[5832,128]{1,0:T(8,128)(2,1)}) %reduce-scatter.4.cloned.1.call-update) | async-done | bytes 1493008
  1218.5 3.2 convert_element_type.158
  (247 shorter events, 45.2 us)
Async XLA Ops:
  7.2 4.7 copy-start.3
  7.2 5.7 copy-start.72
  7.2 267.8 %all-gather.2.cloned.1.call-start = ((), (), s32[]{:S(2)}) async-start(), calls=%async_computation.1 | async-start | bytes 49268736 | tf_op jit(solution)/shard_map/all_gather | solution.py:87
  7.9 795.7 %all-reduce.5.cloned.1.call-start = ((), (), s32[]{:S(2)}) async-start(), calls=%async_computation.2 | async-start | bytes 147456
  359.9 29.5 %copy-start.57 = (bf16[2,1152]{1,0:T(2,128)(2,1)S(1)}, bf16[2,1152]{1,0:T(2,128)(2,1)}, u32[]{:S(2)}) copy-start(bf16[2,1152]{1,0:T(2,128)(2,1)} %param.7) | copy-start | bytes 13828
  389.4 9.2 copy-start.22
  397.9 5.6 copy-start.54
  398.6 4.9 copy-start.40
  480.0 2.4 copy-start.1
  482.6 1.8 copy-start.29
  482.6 1.8 copy-start.33
  482.7 1.8 copy-start.50
  487.9 3.2 copy-start
  487.9 3.2 copy-start.12
  489.5 3.2 copy-start.47
  494.3 3.7 copy-start.24
  502.7 3.1 copy-start.63
  505.7 15.5 %copy-start.35 = (bf16[512,1152]{1,0:T(8,128)(2,1)}, bf16[512,1152]{1,0:T(8,128)(2,1)S(1)}, u32[]{:S(2)}) copy-start(bf16[512,1152]{1,0:T(8,128)(2,1)S(1)} %get-tuple-element.72) | copy-start | bytes 3538948
  505.7 15.5 %copy-start.37 = (bf16[512,1152]{1,0:T(8,128)(2,1)}, bf16[512,1152]{1,0:T(8,128)(2,1)S(1)}, u32[]{:S(2)}) copy-start(bf16[512,1152]{1,0:T(8,128)(2,1)S(1)} %get-tuple-element.71) | copy-start | bytes 3538948
  505.7 33.8 %slice-start.8 = ((s8[7077888]{0:T(1024)(128)(4,1)}), s8[4194304]{0:T(1024)(128)(4,1)S(1)}, s32[]{:S(2)}) async-start(s8[7077888]{0:T(1024)(128)(4,1)} %bitcast.165), calls=%async_computation.12 | async-start | bytes 8388608
  521.2 18.3 %slice-start.9 = ((s8[7077888]{0:T(1024)(128)(4,1)}), s8[2883584]{0:T(1024)(128)(4,1)S(1)}, s32[]{:S(2)}) async-start(s8[7077888]{0:T(1024)(128)(4,1)} %bitcast.165), calls=%async_computation.13 | async-start | bytes 5767168
  534.3 5.3 copy-start.30
  534.3 5.3 copy-start.5
  534.3 5.3 copy-start.23
  534.3 5.3 copy-start.60
  534.3 5.3 copy-start.71
  539.6 8.8 copy-start.66
  567.2 5.1 copy-start.17
  572.3 2.9 copy-start.25
  575.2 3.2 copy-start.38
  575.2 3.2 copy-start.73
  594.7 5.4 copy-start.11
  594.7 5.4 copy-start.13
  594.7 5.4 copy-start.48
  594.7 10.6 slice-start
  600.1 9.7 copy-start.14
  600.1 5.2 slice-start.1
  605.3 2.2 copy-start.10
  623.4 6.7 copy-start.31
  623.4 6.7 copy-start.32
  623.4 6.7 copy-start.36
  630.1 10.6 copy-start.15
  640.8 3.9 copy-start.19
  642.2 4.1 copy-start.39
  642.2 4.1 copy-start.55
  642.2 4.2 copy-start.64
  646.3 9.5 copy-start.6
  646.3 9.5 copy-start.21
  646.3 9.5 copy-start.65
  655.8 2.6 copy-start.69
  655.8 2.6 copy-start.68
  655.8 2.6 copy-start.67
  655.8 3.2 copy-start.58
  671.7 13.6 %copy-start.53 = (f32[6144]{0:T(1024)S(1)}, f32[6144]{0:T(1024)}, u32[]{:S(2)}) copy-start(f32[6144]{0:T(1024)} %convert_reduce_fusion) | copy-start | bytes 73732
  671.7 13.6 %copy-start.56 = (f32[3456]{0:T(1024)S(1)}, f32[3456]{0:T(1024)}, u32[]{:S(2)}) copy-start(f32[3456]{0:T(1024)} %convert_reduce_fusion.1) | copy-start | bytes 41476
  671.8 13.6 %copy-start.62 = (f32[1152]{0:T(1024)S(1)}, f32[1152]{0:T(1024)}, u32[]{:S(2)}) copy-start(f32[1152]{0:T(1024)} %get-tuple-element.15) | copy-start | bytes 13828
  686.0 532.4 %reduce-scatter.4.cloned.1.call-start = ((), (), s32[]{:S(2)}) async-start(), calls=%async_computation.3 | async-start | bytes 49268736
  747.2 11.3 copy-start.4
  754.4 11.2 slice-start.2
  758.5 7.1 slice-start.3
  758.5 8.6 slice-start.4
  758.5 9.6 slice-start.5
  758.5 16.4 %slice-start.6 = ((s8[7077888]{0:T(1024)(128)(4,1)}), s8[2883584]{0:T(1024)(128)(4,1)S(1)}, s32[]{:S(2)}) async-start(s8[7077888]{0:T(1024)(128)(4,1)} %bitcast.157), calls=%async_computation.10 | async-start | bytes 5767168
  768.1 6.8 slice-start.7
  (23 other events, 30.0 us)
Sparse Core Ops, SparseCore 0:
  10.9 264.0 all-gather.1
  686.1 117.4 all-reduce.4
  810.1 408.3 reduce-scatter.3

commit v2 on v1

v2 whole, which is shorter than its diff:
```python
import math

import jax
import jax.numpy as jnp
from jax import lax
from jax.experimental import pallas as pl
from jax.experimental.pallas import tpu as pltpu
import numpy as np
from jax.sharding import PartitionSpec as P

D = 1152
HEADS = 16
HEAD_DIM = 72
FF = 3072
GRID = 16


eps_norm = 1e-06


def unpack_weights(weight_all, bias_all):
    flat = weight_all.reshape(-1)
    layouts = ((D, 3 * D), (D, D), (D, 2 * FF), (D, 6 * D), (FF, D))
    pieces = []
    offset = 0
    for layout in layouts:
        amount = layout[0] * layout[1]
        pieces.append(flat[offset : offset + amount].reshape(layout))
        offset = offset + amount
    offset = 0
    for amount in (3 * D, D, 2 * FF, 6 * D):
        pieces.append(bias_all[offset : offset + amount])
        offset = offset + amount
    return tuple(pieces)


def rope_tables():
    quarter = HEAD_DIM // 4
    places = jnp.arange(GRID * GRID, dtype=jnp.int32)
    rows_at = (places // GRID).astype(jnp.float32)
    cols_at = (places % GRID).astype(jnp.float32)
    freqs = 10000.0 ** (-jnp.arange(quarter, dtype=jnp.float32) / quarter)
    along_rows = rows_at[:, None] * freqs[None, :]
    along_cols = cols_at[:, None] * freqs[None, :]
    angles = jnp.concatenate([along_rows, along_rows, along_cols, along_cols], axis=1)
    return (jnp.cos(angles)[:, None, :], jnp.sin(angles)[:, None, :])


def turn_half(values):
    quarter = values.shape[-1] // 4
    first = values[..., :quarter]
    second = values[..., quarter : 2 * quarter]
    third = values[..., 2 * quarter : 3 * quarter]
    fourth = values[..., 3 * quarter :]
    return jnp.concatenate([-second, first, -fourth, third], axis=-1)


def norm_parts(values):
    centred = values - jnp.mean(values, -1, keepdims=True)
    inverse = lax.rsqrt(jnp.mean(centred * centred, -1, keepdims=True) + eps_norm)
    return (centred * inverse, inverse)


def norm_back(grad_normed, normed, inverse):
    return inverse * (
        grad_normed
        - jnp.mean(grad_normed, -1, keepdims=True)
        - normed * jnp.mean(grad_normed * normed, -1, keepdims=True)
    )


def rms_parts(values):
    inverse = lax.rsqrt(jnp.mean(values * values, -1, keepdims=True) + eps_norm)
    return (values * inverse, inverse)


def rms_back(grad_normed, normed, inverse):
    return inverse * (grad_normed - normed * jnp.mean(grad_normed * normed, -1, keepdims=True))


def compute_block(tokens, cotangent, slot_mask, modulation, weights, biases):
    f32 = jnp.float32
    bf16 = jnp.bfloat16
    w_qkv, w_out, w_mlp, w_down = weights
    b_qkv, b_out, b_mlp = biases
    slots = slot_mask.shape[0]
    length = GRID * GRID
    rows_all = slots * length
    scale = 1.0 / math.sqrt(HEAD_DIM)
    heads_shape = (slots, length, HEADS, HEAD_DIM)
    cosines, sines = rope_tables()
    mask_f = slot_mask.astype(f32)[:, None, None]
    x_f = tokens.astype(f32).reshape(slots, length, D)
    shift_a, scale_a, gate_a, shift_b, scale_b, gate_b = [
        modulation[:, None, place * D : (place + 1) * D] for place in range(6)
    ]
    normed_a, inv_a = norm_parts(x_f)
    attention_input = (normed_a * (1.0 + scale_a) + shift_a).astype(bf16).reshape(rows_all, D)
    projected_output = (
        jnp.dot(attention_input, w_qkv, preferred_element_type=f32) + b_qkv.astype(f32)
    ).reshape(slots, length, 3 * D)
    q_norm, inv_q = rms_parts(projected_output[..., :D].reshape(heads_shape))
    k_norm, inv_k = rms_parts(projected_output[..., D : 2 * D].reshape(heads_shape))
    queries = (q_norm * cosines + turn_half(q_norm) * sines).astype(bf16)
    keys = (k_norm * cosines + turn_half(k_norm) * sines).astype(bf16)
    values = projected_output[..., 2 * D :].reshape(heads_shape).astype(bf16)
    scores = jnp.einsum("slhe,smhe->shlm", queries, keys, preferred_element_type=f32) * scale
    row_max = jnp.max(scores, -1, keepdims=True)
    log_total = row_max + jnp.log(jnp.sum(jnp.exp(scores - row_max), -1, keepdims=True))
    probs_low = jnp.exp(scores - log_total).astype(bf16)
    attention_output = (
        jnp.einsum("shlm,smhe->slhe", probs_low, values, preferred_element_type=f32)
        .astype(bf16)
        .reshape(rows_all, D)
    )
    attention_branch = (
        jnp.dot(attention_output, w_out, preferred_element_type=f32) + b_out.astype(f32)
    ).reshape(slots, length, D)
    middle = x_f + gate_a * attention_branch
    normed_b, inv_b = norm_parts(middle)
    feedforward_input = (normed_b * (1.0 + scale_b) + shift_b).astype(bf16).reshape(rows_all, D)
    mixed_tokens = jnp.dot(feedforward_input, w_mlp, preferred_element_type=f32) + b_mlp.astype(
        f32
    )
    gate_part = mixed_tokens[:, :FF]
    up_part = mixed_tokens[:, FF:]
    hidden_state = (jax.nn.silu(gate_part) * up_part).astype(bf16)
    feedforward_branch = jnp.dot(hidden_state, w_down, preferred_element_type=f32).reshape(
        slots, length, D
    )
    out = ((middle + gate_b * feedforward_branch) * mask_f).astype(bf16).reshape(rows_all, D)
    g_out = cotangent.astype(f32).reshape(slots, length, D) * mask_f
    g_branch_b = (gate_b * g_out).astype(bf16).reshape(rows_all, D)
    g_gate_b = jnp.sum(g_out * feedforward_branch, axis=1)
    g_hidden = jnp.einsum("rd,fd->rf", g_branch_b, w_down, preferred_element_type=f32)
    sigma_gate = jax.nn.sigmoid(gate_part)
    g_mixed = jnp.concatenate(
        [
            g_hidden * up_part * sigma_gate * (1.0 + gate_part * (1.0 - sigma_gate)),
            g_hidden * (gate_part * sigma_gate),
        ],
        axis=1,
    ).astype(bf16)
    grad_b_mlp = jnp.sum(g_mixed.astype(f32), axis=0)
    g_input_b = jnp.einsum("rf,df->rd", g_mixed, w_mlp, preferred_element_type=f32).reshape(
        slots, length, D
    )
    g_shift_b = jnp.sum(g_input_b, axis=1)
    g_scale_b = jnp.sum(g_input_b * normed_b, axis=1)
    g_middle = g_out + norm_back(g_input_b * (1.0 + scale_b), normed_b, inv_b)
    g_branch_a = (gate_a * g_middle).astype(bf16).reshape(rows_all, D)
    g_gate_a = jnp.sum(g_middle * attention_branch, axis=1)
    grad_b_out = jnp.sum(g_branch_a.astype(f32), axis=0)
    g_attended = (
        jnp.einsum("re,de->rd", g_branch_a, w_out, preferred_element_type=f32)
        .astype(bf16)
        .reshape(heads_shape)
    )
    scores = jnp.einsum("slhe,smhe->shlm", queries, keys, preferred_element_type=f32) * scale
    probs = jnp.exp(scores - log_total)
    probs_low = probs.astype(bf16)
    g_probs = jnp.einsum("slhe,smhe->shlm", g_attended, values, preferred_element_type=f32)
    g_values = jnp.einsum("shlm,slhe->smhe", probs_low, g_attended, preferred_element_type=f32)
    g_scores = (probs * (g_probs - jnp.sum(probs * g_probs, -1, keepdims=True))).astype(bf16)
    g_queries = jnp.einsum("shlm,smhe->slhe", g_scores, keys, preferred_element_type=f32) * scale
    g_keys = jnp.einsum("shlm,slhe->smhe", g_scores, queries, preferred_element_type=f32) * scale
    g_q = rms_back(g_queries * cosines - turn_half(g_queries) * sines, q_norm, inv_q)
    g_k = rms_back(g_keys * cosines - turn_half(g_keys) * sines, k_norm, inv_k)
    g_projected = jnp.concatenate(
        [g_q.reshape(rows_all, D), g_k.reshape(rows_all, D), g_values.reshape(rows_all, D)], axis=1
    ).astype(bf16)
    grad_b_qkv = jnp.sum(g_projected.astype(f32), axis=0)
    g_input_a = jnp.einsum("re,de->rd", g_projected, w_qkv, preferred_element_type=f32).reshape(
        slots, length, D
    )
    g_shift_a = jnp.sum(g_input_a, axis=1)
    g_scale_a = jnp.sum(g_input_a * normed_a, axis=1)
    grad_tokens = g_middle + norm_back(g_input_a * (1.0 + scale_a), normed_a, inv_a)
    g_modulation = jnp.concatenate(
        [g_shift_a, g_scale_a, g_gate_a, g_shift_b, g_scale_b, g_gate_b], axis=1
    ).astype(bf16)
    pairs = (
        (attention_input, g_projected),
        (attention_output, g_branch_a),
        (feedforward_input, g_mixed),
        (hidden_state, g_branch_b),
    )
    return (
        out,
        grad_tokens.reshape(rows_all, D),
        g_modulation,
        (grad_b_qkv, grad_b_out, grad_b_mlp),
        pairs,
    )


def weight_grad(pair):
    return jnp.einsum("rd,re->de", pair[0], pair[1], preferred_element_type=jnp.float32)


def on_device_plain(tokens, conditions, cotangent, slot_mask, weight_flat, bias_flat):
    f32 = jnp.float32
    bf16 = jnp.bfloat16
    axes = ("fsdp", "dp")
    weight_all = lax.all_gather(weight_flat, axes, axis=0, tiled=True)
    bias_all = lax.all_gather(bias_flat, axes, axis=0, tiled=True)
    w_qkv, w_out, w_mlp, w_ada, w_down, b_qkv, b_out, b_mlp, b_ada = unpack_weights(
        weight_all, bias_all
    )
    cond_f = conditions.astype(f32)
    cond_act = jax.nn.silu(cond_f).astype(bf16)
    modulation = jnp.dot(cond_act, w_ada, preferred_element_type=f32) + b_ada.astype(f32)
    out, grad_tokens, g_modulation, bias_sums, pairs = compute_block(
        tokens,
        cotangent,
        slot_mask,
        modulation,
        (w_qkv, w_out, w_mlp, w_down),
        (b_qkv, b_out, b_mlp),
    )
    grad_b_ada = jnp.sum(g_modulation.astype(f32), axis=0)
    g_cond = jnp.einsum("se,de->sd", g_modulation, w_ada, preferred_element_type=f32)
    sigma_cond = jax.nn.sigmoid(cond_f)
    grad_conditions = g_cond * sigma_cond * (1.0 + cond_f * (1.0 - sigma_cond))
    grad_qkv, grad_out, grad_mlp, grad_down = [weight_grad(pair) for pair in pairs]
    grad_ada = weight_grad((cond_act, g_modulation))
    grads_big = jnp.concatenate(
        [
            grad.astype(bf16).reshape(-1)
            for grad in (grad_qkv, grad_out, grad_mlp, grad_ada, grad_down)
        ]
    ).reshape(-1, 128)
    grads_small = jnp.concatenate([*bias_sums, grad_b_ada])
    part_weights = lax.psum_scatter(grads_big, axes, scatter_dimension=0, tiled=True)
    part_biases = lax.psum_scatter(grads_small, axes, scatter_dimension=0, tiled=True)
    return (out, grad_tokens, grad_conditions, part_weights.astype(f32), part_biases)


ROWS_QKV = 3 * D * D // 128
ROWS_OUT = D * D // 128
ROWS_MLP = 2 * D * FF // 128
ROWS_ADA = 6 * D * D // 128
ROWS_DOWN = D * FF // 128
FIRST_MLP = ROWS_QKV + ROWS_OUT
FIRST_ADA = FIRST_MLP + ROWS_MLP
FIRST_DOWN = FIRST_ADA + ROWS_ADA
DEVICES = 32
SHARD = 5832
BLOCK_A = 1296
BLOCK_B = 2688
USED_DOWN = 2592
MLP_BLOCKS = 21
QKV_BLOCKS = 24
ADA_ROWS = SHARD * 128 // (6 * D)


def block_a_range(block):
    return (BLOCK_A * block, BLOCK_A * (block + 1))


def block_b_range(block):
    if block < MLP_BLOCKS:
        first = FIRST_MLP + BLOCK_B * block
        return (first, min(first + BLOCK_B, FIRST_ADA))
    first = FIRST_DOWN + USED_DOWN * (block - MLP_BLOCKS)
    return (first, min(first + USED_DOWN, FIRST_DOWN + ROWS_DOWN))


def colour_edges(edges):
    degree = {}
    for left, right in edges:
        degree["l", left] = degree.get(("l", left), 0) + 1
        degree["r", right] = degree.get(("r", right), 0) + 1
    count = max(degree.values())
    at = {}
    for left, right in edges:
        a, b = ("l", left), ("r", right)
        free_a = next(c for c in range(count) if (a, c) not in at)
        free_b = next(c for c in range(count) if (b, c) not in at)
        if free_a != free_b:
            path, node, colour = [], b, free_a
            while (node, colour) in at:
                other = at[node, colour]
                path.append((node, other, colour))
                node, colour = other, free_a + free_b - colour
            for one, two, old in path:
                del at[one, old], at[two, old]
            for one, two, old in path:
                new = free_a + free_b - old
                at[one, new], at[two, new] = two, one
        at[a, free_a], at[b, free_a] = b, a
    rounds = [[] for _ in range(count)]
    for (node, colour), other in at.items():
        if node[0] == "l":
            rounds[colour].append((node[1], other[1]))
    return [sorted(group) for group in rounds]


def plan_rounds(block_range, device_of_block):
    edges, first_row = [], {}
    for block in range(DEVICES):
        first, last = block_range(block)
        for owner in range(first // SHARD, (last - 1) // SHARD + 1):
            edges.append((owner, device_of_block(block)))
            first_row[owner, device_of_block(block)] = first - owner * SHARD
    rounds = colour_edges(edges)
    return rounds, first_row


def device_index():
    return lax.axis_index("fsdp") * lax.axis_size("dp") + lax.axis_index("dp")


def spread(shard, block_rows, block_range):
    me = device_index()
    rounds, first_row = plan_rounds(block_range, lambda block: block)
    padded = jnp.pad(shard, ((block_rows, block_rows), (0, 0)))
    total = None
    for pairs in rounds:
        starts = np.zeros(DEVICES, np.int32)
        for owner, device in pairs:
            starts[owner] = block_rows + first_row[owner, device]
        piece = lax.dynamic_slice_in_dim(padded, jnp.asarray(starts)[me], block_rows, 0)
        got = lax.ppermute(piece, ("fsdp", "dp"), pairs)
        total = got if total is None else total + got
    return total


def collect(buffer, block, block_rows, block_range, places):
    me = device_index()
    rounds, first_row = plan_rounds(block_range, lambda block: device_of(places, block))
    for pairs in rounds:
        starts = np.zeros(DEVICES, np.int32)
        for owner, device in pairs:
            starts[owner] = BLOCK_B + first_row[owner, device]
        got = lax.ppermute(block, ("fsdp", "dp"), [(device, owner) for owner, device in pairs])
        start = jnp.asarray(starts)[me]
        held = lax.dynamic_slice_in_dim(buffer, start, block_rows, 0)
        buffer = lax.dynamic_update_slice_in_dim(
            buffer, held + got.astype(buffer.dtype), start, 0
        )
    return buffer


def to_tiles(rows, chunks):
    return (
        rows.reshape(-1, 8, chunks, 128).transpose(0, 2, 1, 3).reshape(-1, 128)
    )


def from_tiles(rows, chunks):
    return (
        rows.reshape(-1, chunks, 8, 128).transpose(0, 2, 1, 3).reshape(-1, 128)
    )


def matrix_of_tiles(rows, height, width):
    return (
        rows.reshape(height // 8, width // 128, 8, 128)
        .transpose(0, 2, 1, 3)
        .reshape(height, width)
    )


def tiles_of_matrix(matrix):
    height, width = matrix.shape
    return (
        matrix.reshape(height // 8, 8, width // 128, 128)
        .transpose(0, 2, 1, 3)
        .reshape(-1, 128)
    )


SWAP_X = [(0, 1), (1, 0), (2, 3), (3, 2)]
SWAP_Y = [(0, 2), (2, 0), (1, 3), (3, 1)]
SWAP_CORE = [(d, d ^ 1) for d in range(8)]


def along_z(pairs):
    return [(2 * a + e, 2 * b + e) for a, b in pairs for e in range(2)]


def chips_of(*lines):
    place = {}
    for z, line in enumerate(lines):
        for f, block in enumerate(line):
            place[block] = 4 * f + z
    return place


PLACE_A = (
    chips_of((0, 1, 2, 3), (4, 5, 6, 7), (18, 19, 20, 21), (22, 23, 16, 17)),
    chips_of((8, 9, 10, 11), (12, 13, 14, 15), (24, 25, 26, 27), (28, 29, 30, 31)),
)
PLACE_B = (
    chips_of((2, 3, 4, 5), (6, 7, 8, 9), (10, 11, 12, 13), (14, 0, 15, 1)),
    chips_of((20, 16, 17, 18), (21, 22, 23, 24), (25, 26, 27, 28), (29, 19, 30, 31)),
)


def device_of(places, block):
    core = 0 if block in places[0] else 1
    return 2 * places[core][block] + core


def kind_table(places, first_of_second):
    table = np.zeros(DEVICES, np.int32)
    for block in range(DEVICES):
        table[device_of(places, block)] = int(block >= first_of_second)
    return table


def add_low(a, b):
    return (a.astype(jnp.float32) + b.astype(jnp.float32)).astype(jnp.bfloat16)


def pick(array, index, axis):
    return lax.dynamic_index_in_dim(array, index, axis, keepdims=False)


def first_sends(grads, block_rows):
    f = lax.axis_index("fsdp")
    y, x = f // 2, f % 2
    a, b = [part.reshape(2, 2, 4, block_rows // 2, 128) for part in grads]
    return pick(a, 1 - y, 0), pick(b, 1 - x, 1)


def reduce_planes(grads, sends, block_rows):
    f = lax.axis_index("fsdp")
    y, x = f // 2, f % 2
    a, b = [part.reshape(2, 2, 4, block_rows // 2, 128) for part in grads]
    a = add_low(pick(a, y, 0), lax.ppermute(sends[0], "fsdp", SWAP_Y))
    b = add_low(pick(b, x, 1), lax.ppermute(sends[1], "fsdp", SWAP_X))
    a = add_low(pick(a, x, 0), lax.ppermute(pick(a, 1 - x, 0), "fsdp", SWAP_X))
    b = add_low(pick(b, y, 0), lax.ppermute(pick(b, 1 - y, 0), "fsdp", SWAP_Y))
    return jnp.concatenate([a, b], axis=1)


def reduce_line(planes):
    z = lax.axis_index("dp") // 2
    total = pick(planes, z, 0).astype(jnp.float32)
    for k in range(1, 4):
        swap = [(d, d ^ (2 * k)) for d in range(8)]
        total += lax.ppermute(pick(planes, z ^ k, 0), "dp", swap).astype(jnp.float32)
    return total


def gather_column(array):
    parts = [array] + [
        lax.ppermute(array, "dp", [(d, d ^ k) for d in range(8)]) for k in range(1, 8)
    ]
    return jnp.stack(parts)


def gather_columns(part):
    parts = [part] + [
        lax.ppermute(part, "fsdp", [(f, f ^ k) for f in range(4)]) for k in range(1, 4)
    ]
    return jnp.stack(parts).reshape(DEVICES, *part.shape[1:])


ADA_GROUPS = range(FIRST_ADA // (8 * SHARD), (FIRST_DOWN - 1) // (8 * SHARD) + 1)


def sum_to_owners(terms):
    def send(array, change, groups):
        pairs = [(8 * f + d, (8 * f + d) ^ change) for f in groups for d in range(8)]
        return lax.ppermute(array, ("fsdp", "dp"), pairs)

    terms = terms.reshape(4, 4, 2, *terms.shape[1:])
    terms = terms[:, :, 0] + send(terms[:, :, 1], 1, ADA_GROUPS)
    terms = terms[0] + sum(send(terms[k], 8 * k, ADA_GROUPS) for k in range(1, 4))
    return terms[0] + sum(send(terms[k], 2 * k, range(4)) for k in range(1, 4))


def exchange_relative(pieces):
    pieces = pieces.reshape(4, 8, *pieces.shape[1:])
    parts = [pieces[:, 0]] + [
        lax.ppermute(pieces[:, k], "dp", [(d, d ^ k) for d in range(8)]) for k in range(1, 8)
    ]
    part = jnp.stack(parts, axis=1)
    parts = [part[0]] + [
        lax.ppermute(part[k], "fsdp", [(f, f ^ k) for f in range(4)]) for k in range(1, 4)
    ]
    return jnp.stack(parts).reshape(DEVICES, *pieces.shape[2:])


def mlp_kernel(flat_first, blocks, used_tiles, block_tiles):
    def body(x_ref, g_ref, bias_g_ref, bias_u_ref, gate_w, up_w, flat_ref, *rest):
        hid_ref, gg_ref, gu_ref, branch_ref, gin_ref, sum_g_ref, sum_u_ref, down_ref, sem = rest
        f32, bf16 = jnp.float32, jnp.bfloat16
        step = pl.program_id(0)

        def copies():
            return [
                pltpu.make_async_copy(
                    flat_ref.at[pl.ds(flat_first + block_tiles * i, used_tiles)],
                    down_ref.at[pl.ds(used_tiles * i, used_tiles)],
                    sem.at[i],
                )
                for i in range(blocks)
            ]

        @pl.when(step == 0)
        def _():
            for copy in copies():
                copy.start()

        def columns(ref):
            return jnp.concatenate([ref[:, i].reshape(D, 128) for i in range(2)], axis=1)

        x = x_ref[...]
        w_gate, w_up = columns(gate_w), columns(up_w)
        gate = jnp.dot(x, w_gate, preferred_element_type=f32) + bias_g_ref[...]
        up = jnp.dot(x, w_up, preferred_element_type=f32) + bias_u_ref[...]
        sigma = jax.nn.sigmoid(gate)
        silu = gate * sigma
        hid = (silu * up).astype(bf16)
        hid_ref[...] = hid

        @pl.when(step == 0)
        def _():
            for copy in copies():
                copy.wait()
            branch_ref[...] = jnp.zeros_like(branch_ref)
            gin_ref[...] = jnp.zeros_like(gin_ref)

        chunks = D // 128
        rows = down_ref[pl.ds(step * 32 * chunks, 32 * chunks)].reshape(32, chunks, 8, 128)
        w_down = jnp.concatenate([rows[:, j].reshape(256, 128) for j in range(chunks)], axis=1)
        branch_ref[...] += jnp.dot(hid, w_down, preferred_element_type=f32)
        across = (((1,), (1,)), ((), ()))
        g_hid = lax.dot_general(g_ref[...], w_down, across, preferred_element_type=f32)
        g_gate = (g_hid * up * sigma * (1.0 + gate * (1.0 - sigma))).astype(bf16)
        g_up = (g_hid * silu).astype(bf16)
        gg_ref[...] = g_gate
        gu_ref[...] = g_up
        sum_g_ref[...] = jnp.sum(g_gate.astype(f32), axis=0, keepdims=True)
        sum_u_ref[...] = jnp.sum(g_up.astype(f32), axis=0, keepdims=True)
        gin_ref[...] += lax.dot_general(
            g_gate, w_gate, across, preferred_element_type=f32
        ) + lax.dot_general(g_up, w_up, across, preferred_element_type=f32)

    return body


def mlp_both_ways(x, g, bias, all_b):
    f32, bf16 = jnp.float32, jnp.bfloat16
    rows = x.shape[0]
    blocks = DEVICES - MLP_BLOCKS
    used = USED_DOWN // 8
    steps = FF // 256
    tiles = all_b.reshape(-1, 2 * FF // 128, 8, 128)
    whole = pl.BlockSpec((rows, D), lambda t: (0, 0))
    part = pl.BlockSpec((rows, 256), lambda t: (0, t))
    line = pl.BlockSpec((1, 256), lambda t: (0, t))
    return pl.pallas_call(
        mlp_kernel(MLP_BLOCKS * BLOCK_B // 8, blocks, used, BLOCK_B // 8),
        grid=(steps,),
        in_specs=[
            whole,
            whole,
            line,
            pl.BlockSpec((1, 256), lambda t: (0, steps + t)),
            pl.BlockSpec((D // 8, 2, 8, 128), lambda t: (0, t, 0, 0)),
            pl.BlockSpec((D // 8, 2, 8, 128), lambda t: (0, steps + t, 0, 0)),
            pl.BlockSpec(memory_space=pl.ANY),
        ],
        out_specs=[part, part, part, whole, whole, line, line],
        out_shape=[jax.ShapeDtypeStruct((rows, FF), bf16)] * 3
        + [jax.ShapeDtypeStruct((rows, D), f32)] * 2
        + [jax.ShapeDtypeStruct((1, FF), f32)] * 2,
        scratch_shapes=[
            pltpu.VMEM((blocks * used, 8, 128), bf16),
            pltpu.SemaphoreType.DMA((blocks,)),
        ],
        cost_estimate=pl.CostEstimate(
            flops=12 * rows * D * FF, bytes_accessed=30_000_000, transcendentals=rows * FF
        ),
        compiler_params=pltpu.CompilerParams(vmem_limit_bytes=56 << 20),
        name="mlp_both_ways",
    )(x, g, bias, bias, tiles, tiles, all_b.reshape(-1, 8, 128))


def pair_product(xo, xp, go, gp):
    down = (((0,), (0,)), ((), ()))
    total = lax.dot_general(xo[...], go[...], down, preferred_element_type=jnp.float32)
    total += lax.dot_general(xp[...], gp[...], down, preferred_element_type=jnp.float32)
    return total.astype(jnp.bfloat16)


def store_tiles(out_ref, lead, first, value):
    for j in range(value.shape[1] // 128):
        out_ref[(*lead, first + j)] = value[:, 128 * j : 128 * (j + 1)]


def grads_b_core_0(in_b, g_gate, g_up):
    def body(xo, xp, gog, gpg, gou, gpu, out_ref):
        for half, go, gp in ((0, gog, gpg), (1, gou, gpu)):
            value = pair_product(xo, xp, go, gp)
            for j in range(4):
                part = value[:, 128 * j : 128 * (j + 1)].reshape(16, 7, 8, 128)
                for block in range(16):
                    out_ref[half, PLACE_B[0][block], :, j] = part[block]

    rows = in_b[0].shape[0]
    high = 16 * 56
    x_spec = pl.BlockSpec((rows, high), lambda t: (0, 0))
    g_spec = pl.BlockSpec((rows, 512), lambda t: (0, t))
    out = pl.pallas_call(
        body,
        grid=(FF // 512,),
        in_specs=[x_spec] * 2 + [g_spec] * 4,
        out_specs=pl.BlockSpec((2, 16, 7, 4, 8, 128), lambda t: (0, 0, 0, t, 0, 0)),
        out_shape=jax.ShapeDtypeStruct((2, 16, 7, FF // 128, 8, 128), jnp.bfloat16),
        compiler_params=pltpu.CompilerParams(vmem_limit_bytes=56 << 20),
        name="grads_b_core_0",
    )(*in_b, *g_gate, *g_up)
    return out.reshape(2, -1, 128)


def grads_b_core_1(in_b, g_gate, g_up, hidden, g_branch):
    bf16 = jnp.bfloat16
    rows = in_b[0].shape[0]
    mlp_steps = FF // 512
    wide = 384
    down_steps = FF // wide
    half_tiles = BLOCK_B // 16
    mlp_groups = (D - 16 * 56) // 8
    groups = (MLP_BLOCKS - 16) * 7
    half_groups = USED_DOWN // 9 // 16
    down_blocks = DEVICES - MLP_BLOCKS

    place = PLACE_B[1]

    def body(place_ref, xo, xp, gog, gpg, gou, gpu, ho, hp, go, gp, out_ref):
        step = pl.program_id(0)

        @pl.when(step == 0)
        def _():
            for group in range(mlp_groups, groups):
                first = place[16 + group // 7] * half_tiles + group % 7 * (FF // 128)
                for half in range(2):
                    out_ref[half, pl.ds(first, FF // 128)] = jnp.zeros((FF // 128, 8, 128), bf16)
            for block in range(down_blocks):
                for half in range(2):
                    used = min(half_groups, FF // 8 - (2 * block + half) * half_groups) * 9
                    first = place[MLP_BLOCKS + block] * half_tiles + used
                    rest = half_tiles - used
                    out_ref[half, pl.ds(first, rest)] = jnp.zeros((rest, 8, 128), bf16)

        @pl.when(step < mlp_steps)
        def _():
            for half, g_own, g_par in ((0, gog, gpg), (1, gou, gpu)):
                value = pair_product(xo, xp, g_own, g_par)
                skip = value.shape[0] - mlp_groups * 8
                for group in range(mlp_groups):
                    first = place[16 + group // 7] * half_tiles + group % 7 * (FF // 128)
                    store_tiles(
                        out_ref,
                        (half,),
                        first + step * 4,
                        value[skip + 8 * group : skip + 8 * group + 8],
                    )

        @pl.when(step >= mlp_steps)
        def _():
            value = pair_product(ho, hp, go, gp)
            for group in range(wide // 8):
                at = (step - mlp_steps) * (wide // 8) + group
                part = at // half_groups
                first = place_ref[part // 2] * half_tiles + (at % half_groups) * 9
                store_tiles(out_ref, (part % 2,), first, value[8 * group : 8 * group + 8])

    x_spec = pl.BlockSpec((rows, 384), lambda t: (0, 2))
    g_spec = pl.BlockSpec((rows, 512), lambda t: (0, jnp.minimum(t, mlp_steps - 1)))
    h_spec = pl.BlockSpec((rows, wide), lambda t: (0, jnp.maximum(t - mlp_steps, 0)))
    b_spec = pl.BlockSpec((rows, D), lambda t: (0, 0))
    shape = (2, 16 * half_tiles, 8, 128)
    down_place = jnp.asarray([place[MLP_BLOCKS + i] for i in range(down_blocks)], jnp.int32)
    out = pl.pallas_call(
        body,
        grid=(mlp_steps + down_steps,),
        in_specs=[pl.BlockSpec(memory_space=pltpu.SMEM)]
        + [x_spec] * 2
        + [g_spec] * 4
        + [h_spec] * 2
        + [b_spec] * 2,
        out_specs=pl.BlockSpec(shape, lambda t: (0, 0, 0, 0)),
        out_shape=jax.ShapeDtypeStruct(shape, bf16),
        compiler_params=pltpu.CompilerParams(vmem_limit_bytes=56 << 20),
        name="grads_b_core_1",
    )(down_place, *in_b, *g_gate, *g_up, *hidden, *g_branch)
    return out.reshape(2, -1, 128)


def grads_a(core, in_a, g_proj, att, g_branch):
    rows = in_a[0].shape[0]
    steps = 3 * D // 384
    place = PLACE_A[core]

    def store_qkv(value, first_block, step, out_ref):
        for group in range(48):
            block, half, low = first_block + group // 6, group // 3 % 2, group % 3
            store_tiles(
                out_ref,
                (half, place[block]),
                low * 27 + step * 3,
                value[8 * group : 8 * group + 8],
            )

    def body(xo, xp, go, gp, zo, zp, bo, bp, out_ref):
        step = pl.program_id(0)

        @pl.when(step < steps)
        def _():
            store_qkv(pair_product(xo, xp, go, gp), 8 * core, step, out_ref)
            if core == 0:
                store_qkv(pair_product(zo, zp, go, gp), 16, step, out_ref)

        if core == 1:

            @pl.when(step >= steps)
            def _():
                value = pair_product(zo, zp, bo, bp)
                for group in range(144):
                    block, half, low = QKV_BLOCKS + group // 18, group // 9 % 2, group % 9
                    store_tiles(
                        out_ref,
                        (half, place[block]),
                        low * 9 + (step - steps) * 3,
                        value[8 * group : 8 * group + 8],
                    )

    x_spec = pl.BlockSpec((rows, 384), lambda t: (0, core))
    g_spec = pl.BlockSpec((rows, 384), lambda t: (0, jnp.minimum(t, steps - 1)))
    if core == 0:
        z_spec, z = pl.BlockSpec((rows, 384), lambda t: (0, 2)), in_a
        b_spec, count = pl.BlockSpec((rows, 384), lambda t: (0, 0)), steps
    else:
        z_spec, z = pl.BlockSpec((rows, D), lambda t: (0, 0)), att
        b_spec = pl.BlockSpec((rows, 384), lambda t: (0, jnp.maximum(t - steps, 0)))
        count = steps + D // 384
    shape = (2, 16, 81, 8, 128)
    out = pl.pallas_call(
        body,
        grid=(count,),
        in_specs=[x_spec] * 2 + [g_spec] * 2 + [z_spec] * 2 + [b_spec] * 2,
        out_specs=pl.BlockSpec(shape, lambda t: (0, 0, 0, 0, 0)),
        out_shape=jax.ShapeDtypeStruct(shape, jnp.bfloat16),
        compiler_params=pltpu.CompilerParams(vmem_limit_bytes=56 << 20),
        name=f"grads_a_core_{core}",
    )(*in_a, *g_proj, *z, *g_branch)
    return out.reshape(2, -1, 128)


def gathered_weights(flat_a, flat_b):
    axes = ("fsdp", "dp")
    me = device_index()
    block_a = spread(flat_a, BLOCK_A, block_a_range)
    block_a = jnp.where(me < QKV_BLOCKS, to_tiles(block_a, 27), to_tiles(block_a, 9))
    all_a = lax.all_gather(block_a, axes, axis=0, tiled=True)
    block_b = spread(flat_b, BLOCK_B, block_b_range)
    block_b = jnp.where(
        me < MLP_BLOCKS,
        to_tiles(block_b, 48),
        jnp.pad(to_tiles(block_b[:USED_DOWN], 9), ((0, BLOCK_B - USED_DOWN), (0, 0))),
    )
    all_b = lax.all_gather(block_b, axes, axis=0, tiled=True)
    return all_a, all_b


def on_device_32(tokens, conditions, cotangent, slot_mask, weight_flat, bias_flat):
    f32 = jnp.float32
    bf16 = jnp.bfloat16
    axes = ("fsdp", "dp")
    me = device_index()
    core = lax.axis_index("dp") % 2
    slots = conditions.shape[0]
    images = slots * DEVICES
    length = GRID * GRID
    rows_all = slots * length
    scale = 1.0 / math.sqrt(HEAD_DIM)
    heads_shape = (slots, length, HEADS, HEAD_DIM)
    cond_count = slots * D
    bias_count = bias_flat.shape[0]
    packed_rows = -(-(cond_count + bias_count) // 128)
    packed = jnp.concatenate(
        [
            conditions.reshape(-1),
            bias_flat,
            jnp.zeros(packed_rows * 128 - cond_count - bias_count, bf16),
        ]
    ).reshape(packed_rows, 128)
    column, flat_a = lax.optimization_barrier((gather_column(packed), weight_flat))
    packed_all = gather_columns(column).reshape(DEVICES, -1)
    cond_all = packed_all[:, :cond_count].reshape(images, D).astype(f32)
    places = lax.broadcasted_iota(jnp.int32, (DEVICES, DEVICES), 0)
    others = lax.broadcasted_iota(jnp.int32, (DEVICES, DEVICES), 1)
    chosen = ((places ^ me) == others).astype(bf16)
    bias_all = jnp.dot(
        chosen, packed_all[:, cond_count : cond_count + bias_count], preferred_element_type=f32
    ).reshape(-1)
    b_qkv = bias_all[: 3 * D]
    b_out = bias_all[3 * D : 4 * D]
    b_mlp = bias_all[4 * D : 4 * D + 2 * FF]
    b_ada = bias_all[4 * D + 2 * FF :]
    ada_local = weight_flat.reshape(ADA_ROWS, 6 * D)
    ada_start = jnp.clip(
        me * ADA_ROWS - FIRST_ADA * 128 // (6 * D) + ADA_ROWS, 0, D + ADA_ROWS
    )
    cond_act = jax.nn.silu(cond_all).astype(bf16)
    cond_rows = lax.dynamic_slice_in_dim(
        jnp.pad(cond_act.T, ((ADA_ROWS, ADA_ROWS), (0, 0))), ada_start, ADA_ROWS, 0
    )
    terms = jnp.einsum("km,kn->mn", cond_rows, ada_local, preferred_element_type=f32)
    modulation = sum_to_owners(terms.reshape(DEVICES, slots, 6 * D)) + b_ada
    all_a, all_b = gathered_weights(flat_a, flat_a)
    w_qkv = matrix_of_tiles(all_a[:ROWS_QKV], D, 3 * D)
    w_out = matrix_of_tiles(all_a[ROWS_QKV:], D, D)

    def share(array):
        return (array, lax.ppermute(array, "dp", SWAP_CORE))

    cosines, sines = rope_tables()
    mask_f = slot_mask.astype(f32)[:, None, None]
    x_f = tokens.astype(f32).reshape(slots, length, D)
    shift_a, scale_a, gate_a, shift_b, scale_b, gate_b = [
        modulation[:, None, place * D : (place + 1) * D] for place in range(6)
    ]
    g_out = cotangent.astype(f32).reshape(slots, length, D) * mask_f
    g_branch_b = (gate_b * g_out).astype(bf16).reshape(rows_all, D)
    normed_a, inv_a = norm_parts(x_f)
    input_a = (normed_a * (1.0 + scale_a) + shift_a).astype(bf16).reshape(rows_all, D)
    projected = (jnp.dot(input_a, w_qkv, preferred_element_type=f32) + b_qkv).reshape(
        slots, length, 3 * D
    )
    q_norm, inv_q = rms_parts(projected[..., :D].reshape(heads_shape))
    k_norm, inv_k = rms_parts(projected[..., D : 2 * D].reshape(heads_shape))
    queries = (q_norm * cosines + turn_half(q_norm) * sines).astype(bf16)
    keys = (k_norm * cosines + turn_half(k_norm) * sines).astype(bf16)
    values = projected[..., 2 * D :].reshape(heads_shape).astype(bf16)
    scores = jnp.einsum("slhe,smhe->shlm", queries, keys, preferred_element_type=f32) * scale
    row_max = jnp.max(scores, -1, keepdims=True)
    log_total = row_max + jnp.log(jnp.sum(jnp.exp(scores - row_max), -1, keepdims=True))
    probs_low = jnp.exp(scores - log_total).astype(bf16)
    attended = (
        jnp.einsum("shlm,smhe->slhe", probs_low, values, preferred_element_type=f32)
        .astype(bf16)
        .reshape(rows_all, D)
    )
    branch_a = (jnp.dot(attended, w_out, preferred_element_type=f32) + b_out).reshape(
        slots, length, D
    )
    middle = x_f + gate_a * branch_a
    normed_b, inv_b = norm_parts(middle)
    input_b = (normed_b * (1.0 + scale_b) + shift_b).astype(bf16).reshape(rows_all, D)
    early = [share(array) for array in (input_a, attended, input_b, g_branch_b)]
    hidden, g_gate, g_up, branch_b, g_input_b, sum_gate, sum_up = mlp_both_ways(
        input_b, g_branch_b, b_mlp.reshape(1, 2 * FF), all_b
    )
    shared_mlp = [share(array) for array in (g_gate, g_up, hidden)]
    grads_b = lax.cond(
        core == 0,
        lambda: grads_b_core_0(early[2], shared_mlp[0], shared_mlp[1]),
        lambda: grads_b_core_1(early[2], *shared_mlp, early[3]),
    )
    branch_b = branch_b.reshape(slots, length, D)
    g_input_b = g_input_b.reshape(slots, length, D)
    sends_b = first_sends(grads_b, BLOCK_B)
    out = ((middle + gate_b * branch_b) * mask_f).astype(bf16).reshape(rows_all, D)
    g_gate_b = jnp.sum(g_out * branch_b, axis=1)
    g_shift_b = jnp.sum(g_input_b, axis=1)
    g_scale_b = jnp.sum(g_input_b * normed_b, axis=1)
    g_middle = g_out + norm_back(g_input_b * (1.0 + scale_b), normed_b, inv_b)
    g_branch_a = (gate_a * g_middle).astype(bf16).reshape(rows_all, D)
    g_gate_a = jnp.sum(g_middle * branch_a, axis=1)
    grad_b_out = jnp.sum(g_branch_a.astype(f32), axis=0)
    shared_branch_a = share(g_branch_a)
    g_attended = (
        jnp.einsum("re,de->rd", g_branch_a, w_out, preferred_element_type=f32)
        .astype(bf16)
        .reshape(heads_shape)
    )
    g_attended, sends_b = lax.optimization_barrier((g_attended, sends_b))
    planes_b = reduce_planes(grads_b, sends_b, BLOCK_B)
    scores = jnp.einsum("slhe,smhe->shlm", queries, keys, preferred_element_type=f32) * scale
    probs = jnp.exp(scores - log_total)
    probs_low = probs.astype(bf16)
    g_probs = jnp.einsum("slhe,smhe->shlm", g_attended, values, preferred_element_type=f32)
    g_values = jnp.einsum("shlm,slhe->smhe", probs_low, g_attended, preferred_element_type=f32)
    g_scores = (probs * (g_probs - jnp.sum(probs * g_probs, -1, keepdims=True))).astype(bf16)
    g_queries = jnp.einsum("shlm,smhe->slhe", g_scores, keys, preferred_element_type=f32) * scale
    g_keys = jnp.einsum("shlm,slhe->smhe", g_scores, queries, preferred_element_type=f32) * scale
    g_q = rms_back(g_queries * cosines - turn_half(g_queries) * sines, q_norm, inv_q)
    g_k = rms_back(g_keys * cosines - turn_half(g_keys) * sines, k_norm, inv_k)
    g_projected = jnp.concatenate(
        [g_q.reshape(rows_all, D), g_k.reshape(rows_all, D), g_values.reshape(rows_all, D)], axis=1
    ).astype(bf16)
    grad_b_qkv = jnp.sum(g_projected.astype(f32), axis=0)
    shared_proj = share(g_projected)
    g_input_a = jnp.einsum("re,de->rd", g_projected, w_qkv, preferred_element_type=f32).reshape(
        slots, length, D
    )
    made_a = lax.cond(
        core == 0,
        lambda: grads_a(0, early[0], shared_proj, early[1], shared_branch_a),
        lambda: grads_a(1, early[0], shared_proj, early[1], shared_branch_a),
    )
    sends_a = first_sends(made_a, BLOCK_A)
    g_input_a, sends_a = lax.optimization_barrier((g_input_a, sends_a))
    g_shift_a = jnp.sum(g_input_a, axis=1)
    g_scale_a = jnp.sum(g_input_a * normed_a, axis=1)
    planes_a = reduce_planes(made_a, sends_a, BLOCK_A)
    grad_tokens = g_middle + norm_back(g_input_a * (1.0 + scale_a), normed_a, inv_a)
    g_modulation = jnp.concatenate(
        [g_shift_a, g_scale_a, g_gate_a, g_shift_b, g_scale_b, g_gate_b], axis=1
    ).astype(bf16)
    bias_sums = [grad_b_qkv, grad_b_out, sum_gate.reshape(-1), sum_up.reshape(-1)]
    small = jnp.concatenate([g_modulation.reshape(-1)] + [b.astype(bf16) for b in bias_sums])
    small_all = lax.all_gather(small.reshape(-1, 128), axes, axis=0, tiled=False).reshape(
        DEVICES, -1
    )
    sum_b = reduce_line(planes_b).astype(bf16)
    planes_a, small_all = lax.optimization_barrier((planes_a, small_all))
    sum_a = reduce_line(planes_a).astype(bf16)
    is_down = jnp.asarray(kind_table(PLACE_B, MLP_BLOCKS))[me]
    is_out = jnp.asarray(kind_table(PLACE_A, QKV_BLOCKS))[me]
    halves = sum_b.reshape(2, BLOCK_B // 2, 128)
    sum_b = jnp.where(
        is_down == 0,
        jnp.concatenate(
            [from_tiles(half, 24).reshape(-1, 24, 128) for half in halves], axis=1
        ).reshape(-1, 128),
        jnp.pad(
            from_tiles(halves[:, : USED_DOWN // 2].reshape(-1, 128), 9),
            ((0, BLOCK_B - USED_DOWN), (0, 0)),
        ),
    )
    sum_a = jnp.where(is_out == 0, from_tiles(sum_a, 27), from_tiles(sum_a, 9))
    buffer = jnp.zeros((SHARD + 2 * BLOCK_B, 128), f32)
    buffer = collect(buffer, sum_b, BLOCK_B, block_b_range, PLACE_B)
    buffer = collect(buffer, sum_a, BLOCK_A, block_a_range, PLACE_A)
    main = buffer[BLOCK_B : BLOCK_B + SHARD]
    g_mod_all = (
        jnp.dot(chosen, small_all[:, : slots * 6 * D], preferred_element_type=f32)
        .astype(bf16)
        .reshape(images, 6 * D)
    )
    grad_biases = jnp.concatenate(
        [
            jnp.sum(small_all[:, slots * 6 * D :].astype(f32), axis=0),
            jnp.sum(g_mod_all.astype(f32), axis=0),
        ]
    )
    part_biases = lax.dynamic_slice_in_dim(grad_biases, me * bias_count, bias_count, 0)
    grad_ada = jnp.einsum("km,mn->kn", cond_rows, g_mod_all, preferred_element_type=f32)
    g_cond_rows = jnp.einsum("mn,kn->mk", g_mod_all, ada_local, preferred_element_type=f32)
    came = exchange_relative(g_cond_rows.reshape(DEVICES, slots, ADA_ROWS))
    came = jnp.take(came, jnp.arange(DEVICES) ^ me, axis=0)
    first = FIRST_ADA * 128 // (6 * D)
    g_cond = came.transpose(1, 0, 2).reshape(slots, DEVICES * ADA_ROWS)[:, first : first + D]
    cond_f = conditions.astype(f32)
    sigma_cond = jax.nn.sigmoid(cond_f)
    grad_conditions = g_cond * sigma_cond * (1.0 + cond_f * (1.0 - sigma_cond))
    row = me * SHARD + lax.broadcasted_iota(jnp.int32, (SHARD, 128), 0)
    part_weights = jnp.where(
        (row >= FIRST_ADA) & (row < FIRST_DOWN), grad_ada.reshape(SHARD, 128), main
    )
    return (out, grad_tokens.reshape(rows_all, D), grad_conditions, part_weights, part_biases)


def solution(mesh):
    chosen = on_device_32 if dict(mesh.shape) == {"fsdp": 4, "dp": 8} else on_device_plain
    return jax.shard_map(
        chosen,
        mesh=mesh,
        in_specs=(
            P(("fsdp", "dp"), None),
            P(("fsdp", "dp"), None),
            P(("fsdp", "dp"), None),
            P(("fsdp", "dp")),
            P(("fsdp", "dp"), None),
            P(("fsdp", "dp")),
        ),
        out_specs=(
            P(("fsdp", "dp"), None),
            P(("fsdp", "dp"), None),
            P(("fsdp", "dp"), None),
            P(("fsdp", "dp"), None),
            P(("fsdp", "dp")),
        ),
        check_vma=False,
    )
```

time: 1240 us -> 867 us (0.70)
  waiting for transfers between devices: 645 us -> 269 us
  local copies, waits for them, and re-layouts: 333 us -> 157 us
  starting transfers between devices: 0.12 us -> 156 us
  matrix products: 144 us -> 41.8 us
  Pallas kernels: 0 us -> 92.8 us
  other arithmetic: 48.1 us -> 93.8 us
  blocking collectives: 42.9 us -> 0 us
  between operations: 15.4 us -> 44.6 us
    unnamed x5 -> x3, waiting for transfers between devices: 428 us -> 0.05 us
    ppermute x0 -> x68, waiting for transfers between devices: none -> 201 us  [the longest x6 76.1 us: reduce_line(): lax.ppermute(pick(planes, z ^ k, 0), 'dp', swap).astype(jnp.float32)]
    reshape x14 -> x15, local copies, waits for them, and re-layouts: 210 us -> 18.3 us  [the longest x2 6.84 us: on_device_32(): ada_local = weight_flat.reshape(ADA_ROWS, 6 * D)]
    ppermute x0 -> x68, starting transfers between devices: none -> 156 us  [the longest x3 52.4 us: gather_columns(): lax.ppermute(part, 'fsdp', [(f, f ^ k) for f in range(4)])]
    all_gather x1 -> x3, waiting for transfers between devices: 217 us -> 67.6 us  [the longest x1 67.6 us: gathered_weights(): all_b = lax.all_gather(block_b, axes, axis=0, tiled=True)]
    dot_general x21 -> x15, matrix products: 144 us -> 41.8 us  [the longest x1 10.6 us: on_device_32(): jnp.einsum('re,de->rd', g_projected, w_qkv, preferred_element_type=f32)]
    pallas_call x0 -> x3, Pallas kernels: none -> 92.8 us  [the longest x1 49.3 us: mlp_both_ways(): pl.pallas_call(mlp_kernel(MLP_BLOCKS * BLOCK_B // 8, blocks, used, BLOCK_...]
    unnamed x1 -> x0, blocking collectives: 42.9 us -> none
  transfers between devices with their start and end apart: 3 -> 71, of which waited for: 3 -> 25; matrix products, arithmetic and copies ran while one was open for 9% -> 27% of each run, Pallas kernels for 0% -> 2%
where the time goes in v2:
time: 867 us; the launch traced here: 855 us
  waiting for transfers between devices  269 us (31%)
  local copies, waits for them, and re-layouts  157 us (18%)
  starting transfers between devices  156 us (18%)
  other arithmetic  93.8 us (11%)
  Pallas kernels  92.8 us (11%)
  between operations  44.6 us (5%)
  matrix products  41.8 us (5%)
    ppermute x6, waiting for transfers between devices, reduce_line(): lax.ppermute(pick(planes, z ^ k, 0), 'dp', swap).astype(jnp.float32)  76.1 us
    all_gather x1, waiting for transfers between devices, gathered_weights(): all_b = lax.all_gather(block_b, axes, axis=0, tiled=True)  67.6 us
    ppermute x9, waiting for transfers between devices, spread(): got = lax.ppermute(piece, ('fsdp', 'dp'), pairs)  59.4 us
    ppermute x3, starting transfers between devices, gather_columns(): lax.ppermute(part, 'fsdp', [(f, f ^ k) for f in range(4)])  52.4 us
    pallas_call x1, Pallas kernels, mlp_both_ways(): pl.pallas_call(mlp_kernel(MLP_BLOCKS * BLOCK_B // 8, blocks, used, BLOCK_...  49.3 us
    ppermute x9, waiting for transfers between devices, collect(): lax.ppermute(block, ('fsdp', 'dp'), [(device, owner) for owner, device in...  27.7 us
    pallas_call x1, Pallas kernels, grads_b_core_1(): pl.pallas_call(body, grid=(mlp_steps + down_steps,), in_specs=[pl.BlockSp...  26.8 us
    ppermute x3, starting transfers between devices, exchange_relative(): lax.ppermute(part[k], 'fsdp', [(f, f ^ k) for f in range(4)])  23.8 us
  transfers between devices with their start and end apart: 71, of which 25 were waited for; matrix products, arithmetic and copies ran while one was open for 27% of the time, Pallas kernels for 2%

profile of v2, /device:TPU:9, one launch (start us, length us, event | category | flops | bytes accessed | tf_op | source)
XLA Modules:
  0.0 855.5 jit_solution(7607969535068596644)
XLA Ops:
  36.3 5.6 collective-permute-start.21
  50.1 9.3 %collective-permute-done.20 = bf16[1296,128]{1,0:T(8,128)(2,1)S(1)} collective-permute-done((bf16[1296,128]{1,0:T(8,128)(2,1)S(1)}, bf16[1296,128]{1,0:T(8,128)(2,1)S(1)}, u32[]{:S(2)}, u32[]{:S(2)}) %collective-permute-start.20) | collective-permute-done | bytes 331808 | tf_op jit(solution)/shard_map/ppermute | solution.py:324
  59.4 2.5 collective-permute-done.19
  61.9 9.2 %collective-permute-done.17 = bf16[1296,128]{1,0:T(8,128)(2,1)S(1)} collective-permute-done((bf16[1296,128]{1,0:T(8,128)(2,1)S(1)}, bf16[1296,128]{1,0:T(8,128)(2,1)S(1)}, u32[]{:S(2)}, u32[]{:S(2)}) %collective-permute-start.17) | collective-permute-done | bytes 331808 | tf_op jit(solution)/shard_map/ppermute | solution.py:324
  71.1 3.6 collective-permute-done.18
  86.4 6.8 pad_dynamic-slice_fusion.2
  99.0 32.6 %collective-permute-done.24 = bf16[2688,128]{1,0:T(8,128)(2,1)} collective-permute-done((bf16[2688,128]{1,0:T(8,128)(2,1)}, bf16[2688,128]{1,0:T(8,128)(2,1)}, u32[]{:S(2)}, u32[]{:S(2)}) %collective-permute-start.24) | collective-permute-done | bytes 688160 | tf_op jit(solution)/shard_map/ppermute | solution.py:324
  138.1 52.4 %collective-permute-start.8 = (bf16[8,23,128]{2,1,0:T(8,128)(2,1)S(1)}, bf16[8,23,128]{2,1,0:T(8,128)(2,1)S(1)}, u32[]{:S(2)}, u32[]{:S(2)}) collective-permute-start(bf16[8,23,128]{2,1,0:T(8,128)(2,1)S(1)} %constant_dynamic-update-slice_fusion), channel_id=1, source_target_pairs={{0,16},{8,24},{16,0},{24,8},{1,17},{9,25},{17,1},{25,9},{2,18},{10... | collective-permute-start | bytes 141320 | tf_op jit(solution)/shard_map/ppermute | solution.py:457
  190.5 2.7 reshape.637
  202.2 6.2 collective-permute-done.13
  208.3 4.9 collective-permute-done.12
  213.8 2.7 collective-permute-start.15
  225.5 4.1 slice.293
  229.7 4.9 convolution_add_fusion
  234.6 2.9 copy-done.44
  239.1 4.9 fusion.92
  246.1 3.9 copy.173
  267.4 5.7 fusion.88
  276.3 67.6 %all-gather.6.cloned.1.call-done = bf16[86016,128]{1,0:T(8,128)(2,1)} async-done(((bf16[2688,128]{1,0:T(8,128)(2,1)}), bf16[86016,128]{1,0:T(8,128)(2,1)}) %all-gather.6.cloned.1.call-update) | async-done | bytes 22020112 | tf_op jit(solution)/shard_map/all_gather | solution.py:769
  343.9 49.3 %mlp_both_ways.1 = (bf16[512,3072]{1,0:T(8,128)(2,1)}, bf16[512,3072]{1,0:T(8,128)(2,1)}, bf16[512,3072]{1,0:T(8,128)(2,1)}, f32[512,1152]{1,0:T(8,128)}, f32[51...) custom-call(bf16[512,1152]{1,0:T(8,128)(2,1)} %fusion.20.x_ref, bf16[512,1152]{1,0:T(8,128)(2,1)} %fusion.15.g_ref, ...), custom_call_target="tpu_custom_call" | custom-call | flops 21743271936 | bytes 30000000 | tf_op jit(solution)/shard_map/mlp_both_ways/pallas_call | solution.py:557
  396.5 4.1 reshape.639
  422.0 5.2 fusion.29
  427.3 2.7 fusion.86
  430.0 4.2 convolution_convert_fusion.1
  436.6 3.7 reshape.600
  440.3 36.2 %conditional.2 = (bf16[2,2,4,1344,128]{4,3,2,1,0:T(8,128)(2,1)}, bf16[2,2,4,1344,128]{4,3,2,1,0:T(8,128)(2,1)}) conditional(s32[]{:T(128)} %convert_element_type.310, (bf16[512,1152]{1,0:T(8,128)(2,1)}, bf16[512,1152]{1,0:T(8,128)(2,1)}, bf16[512,3072]{1,0:T(8,128)(2,1)}, bf16[512,3072]{1,0:T(8,128)(2,1)}, bf16[512,3072]{1,0:T(8,128)(2,1)}, ...), branch_computations={%region_10.11_spmd.clone, %region_11.12_spmd} | conditional | bytes 22020112 | solution.py:863
  440.3 26.8 %grads_b_core_1.2 = bf16[2,2688,8,128]{3,2,1,0:T(8,128)(2,1)} custom-call(s32[11]{0:T(128)} %constant.289.clone.2.place_ref, bf16[512,1152]{1,0:T(8,128)(2,1)} %get-tuple-element.168.xo, bf16[512,1152]{1,0:T(8,128)(2,1)} %get-tuple-element.169.xp, bf16[512,3072]{1,0:T(8,128)(2,1)} %get-tuple-element.170.gog, bf16[512,3072]{1,0:T(8,128)(2,1)} %get-tuple-element.171.gpg, ...), custom_call_target="tpu_custom_call" | custom-call | tf_op jit(solution)/shard_map/cond/branch_0_fun/grads_b_core_1/pallas_call | solution.py:681
  467.1 9.2 %fusion.91 = (bf16[1,2688,8,128]{3,2,1,0:T(8,128)(2,1)}, bf16[1,2688,8,128]{3,2,1,0:T(8,128)(2,1)}) fusion(bf16[2,2688,8,128]{3,2,1,0:T(8,128)(2,1)} %grads_b_core_1.2), kind=kLoop, calls=%fused_computation.295 | loop fusion | bytes 22020096 | tf_op jit(solution)/shard_map/unstack | solution.py:424
  476.5 3.6 dynamic-slice_bitcast_fusion.1
  480.2 3.6 dynamic-slice_bitcast_fusion
  483.8 4.9 multiply_reduce_fusion
  499.8 4.0 multiply_convert_fusion.2
  521.4 2.7 multiply_reduce_fusion.2
  524.0 3.2 reduce_sum.242
  531.9 2.5 copy.185
  534.5 10.6 %fusion.3 = f32[2,256,1152]{2,1,0:T(8,128)} fusion(bf16[1152,3456,1]{1,0,2:T(8,128)(2,1)} %bitcast.421, bf16[2,256,1152]{2,1,0:T(8,128)(2,1)} %copy.187, bf16[2,256,1152]{2,1,0:T(8,128)(2,1)} %copy.186, bf16[2,256,1152]{2,1,0:T(8,128)(2,1)} %copy.185), kind=kOutput, calls=%fused_computation.25 | convolution fusion | flops 4087480320 | bytes 13860864 | tf_op jit(solution)/shard_map/re,de->rd/dot_general | solution.py:902
  545.1 7.7 collective-permute-done.49
  552.8 3.3 fusion.1
  557.5 6.8 collective-permute-done.51
  564.4 4.3 collective-permute-start.50
  568.7 3.3 fusion
  573.4 5.7 collective-permute-start.52
  579.1 33.1 %conditional.3 = (bf16[2,16,81,8,128]{4,3,2,1,0:T(8,128)(2,1)}) conditional(s32[]{:T(128)} %convert_element_type.310, (bf16[512,1152]{1,0:T(8,128)(2,1)S(1)}, bf16[512,1152]{1,0:T(8,128)(2,1)}, bf16[512,3456]{0,1:T(8,128)(2,1)}, bf16[512,3456]{0,1:T(8,128)(2,1)}, bf16[512,1152]{0,1:T(8,128)(2,1)}, /*index=5*/bf16[512,1152]{0,1:T(8,128)(2,1)}, ...), branch_computations={%region_15.16_spmd, %region_16.17_spmd} | conditional | bytes 18874376 | solution.py:905
  579.1 5.8 copy.191.go
  584.9 5.8 copy.192.gp
  595.5 16.8 %grads_a_core_1.3 = bf16[2,16,81,8,128]{4,3,2,1,0:T(8,128)(2,1)} custom-call(bf16[512,1152]{1,0:T(8,128)(2,1)S(1)} %get-tuple-element.109.xo, bf16[512,1152]{1,0:T(8,128)(2,1)} %get-tuple-element.110.xp, bf16[512,3456]{1,0:T(8,128)(2,1)} %copy.191.go, bf16[512,3456]{1,0:T(8,128)(2,1)} %copy.192.gp, bf16[512,1152]{1,0:T(8,128)(2,1)} %copy.193.zo, ...), custom_call_target="tpu_custom_call" | custom-call | tf_op jit(solution)/shard_map/cond/branch_0_fun/grads_a_core_1/pallas_call | solution.py:745
  612.2 3.0 fusion.93
  621.8 4.4 multiply_reduce_fusion.13
  638.3 39.2 %collective-permute-done.55 = bf16[2688,128]{1,0:T(8,128)(2,1)S(1)} collective-permute-done((bf16[2688,128]{1,0:T(8,128)(2,1)S(1)}, bf16[2688,128]{1,0:T(8,128)(2,1)S(1)}, u32[]{:S(2)}, u32[]{:S(2)}) %collective-permute-start.55) | collective-permute-done | bytes 688160 | tf_op jit(solution)/shard_map/ppermute | solution.py:444
  677.4 16.4 %collective-permute-done.54 = bf16[2688,128]{1,0:T(8,128)(2,1)S(1)} collective-permute-done((bf16[2688,128]{1,0:T(8,128)(2,1)S(1)}, bf16[2688,128]{1,0:T(8,128)(2,1)S(1)}, u32[]{:S(2)}, u32[]{:S(2)}) %collective-permute-start.54) | collective-permute-done | bytes 688160 | tf_op jit(solution)/shard_map/ppermute | solution.py:444
  703.5 14.4 %collective-permute-done.56 = bf16[2688,128]{1,0:T(8,128)(2,1)S(1)} collective-permute-done((bf16[2688,128]{1,0:T(8,128)(2,1)S(1)}, bf16[2688,128]{1,0:T(8,128)(2,1)S(1)}, u32[]{:S(2)}, u32[]{:S(2)}) %collective-permute-start.56) | collective-permute-done | bytes 688160 | tf_op jit(solution)/shard_map/ppermute | solution.py:336
  717.9 2.9 broadcast_in_dim.14
  722.0 2.6 add_dynamic-update-slice_fusion.2
  724.6 2.5 add_dynamic-update-slice_fusion.1
  727.1 2.6 add_dynamic-update-slice_fusion
  729.9 3.6 collective-permute-done.36
  750.0 23.4 %collective-permute-start.48 = (f32[8,2,108]{2,1,0:T(2,128)S(1)}, f32[8,2,108]{2,1,0:T(2,128)S(1)}, u32[]{:S(2)}, u32[]{:S(2)}) collective-permute-start(f32[8,2,108]{2,1,0:T(2,128)S(1)} %get-tuple-element.313), channel_id=1, source_target_pairs={{0,24},{8,16},{16,8},{24,0},{1,25},{9,17},{17,9},{25,1},{2,26},{10... | collective-permute-start | bytes 20744 | tf_op jit(solution)/shard_map/ppermute | solution.py:483
  774.5 4.2 reshape.610
  778.9 6.0 collective-permute-start.61
  785.8 15.6 %collective-permute-done.62 = bf16[1296,128]{1,0:T(8,128)(2,1)S(1)} collective-permute-done((bf16[1296,128]{1,0:T(8,128)(2,1)S(1)}, bf16[1296,128]{1,0:T(8,128)(2,1)S(1)}, u32[]{:S(2)}, u32[]{:S(2)}) %collective-permute-start.62) | collective-permute-done | bytes 331808 | tf_op jit(solution)/shard_map/ppermute | solution.py:444
  801.5 4.9 collective-permute-done.61
  811.6 6.4 collective-permute-start.66
  821.4 13.3 %collective-permute-done.64 = bf16[1296,128]{1,0:T(8,128)(2,1)S(1)} collective-permute-done((bf16[1296,128]{1,0:T(8,128)(2,1)S(1)}, bf16[1296,128]{1,0:T(8,128)(2,1)S(1)}, u32[]{:S(2)}, u32[]{:S(2)}) %collective-permute-start.64) | collective-permute-done | bytes 331808 | tf_op jit(solution)/shard_map/ppermute | solution.py:336
  842.8 5.7 slice_select_fusion
  (537 shorter events, 207.4 us)
Async XLA Ops:
  7.2 218.4 %all-gather.4.cloned.1.call-start = ((), (), s32[]{:S(2)}) async-start(), calls=%async_computation | async-start | bytes 10948608 | tf_op jit(solution)/shard_map/all_gather | solution.py:762
  8.7 21.0 %collective-permute-start = (bf16[23,128]{1,0:T(8,128)(2,1)S(1)}, bf16[23,128]{1,0:T(8,128)(2,1)S(1)}, u32[]{:S(2)}, u32[]{:S(2)}) collective-permute-start(bf16[23,128]{1,0:T(8,128)(2,1)S(1)} %bitcast.466), channel_id=1, source_target_pairs={{0,1},{1,0},{2,3},{3,2},{4,5},{5,4},{6,7},{7,6},{8,9},{9,8},{10,11... | collective-permute-start | bytes 17672 | tf_op jit(solution)/shard_map/ppermute | solution.py:450
  9.4 21.7 %collective-permute-start.1 = (bf16[23,128]{1,0:T(8,128)(2,1)S(1)}, bf16[23,128]{1,0:T(8,128)(2,1)S(1)}, u32[]{:S(2)}, u32[]{:S(2)}) collective-permute-start(bf16[23,128]{1,0:T(8,128)(2,1)S(1)} %bitcast.467), channel_id=1, source_target_pairs={{0,2},{1,3},{2,0},{3,1},{4,6},{5,7},{6,4},{7,5},{8,10},{9,11},{10,... | collective-permute-start | bytes 17672 | tf_op jit(solution)/shard_map/ppermute | solution.py:450
  9.4 22.1 %collective-permute-start.2 = (bf16[23,128]{1,0:T(8,128)(2,1)S(1)}, bf16[23,128]{1,0:T(8,128)(2,1)S(1)}, u32[]{:S(2)}, u32[]{:S(2)}) collective-permute-start(bf16[23,128]{1,0:T(8,128)(2,1)S(1)} %bitcast.468), channel_id=1, source_target_pairs={{0,3},{1,2},{2,1},{3,0},{4,7},{5,6},{6,5},{7,4},{8,11},{9,10},{10,... | collective-permute-start | bytes 17672 | tf_op jit(solution)/shard_map/ppermute | solution.py:450
  11.0 20.5 %collective-permute-start.3 = (bf16[23,128]{1,0:T(8,128)(2,1)S(1)}, bf16[23,128]{1,0:T(8,128)(2,1)S(1)}, u32[]{:S(2)}, u32[]{:S(2)}) collective-permute-start(bf16[23,128]{1,0:T(8,128)(2,1)S(1)} %bitcast.469), channel_id=1, source_target_pairs={{0,4},{1,5},{2,6},{3,7},{4,0},{5,1},{6,2},{7,3},{8,12},{9,13},{10,... | collective-permute-start | bytes 17672 | tf_op jit(solution)/shard_map/ppermute | solution.py:450
  13.3 18.2 %collective-permute-start.4 = (bf16[23,128]{1,0:T(8,128)(2,1)S(1)}, bf16[23,128]{1,0:T(8,128)(2,1)S(1)}, u32[]{:S(2)}, u32[]{:S(2)}) collective-permute-start(bf16[23,128]{1,0:T(8,128)(2,1)S(1)} %bitcast.470), channel_id=1, source_target_pairs={{0,5},{1,4},{2,7},{3,6},{4,1},{5,0},{6,3},{7,2},{8,13},{9,12},{10,... | collective-permute-start | bytes 17672 | tf_op jit(solution)/shard_map/ppermute | solution.py:450
  36.3 13.7 %collective-permute-start.21 = (bf16[1296,128]{1,0:T(8,128)(2,1)S(1)}, bf16[1296,128]{1,0:T(8,128)(2,1)S(1)}, u32[]{:S(2)}, u32[]{:S(2)}) collective-permute-start(bf16[1296,128]{1,0:T(8,128)(2,1)S(1)} %get-tuple-element.284), channel_id=1, source_target_pairs={{0,4},{1,8},{2,13},{3,17},{4,22},{5,26},{6,31}} | collective-permute-start | bytes 995336 | tf_op jit(solution)/shard_map/ppermute | solution.py:324
  41.9 17.5 %collective-permute-start.20 = (bf16[1296,128]{1,0:T(8,128)(2,1)S(1)}, bf16[1296,128]{1,0:T(8,128)(2,1)S(1)}, u32[]{:S(2)}, u32[]{:S(2)}) collective-permute-start(bf16[1296,128]{1,0:T(8,128)(2,1)S(1)} %get-tuple-element.283), channel_id=1, source_target_pairs={{0,3},{1,7},{2,12},{3,16},{4,21},{5,25},{6,30}} | collective-permute-start | bytes 995336 | tf_op jit(solution)/shard_map/ppermute | solution.py:324
  43.8 18.0 %collective-permute-start.19 = (bf16[1296,128]{1,0:T(8,128)(2,1)S(1)}, bf16[1296,128]{1,0:T(8,128)(2,1)S(1)}, u32[]{:S(2)}, u32[]{:S(2)}) collective-permute-start(bf16[1296,128]{1,0:T(8,128)(2,1)S(1)} %get-tuple-element.282), channel_id=1, source_target_pairs={{0,2},{1,6},{2,11},{3,15},{4,20},{5,24},{6,29}} | collective-permute-start | bytes 995336 | tf_op jit(solution)/shard_map/ppermute | solution.py:324
  45.2 26.0 %collective-permute-start.17 = (bf16[1296,128]{1,0:T(8,128)(2,1)S(1)}, bf16[1296,128]{1,0:T(8,128)(2,1)S(1)}, u32[]{:S(2)}, u32[]{:S(2)}) collective-permute-start(bf16[1296,128]{1,0:T(8,128)(2,1)S(1)} %get-tuple-element.285), channel_id=1, source_target_pairs={{0,0},{1,4},{2,9},{3,13},{4,18},{5,22},{6,27},{7,31}} | collective-permute-start | bytes 995336 | tf_op jit(solution)/shard_map/ppermute | solution.py:324
  46.5 28.2 %collective-permute-start.18 = (bf16[1296,128]{1,0:T(8,128)(2,1)S(1)}, bf16[1296,128]{1,0:T(8,128)(2,1)S(1)}, u32[]{:S(2)}, u32[]{:S(2)}) collective-permute-start(bf16[1296,128]{1,0:T(8,128)(2,1)S(1)} %get-tuple-element.281), channel_id=1, source_target_pairs={{0,1},{1,5},{2,10},{3,14},{4,19},{5,23},{6,28}} | collective-permute-start | bytes 995336 | tf_op jit(solution)/shard_map/ppermute | solution.py:324
  76.2 267.7 %all-gather.6.cloned.1.call-start = ((), (), s32[]{:S(2)}) async-start(), calls=%async_computation.1 | async-start | bytes 22708224 | tf_op jit(solution)/shard_map/all_gather | solution.py:769
  93.2 5.8 collective-permute-start.25
  94.7 36.9 %collective-permute-start.24 = (bf16[2688,128]{1,0:T(8,128)(2,1)}, bf16[2688,128]{1,0:T(8,128)(2,1)}, u32[]{:S(2)}, u32[]{:S(2)}) collective-permute-start(bf16[2688,128]{1,0:T(8,128)(2,1)} %get-tuple-element.278), channel_id=1, source_target_pairs={{8,3},{9,6},{10,8},{11,10},{12,12},{13,14},{14,16},{15,19},{28,24}... | collective-permute-start | bytes 2064392 | tf_op jit(solution)/shard_map/ppermute | solution.py:324
  96.0 35.6 %collective-permute-start.22 = (bf16[2688,128]{1,0:T(8,128)(2,1)S(1)}, bf16[2688,128]{1,0:T(8,128)(2,1)}, u32[]{:S(2)}, u32[]{:S(2)}) collective-permute-start(bf16[2688,128]{1,0:T(8,128)(2,1)S(1)} %get-tuple-element.280), channel_id=1, source_target_pairs={{7,0},{8,1},{9,4},{10,6},{11,8},{12,10},{13,12},{14,14},{15,17},{1... | collective-permute-start | bytes 2064392 | tf_op jit(solution)/shard_map/ppermute | solution.py:324
  97.5 34.1 %collective-permute-start.23 = (bf16[2688,128]{1,0:T(8,128)(2,1)S(1)}, bf16[2688,128]{1,0:T(8,128)(2,1)}, u32[]{:S(2)}, u32[]{:S(2)}) collective-permute-start(bf16[2688,128]{1,0:T(8,128)(2,1)S(1)} %get-tuple-element.277), channel_id=1, source_target_pairs={{7,1},{8,2},{9,5},{10,7},{11,9},{12,11},{13,13},{14,15},{15,18},{1... | collective-permute-start | bytes 2064392 | tf_op jit(solution)/shard_map/ppermute | solution.py:324
  137.2 596.6 %all-gather.8.cloned.1.call-start = ((), (), s32[]{:S(2)}) async-start(), calls=%async_computation.2 | async-start | bytes 1622016 | tf_op jit(solution)/shard_map/all_gather | solution.py:921
  138.1 55.2 %collective-permute-start.9 = (bf16[8,23,128]{2,1,0:T(8,128)(2,1)S(1)}, bf16[8,23,128]{2,1,0:T(8,128)(2,1)S(1)}, u32[]{:S(2)}, u32[]{:S(2)}) collective-permute-start(bf16[8,23,128]{2,1,0:T(8,128)(2,1)S(1)} %constant_dynamic-update-slice_fusion), channel_id=1, source_target_pairs={{0,24},{8,16},{16,8},{24,0},{1,25},{9,17},{17,9},{25,1},{2,26},{10... | collective-permute-start | bytes 141320 | tf_op jit(solution)/shard_map/ppermute | solution.py:457
  138.1 55.2 %collective-permute-start.8 = (bf16[8,23,128]{2,1,0:T(8,128)(2,1)S(1)}, bf16[8,23,128]{2,1,0:T(8,128)(2,1)S(1)}, u32[]{:S(2)}, u32[]{:S(2)}) collective-permute-start(bf16[8,23,128]{2,1,0:T(8,128)(2,1)S(1)} %constant_dynamic-update-slice_fusion), channel_id=1, source_target_pairs={{0,16},{8,24},{16,0},{24,8},{1,17},{9,25},{17,1},{25,9},{2,18},{10... | collective-permute-start | bytes 141320 | tf_op jit(solution)/shard_map/ppermute | solution.py:457
  198.3 10.0 %collective-permute-start.13 = (f32[4,2,6912]{2,0,1:T(4,128)S(1)}, f32[4,2,6912]{2,0,1:T(4,128)S(1)}, u32[]{:S(2)}, u32[]{:S(2)}) collective-permute-start(f32[4,2,6912]{2,0,1:T(4,128)S(1)} %get-tuple-element.290), channel_id=1, source_target_pairs={{16,8},{17,9},{18,10},{19,11},{20,12},{21,13},{22,14},{23,15},{24,... | collective-permute-start | bytes 663560 | tf_op jit(solution)/shard_map/ppermute | solution.py:468
  199.6 8.8 %collective-permute-start.11 = (f32[4,2,6912]{2,0,1:T(4,128)S(1)}, f32[4,2,6912]{2,0,1:T(4,128)S(1)}, u32[]{:S(2)}, u32[]{:S(2)}) collective-permute-start(f32[4,2,6912]{2,0,1:T(4,128)S(1)} %get-tuple-element.291), channel_id=1, source_target_pairs={{16,24},{17,25},{18,26},{19,27},{20,28},{21,29},{22,30},{23,31},{2... | collective-permute-start | bytes 663560 | tf_op jit(solution)/shard_map/ppermute | solution.py:468
  200.3 13.0 %collective-permute-start.12 = (f32[4,2,6912]{2,0,1:T(4,128)S(1)}, f32[4,2,6912]{2,0,1:T(4,128)S(1)}, u32[]{:S(2)}, u32[]{:S(2)}) collective-permute-start(f32[4,2,6912]{2,0,1:T(4,128)S(1)} %get-tuple-element.289), channel_id=1, source_target_pairs={{16,0},{17,1},{18,2},{19,3},{20,4},{21,5},{22,6},{23,7},{24,8},{25... | collective-permute-start | bytes 663560 | tf_op jit(solution)/shard_map/ppermute | solution.py:468
  213.5 6.4 collective-permute-start.16
  213.6 6.3 collective-permute-start.14
  213.8 8.3 collective-permute-start.15
  393.2 47.1 %collective-permute-start.27 = (bf16[512,3072]{1,0:T(8,128)(2,1)}, bf16[512,3072]{1,0:T(8,128)(2,1)}, u32[]{:S(2)}, u32[]{:S(2)}) collective-permute-start(bf16[512,3072]{1,0:T(8,128)(2,1)} %get-tuple-element.180), channel_id=1, source_target_pairs={{0,1},{1,0},{2,3},{3,2},{4,5},{5,4},{6,7},{7,6},{8,9},{9,8},{10,11... | collective-permute-start | bytes 9437192 | tf_op jit(solution)/shard_map/ppermute | solution.py:823
  393.5 46.8 %collective-permute-start.28 = (bf16[512,3072]{1,0:T(8,128)(2,1)}, bf16[512,3072]{1,0:T(8,128)(2,1)}, u32[]{:S(2)}, u32[]{:S(2)}) collective-permute-start(bf16[512,3072]{1,0:T(8,128)(2,1)} %get-tuple-element.182), channel_id=1, source_target_pairs={{0,1},{1,0},{2,3},{3,2},{4,5},{5,4},{6,7},{7,6},{8,9},{9,8},{10,11... | collective-permute-start | bytes 9437192 | tf_op jit(solution)/shard_map/ppermute | solution.py:823
  393.8 46.6 %collective-permute-start.29 = (bf16[512,3072]{1,0:T(8,128)(2,1)}, bf16[512,3072]{1,0:T(8,128)(2,1)}, u32[]{:S(2)}, u32[]{:S(2)}) collective-permute-start(bf16[512,3072]{1,0:T(8,128)(2,1)} %get-tuple-element.184), channel_id=1, source_target_pairs={{0,1},{1,0},{2,3},{3,2},{4,5},{5,4},{6,7},{7,6},{8,9},{9,8},{10,11... | collective-permute-start | bytes 9437192 | tf_op jit(solution)/shard_map/ppermute | solution.py:823
  420.2 20.1 %collective-permute-start.30 = (bf16[512,1152]{1,0:T(8,128)(2,1)}, bf16[512,1152]{1,0:T(8,128)(2,1)}, u32[]{:S(2)}, u32[]{:S(2)}) collective-permute-start(bf16[512,1152]{1,0:T(8,128)(2,1)} %fusion.15.g_ref), channel_id=1, source_target_pairs={{0,1},{1,0},{2,3},{3,2},{4,5},{5,4},{6,7},{7,6},{8,9},{9,8},{10,11... | collective-permute-start | bytes 3538952 | tf_op jit(solution)/shard_map/ppermute | solution.py:823
  420.5 19.8 %collective-permute-start.26 = (bf16[512,1152]{1,0:T(8,128)(2,1)}, bf16[512,1152]{1,0:T(8,128)(2,1)}, u32[]{:S(2)}, u32[]{:S(2)}) collective-permute-start(bf16[512,1152]{1,0:T(8,128)(2,1)} %fusion.20.x_ref), channel_id=1, source_target_pairs={{0,1},{1,0},{2,3},{3,2},{4,5},{5,4},{6,7},{7,6},{8,9},{9,8},{10,11... | collective-permute-start | bytes 3538952 | tf_op jit(solution)/shard_map/ppermute | solution.py:823
  498.6 54.2 %collective-permute-start.49 = (bf16[2,4,1344,128]{3,2,1,0:T(8,128)(2,1)}, bf16[2,4,1344,128]{3,2,1,0:T(8,128)(2,1)}, u32[]{:S(2)}, u32[]{:S(2)}) collective-permute-start(bf16[2,4,1344,128]{3,2,1,0:T(8,128)(2,1)} %dynamic-slice_bitcast_fusion.1), channel_id=1, source_target_pairs={{0,16},{16,0},{8,24},{24,8},{1,17},{17,1},{9,25},{25,9},{2,18},{18... | collective-permute-start | bytes 8257544 | tf_op jit(solution)/shard_map/ppermute | solution.py:432
  510.1 54.2 %collective-permute-start.51 = (bf16[2,4,1344,128]{3,2,1,0:T(8,128)(2,1)}, bf16[2,4,1344,128]{3,2,1,0:T(8,128)(2,1)}, u32[]{:S(2)}, u32[]{:S(2)}) collective-permute-start(bf16[2,4,1344,128]{3,2,1,0:T(8,128)(2,1)} %dynamic-slice_bitcast_fusion), channel_id=1, source_target_pairs={{0,8},{8,0},{16,24},{24,16},{1,9},{9,1},{17,25},{25,17},{2,10},{10... | collective-permute-start | bytes 8257544 | tf_op jit(solution)/shard_map/ppermute | solution.py:433
  513.8 65.3 %collective-permute-start.32 = (bf16[512,3456]{0,1:T(8,128)(2,1)}, bf16[512,3456]{0,1:T(8,128)(2,1)}, u32[]{:S(2)}, u32[]{:S(2)}) collective-permute-start(bf16[512,3456]{0,1:T(8,128)(2,1)} %constant_dynamic-update-slice_fusion.8), channel_id=1, source_target_pairs={{0,1},{1,0},{2,3},{3,2},{4,5},{5,4},{6,7},{7,6},{8,9},{9,8},{10,11... | collective-permute-start | bytes 10616840 | tf_op jit(solution)/shard_map/ppermute | solution.py:823
  514.4 59.0 %collective-permute-start.31 = (bf16[512,1152]{1,0:T(8,128)(2,1)S(1)}, bf16[512,1152]{1,0:T(8,128)(2,1)}, u32[]{:S(2)}, u32[]{:S(2)}) collective-permute-start(bf16[512,1152]{1,0:T(8,128)(2,1)S(1)} %copy-done.13), channel_id=1, source_target_pairs={{0,1},{1,0},{2,3},{3,2},{4,5},{5,4},{6,7},{7,6},{8,9},{9,8},{10,11... | collective-permute-start | bytes 3538952 | tf_op jit(solution)/shard_map/ppermute | solution.py:823
  514.9 64.2 %collective-permute-start.33 = (bf16[512,1152]{0,1:T(8,128)(2,1)}, bf16[512,1152]{0,1:T(8,128)(2,1)}, u32[]{:S(2)}, u32[]{:S(2)}) collective-permute-start(bf16[512,1152]{0,1:T(8,128)(2,1)} %bitcast.205), channel_id=1, source_target_pairs={{0,1},{1,0},{2,3},{3,2},{4,5},{5,4},{6,7},{7,6},{8,9},{9,8},{10,11... | collective-permute-start | bytes 3538952 | tf_op jit(solution)/shard_map/ppermute | solution.py:823
  552.8 26.2 %collective-permute-start.34 = (bf16[512,1152]{1,0:T(8,128)(2,1)}, bf16[512,1152]{1,0:T(8,128)(2,1)}, u32[]{:S(2)}, u32[]{:S(2)}) collective-permute-start(bf16[512,1152]{1,0:T(8,128)(2,1)} %get-tuple-element.245), channel_id=1, source_target_pairs={{0,1},{1,0},{2,3},{3,2},{4,5},{5,4},{6,7},{7,6},{8,9},{9,8},{10,11... | collective-permute-start | bytes 3538952 | tf_op jit(solution)/shard_map/ppermute | solution.py:823
  564.4 63.9 %collective-permute-start.50 = (bf16[4,1344,128]{2,1,0:T(8,128)(2,1)}, bf16[4,1344,128]{2,1,0:T(8,128)(2,1)}, u32[]{:S(2)}, u32[]{:S(2)}) collective-permute-start(bf16[4,1344,128]{2,1,0:T(8,128)(2,1)} %dynamic-slice_bitcast_fusion.3), channel_id=1, source_target_pairs={{0,8},{8,0},{16,24},{24,16},{1,9},{9,1},{17,25},{25,17},{2,10},{10... | collective-permute-start | bytes 4128776 | tf_op jit(solution)/shard_map/ppermute | solution.py:434
  573.4 57.1 %collective-permute-start.52 = (bf16[4,1344,128]{2,1,0:T(8,128)(2,1)}, bf16[4,1344,128]{2,1,0:T(8,128)(2,1)}, u32[]{:S(2)}, u32[]{:S(2)}) collective-permute-start(bf16[4,1344,128]{2,1,0:T(8,128)(2,1)} %dynamic-slice_bitcast_fusion.2), channel_id=1, source_target_pairs={{0,16},{16,0},{8,24},{24,8},{1,17},{17,1},{9,25},{25,9},{2,18},{18... | collective-permute-start | bytes 4128776 | tf_op jit(solution)/shard_map/ppermute | solution.py:435
  619.3 79.8 %collective-permute-start.37 = (bf16[2,4,648,128]{3,2,1,0:T(8,128)(2,1)}, bf16[2,4,648,128]{3,2,1,0:T(8,128)(2,1)}, u32[]{:S(2)}, u32[]{:S(2)}) collective-permute-start(bf16[2,4,648,128]{3,2,1,0:T(8,128)(2,1)} %dynamic-slice_bitcast_fusion.4), channel_id=1, source_target_pairs={{0,8},{8,0},{16,24},{24,16},{1,9},{9,1},{17,25},{25,17},{2,10},{10... | collective-permute-start | bytes 3981320 | tf_op jit(solution)/shard_map/ppermute | solution.py:433
  620.4 81.2 %collective-permute-start.35 = (bf16[2,4,648,128]{3,2,1,0:T(8,128)(2,1)}, bf16[2,4,648,128]{3,2,1,0:T(8,128)(2,1)}, u32[]{:S(2)}, u32[]{:S(2)}) collective-permute-start(bf16[2,4,648,128]{3,2,1,0:T(8,128)(2,1)} %dynamic-slice_bitcast_fusion.5), channel_id=1, source_target_pairs={{0,16},{16,0},{8,24},{24,8},{1,17},{17,1},{9,25},{25,9},{2,18},{18... | collective-permute-start | bytes 3981320 | tf_op jit(solution)/shard_map/ppermute | solution.py:432
  632.7 44.8 %collective-permute-start.55 = (bf16[2688,128]{1,0:T(8,128)(2,1)S(1)}, bf16[2688,128]{1,0:T(8,128)(2,1)S(1)}, u32[]{:S(2)}, u32[]{:S(2)}) collective-permute-start(bf16[2688,128]{1,0:T(8,128)(2,1)S(1)} %get-tuple-element.259), channel_id=1, source_target_pairs={{0,6},{1,7},{2,4},{3,5},{4,2},{5,3},{6,0},{7,1},{8,14},{9,15},{10,... | collective-permute-start | bytes 2064392 | tf_op jit(solution)/shard_map/ppermute | solution.py:444
  633.9 59.9 %collective-permute-start.54 = (bf16[2688,128]{1,0:T(8,128)(2,1)S(1)}, bf16[2688,128]{1,0:T(8,128)(2,1)S(1)}, u32[]{:S(2)}, u32[]{:S(2)}) collective-permute-start(bf16[2688,128]{1,0:T(8,128)(2,1)S(1)} %get-tuple-element.258), channel_id=1, source_target_pairs={{0,4},{1,5},{2,6},{3,7},{4,0},{5,1},{6,2},{7,3},{8,12},{9,13},{10,... | collective-permute-start | bytes 2064392 | tf_op jit(solution)/shard_map/ppermute | solution.py:444
  635.1 58.7 %collective-permute-start.53 = (bf16[2688,128]{1,0:T(8,128)(2,1)S(1)}, bf16[2688,128]{1,0:T(8,128)(2,1)S(1)}, u32[]{:S(2)}, u32[]{:S(2)}) collective-permute-start(bf16[2688,128]{1,0:T(8,128)(2,1)S(1)} %get-tuple-element.257), channel_id=1, source_target_pairs={{0,2},{1,3},{2,0},{3,1},{4,6},{5,7},{6,4},{7,5},{8,10},{9,11},{10,... | collective-permute-start | bytes 2064392 | tf_op jit(solution)/shard_map/ppermute | solution.py:444
  695.3 22.6 %collective-permute-start.56 = (bf16[2688,128]{1,0:T(8,128)(2,1)S(1)}, bf16[2688,128]{1,0:T(8,128)(2,1)S(1)}, u32[]{:S(2)}, u32[]{:S(2)}) collective-permute-start(bf16[2688,128]{1,0:T(8,128)(2,1)S(1)} %bitcast_select_fusion.1), channel_id=1, source_target_pairs={{14,7},{30,8},{16,9},{2,10},{18,11},{4,12},{20,13},{6,14},{17,15},... | collective-permute-start | bytes 2064392 | tf_op jit(solution)/shard_map/ppermute | solution.py:336
  697.7 24.4 %collective-permute-start.57 = (bf16[2688,128]{1,0:T(8,128)(2,1)S(1)}, bf16[2688,128]{1,0:T(8,128)(2,1)S(1)}, u32[]{:S(2)}, u32[]{:S(2)}) collective-permute-start(bf16[2688,128]{1,0:T(8,128)(2,1)S(1)} %bitcast_select_fusion.1), channel_id=1, source_target_pairs={{30,7},{0,8},{24,9},{10,10},{26,11},{12,12},{28,13},{22,14},{25,15... | collective-permute-start | bytes 2064392 | tf_op jit(solution)/shard_map/ppermute | solution.py:336
  698.4 26.2 %collective-permute-start.58 = (bf16[2688,128]{1,0:T(8,128)(2,1)S(1)}, bf16[2688,128]{1,0:T(8,128)(2,1)S(1)}, u32[]{:S(2)}, u32[]{:S(2)}) collective-permute-start(bf16[2688,128]{1,0:T(8,128)(2,1)S(1)} %bitcast_select_fusion.1), channel_id=1, source_target_pairs={{8,8},{2,9},{18,10},{4,11},{20,12},{6,13},{9,14},{15,15},{27,28},{... | collective-permute-start | bytes 2064392 | tf_op jit(solution)/shard_map/ppermute | solution.py:336
  699.1 28.0 %collective-permute-start.59 = (bf16[2688,128]{1,0:T(8,128)(2,1)S(1)}, bf16[2688,128]{1,0:T(8,128)(2,1)S(1)}, u32[]{:S(2)}, u32[]{:S(2)}) collective-permute-start(bf16[2688,128]{1,0:T(8,128)(2,1)S(1)} %bitcast_select_fusion.1), channel_id=1, source_target_pairs={{16,8},{17,14},{21,29}} | collective-permute-start | bytes 2064392 | tf_op jit(solution)/shard_map/ppermute | solution.py:336
  701.6 28.1 %collective-permute-start.38 = (bf16[4,648,128]{2,1,0:T(8,128)(2,1)S(1)}, bf16[4,648,128]{2,1,0:T(8,128)(2,1)S(1)}, u32[]{:S(2)}, u32[]{:S(2)}) collective-permute-start(bf16[4,648,128]{2,1,0:T(8,128)(2,1)S(1)} %dynamic-slice_bitcast_fusion.6), channel_id=1, source_target_pairs={{0,16},{16,0},{8,24},{24,8},{1,17},{17,1},{9,25},{25,9},{2,18},{18... | collective-permute-start | bytes 1990664 | tf_op jit(solution)/shard_map/ppermute | solution.py:435
  717.9 15.5 %collective-permute-start.36 = (bf16[4,648,128]{2,1,0:T(8,128)(2,1)S(1)}, bf16[4,648,128]{2,1,0:T(8,128)(2,1)S(1)}, u32[]{:S(2)}, u32[]{:S(2)}) collective-permute-start(bf16[4,648,128]{2,1,0:T(8,128)(2,1)S(1)} %dynamic-slice_bitcast_fusion.7), channel_id=1, source_target_pairs={{0,8},{8,0},{16,24},{24,16},{1,9},{9,1},{17,25},{25,17},{2,10},{10... | collective-permute-start | bytes 1990664 | tf_op jit(solution)/shard_map/ppermute | solution.py:434
  740.4 4.6 collective-permute-start.39
  740.5 6.3 collective-permute-start.40
  740.6 6.5 collective-permute-start.41
  742.7 4.4 collective-permute-start.42
  750.0 34.8 %collective-permute-start.48 = (f32[8,2,108]{2,1,0:T(2,128)S(1)}, f32[8,2,108]{2,1,0:T(2,128)S(1)}, u32[]{:S(2)}, u32[]{:S(2)}) collective-permute-start(f32[8,2,108]{2,1,0:T(2,128)S(1)} %get-tuple-element.313), channel_id=1, source_target_pairs={{0,24},{8,16},{16,8},{24,0},{1,25},{9,17},{17,9},{25,1},{2,26},{10... | collective-permute-start | bytes 20744 | tf_op jit(solution)/shard_map/ppermute | solution.py:483
  773.4 11.4 %collective-permute-start.47 = (f32[8,2,108]{2,1,0:T(2,128)S(1)}, f32[8,2,108]{2,1,0:T(2,128)S(1)}, u32[]{:S(2)}, u32[]{:S(2)}) collective-permute-start(f32[8,2,108]{2,1,0:T(2,128)S(1)} %get-tuple-element.314), channel_id=1, source_target_pairs={{0,16},{8,24},{16,0},{24,8},{1,17},{9,25},{17,1},{25,9},{2,18},{10... | collective-permute-start | bytes 20744 | tf_op jit(solution)/shard_map/ppermute | solution.py:483
  773.4 11.4 %collective-permute-start.46 = (f32[8,2,108]{2,1,0:T(2,128)S(1)}, f32[8,2,108]{2,1,0:T(2,128)S(1)}, u32[]{:S(2)}, u32[]{:S(2)}) collective-permute-start(f32[8,2,108]{2,1,0:T(2,128)S(1)} %get-tuple-element.312), channel_id=1, source_target_pairs={{0,8},{8,0},{16,24},{24,16},{1,9},{9,1},{17,25},{25,17},{2,10},{10... | collective-permute-start | bytes 20744 | tf_op jit(solution)/shard_map/ppermute | solution.py:483
  778.6 22.8 %collective-permute-start.62 = (bf16[1296,128]{1,0:T(8,128)(2,1)S(1)}, bf16[1296,128]{1,0:T(8,128)(2,1)S(1)}, u32[]{:S(2)}, u32[]{:S(2)}) collective-permute-start(bf16[1296,128]{1,0:T(8,128)(2,1)S(1)} %get-tuple-element.287), channel_id=1, source_target_pairs={{0,6},{1,7},{2,4},{3,5},{4,2},{5,3},{6,0},{7,1},{8,14},{9,15},{10,... | collective-permute-start | bytes 995336 | tf_op jit(solution)/shard_map/ppermute | solution.py:444
  778.9 27.5 %collective-permute-start.61 = (bf16[1296,128]{1,0:T(8,128)(2,1)S(1)}, bf16[1296,128]{1,0:T(8,128)(2,1)S(1)}, u32[]{:S(2)}, u32[]{:S(2)}) collective-permute-start(bf16[1296,128]{1,0:T(8,128)(2,1)S(1)} %get-tuple-element.288), channel_id=1, source_target_pairs={{0,4},{1,5},{2,6},{3,7},{4,0},{5,1},{6,2},{7,3},{8,12},{9,13},{10,... | collective-permute-start | bytes 995336 | tf_op jit(solution)/shard_map/ppermute | solution.py:444
  784.8 21.5 %collective-permute-start.60 = (bf16[1296,128]{1,0:T(8,128)(2,1)S(1)}, bf16[1296,128]{1,0:T(8,128)(2,1)S(1)}, u32[]{:S(2)}, u32[]{:S(2)}) collective-permute-start(bf16[1296,128]{1,0:T(8,128)(2,1)S(1)} %get-tuple-element.286), channel_id=1, source_target_pairs={{0,2},{1,3},{2,0},{3,1},{4,6},{5,7},{6,4},{7,5},{8,10},{9,11},{10,... | collective-permute-start | bytes 995336 | tf_op jit(solution)/shard_map/ppermute | solution.py:444
  807.1 12.3 %collective-permute-start.63 = (bf16[1296,128]{1,0:T(8,128)(2,1)S(1)}, bf16[1296,128]{1,0:T(8,128)(2,1)S(1)}, u32[]{:S(2)}, u32[]{:S(2)}) collective-permute-start(bf16[1296,128]{1,0:T(8,128)(2,1)S(1)} %broadcast_select_fusion), channel_id=1, source_target_pairs={{0,0},{2,1},{9,2},{11,3},{4,4},{6,5},{29,6},{31,7}} | collective-permute-start | bytes 995336 | tf_op jit(solution)/shard_map/ppermute | solution.py:336
  809.0 25.6 %collective-permute-start.64 = (bf16[1296,128]{1,0:T(8,128)(2,1)S(1)}, bf16[1296,128]{1,0:T(8,128)(2,1)S(1)}, u32[]{:S(2)}, u32[]{:S(2)}) collective-permute-start(bf16[1296,128]{1,0:T(8,128)(2,1)S(1)} %broadcast_select_fusion), channel_id=1, source_target_pairs={{8,0},{10,1},{17,2},{19,3},{12,4},{14,5},{7,6}} | collective-permute-start | bytes 995336 | tf_op jit(solution)/shard_map/ppermute | solution.py:336
  810.3 26.4 %collective-permute-start.65 = (bf16[1296,128]{1,0:T(8,128)(2,1)S(1)}, bf16[1296,128]{1,0:T(8,128)(2,1)S(1)}, u32[]{:S(2)}, u32[]{:S(2)}) collective-permute-start(bf16[1296,128]{1,0:T(8,128)(2,1)S(1)} %broadcast_select_fusion), channel_id=1, source_target_pairs={{16,0},{18,1},{25,2},{27,3},{20,4},{5,5},{15,6}} | collective-permute-start | bytes 995336 | tf_op jit(solution)/shard_map/ppermute | solution.py:336
  811.6 27.2 %collective-permute-start.66 = (bf16[1296,128]{1,0:T(8,128)(2,1)S(1)}, bf16[1296,128]{1,0:T(8,128)(2,1)S(1)}, u32[]{:S(2)}, u32[]{:S(2)}) collective-permute-start(bf16[1296,128]{1,0:T(8,128)(2,1)S(1)} %broadcast_select_fusion), channel_id=1, source_target_pairs={{24,0},{26,1},{3,2},{22,3},{28,4},{13,5},{23,6}} | collective-permute-start | bytes 995336 | tf_op jit(solution)/shard_map/ppermute | solution.py:336
  818.0 22.8 %collective-permute-start.67 = (bf16[1296,128]{1,0:T(8,128)(2,1)S(1)}, bf16[1296,128]{1,0:T(8,128)(2,1)S(1)}, u32[]{:S(2)}, u32[]{:S(2)}) collective-permute-start(bf16[1296,128]{1,0:T(8,128)(2,1)S(1)} %broadcast_select_fusion), channel_id=1, source_target_pairs={{2,0},{1,1},{11,2},{30,3},{6,4},{21,5},{31,6}} | collective-permute-start | bytes 995336 | tf_op jit(solution)/shard_map/ppermute | solution.py:336
  (110 other events, 547.1 us)
Sparse Core Ops, SparseCore 0:
  76.3 124.6 all-gather.3
  204.6 139.2 all-gather.5
  628.3 70.8 all-gather.7

commit v3 on v2

--- a/solution.py
+++ b/solution.py
@@ -266,80 +266,80 @@
     return (first, min(first + USED_DOWN, FIRST_DOWN + ROWS_DOWN))
 
 
-def colour_edges(edges):
-    degree = {}
-    for left, right in edges:
-        degree["l", left] = degree.get(("l", left), 0) + 1
-        degree["r", right] = degree.get(("r", right), 0) + 1
-    count = max(degree.values())
-    at = {}
-    for left, right in edges:
-        a, b = ("l", left), ("r", right)
-        free_a = next(c for c in range(count) if (a, c) not in at)
-        free_b = next(c for c in range(count) if (b, c) not in at)
-        if free_a != free_b:
-            path, node, colour = [], b, free_a
-            while (node, colour) in at:
-                other = at[node, colour]
-                path.append((node, other, colour))
-                node, colour = other, free_a + free_b - colour
-            for one, two, old in path:
-                del at[one, old], at[two, old]
-            for one, two, old in path:
-                new = free_a + free_b - old
-                at[one, new], at[two, new] = two, one
-        at[a, free_a], at[b, free_a] = b, a
-    rounds = [[] for _ in range(count)]
-    for (node, colour), other in at.items():
-        if node[0] == "l":
-            rounds[colour].append((node[1], other[1]))
-    return [sorted(group) for group in rounds]
-
-
-def plan_rounds(block_range, device_of_block):
-    edges, first_row = [], {}
-    for block in range(DEVICES):
-        first, last = block_range(block)
-        for owner in range(first // SHARD, (last - 1) // SHARD + 1):
-            edges.append((owner, device_of_block(block)))
-            first_row[owner, device_of_block(block)] = first - owner * SHARD
-    rounds = colour_edges(edges)
-    return rounds, first_row
+def plan_rounds(block_range, first_block, count, device_of_block):
+    rounds = []
+    for k in range(count):
+        pairs = []
+        for owner in range(DEVICES):
+            block = first_block(owner) + k
+            if 0 <= block < DEVICES:
+                first, last = block_range(block)
+                if first < (owner + 1) * SHARD and last > owner * SHARD:
+                    pairs.append((owner, device_of_block(block)))
+        rounds.append(pairs)
+    return rounds
+
+
+DOWN_OWNER = FIRST_DOWN // SHARD
+
+
+def first_block_a(owner):
+    return owner * SHARD // BLOCK_A
+
+
+def first_block_b(owner):
+    if owner < DOWN_OWNER:
+        return (owner * SHARD - FIRST_MLP) // BLOCK_B
+    return MLP_BLOCKS + max((owner * SHARD - FIRST_DOWN) // USED_DOWN, -1)
+
+
+def starts_a():
+    return -(device_index() * SHARD % BLOCK_A), BLOCK_A
+
+
+def starts_b():
+    me = device_index()
+    low = me >= DOWN_OWNER
+    first = jnp.where(low, FIRST_DOWN, FIRST_MLP)
+    step = jnp.where(low, USED_DOWN, BLOCK_B)
+    return -((me * SHARD - first) % step), step
+
+
+PLAN_A = (BLOCK_A, block_a_range, first_block_a, 5, starts_a)
+PLAN_B = (BLOCK_B, block_b_range, first_block_b, 4, starts_b)
 
 
 def device_index():
     return lax.axis_index("fsdp") * lax.axis_size("dp") + lax.axis_index("dp")
 
 
-def spread(shard, block_rows, block_range):
-    me = device_index()
-    rounds, first_row = plan_rounds(block_range, lambda block: block)
+def cut_pieces(shard, plan):
+    block_rows, _, _, count, starts = plan
     padded = jnp.pad(shard, ((block_rows, block_rows), (0, 0)))
+    first, step = starts()
+    return [
+        lax.dynamic_slice_in_dim(padded, block_rows + first + k * step, block_rows, 0)
+        for k in range(count)
+    ]
+
+
+def spread(pieces, plan):
+    _, block_range, first_block, count, _ = plan
+    rounds = plan_rounds(block_range, first_block, count, lambda block: block)
     total = None
-    for pairs in rounds:
-        starts = np.zeros(DEVICES, np.int32)
-        for owner, device in pairs:
-            starts[owner] = block_rows + first_row[owner, device]
-        piece = lax.dynamic_slice_in_dim(padded, jnp.asarray(starts)[me], block_rows, 0)
+    for piece, pairs in zip(pieces, rounds, strict=True):
         got = lax.ppermute(piece, ("fsdp", "dp"), pairs)
         total = got if total is None else total + got
     return total
 
 
-def collect(buffer, block, block_rows, block_range, places):
-    me = device_index()
-    rounds, first_row = plan_rounds(block_range, lambda block: device_of(places, block))
-    for pairs in rounds:
-        starts = np.zeros(DEVICES, np.int32)
-        for owner, device in pairs:
-            starts[owner] = BLOCK_B + first_row[owner, device]
-        got = lax.ppermute(block, ("fsdp", "dp"), [(device, owner) for owner, device in pairs])
-        start = jnp.asarray(starts)[me]
-        held = lax.dynamic_slice_in_dim(buffer, start, block_rows, 0)
-        buffer = lax.dynamic_update_slice_in_dim(
-            buffer, held + got.astype(buffer.dtype), start, 0
-        )
-    return buffer
+def send_back(block, plan, places):
+    _, block_range, first_block, count, _ = plan
+    rounds = plan_rounds(block_range, first_block, count, lambda block: device_of(places, block))
+    return [
+        lax.ppermute(block, ("fsdp", "dp"), [(device, owner) for owner, device in pairs])
+        for pairs in rounds
+    ]
 
 
 def to_tiles(rows, chunks):
@@ -403,11 +403,10 @@
     return 2 * places[core][block] + core
 
 
-def kind_table(places, first_of_second):
-    table = np.zeros(DEVICES, np.int32)
-    for block in range(DEVICES):
-        table[device_of(places, block)] = int(block >= first_of_second)
-    return table
+def is_kind(places, first_of_second):
+    mask = sum(1 << device_of(places, block) for block in range(first_of_second, DEVICES))
+    bits = jnp.uint32(mask) >> device_index().astype(jnp.uint32)
+    return bits % 2 == 1
 
 
 def add_low(a, b):
@@ -425,23 +424,42 @@
     return pick(a, 1 - y, 0), pick(b, 1 - x, 1)
 
 
-def reduce_planes(grads, sends, block_rows):
+def over_planes(sends, axes):
+    return [lax.ppermute(send, "fsdp", axis) for send, axis in zip(sends, axes, strict=True)]
+
+
+def second_sends(grads, arrived, block_rows):
     f = lax.axis_index("fsdp")
     y, x = f // 2, f % 2
     a, b = [part.reshape(2, 2, 4, block_rows // 2, 128) for part in grads]
-    a = add_low(pick(a, y, 0), lax.ppermute(sends[0], "fsdp", SWAP_Y))
-    b = add_low(pick(b, x, 1), lax.ppermute(sends[1], "fsdp", SWAP_X))
-    a = add_low(pick(a, x, 0), lax.ppermute(pick(a, 1 - x, 0), "fsdp", SWAP_X))
-    b = add_low(pick(b, y, 0), lax.ppermute(pick(b, 1 - y, 0), "fsdp", SWAP_Y))
-    return jnp.concatenate([a, b], axis=1)
-
-
-def reduce_line(planes):
+    a = add_low(pick(a, y, 0), arrived[0])
+    b = add_low(pick(b, x, 1), arrived[1])
+    return (pick(a, x, 0), pick(b, y, 0)), (pick(a, 1 - x, 0), pick(b, 1 - y, 0))
+
+
+def plane_sums(kept, arrived):
+    return jnp.concatenate([add_low(k, a) for k, a in zip(kept, arrived, strict=True)], axis=1)
+
+
+def after(value, *others):
+    return lax.optimization_barrier((value, others))[0]
+
+
+def line_sends(planes):
     z = lax.axis_index("dp") // 2
-    total = pick(planes, z, 0).astype(jnp.float32)
-    for k in range(1, 4):
-        swap = [(d, d ^ (2 * k)) for d in range(8)]
-        total += lax.ppermute(pick(planes, z ^ k, 0), "dp", swap).astype(jnp.float32)
+    return [pick(planes, z ^ k, 0) for k in range(4)]
+
+
+def from_line(sends):
+    return [
+        lax.ppermute(sends[k], "dp", [(d, d ^ (2 * k)) for d in range(8)]) for k in range(1, 4)
+    ]
+
+
+def sum_line(own, others):
+    total = own.astype(jnp.float32)
+    for other in others:
+        total += other.astype(jnp.float32)
     return total
 
 
@@ -473,63 +491,61 @@
     return terms[0] + sum(send(terms[k], 2 * k, range(4)) for k in range(1, 4))
 
 
-def exchange_relative(pieces):
-    pieces = pieces.reshape(4, 8, *pieces.shape[1:])
-    parts = [pieces[:, 0]] + [
-        lax.ppermute(pieces[:, k], "dp", [(d, d ^ k) for d in range(8)]) for k in range(1, 8)
-    ]
-    part = jnp.stack(parts, axis=1)
-    parts = [part[0]] + [
-        lax.ppermute(part[k], "fsdp", [(f, f ^ k) for f in range(4)]) for k in range(1, 4)
-    ]
-    return jnp.stack(parts).reshape(DEVICES, *pieces.shape[2:])
-
-
-def mlp_kernel(flat_first, blocks, used_tiles, block_tiles):
-    def body(x_ref, g_ref, bias_g_ref, bias_u_ref, gate_w, up_w, flat_ref, *rest):
-        hid_ref, gg_ref, gu_ref, branch_ref, gin_ref, sum_g_ref, sum_u_ref, down_ref, sem = rest
-        f32, bf16 = jnp.float32, jnp.bfloat16
+def mlp_both_ways(x, g, bias, gathered):
+    f32, bf16 = jnp.float32, jnp.bfloat16
+    rows = x.shape[0]
+    steps = FF // 256
+    full = BLOCK_B // 8
+    used = USED_DOWN // 8
+    wide = 2 * FF // 128
+    chunks = D // 128
+    across = (((1,), (1,)), ((), ()))
+
+    def body(x_ref, g_ref, bias_g_ref, bias_u_ref, source, *rest):
+        hid_ref, gg_ref, gu_ref, branch_ref, gin_ref, sum_g_ref, sum_u_ref, *rest = rest
+        mix_ref, down_ref, sem = rest
         step = pl.program_id(0)
 
-        def copies():
-            return [
-                pltpu.make_async_copy(
-                    flat_ref.at[pl.ds(flat_first + block_tiles * i, used_tiles)],
-                    down_ref.at[pl.ds(used_tiles * i, used_tiles)],
-                    sem.at[i],
-                )
-                for i in range(blocks)
-            ]
+        def each(act):
+            stride = (BLOCK_A + BLOCK_B) // 8
+            for i in range(DEVICES):
+                first = i * stride + BLOCK_A // 8
+                if i < MLP_BLOCKS:
+                    piece = source.at[pl.ds(first, full)]
+                    flat = mix_ref.reshape(MLP_BLOCKS * full, 8, 128)
+                    target = flat.at[pl.ds(i * full, full)]
+                else:
+                    piece = source.at[pl.ds(first, used)]
+                    target = down_ref.at[pl.ds((i - MLP_BLOCKS) * used, used)]
+                act(pltpu.make_async_copy(piece, target, sem.at[i]))
 
         @pl.when(step == 0)
         def _():
-            for copy in copies():
-                copy.start()
-
-        def columns(ref):
-            return jnp.concatenate([ref[:, i].reshape(D, 128) for i in range(2)], axis=1)
+            each(lambda copy: copy.start())
+            branch_ref[...] = jnp.zeros_like(branch_ref)
+            gin_ref[...] = jnp.zeros_like(gin_ref)
+            each(lambda copy: copy.wait())
+
+        def columns(first):
+            return jnp.concatenate(
+                [
+                    mix_ref[: D // 8, first + i].reshape(D, 128)
+                    for i in range(2)
+                ],
+                axis=1,
+            )
 
         x = x_ref[...]
-        w_gate, w_up = columns(gate_w), columns(up_w)
+        w_gate, w_up = columns(2 * step), columns(wide // 2 + 2 * step)
         gate = jnp.dot(x, w_gate, preferred_element_type=f32) + bias_g_ref[...]
         up = jnp.dot(x, w_up, preferred_element_type=f32) + bias_u_ref[...]
         sigma = jax.nn.sigmoid(gate)
         silu = gate * sigma
         hid = (silu * up).astype(bf16)
         hid_ref[...] = hid
-
-        @pl.when(step == 0)
-        def _():
-            for copy in copies():
-                copy.wait()
-            branch_ref[...] = jnp.zeros_like(branch_ref)
-            gin_ref[...] = jnp.zeros_like(gin_ref)
-
-        chunks = D // 128
-        rows = down_ref[pl.ds(step * 32 * chunks, 32 * chunks)].reshape(32, chunks, 8, 128)
-        w_down = jnp.concatenate([rows[:, j].reshape(256, 128) for j in range(chunks)], axis=1)
+        low_rows = down_ref[pl.ds(step * 32 * chunks, 32 * chunks)].reshape(32, chunks, 8, 128)
+        w_down = jnp.concatenate([low_rows[:, j].reshape(256, 128) for j in range(chunks)], axis=1)
         branch_ref[...] += jnp.dot(hid, w_down, preferred_element_type=f32)
-        across = (((1,), (1,)), ((), ()))
         g_hid = lax.dot_general(g_ref[...], w_down, across, preferred_element_type=f32)
         g_gate = (g_hid * up * sigma * (1.0 + gate * (1.0 - sigma))).astype(bf16)
         g_up = (g_hid * silu).astype(bf16)
@@ -541,29 +557,17 @@
             g_gate, w_gate, across, preferred_element_type=f32
         ) + lax.dot_general(g_up, w_up, across, preferred_element_type=f32)
 
-    return body
-
-
-def mlp_both_ways(x, g, bias, all_b):
-    f32, bf16 = jnp.float32, jnp.bfloat16
-    rows = x.shape[0]
-    blocks = DEVICES - MLP_BLOCKS
-    used = USED_DOWN // 8
-    steps = FF // 256
-    tiles = all_b.reshape(-1, 2 * FF // 128, 8, 128)
     whole = pl.BlockSpec((rows, D), lambda t: (0, 0))
     part = pl.BlockSpec((rows, 256), lambda t: (0, t))
     line = pl.BlockSpec((1, 256), lambda t: (0, t))
     return pl.pallas_call(
-        mlp_kernel(MLP_BLOCKS * BLOCK_B // 8, blocks, used, BLOCK_B // 8),
+        body,
         grid=(steps,),
         in_specs=[
             whole,
             whole,
             line,
             pl.BlockSpec((1, 256), lambda t: (0, steps + t)),
-            pl.BlockSpec((D // 8, 2, 8, 128), lambda t: (0, t, 0, 0)),
-            pl.BlockSpec((D // 8, 2, 8, 128), lambda t: (0, steps + t, 0, 0)),
             pl.BlockSpec(memory_space=pl.ANY),
         ],
         out_specs=[part, part, part, whole, whole, line, line],
@@ -571,15 +575,16 @@
         + [jax.ShapeDtypeStruct((rows, D), f32)] * 2
         + [jax.ShapeDtypeStruct((1, FF), f32)] * 2,
         scratch_shapes=[
-            pltpu.VMEM((blocks * used, 8, 128), bf16),
-            pltpu.SemaphoreType.DMA((blocks,)),
+            pltpu.VMEM((MLP_BLOCKS * full // wide, wide, 8, 128), bf16),
+            pltpu.VMEM(((DEVICES - MLP_BLOCKS) * used, 8, 128), bf16),
+            pltpu.SemaphoreType.DMA((DEVICES,)),
         ],
         cost_estimate=pl.CostEstimate(
             flops=12 * rows * D * FF, bytes_accessed=30_000_000, transcendentals=rows * FF
         ),
-        compiler_params=pltpu.CompilerParams(vmem_limit_bytes=56 << 20),
+        compiler_params=pltpu.CompilerParams(vmem_limit_bytes=46 << 20),
         name="mlp_both_ways",
-    )(x, g, bias, bias, tiles, tiles, all_b.reshape(-1, 8, 128))
+    )(x, g, bias, bias, gathered)
 
 
 def pair_product(xo, xp, go, gp):
@@ -595,13 +600,13 @@
 
 
 def grads_b_core_0(in_b, g_gate, g_up):
-    def body(xo, xp, gog, gpg, gou, gpu, out_ref):
-        for half, go, gp in ((0, gog, gpg), (1, gou, gpu)):
+    def body(xo, xp, gog, gpg, gou, gpu, *outs):
+        for out_ref, go, gp in ((outs[0], gog, gpg), (outs[1], gou, gpu)):
             value = pair_product(xo, xp, go, gp)
             for j in range(4):
                 part = value[:, 128 * j : 128 * (j + 1)].reshape(16, 7, 8, 128)
                 for block in range(16):
-                    out_ref[half, PLACE_B[0][block], :, j] = part[block]
+                    out_ref[PLACE_B[0][block], :, j] = part[block]
 
     rows = in_b[0].shape[0]
     high = 16 * 56
@@ -611,12 +616,12 @@
         body,
         grid=(FF // 512,),
         in_specs=[x_spec] * 2 + [g_spec] * 4,
-        out_specs=pl.BlockSpec((2, 16, 7, 4, 8, 128), lambda t: (0, 0, 0, t, 0, 0)),
-        out_shape=jax.ShapeDtypeStruct((2, 16, 7, FF // 128, 8, 128), jnp.bfloat16),
-        compiler_params=pltpu.CompilerParams(vmem_limit_bytes=56 << 20),
+        out_specs=[pl.BlockSpec((16, 7, 4, 8, 128), lambda t: (0, 0, t, 0, 0))] * 2,
+        out_shape=[jax.ShapeDtypeStruct((16, 7, FF // 128, 8, 128), jnp.bfloat16)] * 2,
+        compiler_params=pltpu.CompilerParams(vmem_limit_bytes=44 << 20),
         name="grads_b_core_0",
     )(*in_b, *g_gate, *g_up)
-    return out.reshape(2, -1, 128)
+    return [part.reshape(-1, 128) for part in out]
 
 
 def grads_b_core_1(in_b, g_gate, g_up, hidden, g_branch):
@@ -633,32 +638,32 @@
 
     place = PLACE_B[1]
 
-    def body(place_ref, xo, xp, gog, gpg, gou, gpu, ho, hp, go, gp, out_ref):
+    def body(place_ref, xo, xp, gog, gpg, gou, gpu, ho, hp, go, gp, *outs):
         step = pl.program_id(0)
 
         @pl.when(step == 0)
         def _():
             for group in range(mlp_groups, groups):
                 first = place[16 + group // 7] * half_tiles + group % 7 * (FF // 128)
-                for half in range(2):
-                    out_ref[half, pl.ds(first, FF // 128)] = jnp.zeros((FF // 128, 8, 128), bf16)
+                for out_ref in outs:
+                    out_ref[pl.ds(first, FF // 128)] = jnp.zeros((FF // 128, 8, 128), bf16)
             for block in range(down_blocks):
                 for half in range(2):
                     used = min(half_groups, FF // 8 - (2 * block + half) * half_groups) * 9
                     first = place[MLP_BLOCKS + block] * half_tiles + used
                     rest = half_tiles - used
-                    out_ref[half, pl.ds(first, rest)] = jnp.zeros((rest, 8, 128), bf16)
+                    outs[half][pl.ds(first, rest)] = jnp.zeros((rest, 8, 128), bf16)
 
         @pl.when(step < mlp_steps)
         def _():
-            for half, g_own, g_par in ((0, gog, gpg), (1, gou, gpu)):
+            for out_ref, g_own, g_par in ((outs[0], gog, gpg), (outs[1], gou, gpu)):
                 value = pair_product(xo, xp, g_own, g_par)
                 skip = value.shape[0] - mlp_groups * 8
                 for group in range(mlp_groups):
                     first = place[16 + group // 7] * half_tiles + group % 7 * (FF // 128)
                     store_tiles(
                         out_ref,
-                        (half,),
+                        (),
                         first + step * 4,
                         value[skip + 8 * group : skip + 8 * group + 8],
                     )
@@ -670,13 +675,19 @@
                 at = (step - mlp_steps) * (wide // 8) + group
                 part = at // half_groups
                 first = place_ref[part // 2] * half_tiles + (at % half_groups) * 9
-                store_tiles(out_ref, (part % 2,), first, value[8 * group : 8 * group + 8])
+                piece = value[8 * group : 8 * group + 8]
+
+                def put(out_ref, first=first, piece=piece):
+                    store_tiles(out_ref, (), first, piece)
+
+                pl.when(part % 2 == 0)(lambda put=put: put(outs[0]))
+                pl.when(part % 2 == 1)(lambda put=put: put(outs[1]))
 
     x_spec = pl.BlockSpec((rows, 384), lambda t: (0, 2))
     g_spec = pl.BlockSpec((rows, 512), lambda t: (0, jnp.minimum(t, mlp_steps - 1)))
     h_spec = pl.BlockSpec((rows, wide), lambda t: (0, jnp.maximum(t - mlp_steps, 0)))
     b_spec = pl.BlockSpec((rows, D), lambda t: (0, 0))
-    shape = (2, 16 * half_tiles, 8, 128)
+    shape = (16 * half_tiles, 8, 128)
     down_place = jnp.asarray([place[MLP_BLOCKS + i] for i in range(down_blocks)], jnp.int32)
     out = pl.pallas_call(
         body,
@@ -686,12 +697,12 @@
         + [g_spec] * 4
         + [h_spec] * 2
         + [b_spec] * 2,
-        out_specs=pl.BlockSpec(shape, lambda t: (0, 0, 0, 0)),
-        out_shape=jax.ShapeDtypeStruct(shape, bf16),
-        compiler_params=pltpu.CompilerParams(vmem_limit_bytes=56 << 20),
+        out_specs=[pl.BlockSpec(shape, lambda t: (0, 0, 0))] * 2,
+        out_shape=[jax.ShapeDtypeStruct(shape, bf16)] * 2,
+        compiler_params=pltpu.CompilerParams(vmem_limit_bytes=44 << 20),
         name="grads_b_core_1",
     )(down_place, *in_b, *g_gate, *g_up, *hidden, *g_branch)
-    return out.reshape(2, -1, 128)
+    return [part.reshape(-1, 128) for part in out]
 
 
 def grads_a(core, in_a, g_proj, att, g_branch):
@@ -699,24 +710,24 @@
     steps = 3 * D // 384
     place = PLACE_A[core]
 
-    def store_qkv(value, first_block, step, out_ref):
+    def store_qkv(value, first_block, step, outs):
         for group in range(48):
             block, half, low = first_block + group // 6, group // 3 % 2, group % 3
             store_tiles(
-                out_ref,
-                (half, place[block]),
+                outs[half],
+                (place[block],),
                 low * 27 + step * 3,
                 value[8 * group : 8 * group + 8],
             )
 
-    def body(xo, xp, go, gp, zo, zp, bo, bp, out_ref):
+    def body(xo, xp, go, gp, zo, zp, bo, bp, *outs):
         step = pl.program_id(0)
 
         @pl.when(step < steps)
         def _():
-            store_qkv(pair_product(xo, xp, go, gp), 8 * core, step, out_ref)
+            store_qkv(pair_product(xo, xp, go, gp), 8 * core, step, outs)
             if core == 0:
-                store_qkv(pair_product(zo, zp, go, gp), 16, step, out_ref)
+                store_qkv(pair_product(zo, zp, go, gp), 16, step, outs)
 
         if core == 1:
 
@@ -726,8 +737,8 @@
                 for group in range(144):
                     block, half, low = QKV_BLOCKS + group // 18, group // 9 % 2, group % 9
                     store_tiles(
-                        out_ref,
-                        (half, place[block]),
+                        outs[half],
+                        (place[block],),
                         low * 9 + (step - steps) * 3,
                         value[8 * group : 8 * group + 8],
                     )
@@ -741,33 +752,262 @@
         z_spec, z = pl.BlockSpec((rows, D), lambda t: (0, 0)), att
         b_spec = pl.BlockSpec((rows, 384), lambda t: (0, jnp.maximum(t - steps, 0)))
         count = steps + D // 384
-    shape = (2, 16, 81, 8, 128)
+    shape = (16, 81, 8, 128)
     out = pl.pallas_call(
         body,
         grid=(count,),
         in_specs=[x_spec] * 2 + [g_spec] * 2 + [z_spec] * 2 + [b_spec] * 2,
-        out_specs=pl.BlockSpec(shape, lambda t: (0, 0, 0, 0, 0)),
-        out_shape=jax.ShapeDtypeStruct(shape, jnp.bfloat16),
-        compiler_params=pltpu.CompilerParams(vmem_limit_bytes=56 << 20),
+        out_specs=[pl.BlockSpec(shape, lambda t: (0, 0, 0, 0))] * 2,
+        out_shape=[jax.ShapeDtypeStruct(shape, jnp.bfloat16)] * 2,
+        compiler_params=pltpu.CompilerParams(vmem_limit_bytes=44 << 20),
         name=f"grads_a_core_{core}",
     )(*in_a, *g_proj, *z, *g_branch)
-    return out.reshape(2, -1, 128)
-
-
-def gathered_weights(flat_a, flat_b):
-    axes = ("fsdp", "dp")
+    return [part.reshape(-1, 128) for part in out]
+
+
+def gathered_weights(pieces_a, pieces_b):
     me = device_index()
-    block_a = spread(flat_a, BLOCK_A, block_a_range)
+    block_a = spread(pieces_a, PLAN_A)
     block_a = jnp.where(me < QKV_BLOCKS, to_tiles(block_a, 27), to_tiles(block_a, 9))
-    all_a = lax.all_gather(block_a, axes, axis=0, tiled=True)
-    block_b = spread(flat_b, BLOCK_B, block_b_range)
+    block_b = spread(pieces_b, PLAN_B)
     block_b = jnp.where(
         me < MLP_BLOCKS,
         to_tiles(block_b, 48),
         jnp.pad(to_tiles(block_b[:USED_DOWN], 9), ((0, BLOCK_B - USED_DOWN), (0, 0))),
     )
-    all_b = lax.all_gather(block_b, axes, axis=0, tiled=True)
-    return all_a, all_b
+    block = jnp.concatenate([block_a, block_b])
+    return lax.all_gather(block, ("fsdp", "dp"), axis=0, tiled=True).reshape(-1, 8, 128)
+
+
+def head_indicator():
+    feature = lax.broadcasted_iota(jnp.int32, (D, 128), 0)
+    head = lax.broadcasted_iota(jnp.int32, (D, 128), 1)
+    return ((feature >= head * HEAD_DIM) & (feature < (head + 1) * HEAD_DIM)).astype(jnp.bfloat16)
+
+
+def two_parts(value):
+    high = value.astype(jnp.bfloat16)
+    return high, (value - high.astype(jnp.float32)).astype(jnp.bfloat16)
+
+
+def head_means(value, indicator):
+    high, low = two_parts(value)
+    total = jnp.dot(high, indicator, preferred_element_type=jnp.float32)
+    total += jnp.dot(low, indicator, preferred_element_type=jnp.float32)
+    return total * (1.0 / HEAD_DIM)
+
+
+def over_heads(value, indicator):
+    high, low = two_parts(value)
+    across = (((1,), (1,)), ((), ()))
+    total = lax.dot_general(high, indicator, across, preferred_element_type=jnp.float32)
+    return total + lax.dot_general(low, indicator, across, preferred_element_type=jnp.float32)
+
+
+def turned(value):
+    quarter = HEAD_DIM // 4
+    feature = lax.broadcasted_iota(jnp.int32, value.shape, 1) % (2 * quarter)
+    ahead = pltpu.roll(value, D - quarter, 1)
+    behind = pltpu.roll(value, quarter, 1)
+    return jnp.where(feature < quarter, -ahead, behind)
+
+
+def heads_of(ref):
+    return [ref[:, HEAD_DIM * h : HEAD_DIM * (h + 1)] for h in range(HEADS)]
+
+
+ACROSS = (((1,), (1,)), ((), ()))
+DOWN = (((0,), (0,)), ((), ()))
+
+
+def attention_forward(projected, cosines, sines):
+    f32, bf16 = jnp.float32, jnp.bfloat16
+    rows = projected.shape[0]
+    length = cosines.shape[0]
+    scale = 1.0 / math.sqrt(HEAD_DIM)
+
+    def body(proj_ref, cos_ref, sin_ref, ind_ref, q_ref, k_ref, v_ref, att_ref, log_ref):
+        indicator = ind_ref[...]
+        for part, ref in ((0, q_ref), (1, k_ref)):
+            value = proj_ref[:, D * part : D * (part + 1)]
+            inverse = lax.rsqrt(head_means(value * value, indicator) + eps_norm)
+            norm = value * over_heads(inverse, indicator)
+            ref[...] = (norm * cos_ref[...] + turned(norm) * sin_ref[...]).astype(bf16)
+        v_ref[...] = proj_ref[:, 2 * D :].astype(bf16)
+        logs = []
+        for h in range(HEADS):
+            at = slice(HEAD_DIM * h, HEAD_DIM * (h + 1))
+            scores = (
+                lax.dot_general(q_ref[:, at], k_ref[:, at], ACROSS, preferred_element_type=f32)
+                * scale
+            )
+            top = jnp.max(scores, axis=1, keepdims=True)
+            log_total = top + jnp.log(jnp.sum(jnp.exp(scores - top), axis=1, keepdims=True))
+            probs = jnp.exp(scores - log_total).astype(bf16)
+            att_ref[:, at] = jnp.dot(probs, v_ref[:, at], preferred_element_type=f32).astype(bf16)
+            log_ref[:, h : h + 1] = log_total
+
+    wide = pl.BlockSpec((length, D), lambda i: (i, 0))
+    table = pl.BlockSpec((length, D), lambda i: (0, 0))
+    return pl.pallas_call(
+        body,
+        grid=(rows // length,),
+        in_specs=[
+            pl.BlockSpec((length, 3 * D), lambda i: (i, 0)),
+            table,
+            table,
+            pl.BlockSpec((D, 128), lambda i: (0, 0)),
+        ],
+        out_specs=[wide] * 4 + [pl.BlockSpec((length, HEADS), lambda i: (i, 0))],
+        out_shape=[jax.ShapeDtypeStruct((rows, D), bf16)] * 4
+        + [jax.ShapeDtypeStruct((rows, HEADS), f32)],
+        cost_estimate=pl.CostEstimate(
+            flops=8 * rows * length * D, bytes_accessed=20_000_000, transcendentals=40_000_000
+        ),
+        compiler_params=pltpu.CompilerParams(vmem_limit_bytes=44 << 20),
+        name="attention_forward",
+    )(projected, cosines, sines, head_indicator())
+
+
+def attention_backward(projected, queries, keys, values, log_total, g_attended, cosines, sines):
+    f32, bf16 = jnp.float32, jnp.bfloat16
+    rows = projected.shape[0]
+    length = cosines.shape[0]
+    scale = 1.0 / math.sqrt(HEAD_DIM)
+
+    def body(proj_ref, q_ref, k_ref, v_ref, log_ref, g_ref, cos_ref, sin_ref, ind_ref, *rest):
+        out_ref, sum_ref, gq_ref, gk_ref, gv_ref = rest
+        for h in range(HEADS):
+            at = slice(HEAD_DIM * h, HEAD_DIM * (h + 1))
+            q, k, v, g = q_ref[:, at], k_ref[:, at], v_ref[:, at], g_ref[:, at]
+            scores = lax.dot_general(q, k, ACROSS, preferred_element_type=f32) * scale
+            probs = jnp.exp(scores - log_ref[:, h : h + 1])
+            g_probs = lax.dot_general(g, v, ACROSS, preferred_element_type=f32)
+            gv_ref[:, at] = lax.dot_general(
+                probs.astype(bf16), g, DOWN, preferred_element_type=f32
+            )
+            inner = jnp.sum(probs * g_probs, axis=1, keepdims=True)
+            g_scores = (probs * (g_probs - inner)).astype(bf16)
+            gq_ref[:, at] = jnp.dot(g_scores, k, preferred_element_type=f32) * scale
+            gk_ref[:, at] = (
+                lax.dot_general(g_scores, q, DOWN, preferred_element_type=f32) * scale
+            )
+        indicator = ind_ref[...]
+        for part, ref in ((0, gq_ref), (1, gk_ref)):
+            value = proj_ref[:, D * part : D * (part + 1)]
+            inverse = over_heads(
+                lax.rsqrt(head_means(value * value, indicator) + eps_norm), indicator
+            )
+            norm = value * inverse
+            back = ref[...] * cos_ref[...] - turned(ref[...]) * sin_ref[...]
+            mean = over_heads(head_means(back * norm, indicator), indicator)
+            out_ref[:, D * part : D * (part + 1)] = (inverse * (back - norm * mean)).astype(bf16)
+        out_ref[:, 2 * D :] = gv_ref[...].astype(bf16)
+        sum_ref[0] = jnp.sum(out_ref[...].astype(f32), axis=0, keepdims=True)
+
+    wide = pl.BlockSpec((length, D), lambda i: (i, 0))
+    table = pl.BlockSpec((length, D), lambda i: (0, 0))
+    images = rows // length
+    return pl.pallas_call(
+        body,
+        grid=(images,),
+        in_specs=[
+            pl.BlockSpec((length, 2 * D), lambda i: (i, 0)),
+            wide,
+            wide,
+            wide,
+            pl.BlockSpec((length, HEADS), lambda i: (i, 0)),
+            wide,
+            table,
+            table,
+            pl.BlockSpec((D, 128), lambda i: (0, 0)),
+        ],
+        out_specs=[
+            pl.BlockSpec((length, 3 * D), lambda i: (i, 0)),
+            pl.BlockSpec((1, 1, 3 * D), lambda i: (i, 0, 0)),
+        ],
+        out_shape=[
+            jax.ShapeDtypeStruct((rows, 3 * D), bf16),
+            jax.ShapeDtypeStruct((images, 1, 3 * D), f32),
+        ],
+        scratch_shapes=[pltpu.VMEM((length, D), f32)] * 3,
+        cost_estimate=pl.CostEstimate(flops=1000, bytes_accessed=1000, transcendentals=0),
+        compiler_params=pltpu.CompilerParams(vmem_limit_bytes=44 << 20),
+        name="attention_backward",
+    )(projected, queries, keys, values, log_total, g_attended, cosines, sines, head_indicator())
+
+
+def split_a(gathered):
+    block = BLOCK_A // 8
+
+    def body(all_ref, qkv_ref, out_ref, sem):
+        copies = []
+        for i in range(DEVICES):
+            ref, first = (qkv_ref, 0) if i < QKV_BLOCKS else (out_ref, QKV_BLOCKS)
+            copies.append(
+                pltpu.make_async_copy(
+                    all_ref.at[pl.ds(i * (BLOCK_A + BLOCK_B) // 8, block)],
+                    ref.at[pl.ds((i - first) * block, block)],
+                    sem.at[i],
+                )
+            )
+        for copy in copies:
+            copy.start()
+        for copy in copies:
+            copy.wait()
+
+    w_qkv, w_out = pl.pallas_call(
+        body,
+        in_specs=[pl.BlockSpec(memory_space=pl.ANY)],
+        out_specs=[pl.BlockSpec(memory_space=pltpu.VMEM)] * 2,
+        out_shape=[
+            jax.ShapeDtypeStruct((ROWS_QKV // 8, 8, 128), jnp.bfloat16),
+            jax.ShapeDtypeStruct((ROWS_OUT // 8, 8, 128), jnp.bfloat16),
+        ],
+        scratch_shapes=[pltpu.SemaphoreType.DMA((DEVICES,))],
+        compiler_params=pltpu.CompilerParams(vmem_limit_bytes=40 << 20),
+        name="split_a",
+    )(gathered)
+    return matrix_of_tiles(w_qkv, D, 3 * D), matrix_of_tiles(w_out, D, D)
+
+
+def owned_rows(back_a, back_b, grad_ada):
+    first_a, step_a = starts_a()
+    first_b, step_b = starts_b()
+    me = device_index()
+    numbers = jnp.stack(
+        [jnp.asarray(v, jnp.int32) for v in (first_a, step_a, first_b, step_b, me * SHARD)]
+    )
+    total = SHARD + 2 * BLOCK_B
+
+    def body(numbers_ref, *refs):
+        out_ref, sum_ref = refs[-2:]
+        sum_ref[...] = jnp.zeros_like(sum_ref)
+        for refs_of, at, rows in (
+            (refs[: len(back_b)], 2, BLOCK_B),
+            (refs[len(back_b) : len(back_b) + len(back_a)], 0, BLOCK_A),
+        ):
+            for k, ref in enumerate(refs_of):
+                start = BLOCK_B + numbers_ref[at] + k * numbers_ref[at + 1]
+                start = pl.multiple_of(jnp.clip(start, 0, total - rows), 8)
+                sum_ref[pl.ds(start, rows)] += ref[...].astype(jnp.float32)
+        row = numbers_ref[4] + lax.broadcasted_iota(jnp.int32, (SHARD, 128), 0)
+        out_ref[...] = jnp.where(
+            (row >= FIRST_ADA) & (row < FIRST_DOWN),
+            refs[-3][...],
+            sum_ref[pl.ds(BLOCK_B, SHARD)],
+        )
+
+    return pl.pallas_call(
+        body,
+        in_specs=[pl.BlockSpec(memory_space=pltpu.SMEM)]
+        + [pl.BlockSpec(memory_space=pltpu.VMEM)] * (len(back_a) + len(back_b) + 1),
+        out_specs=pl.BlockSpec(memory_space=pltpu.VMEM),
+        out_shape=jax.ShapeDtypeStruct((SHARD, 128), jnp.float32),
+        scratch_shapes=[pltpu.VMEM((total, 128), jnp.float32)],
+        compiler_params=pltpu.CompilerParams(vmem_limit_bytes=40 << 20),
+        name="owned_rows",
+    )(numbers, *back_b, *back_a, grad_ada)
 
 
 def on_device_32(tokens, conditions, cotangent, slot_mask, weight_flat, bias_flat):
@@ -780,8 +1020,6 @@
     images = slots * DEVICES
     length = GRID * GRID
     rows_all = slots * length
-    scale = 1.0 / math.sqrt(HEAD_DIM)
-    heads_shape = (slots, length, HEADS, HEAD_DIM)
     cond_count = slots * D
     bias_count = bias_flat.shape[0]
     packed_rows = -(-(cond_count + bias_count) // 128)
@@ -792,8 +1030,10 @@
             jnp.zeros(packed_rows * 128 - cond_count - bias_count, bf16),
         ]
     ).reshape(packed_rows, 128)
-    column, flat_a = lax.optimization_barrier((gather_column(packed), weight_flat))
-    packed_all = gather_columns(column).reshape(DEVICES, -1)
+    pieces_a = cut_pieces(weight_flat, PLAN_A)
+    packed, pieces_a = lax.optimization_barrier((packed, pieces_a))
+    gathered = gathered_weights(pieces_a, cut_pieces(weight_flat, PLAN_B))
+    packed_all = gather_columns(gather_column(packed)).reshape(DEVICES, -1)
     cond_all = packed_all[:, :cond_count].reshape(images, D).astype(f32)
     places = lax.broadcasted_iota(jnp.int32, (DEVICES, DEVICES), 0)
     others = lax.broadcasted_iota(jnp.int32, (DEVICES, DEVICES), 1)
@@ -815,14 +1055,12 @@
     )
     terms = jnp.einsum("km,kn->mn", cond_rows, ada_local, preferred_element_type=f32)
     modulation = sum_to_owners(terms.reshape(DEVICES, slots, 6 * D)) + b_ada
-    all_a, all_b = gathered_weights(flat_a, flat_a)
-    w_qkv = matrix_of_tiles(all_a[:ROWS_QKV], D, 3 * D)
-    w_out = matrix_of_tiles(all_a[ROWS_QKV:], D, D)
+    w_qkv, w_out = split_a(gathered)
 
     def share(array):
         return (array, lax.ppermute(array, "dp", SWAP_CORE))
 
-    cosines, sines = rope_tables()
+    cosines, sines = [jnp.tile(table[:, 0], (1, HEADS)) for table in rope_tables()]
     mask_f = slot_mask.astype(f32)[:, None, None]
     x_f = tokens.astype(f32).reshape(slots, length, D)
     shift_a, scale_a, gate_a, shift_b, scale_b, gate_b = [
@@ -832,23 +1070,8 @@
     g_branch_b = (gate_b * g_out).astype(bf16).reshape(rows_all, D)
     normed_a, inv_a = norm_parts(x_f)
     input_a = (normed_a * (1.0 + scale_a) + shift_a).astype(bf16).reshape(rows_all, D)
-    projected = (jnp.dot(input_a, w_qkv, preferred_element_type=f32) + b_qkv).reshape(
-        slots, length, 3 * D
-    )
-    q_norm, inv_q = rms_parts(projected[..., :D].reshape(heads_shape))
-    k_norm, inv_k = rms_parts(projected[..., D : 2 * D].reshape(heads_shape))
-    queries = (q_norm * cosines + turn_half(q_norm) * sines).astype(bf16)
-    keys = (k_norm * cosines + turn_half(k_norm) * sines).astype(bf16)
-    values = projected[..., 2 * D :].reshape(heads_shape).astype(bf16)
-    scores = jnp.einsum("slhe,smhe->shlm", queries, keys, preferred_element_type=f32) * scale
-    row_max = jnp.max(scores, -1, keepdims=True)
-    log_total = row_max + jnp.log(jnp.sum(jnp.exp(scores - row_max), -1, keepdims=True))
-    probs_low = jnp.exp(scores - log_total).astype(bf16)
-    attended = (
-        jnp.einsum("shlm,smhe->slhe", probs_low, values, preferred_element_type=f32)
-        .astype(bf16)
-        .reshape(rows_all, D)
-    )
+    projected = jnp.dot(input_a, w_qkv, preferred_element_type=f32) + b_qkv
+    queries, keys, values, attended, log_total = attention_forward(projected, cosines, sines)
     branch_a = (jnp.dot(attended, w_out, preferred_element_type=f32) + b_out).reshape(
         slots, length, D
     )
@@ -857,17 +1080,11 @@
     input_b = (normed_b * (1.0 + scale_b) + shift_b).astype(bf16).reshape(rows_all, D)
     early = [share(array) for array in (input_a, attended, input_b, g_branch_b)]
     hidden, g_gate, g_up, branch_b, g_input_b, sum_gate, sum_up = mlp_both_ways(
-        input_b, g_branch_b, b_mlp.reshape(1, 2 * FF), all_b
+        input_b, g_branch_b, b_mlp.reshape(1, 2 * FF), gathered
     )
     shared_mlp = [share(array) for array in (g_gate, g_up, hidden)]
-    grads_b = lax.cond(
-        core == 0,
-        lambda: grads_b_core_0(early[2], shared_mlp[0], shared_mlp[1]),
-        lambda: grads_b_core_1(early[2], *shared_mlp, early[3]),
-    )
     branch_b = branch_b.reshape(slots, length, D)
     g_input_b = g_input_b.reshape(slots, length, D)
-    sends_b = first_sends(grads_b, BLOCK_B)
     out = ((middle + gate_b * branch_b) * mask_f).astype(bf16).reshape(rows_all, D)
     g_gate_b = jnp.sum(g_out * branch_b, axis=1)
     g_shift_b = jnp.sum(g_input_b, axis=1)
@@ -877,58 +1094,52 @@
     g_gate_a = jnp.sum(g_middle * branch_a, axis=1)
     grad_b_out = jnp.sum(g_branch_a.astype(f32), axis=0)
     shared_branch_a = share(g_branch_a)
-    g_attended = (
-        jnp.einsum("re,de->rd", g_branch_a, w_out, preferred_element_type=f32)
-        .astype(bf16)
-        .reshape(heads_shape)
-    )
-    g_attended, sends_b = lax.optimization_barrier((g_attended, sends_b))
-    planes_b = reduce_planes(grads_b, sends_b, BLOCK_B)
-    scores = jnp.einsum("slhe,smhe->shlm", queries, keys, preferred_element_type=f32) * scale
-    probs = jnp.exp(scores - log_total)
-    probs_low = probs.astype(bf16)
-    g_probs = jnp.einsum("slhe,smhe->shlm", g_attended, values, preferred_element_type=f32)
-    g_values = jnp.einsum("shlm,slhe->smhe", probs_low, g_attended, preferred_element_type=f32)
-    g_scores = (probs * (g_probs - jnp.sum(probs * g_probs, -1, keepdims=True))).astype(bf16)
-    g_queries = jnp.einsum("shlm,smhe->slhe", g_scores, keys, preferred_element_type=f32) * scale
-    g_keys = jnp.einsum("shlm,slhe->smhe", g_scores, queries, preferred_element_type=f32) * scale
-    g_q = rms_back(g_queries * cosines - turn_half(g_queries) * sines, q_norm, inv_q)
-    g_k = rms_back(g_keys * cosines - turn_half(g_keys) * sines, k_norm, inv_k)
-    g_projected = jnp.concatenate(
-        [g_q.reshape(rows_all, D), g_k.reshape(rows_all, D), g_values.reshape(rows_all, D)], axis=1
-    ).astype(bf16)
-    grad_b_qkv = jnp.sum(g_projected.astype(f32), axis=0)
+    grads_b = lax.cond(
+        core == 0,
+        lambda: grads_b_core_0(early[2], shared_mlp[0], shared_mlp[1]),
+        lambda: grads_b_core_1(early[2], *shared_mlp, early[3]),
+    )
+    orders = (SWAP_Y, SWAP_X), (SWAP_X, SWAP_Y)
+    sends_b = first_sends(grads_b, BLOCK_B)
+    arrived = over_planes(sends_b, orders[0])
+    g_attended = jnp.einsum("re,de->rd", g_branch_a, w_out, preferred_element_type=f32)
+    g_attended = after(g_attended.astype(bf16), sends_b)
+    g_projected, proj_sums = attention_backward(
+        projected, queries, keys, values, log_total, g_attended, cosines, sines
+    )
+    grad_b_qkv = jnp.sum(proj_sums, axis=(0, 1))
     shared_proj = share(g_projected)
-    g_input_a = jnp.einsum("re,de->rd", g_projected, w_qkv, preferred_element_type=f32).reshape(
-        slots, length, D
-    )
-    made_a = lax.cond(
-        core == 0,
-        lambda: grads_a(0, early[0], shared_proj, early[1], shared_branch_a),
-        lambda: grads_a(1, early[0], shared_proj, early[1], shared_branch_a),
-    )
-    sends_a = first_sends(made_a, BLOCK_A)
-    g_input_a, sends_a = lax.optimization_barrier((g_input_a, sends_a))
+    kept_b, sends_b = second_sends(grads_b, after(arrived, g_projected), BLOCK_B)
+    g_projected, shared_proj = after((g_projected, shared_proj), sends_b)
+    g_input_a = jnp.einsum("re,de->rd", g_projected, w_qkv, preferred_element_type=f32)
+    g_input_a = lax.optimization_barrier(g_input_a).reshape(slots, length, D)
     g_shift_a = jnp.sum(g_input_a, axis=1)
     g_scale_a = jnp.sum(g_input_a * normed_a, axis=1)
-    planes_a = reduce_planes(made_a, sends_a, BLOCK_A)
-    grad_tokens = g_middle + norm_back(g_input_a * (1.0 + scale_a), normed_a, inv_a)
     g_modulation = jnp.concatenate(
         [g_shift_a, g_scale_a, g_gate_a, g_shift_b, g_scale_b, g_gate_b], axis=1
     ).astype(bf16)
     bias_sums = [grad_b_qkv, grad_b_out, sum_gate.reshape(-1), sum_up.reshape(-1)]
     small = jnp.concatenate([g_modulation.reshape(-1)] + [b.astype(bf16) for b in bias_sums])
+    shared_proj = after(shared_proj, small)
     small_all = lax.all_gather(small.reshape(-1, 128), axes, axis=0, tiled=False).reshape(
         DEVICES, -1
     )
-    sum_b = reduce_line(planes_b).astype(bf16)
-    planes_a, small_all = lax.optimization_barrier((planes_a, small_all))
-    sum_a = reduce_line(planes_a).astype(bf16)
-    is_down = jnp.asarray(kind_table(PLACE_B, MLP_BLOCKS))[me]
-    is_out = jnp.asarray(kind_table(PLACE_A, QKV_BLOCKS))[me]
+    made_a = lax.cond(
+        core == 0,
+        lambda: grads_a(0, early[0], shared_proj, early[1], shared_branch_a),
+        lambda: grads_a(1, early[0], shared_proj, early[1], shared_branch_a),
+    )
+    sends_a = first_sends(made_a, BLOCK_A)
+    planes_b = plane_sums(kept_b, after(over_planes(sends_b, orders[1]), sends_a))
+    sends_b = line_sends(planes_b)
+    arrived = after(over_planes(sends_a, orders[0]), sends_b)
+    kept_a, sends_a = second_sends(made_a, arrived, BLOCK_A)
+    line_b = after(from_line(sends_b), sends_a)
+    grad_tokens = g_middle + norm_back(g_input_a * (1.0 + scale_a), normed_a, inv_a)
+    sum_b = sum_line(sends_b[0], line_b).astype(bf16)
     halves = sum_b.reshape(2, BLOCK_B // 2, 128)
     sum_b = jnp.where(
-        is_down == 0,
+        jnp.logical_not(is_kind(PLACE_B, MLP_BLOCKS)),
         jnp.concatenate(
             [from_tiles(half, 24).reshape(-1, 24, 128) for half in halves], axis=1
         ).reshape(-1, 128),
@@ -937,11 +1148,12 @@
             ((0, BLOCK_B - USED_DOWN), (0, 0)),
         ),
     )
-    sum_a = jnp.where(is_out == 0, from_tiles(sum_a, 27), from_tiles(sum_a, 9))
-    buffer = jnp.zeros((SHARD + 2 * BLOCK_B, 128), f32)
-    buffer = collect(buffer, sum_b, BLOCK_B, block_b_range, PLACE_B)
-    buffer = collect(buffer, sum_a, BLOCK_A, block_a_range, PLACE_A)
-    main = buffer[BLOCK_B : BLOCK_B + SHARD]
+    planes_a = plane_sums(kept_a, after(over_planes(sends_a, orders[1]), sum_b))
+    sends_a = line_sends(planes_a)
+    back_b = send_back(after(sum_b, sends_a), PLAN_B, PLACE_B)
+    sum_a = sum_line(sends_a[0], after(from_line(sends_a), back_b)).astype(bf16)
+    sum_a = jnp.where(is_kind(PLACE_A, QKV_BLOCKS), from_tiles(sum_a, 9), from_tiles(sum_a, 27))
+    back_a = send_back(sum_a, PLAN_A, PLACE_A)
     g_mod_all = (
         jnp.dot(chosen, small_all[:, : slots * 6 * D], preferred_element_type=f32)
         .astype(bf16)
@@ -956,17 +1168,19 @@
     part_biases = lax.dynamic_slice_in_dim(grad_biases, me * bias_count, bias_count, 0)
     grad_ada = jnp.einsum("km,mn->kn", cond_rows, g_mod_all, preferred_element_type=f32)
     g_cond_rows = jnp.einsum("mn,kn->mk", g_mod_all, ada_local, preferred_element_type=f32)
-    came = exchange_relative(g_cond_rows.reshape(DEVICES, slots, ADA_ROWS))
-    came = jnp.take(came, jnp.arange(DEVICES) ^ me, axis=0)
+    rows_of_all = lax.all_gather(
+        jnp.pad(g_cond_rows, ((0, 0), (0, 128 - ADA_ROWS))), axes, axis=0, tiled=False
+    )
+    came = jnp.where(
+        (jnp.arange(DEVICES)[:, None] ^ me) == jnp.arange(DEVICES)[None, :], 1.0, 0.0
+    )[:, :, None, None] * rows_of_all[:, :, :ADA_ROWS].reshape(DEVICES, DEVICES, slots, ADA_ROWS)
+    came = jnp.sum(came, axis=1)
     first = FIRST_ADA * 128 // (6 * D)
     g_cond = came.transpose(1, 0, 2).reshape(slots, DEVICES * ADA_ROWS)[:, first : first + D]
     cond_f = conditions.astype(f32)
     sigma_cond = jax.nn.sigmoid(cond_f)
     grad_conditions = g_cond * sigma_cond * (1.0 + cond_f * (1.0 - sigma_cond))
-    row = me * SHARD + lax.broadcasted_iota(jnp.int32, (SHARD, 128), 0)
-    part_weights = jnp.where(
-        (row >= FIRST_ADA) & (row < FIRST_DOWN), grad_ada.reshape(SHARD, 128), main
-    )
+    part_weights = owned_rows(back_a, back_b, grad_ada.reshape(SHARD, 128))
     return (out, grad_tokens.reshape(rows_all, D), grad_conditions, part_weights, part_biases)
 
 

time: 867 us -> 741 us (0.85)
  local copies, waits for them, and re-layouts: 157 us -> 81.9 us
  starting transfers between devices: 156 us -> 86.7 us
  Pallas kernels: 92.8 us -> 156 us
  other arithmetic: 93.8 us -> 61.4 us
  between operations: 44.6 us -> 15.9 us
  waiting for transfers between devices: 269 us -> 297 us
  matrix products: 41.8 us -> 28.7 us
    pallas_call x1 -> x5, Pallas kernels: 49.3 us -> 109 us  [the longest x1 50.4 us: mlp_both_ways(): pl.pallas_call(body, grid=(steps,), in_specs=[whole, whole, line, pl.Bloc...]
    all_gather x2, waiting for transfers between devices: 67.6 us -> 125 us  [the longest x1 116 us: gathered_weights(): lax.all_gather(block, ('fsdp', 'dp'), axis=0, tiled=True)]
    ppermute x3, starting transfers between devices: 52.4 us -> 7.43 us  [gather_columns(): lax.ppermute(part, 'fsdp', [(f, f ^ k) for f in range(4)])]
    ppermute x33 -> x23, starting transfers between devices: 70.2 us -> 34.7 us  [the longest x9 18.9 us: send_back(): lax.ppermute(block, ('fsdp', 'dp'), [(device, owner) for owner, device in...]
    ppermute x33 -> x23, waiting for transfers between devices: 125 us -> 90.9 us  [the longest x6 50.7 us: from_line(): lax.ppermute(sends[k], 'dp', [(d, d ^ 2 * k) for d in range(8)])]
    another operation x11 -> x6, local copies, waits for them, and re-layouts: 32.3 us -> 4.18 us  [the longest x4 4.05 us: on_device_32(): jnp.tile(table[:, 0], (1, HEADS))]
    ppermute x9, waiting for transfers between devices: 59.4 us -> 33 us  [spread(): got = lax.ppermute(piece, ('fsdp', 'dp'), pairs)]
    dynamic_update_slice x9 -> x0, other arithmetic: 19 us -> none  [collect(): lax.dynamic_update_slice_in_dim(buffer, held + got.astype(buffer.dtype),...]
  transfers between devices with their start and end apart: 71 -> 61, of which waited for: 25 -> 19; matrix products, arithmetic and copies ran while one was open for 27% -> 17% of each run, Pallas kernels for 2% -> 6%
where the time goes in v3:
time: 741 us; the launch traced here: 728 us
  waiting for transfers between devices  297 us (40%)
  Pallas kernels  156 us (21%)
  starting transfers between devices  86.7 us (12%)
  local copies, waits for them, and re-layouts  81.9 us (11%)
  other arithmetic  61.4 us (8%)
  matrix products  28.7 us (4%)
  between operations  15.9 us (2%)
    all_gather x1, waiting for transfers between devices, gathered_weights(): lax.all_gather(block, ('fsdp', 'dp'), axis=0, tiled=True)  116 us
    ppermute x6, waiting for transfers between devices, from_line(): lax.ppermute(sends[k], 'dp', [(d, d ^ 2 * k) for d in range(8)])  50.7 us
    pallas_call x1, Pallas kernels, mlp_both_ways(): pl.pallas_call(body, grid=(steps,), in_specs=[whole, whole, line, pl.Bloc...  50.4 us
    ppermute x9, waiting for transfers between devices, spread(): got = lax.ppermute(piece, ('fsdp', 'dp'), pairs)  33 us
    pallas_call x1, Pallas kernels, grads_b_core_1(): pl.pallas_call(body, grid=(mlp_steps + down_steps,), in_specs=[pl.BlockSp...  32.5 us
    ppermute x7, waiting for transfers between devices, send(): return lax.ppermute(array, ('fsdp', 'dp'), pairs)  29.9 us
    unnamed x225, local copies, waits for them, and re-layouts  27.7 us
    pallas_call x1, Pallas kernels, attention_backward(): pl.pallas_call(body, grid=(images,), in_specs=[pl.BlockSpec((length, 2 *...  26.4 us
  transfers between devices with their start and end apart: 61, of which 19 were waited for; matrix products, arithmetic and copies ran while one was open for 17% of the time, Pallas kernels for 6%

profile of v3, /device:TPU:9, one launch (start us, length us, event | category | flops | bytes accessed | tf_op | source)
XLA Modules:
  0.0 727.9 jit_solution(242276024111396169)
XLA Ops:
  8.9 3.0 pad_dynamic-slice_fusion.12
  11.9 4.1 collective-permute-start.17
  16.0 3.0 collective-permute-start.18
  19.0 2.0 collective-permute-start.19
  21.1 1.9 collective-permute-start.20
  23.0 2.0 collective-permute-start.21
  25.0 6.7 pad_dynamic-slice_fusion.2
  33.3 14.5 %collective-permute-done.18 = bf16[1296,128]{1,0:T(8,128)(2,1)} collective-permute-done((bf16[1296,128]{1,0:T(8,128)(2,1)}, bf16[1296,128]{1,0:T(8,128)(2,1)}, u32[]{:S(2)}, u32[]{:S(2)}) %collective-permute-start.18) | collective-permute-done | bytes 331808 | tf_op jit(solution)/shard_map/ppermute | solution.py:331
  49.2 3.1 collective-permute-done.19
  57.9 15.4 %collective-permute-done.24 = bf16[2688,128]{1,0:T(8,128)(2,1)} collective-permute-done((bf16[2688,128]{1,0:T(8,128)(2,1)}, bf16[2688,128]{1,0:T(8,128)(2,1)}, u32[]{:S(2)}, u32[]{:S(2)}) %collective-permute-start.24) | collective-permute-done | bytes 688160 | tf_op jit(solution)/shard_map/ppermute | solution.py:331
  79.6 2.0 collective-permute-start.2
  81.6 10.1 %collective-permute-start.3 = (bf16[23,128]{1,0:T(8,128)(2,1)S(1)}, bf16[23,128]{1,0:T(8,128)(2,1)S(1)}, u32[]{:S(2)}, u32[]{:S(2)}) collective-permute-start(bf16[23,128]{1,0:T(8,128)(2,1)S(1)} %bitcast.332), channel_id=1, source_target_pairs={{0,4},{1,5},{2,6},{3,7},{4,0},{5,1},{6,2},{7,3},{8,12},{9,13},{10,... | collective-permute-start | bytes 17672 | tf_op jit(solution)/shard_map/ppermute | solution.py:468
  94.5 2.9 collective-permute-start.5
  102.9 6.7 collective-permute-start.9
  110.1 2.7 reshape.594
  129.2 14.4 %collective-permute-done.12 = f32[4,2,6912]{2,0,1:T(4,128)S(1)} collective-permute-done((f32[4,2,6912]{2,0,1:T(4,128)S(1)}, f32[4,2,6912]{2,0,1:T(4,128)S(1)}, u32[]{:S(2)}, u32[]{:S(2)}) %collective-permute-start.12) | collective-permute-done | bytes 221216 | tf_op jit(solution)/shard_map/ppermute | solution.py:486
  143.6 7.2 collective-permute-done.13
  151.5 2.0 collective-permute-start.15
  155.7 3.4 collective-permute-done.15
  159.1 5.0 collective-permute-done.16
  164.7 3.0 fusion.9
  169.1 116.3 %all-gather.5.cloned.1.call-done = bf16[127488,128]{1,0:T(8,128)(2,1)} async-done(((bf16[3984,128]{1,0:T(8,128)(2,1)}), bf16[127488,128]{1,0:T(8,128)(2,1)}) %all-gather.5.cloned.1.call-update) | async-done | bytes 32636944 | tf_op jit(solution)/shard_map/all_gather | solution.py:779
  285.4 4.4 split_a.1
  289.8 3.1 copy-done.29
  292.9 7.2 convolution_add_fusion.proj_ref
  300.1 23.1 %attention_forward.1 = (bf16[512,1152]{1,0:T(8,128)(2,1)S(1)}, bf16[512,1152]{1,0:T(8,128)(2,1)S(1)}, bf16[512,1152]{1,0:T(8,128)(2,1)S(1)}, bf16[512,1152]{1,0:T(8,128)(2,1)S(1)}, f32[512,16]{1,0:T(8,128)S(1)}) custom-call(f32[512,3456]{1,0:T(8,128)} %convolution_add_fusion.proj_ref, f32[256,1152]{1,0:T(8,128)S(1)} %copy.69.cos_ref, ...), custom_call_target="tpu_custom_call" | custom-call | flops 1207959552 | bytes 20000000 | tf_op jit(solution)/shard_map/attention_forward/pallas_call | solution.py:852
  323.2 3.3 fusion.69
  328.6 50.4 %mlp_both_ways.1 = (bf16[512,3072]{1,0:T(8,128)(2,1)}, bf16[512,3072]{1,0:T(8,128)(2,1)}, bf16[512,3072]{1,0:T(8,128)(2,1)}, f32[512,1152]{1,0:T(8,128)S(1)}, f3...) custom-call(bf16[512,1152]{1,0:T(8,128)(2,1)} %fusion.15.x_ref, ...), custom_call_target="tpu_custom_call" | custom-call | flops 21743271936 | bytes 30000000 | tf_op jit(solution)/shard_map/mlp_both_ways/pallas_call | solution.py:563
  382.3 15.4 %collective-permute-done.26 = bf16[512,1152]{1,0:T(8,128)(2,1)} collective-permute-done((bf16[512,1152]{1,0:T(8,128)(2,1)}, bf16[512,1152]{1,0:T(8,128)(2,1)}, u32[]{:S(2)}, u32[]{:S(2)}) %collective-permute-start.26) | collective-permute-done | bytes 1179680 | tf_op jit(solution)/shard_map/ppermute | solution.py:1061
  399.4 33.4 %conditional.2 = (bf16[2,2,4,1344,128]{4,3,2,1,0:T(8,128)(2,1)S(1)}, bf16[2,2,4,1344,128]{4,3,2,1,0:T(8,128)(2,1)S(1)}) conditional(s32[]{:T(128)} %convert_element_type.263, (bf16[512,1152]{1,0:T(8,128)(2,1)}, bf16[512,1152]{1,0:T(8,128)(2,1)}, bf16[512,3072]{1,0:T(8,128)(2,1)}, bf16[512,3072]{1,0:T(8,128)(2,1)}, bf16[512,3072]{1,0:T(8,128)(2,1)}, ...), branch_computations={%region_6.7_spmd.clone, %region_7.8_spmd} | conditional | bytes 220 | solution.py:1097
  400.0 32.5 %grads_b_core_1.1 = (bf16[2688,8,128]{2,1,0:T(8,128)(2,1)S(1)}, bf16[2688,8,128]{2,1,0:T(8,128)(2,1)S(1)}) custom-call(s32[11]{0:T(128)S(1)} %copy-done.28, bf16[512,1152]{1,0:T(8,128)(2,1)} %get-tuple-element.209.xo, bf16[512,1152]{1,0:T(8,128)(2,1)} %get-tuple-element.210.xp, bf16[512,3072]{1,0:T(8,128)(2,1)} %get-tuple-element.211.gog, ...), custom_call_target="tpu_custom_call" | custom-call | tf_op jit(solution)/shard_map/cond/branch_0_fun/grads_b_core_1/pallas_call | solution.py:692
  432.7 1.9 dynamic-slice_bitcast_fusion
  440.5 2.1 fusion.19
  442.6 3.1 fusion.67
  448.5 26.4 %attention_backward.1 = (bf16[512,3456]{1,0:T(8,128)(2,1)}, f32[2,1,3456]{2,1,0:T(1,128)S(1)}) custom-call(f32[512,3456]{1,0:T(8,128)} %convolution_add_fusion.proj_ref, bf16[512,1152]{1,0:T(8,128)(2,1)S(1)} %copy-done.8, bf16[512,1152]{1,0:T(8,128)(2,1)S(1)} %copy-done.10, bf16[512,1152]{1,0:T(8,128)(2,1)S(1)} %copy-done.12, f32[512,16]{1,0:T(8,128)S(1)} %copy-done.24, ...), custom_call_target="tpu_custom_call" | custom-call | flops 1000 | bytes 1000 | tf_op jit(solution)/shard_map/attention_backward/pallas_call | solution.py:911
  486.1 3.5 fusion
  492.1 3.3 fusion.1
  498.0 7.5 %fusion.74 = f32[512,1152]{1,0:T(8,128)S(1)} fusion(bf16[512,3456]{1,0:T(8,128)(2,1)} %get-tuple-element.184, bf16[1152,3456]{1,0:T(8,128)(2,1)S(1)} %bitcast.288), kind=kOutput, calls=%fused_computation.220 | convolution fusion | flops 4076863488 | bytes 13860864 | tf_op jit(solution)/shard_map/re,de->rd/dot_general | solution.py:1114
  505.7 2.9 fusion.17
  515.2 14.5 %conditional.3 = (bf16[2,2,4,648,128]{4,3,2,1,0:T(8,128)(2,1)S(1)}, bf16[2,2,4,648,128]{4,3,2,1,0:T(8,128)(2,1)S(1)}) conditional(s32[]{:T(128)} %convert_element_type.263, (bf16[512,1152]{1,0:T(8,128)(2,1)S(1)}, bf16[512,1152]{1,0:T(8,128)(2,1)}, bf16[512,3456]{1,0:T(8,128)(2,1)}, bf16[512,3456]{1,0:T(8,128)(2,1)}, bf16[512,1152]{1,0:T(8,128)(2,1)}, ...), branch_computations={%region_19.20_spmd, %region_20.21_spmd} | conditional | bytes 16 | solution.py:1127
  515.3 14.5 %grads_a_core_1.1 = (bf16[16,81,8,128]{3,2,1,0:T(8,128)(2,1)S(1)}, bf16[16,81,8,128]{3,2,1,0:T(8,128)(2,1)S(1)}) custom-call(bf16[512,1152]{1,0:T(8,128)(2,1)S(1)} %get-tuple-element.88.xo, bf16[512,1152]{1,0:T(8,128)(2,1)} %get-tuple-element.89.xp, bf16[512,3456]{1,0:T(8,128)(2,1)} %get-tuple-element.90.go, bf16[512,3456]{1,0:T(8,128)(2,1)} %get-tuple-element.91.gp, ...), custom_call_target="tpu_custom_call" | custom-call | tf_op jit(solution)/shard_map/cond/branch_0_fun/grads_a_core_1/pallas_call | solution.py:756
  530.9 4.7 collective-permute-start.42
  539.5 2.3 collective-permute-start.40
  542.1 18.4 %collective-permute-done.43 = bf16[2,4,648,128]{3,2,1,0:T(8,128)(2,1)S(1)} collective-permute-done((bf16[2,4,648,128]{3,2,1,0:T(8,128)(2,1)S(1)}, bf16[2,4,648,128]{3,2,1,0:T(8,128)(2,1)S(1)}, u32[]{:S(2)}, u32[]{:S(2)}) %collective-permute-start.43) | collective-permute-done | bytes 1327136 | tf_op jit(solution)/shard_map/ppermute | solution.py:428
  560.5 6.3 collective-permute-done.42
  571.3 4.4 collective-permute-done.40
  575.7 31.7 %collective-permute-done.41 = bf16[2688,128]{1,0:T(8,128)(2,1)S(1)} collective-permute-done((bf16[2688,128]{1,0:T(8,128)(2,1)S(1)}, bf16[2688,128]{1,0:T(8,128)(2,1)S(1)}, u32[]{:S(2)}, u32[]{:S(2)}) %collective-permute-start.41) | collective-permute-done | bytes 688160 | tf_op jit(solution)/shard_map/ppermute | solution.py:455
  617.1 2.7 reshape.542
  619.9 2.5 fusion.18
  623.1 6.1 collective-permute-start.47
  630.0 2.4 copy.100
  634.9 2.4 reshape.565
  637.3 2.4 fusion.75
  640.5 14.2 %collective-permute-done.52 = bf16[1296,128]{1,0:T(8,128)(2,1)} collective-permute-done((bf16[1296,128]{1,0:T(8,128)(2,1)}, bf16[1296,128]{1,0:T(8,128)(2,1)}, u32[]{:S(2)}, u32[]{:S(2)}) %collective-permute-start.52) | collective-permute-done | bytes 331808 | tf_op jit(solution)/shard_map/ppermute | solution.py:455
  654.7 2.1 add_convert_fusion.1
  657.8 1.9 reshape.574
  664.6 5.3 collective-permute-start.56
  671.5 5.0 multiply_add_fusion
  676.5 2.3 fusion.76
  678.8 2.6 reshape.577.refs_9_
  681.5 15.4 %collective-permute-done.54.refs_5_ = bf16[1296,128]{1,0:T(8,128)(2,1)} collective-permute-done((bf16[1296,128]{1,0:T(8,128)(2,1)}, bf16[1296,128]{1,0:T(8,128)(2,1)}, u32[]{:S(2)}, u32[]{:S(2)}) %collective-permute-start.54) | collective-permute-done | bytes 331808 | tf_op jit(solution)/shard_map/ppermute | solution.py:340
  701.3 5.3 owned_rows.1
  708.7 8.7 %all-gather.9.cloned.1.call-done = f32[2048,128]{1,0:T(8,128)} async-done(((f32[64,128]{1,0:T(8,128)}), f32[2048,128]{1,0:T(8,128)}) %all-gather.9.cloned.1.call-update) | async-done | bytes 1048592 | tf_op jit(solution)/shard_map/all_gather | solution.py:1171
  717.4 2.9 multiply_reduce_fusion.6
  (435 shorter events, 123.6 us)
Async XLA Ops:
  7.2 278.2 %all-gather.5.cloned.1.call-start = ((), (), s32[]{:S(2)}) async-start(), calls=%async_computation | async-start | bytes 33656832 | tf_op jit(solution)/shard_map/all_gather | solution.py:779
  11.9 19.9 %collective-permute-start.17 = (bf16[1296,128]{1,0:T(8,128)(2,1)}, bf16[1296,128]{1,0:T(8,128)(2,1)S(1)}, u32[]{:S(2)}, u32[]{:S(2)}) collective-permute-start(bf16[1296,128]{1,0:T(8,128)(2,1)} %get-tuple-element.155), channel_id=1, source_target_pairs={{0,0},{1,4},{2,9},{3,13},{4,18},{5,22},{6,27},{7,31}} | collective-permute-start | bytes 995336 | tf_op jit(solution)/shard_map/ppermute | solution.py:331
  16.0 31.7 %collective-permute-start.18 = (bf16[1296,128]{1,0:T(8,128)(2,1)}, bf16[1296,128]{1,0:T(8,128)(2,1)}, u32[]{:S(2)}, u32[]{:S(2)}) collective-permute-start(bf16[1296,128]{1,0:T(8,128)(2,1)} %get-tuple-element.156), channel_id=1, source_target_pairs={{0,1},{1,5},{2,10},{3,14},{4,19},{5,23},{6,28}} | collective-permute-start | bytes 995336 | tf_op jit(solution)/shard_map/ppermute | solution.py:331
  19.0 33.3 %collective-permute-start.19 = (bf16[1296,128]{1,0:T(8,128)(2,1)}, bf16[1296,128]{1,0:T(8,128)(2,1)}, u32[]{:S(2)}, u32[]{:S(2)}) collective-permute-start(bf16[1296,128]{1,0:T(8,128)(2,1)} %get-tuple-element.157), channel_id=1, source_target_pairs={{0,2},{1,6},{2,11},{3,15},{4,20},{5,24},{6,29}} | collective-permute-start | bytes 995336 | tf_op jit(solution)/shard_map/ppermute | solution.py:331
  21.1 32.6 %collective-permute-start.20 = (bf16[1296,128]{1,0:T(8,128)(2,1)S(1)}, bf16[1296,128]{1,0:T(8,128)(2,1)}, u32[]{:S(2)}, u32[]{:S(2)}) collective-permute-start(bf16[1296,128]{1,0:T(8,128)(2,1)S(1)} %get-tuple-element.158), channel_id=1, source_target_pairs={{0,3},{1,7},{2,12},{3,16},{4,21},{5,25},{6,30}} | collective-permute-start | bytes 995336 | tf_op jit(solution)/shard_map/ppermute | solution.py:331
  23.0 32.2 %collective-permute-start.21 = (bf16[1296,128]{1,0:T(8,128)(2,1)S(1)}, bf16[1296,128]{1,0:T(8,128)(2,1)}, u32[]{:S(2)}, u32[]{:S(2)}) collective-permute-start(bf16[1296,128]{1,0:T(8,128)(2,1)S(1)} %get-tuple-element.159), channel_id=1, source_target_pairs={{0,4},{1,8},{2,13},{3,17},{4,22},{5,26},{6,31}} | collective-permute-start | bytes 995336 | tf_op jit(solution)/shard_map/ppermute | solution.py:331
  31.8 26.1 %collective-permute-start.22 = (bf16[2688,128]{1,0:T(8,128)(2,1)}, bf16[2688,128]{1,0:T(8,128)(2,1)}, u32[]{:S(2)}, u32[]{:S(2)}) collective-permute-start(bf16[2688,128]{1,0:T(8,128)(2,1)} %get-tuple-element.256), channel_id=1, source_target_pairs={{8,1},{9,4},{10,6},{11,8},{12,10},{13,12},{14,14},{15,17},{16,19},... | collective-permute-start | bytes 2064392 | tf_op jit(solution)/shard_map/ppermute | solution.py:331
  47.7 10.2 %collective-permute-start.23 = (bf16[2688,128]{1,0:T(8,128)(2,1)}, bf16[2688,128]{1,0:T(8,128)(2,1)}, u32[]{:S(2)}, u32[]{:S(2)}) collective-permute-start(bf16[2688,128]{1,0:T(8,128)(2,1)} %get-tuple-element.253), channel_id=1, source_target_pairs={{7,0},{8,2},{9,5},{10,7},{11,9},{12,11},{13,13},{14,15},{15,18},{1... | collective-permute-start | bytes 2064392 | tf_op jit(solution)/shard_map/ppermute | solution.py:331
  52.4 20.9 %collective-permute-start.24 = (bf16[2688,128]{1,0:T(8,128)(2,1)}, bf16[2688,128]{1,0:T(8,128)(2,1)}, u32[]{:S(2)}, u32[]{:S(2)}) collective-permute-start(bf16[2688,128]{1,0:T(8,128)(2,1)} %get-tuple-element.254), channel_id=1, source_target_pairs={{7,1},{8,3},{9,6},{10,8},{11,10},{12,12},{13,14},{14,16},{15,19},{... | collective-permute-start | bytes 2064392 | tf_op jit(solution)/shard_map/ppermute | solution.py:331
  53.7 19.6 %collective-permute-start.25 = (bf16[2688,128]{1,0:T(8,128)(2,1)S(1)}, bf16[2688,128]{1,0:T(8,128)(2,1)}, u32[]{:S(2)}, u32[]{:S(2)}) collective-permute-start(bf16[2688,128]{1,0:T(8,128)(2,1)S(1)} %get-tuple-element.255), channel_id=1, source_target_pairs={{8,4},{14,17},{29,27}} | collective-permute-start | bytes 2064392 | tf_op jit(solution)/shard_map/ppermute | solution.py:331
  79.3 550.6 %all-gather.7.cloned.1.call-start = ((), (), s32[]{:S(2)}) async-start(), calls=%async_computation.1 | async-start | bytes 1622016 | tf_op jit(solution)/shard_map/all_gather | solution.py:1124
  79.4 15.1 %collective-permute-start = (bf16[23,128]{1,0:T(8,128)(2,1)S(1)}, bf16[23,128]{1,0:T(8,128)(2,1)S(1)}, u32[]{:S(2)}, u32[]{:S(2)}) collective-permute-start(bf16[23,128]{1,0:T(8,128)(2,1)S(1)} %bitcast.329), channel_id=1, source_target_pairs={{0,1},{1,0},{2,3},{3,2},{4,5},{5,4},{6,7},{7,6},{8,9},{9,8},{10,11... | collective-permute-start | bytes 17672 | tf_op jit(solution)/shard_map/ppermute | solution.py:468
  79.5 18.6 %collective-permute-start.1 = (bf16[23,128]{1,0:T(8,128)(2,1)S(1)}, bf16[23,128]{1,0:T(8,128)(2,1)S(1)}, u32[]{:S(2)}, u32[]{:S(2)}) collective-permute-start(bf16[23,128]{1,0:T(8,128)(2,1)S(1)} %bitcast.330), channel_id=1, source_target_pairs={{0,2},{1,3},{2,0},{3,1},{4,6},{5,7},{6,4},{7,5},{8,10},{9,11},{10,... | collective-permute-start | bytes 17672 | tf_op jit(solution)/shard_map/ppermute | solution.py:468
  79.6 19.1 %collective-permute-start.2 = (bf16[23,128]{1,0:T(8,128)(2,1)S(1)}, bf16[23,128]{1,0:T(8,128)(2,1)S(1)}, u32[]{:S(2)}, u32[]{:S(2)}) collective-permute-start(bf16[23,128]{1,0:T(8,128)(2,1)S(1)} %bitcast.331), channel_id=1, source_target_pairs={{0,3},{1,2},{2,1},{3,0},{4,7},{5,6},{6,5},{7,4},{8,11},{9,10},{10,... | collective-permute-start | bytes 17672 | tf_op jit(solution)/shard_map/ppermute | solution.py:468
  81.6 17.6 %collective-permute-start.3 = (bf16[23,128]{1,0:T(8,128)(2,1)S(1)}, bf16[23,128]{1,0:T(8,128)(2,1)S(1)}, u32[]{:S(2)}, u32[]{:S(2)}) collective-permute-start(bf16[23,128]{1,0:T(8,128)(2,1)S(1)} %bitcast.332), channel_id=1, source_target_pairs={{0,4},{1,5},{2,6},{3,7},{4,0},{5,1},{6,2},{7,3},{8,12},{9,13},{10,... | collective-permute-start | bytes 17672 | tf_op jit(solution)/shard_map/ppermute | solution.py:468
  91.7 8.1 %collective-permute-start.4 = (bf16[23,128]{1,0:T(8,128)(2,1)S(1)}, bf16[23,128]{1,0:T(8,128)(2,1)S(1)}, u32[]{:S(2)}, u32[]{:S(2)}) collective-permute-start(bf16[23,128]{1,0:T(8,128)(2,1)S(1)} %bitcast.333), channel_id=1, source_target_pairs={{0,5},{1,4},{2,7},{3,6},{4,1},{5,0},{6,3},{7,2},{8,13},{9,12},{10,... | collective-permute-start | bytes 17672 | tf_op jit(solution)/shard_map/ppermute | solution.py:468
  94.5 5.9 collective-permute-start.5
  98.0 3.5 collective-permute-start.6
  102.1 12.0 %collective-permute-start.7 = (bf16[8,23,128]{2,1,0:T(8,128)(2,1)}, bf16[8,23,128]{2,1,0:T(8,128)(2,1)}, u32[]{:S(2)}, u32[]{:S(2)}) collective-permute-start(bf16[8,23,128]{2,1,0:T(8,128)(2,1)} %constant_dynamic-update-slice_fusion), channel_id=1, source_target_pairs={{0,8},{8,0},{16,24},{24,16},{1,9},{9,1},{17,25},{25,17},{2,10},{10... | collective-permute-start | bytes 141320 | tf_op jit(solution)/shard_map/ppermute | solution.py:475
  102.9 11.3 %collective-permute-start.8 = (bf16[8,23,128]{2,1,0:T(8,128)(2,1)}, bf16[8,23,128]{2,1,0:T(8,128)(2,1)}, u32[]{:S(2)}, u32[]{:S(2)}) collective-permute-start(bf16[8,23,128]{2,1,0:T(8,128)(2,1)} %constant_dynamic-update-slice_fusion), channel_id=1, source_target_pairs={{0,16},{8,24},{16,0},{24,8},{1,17},{9,25},{17,1},{25,9},{2,18},{10... | collective-permute-start | bytes 141320 | tf_op jit(solution)/shard_map/ppermute | solution.py:475
  102.9 11.3 %collective-permute-start.9 = (bf16[8,23,128]{2,1,0:T(8,128)(2,1)}, bf16[8,23,128]{2,1,0:T(8,128)(2,1)}, u32[]{:S(2)}, u32[]{:S(2)}) collective-permute-start(bf16[8,23,128]{2,1,0:T(8,128)(2,1)} %constant_dynamic-update-slice_fusion), channel_id=1, source_target_pairs={{0,24},{8,16},{16,8},{24,0},{1,25},{9,17},{17,9},{25,1},{2,26},{10... | collective-permute-start | bytes 141320 | tf_op jit(solution)/shard_map/ppermute | solution.py:475
  118.3 5.7 collective-permute-start.10
  122.7 177.4 %copy-start.3 = (f32[256,1152]{1,0:T(8,128)}, f32[256,1152]{1,0:T(8,128)S(1)}, u32[]{:S(2)}) copy-start(f32[256,1152]{1,0:T(8,128)S(1)} %copy.70.sin_ref) | copy-start | bytes 3538948
  124.0 176.1 %copy-start.13 = (bf16[1152,128]{1,0:T(8,128)(2,1)}, bf16[1152,128]{1,0:T(8,128)(2,1)S(1)}, u32[]{:S(2)}) copy-start(bf16[1152,128]{1,0:T(8,128)(2,1)S(1)} %fusion.35.ind_ref) | copy-start | bytes 884740
  125.9 3.3 collective-permute-start.11
  126.5 17.0 %collective-permute-start.12 = (f32[4,2,6912]{2,0,1:T(4,128)S(1)}, f32[4,2,6912]{2,0,1:T(4,128)S(1)}, u32[]{:S(2)}, u32[]{:S(2)}) collective-permute-start(f32[4,2,6912]{2,0,1:T(4,128)S(1)} %get-tuple-element.266), channel_id=1, source_target_pairs={{16,0},{17,1},{18,2},{19,3},{20,4},{21,5},{22,6},{23,7},{24,8},{25... | collective-permute-start | bytes 663560 | tf_op jit(solution)/shard_map/ppermute | solution.py:486
  127.8 22.9 %collective-permute-start.13 = (f32[4,2,6912]{2,0,1:T(4,128)S(1)}, f32[4,2,6912]{2,0,1:T(4,128)S(1)}, u32[]{:S(2)}, u32[]{:S(2)}) collective-permute-start(f32[4,2,6912]{2,0,1:T(4,128)S(1)} %get-tuple-element.267), channel_id=1, source_target_pairs={{16,8},{17,9},{18,10},{19,11},{20,12},{21,13},{22,14},{23,15},{24,... | collective-permute-start | bytes 663560 | tf_op jit(solution)/shard_map/ppermute | solution.py:486
  151.0 4.6 collective-permute-start.14
  151.5 7.6 %collective-permute-start.15 = (f32[2,6912]{1,0:T(2,128)S(1)}, f32[2,6912]{1,0:T(2,128)S(1)}, u32[]{:S(2)}, u32[]{:S(2)}) collective-permute-start(f32[2,6912]{1,0:T(2,128)S(1)} %bitcast.323), channel_id=1, source_target_pairs={{0,4},{1,5},{2,6},{3,7},{4,0},{5,1},{6,2},{7,3},{8,12},{9,13},{10,... | collective-permute-start | bytes 165896 | tf_op jit(solution)/shard_map/ppermute | solution.py:486
  153.6 10.5 %collective-permute-start.16 = (f32[2,6912]{1,0:T(2,128)S(1)}, f32[2,6912]{1,0:T(2,128)S(1)}, u32[]{:S(2)}, u32[]{:S(2)}) collective-permute-start(f32[2,6912]{1,0:T(2,128)S(1)} %bitcast.324), channel_id=1, source_target_pairs={{0,6},{1,7},{2,4},{3,5},{4,2},{5,3},{6,0},{7,1},{8,14},{9,15},{10,... | collective-permute-start | bytes 165896 | tf_op jit(solution)/shard_map/ppermute | solution.py:486
  164.2 162.7 %copy-start.65 = (f32[2,1152]{1,0:T(2,128)}, f32[2,1152]{1,0:T(2,128)S(1)}, u32[]{:S(2)}) copy-start(f32[2,1152]{1,0:T(2,128)S(1)} %get-tuple-element.277) | copy-start | bytes 27652
  381.0 16.7 %collective-permute-start.27 = (bf16[512,3072]{1,0:T(8,128)(2,1)}, bf16[512,3072]{1,0:T(8,128)(2,1)}, u32[]{:S(2)}, u32[]{:S(2)}) collective-permute-start(bf16[512,3072]{1,0:T(8,128)(2,1)} %get-tuple-element.223), channel_id=1, source_target_pairs={{0,1},{1,0},{2,3},{3,2},{4,5},{5,4},{6,7},{7,6},{8,9},{9,8},{10,11... | collective-permute-start | bytes 9437192 | tf_op jit(solution)/shard_map/ppermute | solution.py:1061
  381.2 16.4 %collective-permute-start.28 = (bf16[512,3072]{1,0:T(8,128)(2,1)}, bf16[512,3072]{1,0:T(8,128)(2,1)}, u32[]{:S(2)}, u32[]{:S(2)}) collective-permute-start(bf16[512,3072]{1,0:T(8,128)(2,1)} %get-tuple-element.225), channel_id=1, source_target_pairs={{0,1},{1,0},{2,3},{3,2},{4,5},{5,4},{6,7},{7,6},{8,9},{9,8},{10,11... | collective-permute-start | bytes 9437192 | tf_op jit(solution)/shard_map/ppermute | solution.py:1061
  381.5 17.9 %collective-permute-start.29 = (bf16[512,3072]{1,0:T(8,128)(2,1)}, bf16[512,3072]{1,0:T(8,128)(2,1)}, u32[]{:S(2)}, u32[]{:S(2)}) collective-permute-start(bf16[512,3072]{1,0:T(8,128)(2,1)} %get-tuple-element.227), channel_id=1, source_target_pairs={{0,1},{1,0},{2,3},{3,2},{4,5},{5,4},{6,7},{7,6},{8,9},{9,8},{10,11... | collective-permute-start | bytes 9437192 | tf_op jit(solution)/shard_map/ppermute | solution.py:1061
  381.7 15.9 %collective-permute-start.26 = (bf16[512,1152]{1,0:T(8,128)(2,1)}, bf16[512,1152]{1,0:T(8,128)(2,1)}, u32[]{:S(2)}, u32[]{:S(2)}) collective-permute-start(bf16[512,1152]{1,0:T(8,128)(2,1)} %fusion.15.x_ref), channel_id=1, source_target_pairs={{0,1},{1,0},{2,3},{3,2},{4,5},{5,4},{6,7},{7,6},{8,9},{9,8},{10,11... | collective-permute-start | bytes 3538952 | tf_op jit(solution)/shard_map/ppermute | solution.py:1061
  382.0 17.4 %collective-permute-start.30 = (bf16[512,1152]{1,0:T(8,128)(2,1)}, bf16[512,1152]{1,0:T(8,128)(2,1)}, u32[]{:S(2)}, u32[]{:S(2)}) collective-permute-start(bf16[512,1152]{1,0:T(8,128)(2,1)} %fusion.10.g_ref), channel_id=1, source_target_pairs={{0,1},{1,0},{2,3},{3,2},{4,5},{5,4},{6,7},{7,6},{8,9},{9,8},{10,11... | collective-permute-start | bytes 3538952 | tf_op jit(solution)/shard_map/ppermute | solution.py:1061
  434.7 50.9 %collective-permute-start.33 = (bf16[2,4,1344,128]{3,2,1,0:T(8,128)(2,1)}, bf16[2,4,1344,128]{3,2,1,0:T(8,128)(2,1)}, u32[]{:S(2)}, u32[]{:S(2)}) collective-permute-start(bf16[2,4,1344,128]{3,2,1,0:T(8,128)(2,1)} %dynamic-slice_bitcast_fusion), channel_id=1, source_target_pairs={{0,8},{8,0},{16,24},{24,16},{1,9},{9,1},{17,25},{25,17},{2,10},{10... | collective-permute-start | bytes 8257544 | tf_op jit(solution)/shard_map/ppermute | solution.py:428
  437.8 48.4 %collective-permute-start.32 = (bf16[2,4,1344,128]{3,2,1,0:T(8,128)(2,1)}, bf16[2,4,1344,128]{3,2,1,0:T(8,128)(2,1)}, u32[]{:S(2)}, u32[]{:S(2)}) collective-permute-start(bf16[2,4,1344,128]{3,2,1,0:T(8,128)(2,1)} %dynamic-slice_bitcast_fusion.1), channel_id=1, source_target_pairs={{0,16},{16,0},{8,24},{24,8},{1,17},{17,1},{9,25},{25,9},{2,18},{18... | collective-permute-start | bytes 8257544 | tf_op jit(solution)/shard_map/ppermute | solution.py:428
  475.5 21.4 %collective-permute-start.31 = (bf16[512,3456]{1,0:T(8,128)(2,1)}, bf16[512,3456]{1,0:T(8,128)(2,1)}, u32[]{:S(2)}, u32[]{:S(2)}) collective-permute-start(bf16[512,3456]{1,0:T(8,128)(2,1)} %get-tuple-element.184), channel_id=1, source_target_pairs={{0,1},{1,0},{2,3},{3,2},{4,5},{5,4},{6,7},{7,6},{8,9},{9,8},{10,11... | collective-permute-start | bytes 10616840 | tf_op jit(solution)/shard_map/ppermute | solution.py:1061
  478.0 37.2 %collective-permute-start.36 = (bf16[512,1152]{1,0:T(8,128)(2,1)}, bf16[512,1152]{1,0:T(8,128)(2,1)}, u32[]{:S(2)}, u32[]{:S(2)}) collective-permute-start(bf16[512,1152]{1,0:T(8,128)(2,1)} %fusion.9), channel_id=1, source_target_pairs={{0,1},{1,0},{2,3},{3,2},{4,5},{5,4},{6,7},{7,6},{8,9},{9,8},{10,11... | collective-permute-start | bytes 3538952 | tf_op jit(solution)/shard_map/ppermute | solution.py:1061
  482.8 32.4 %collective-permute-start.38 = (bf16[512,1152]{1,0:T(8,128)(2,1)}, bf16[512,1152]{1,0:T(8,128)(2,1)}, u32[]{:S(2)}, u32[]{:S(2)}) collective-permute-start(bf16[512,1152]{1,0:T(8,128)(2,1)} %copy-done.47), channel_id=1, source_target_pairs={{0,1},{1,0},{2,3},{3,2},{4,5},{5,4},{6,7},{7,6},{8,9},{9,8},{10,11... | collective-permute-start | bytes 3538952 | tf_op jit(solution)/shard_map/ppermute | solution.py:1061
  485.6 29.7 %collective-permute-start.37 = (bf16[512,1152]{1,0:T(8,128)(2,1)}, bf16[512,1152]{1,0:T(8,128)(2,1)}, u32[]{:S(2)}, u32[]{:S(2)}) collective-permute-start(bf16[512,1152]{1,0:T(8,128)(2,1)} %copy-done.57), channel_id=1, source_target_pairs={{0,1},{1,0},{2,3},{3,2},{4,5},{5,4},{6,7},{7,6},{8,9},{9,8},{10,11... | collective-permute-start | bytes 3538952 | tf_op jit(solution)/shard_map/ppermute | solution.py:1061
  490.9 44.8 %collective-permute-start.35 = (bf16[4,1344,128]{2,1,0:T(8,128)(2,1)}, bf16[4,1344,128]{2,1,0:T(8,128)(2,1)}, u32[]{:S(2)}, u32[]{:S(2)}) collective-permute-start(bf16[4,1344,128]{2,1,0:T(8,128)(2,1)} %dynamic-slice_bitcast_fusion.2), channel_id=1, source_target_pairs={{0,16},{16,0},{8,24},{24,8},{1,17},{17,1},{9,25},{25,9},{2,18},{18... | collective-permute-start | bytes 4128776 | tf_op jit(solution)/shard_map/ppermute | solution.py:428
  497.5 38.2 %collective-permute-start.34 = (bf16[4,1344,128]{2,1,0:T(8,128)(2,1)}, bf16[4,1344,128]{2,1,0:T(8,128)(2,1)}, u32[]{:S(2)}, u32[]{:S(2)}) collective-permute-start(bf16[4,1344,128]{2,1,0:T(8,128)(2,1)} %dynamic-slice_bitcast_fusion.3), channel_id=1, source_target_pairs={{0,8},{8,0},{16,24},{24,16},{1,9},{9,1},{17,25},{25,17},{2,10},{10... | collective-permute-start | bytes 4128776 | tf_op jit(solution)/shard_map/ppermute | solution.py:428
  515.1 202.3 %all-gather.9.cloned.1.call-start = ((), (), s32[]{:S(2)}) async-start(), calls=%async_computation.2 | async-start | bytes 1081344 | tf_op jit(solution)/shard_map/all_gather | solution.py:1171
  529.9 30.6 %collective-permute-start.43 = (bf16[2,4,648,128]{3,2,1,0:T(8,128)(2,1)S(1)}, bf16[2,4,648,128]{3,2,1,0:T(8,128)(2,1)S(1)}, u32[]{:S(2)}, u32[]{:S(2)}) collective-permute-start(bf16[2,4,648,128]{3,2,1,0:T(8,128)(2,1)S(1)} %dynamic-slice_bitcast_fusion.4), channel_id=1, source_target_pairs={{0,8},{8,0},{16,24},{24,16},{1,9},{9,1},{17,25},{25,17},{2,10},{10... | collective-permute-start | bytes 3981320 | tf_op jit(solution)/shard_map/ppermute | solution.py:428
  530.9 35.8 %collective-permute-start.42 = (bf16[2,4,648,128]{3,2,1,0:T(8,128)(2,1)S(1)}, bf16[2,4,648,128]{3,2,1,0:T(8,128)(2,1)S(1)}, u32[]{:S(2)}, u32[]{:S(2)}) collective-permute-start(bf16[2,4,648,128]{3,2,1,0:T(8,128)(2,1)S(1)} %dynamic-slice_bitcast_fusion.5), channel_id=1, source_target_pairs={{0,16},{16,0},{8,24},{24,8},{1,17},{17,1},{9,25},{25,9},{2,18},{18... | collective-permute-start | bytes 3981320 | tf_op jit(solution)/shard_map/ppermute | solution.py:428
  539.3 32.0 %collective-permute-start.39 = (bf16[2688,128]{1,0:T(8,128)(2,1)S(1)}, bf16[2688,128]{1,0:T(8,128)(2,1)S(1)}, u32[]{:S(2)}, u32[]{:S(2)}) collective-permute-start(bf16[2688,128]{1,0:T(8,128)(2,1)S(1)} %get-tuple-element.249), channel_id=1, source_target_pairs={{0,2},{1,3},{2,0},{3,1},{4,6},{5,7},{6,4},{7,5},{8,10},{9,11},{10,... | collective-permute-start | bytes 2064392 | tf_op jit(solution)/shard_map/ppermute | solution.py:455
  539.5 36.2 %collective-permute-start.40 = (bf16[2688,128]{1,0:T(8,128)(2,1)S(1)}, bf16[2688,128]{1,0:T(8,128)(2,1)S(1)}, u32[]{:S(2)}, u32[]{:S(2)}) collective-permute-start(bf16[2688,128]{1,0:T(8,128)(2,1)S(1)} %get-tuple-element.250), channel_id=1, source_target_pairs={{0,4},{1,5},{2,6},{3,7},{4,0},{5,1},{6,2},{7,3},{8,12},{9,13},{10,... | collective-permute-start | bytes 2064392 | tf_op jit(solution)/shard_map/ppermute | solution.py:455
  541.8 65.6 %collective-permute-start.41 = (bf16[2688,128]{1,0:T(8,128)(2,1)S(1)}, bf16[2688,128]{1,0:T(8,128)(2,1)S(1)}, u32[]{:S(2)}, u32[]{:S(2)}) collective-permute-start(bf16[2688,128]{1,0:T(8,128)(2,1)S(1)} %get-tuple-element.251), channel_id=1, source_target_pairs={{0,6},{1,7},{2,4},{3,5},{4,2},{5,3},{6,0},{7,1},{8,14},{9,15},{10,... | collective-permute-start | bytes 2064392 | tf_op jit(solution)/shard_map/ppermute | solution.py:455
  568.0 43.4 %collective-permute-start.45 = (bf16[4,648,128]{2,1,0:T(8,128)(2,1)}, bf16[4,648,128]{2,1,0:T(8,128)(2,1)}, u32[]{:S(2)}, u32[]{:S(2)}) collective-permute-start(bf16[4,648,128]{2,1,0:T(8,128)(2,1)} %dynamic-slice_bitcast_fusion.6), channel_id=1, source_target_pairs={{0,16},{16,0},{8,24},{24,8},{1,17},{17,1},{9,25},{25,9},{2,18},{18... | collective-permute-start | bytes 1990664 | tf_op jit(solution)/shard_map/ppermute | solution.py:428
  569.7 41.7 %collective-permute-start.44 = (bf16[4,648,128]{2,1,0:T(8,128)(2,1)}, bf16[4,648,128]{2,1,0:T(8,128)(2,1)}, u32[]{:S(2)}, u32[]{:S(2)}) collective-permute-start(bf16[4,648,128]{2,1,0:T(8,128)(2,1)} %dynamic-slice_bitcast_fusion.7), channel_id=1, source_target_pairs={{0,8},{8,0},{16,24},{24,16},{1,9},{9,1},{17,25},{25,17},{2,10},{10... | collective-permute-start | bytes 1990664 | tf_op jit(solution)/shard_map/ppermute | solution.py:428
  615.1 17.2 %collective-permute-start.50 = (bf16[1296,128]{1,0:T(8,128)(2,1)}, bf16[1296,128]{1,0:T(8,128)(2,1)}, u32[]{:S(2)}, u32[]{:S(2)}) collective-permute-start(bf16[1296,128]{1,0:T(8,128)(2,1)} %get-tuple-element.264), channel_id=1, source_target_pairs={{0,2},{1,3},{2,0},{3,1},{4,6},{5,7},{6,4},{7,5},{8,10},{9,11},{10,... | collective-permute-start | bytes 995336 | tf_op jit(solution)/shard_map/ppermute | solution.py:455
  615.2 22.2 %collective-permute-start.51 = (bf16[1296,128]{1,0:T(8,128)(2,1)}, bf16[1296,128]{1,0:T(8,128)(2,1)S(1)}, u32[]{:S(2)}, u32[]{:S(2)}) collective-permute-start(bf16[1296,128]{1,0:T(8,128)(2,1)} %get-tuple-element.265), channel_id=1, source_target_pairs={{0,4},{1,5},{2,6},{3,7},{4,0},{5,1},{6,2},{7,3},{8,12},{9,13},{10,... | collective-permute-start | bytes 995336 | tf_op jit(solution)/shard_map/ppermute | solution.py:455
  622.4 32.3 %collective-permute-start.46 = (bf16[2688,128]{1,0:T(8,128)(2,1)}, bf16[2688,128]{1,0:T(8,128)(2,1)S(1)}, u32[]{:S(2)}, u32[]{:S(2)}) collective-permute-start(bf16[2688,128]{1,0:T(8,128)(2,1)} %bitcast_select_fusion.1), channel_id=1, source_target_pairs={{30,8},{16,9},{2,10},{18,11},{4,12},{20,13},{6,14},{17,15},{15,16}... | collective-permute-start | bytes 2064392 | tf_op jit(solution)/shard_map/ppermute | solution.py:340
  623.1 31.6 %collective-permute-start.47 = (bf16[2688,128]{1,0:T(8,128)(2,1)}, bf16[2688,128]{1,0:T(8,128)(2,1)S(1)}, u32[]{:S(2)}, u32[]{:S(2)}) collective-permute-start(bf16[2688,128]{1,0:T(8,128)(2,1)} %bitcast_select_fusion.1), channel_id=1, source_target_pairs={{14,7},{0,8},{24,9},{10,10},{26,11},{12,12},{28,13},{22,14},{25,15... | collective-permute-start | bytes 2064392 | tf_op jit(solution)/shard_map/ppermute | solution.py:340
  629.2 25.4 %collective-permute-start.48 = (bf16[2688,128]{1,0:T(8,128)(2,1)}, bf16[2688,128]{1,0:T(8,128)(2,1)S(1)}, u32[]{:S(2)}, u32[]{:S(2)}) collective-permute-start(bf16[2688,128]{1,0:T(8,128)(2,1)} %bitcast_select_fusion.1), channel_id=1, source_target_pairs={{30,7},{8,8},{2,9},{18,10},{4,11},{20,12},{6,13},{9,14},{15,15},{1... | collective-permute-start | bytes 2064392 | tf_op jit(solution)/shard_map/ppermute | solution.py:340
  632.4 22.3 %collective-permute-start.49 = (bf16[2688,128]{1,0:T(8,128)(2,1)}, bf16[2688,128]{1,0:T(8,128)(2,1)S(1)}, u32[]{:S(2)}, u32[]{:S(2)}) collective-permute-start(bf16[2688,128]{1,0:T(8,128)(2,1)} %bitcast_select_fusion.1), channel_id=1, source_target_pairs={{16,8},{17,14},{21,29}} | collective-permute-start | bytes 2064392 | tf_op jit(solution)/shard_map/ppermute | solution.py:340
  637.3 17.3 %collective-permute-start.52 = (bf16[1296,128]{1,0:T(8,128)(2,1)}, bf16[1296,128]{1,0:T(8,128)(2,1)}, u32[]{:S(2)}, u32[]{:S(2)}) collective-permute-start(bf16[1296,128]{1,0:T(8,128)(2,1)} %get-tuple-element.262), channel_id=1, source_target_pairs={{0,6},{1,7},{2,4},{3,5},{4,2},{5,3},{6,0},{7,1},{8,14},{9,15},{10,... | collective-permute-start | bytes 995336 | tf_op jit(solution)/shard_map/ppermute | solution.py:455
  660.7 20.7 %collective-permute-start.53 = (bf16[1296,128]{1,0:T(8,128)(2,1)}, bf16[1296,128]{1,0:T(8,128)(2,1)S(1)}, u32[]{:S(2)}, u32[]{:S(2)}) collective-permute-start(bf16[1296,128]{1,0:T(8,128)(2,1)} %broadcast_select_fusion), channel_id=1, source_target_pairs={{0,0},{2,1},{9,2},{11,3},{4,4},{6,5},{29,6},{31,7}} | collective-permute-start | bytes 995336 | tf_op jit(solution)/shard_map/ppermute | solution.py:340
  662.0 34.9 %collective-permute-start.54 = (bf16[1296,128]{1,0:T(8,128)(2,1)}, bf16[1296,128]{1,0:T(8,128)(2,1)}, u32[]{:S(2)}, u32[]{:S(2)}) collective-permute-start(bf16[1296,128]{1,0:T(8,128)(2,1)} %broadcast_select_fusion), channel_id=1, source_target_pairs={{8,0},{10,1},{17,2},{19,3},{12,4},{14,5},{7,6}} | collective-permute-start | bytes 995336 | tf_op jit(solution)/shard_map/ppermute | solution.py:340
  663.3 33.6 %collective-permute-start.55 = (bf16[1296,128]{1,0:T(8,128)(2,1)}, bf16[1296,128]{1,0:T(8,128)(2,1)}, u32[]{:S(2)}, u32[]{:S(2)}) collective-permute-start(bf16[1296,128]{1,0:T(8,128)(2,1)} %broadcast_select_fusion), channel_id=1, source_target_pairs={{16,0},{18,1},{25,2},{27,3},{20,4},{5,5},{15,6}} | collective-permute-start | bytes 995336 | tf_op jit(solution)/shard_map/ppermute | solution.py:340
  664.6 32.3 %collective-permute-start.56 = (bf16[1296,128]{1,0:T(8,128)(2,1)}, bf16[1296,128]{1,0:T(8,128)(2,1)}, u32[]{:S(2)}, u32[]{:S(2)}) collective-permute-start(bf16[1296,128]{1,0:T(8,128)(2,1)} %broadcast_select_fusion), channel_id=1, source_target_pairs={{24,0},{26,1},{3,2},{22,3},{28,4},{13,5},{23,6}} | collective-permute-start | bytes 995336 | tf_op jit(solution)/shard_map/ppermute | solution.py:340
  670.0 26.9 %collective-permute-start.57 = (bf16[1296,128]{1,0:T(8,128)(2,1)}, bf16[1296,128]{1,0:T(8,128)(2,1)}, u32[]{:S(2)}, u32[]{:S(2)}) collective-permute-start(bf16[1296,128]{1,0:T(8,128)(2,1)} %broadcast_select_fusion), channel_id=1, source_target_pairs={{2,0},{1,1},{11,2},{30,3},{6,4},{21,5},{31,6}} | collective-permute-start | bytes 995336 | tf_op jit(solution)/shard_map/ppermute | solution.py:340
  (100 other events, 917.2 us)
Sparse Core Ops, SparseCore 0:
  79.5 205.8 all-gather.4
  515.3 83.4 all-gather.6
  640.6 76.8 all-gather.8

commit v4 on v3

--- a/solution.py
+++ b/solution.py
@@ -494,7 +494,8 @@
 def mlp_both_ways(x, g, bias, gathered):
     f32, bf16 = jnp.float32, jnp.bfloat16
     rows = x.shape[0]
-    steps = FF // 256
+    tile = 512
+    steps = FF // tile
     full = BLOCK_B // 8
     used = USED_DOWN // 8
     wide = 2 * FF // 128
@@ -530,21 +531,23 @@
             return jnp.concatenate(
                 [
                     mix_ref[: D // 8, first + i].reshape(D, 128)
-                    for i in range(2)
+                    for i in range(tile // 128)
                 ],
                 axis=1,
             )
 
         x = x_ref[...]
-        w_gate, w_up = columns(2 * step), columns(wide // 2 + 2 * step)
+        w_gate, w_up = columns(tile // 128 * step), columns(wide // 2 + tile // 128 * step)
         gate = jnp.dot(x, w_gate, preferred_element_type=f32) + bias_g_ref[...]
         up = jnp.dot(x, w_up, preferred_element_type=f32) + bias_u_ref[...]
         sigma = jax.nn.sigmoid(gate)
         silu = gate * sigma
         hid = (silu * up).astype(bf16)
         hid_ref[...] = hid
-        low_rows = down_ref[pl.ds(step * 32 * chunks, 32 * chunks)].reshape(32, chunks, 8, 128)
-        w_down = jnp.concatenate([low_rows[:, j].reshape(256, 128) for j in range(chunks)], axis=1)
+        groups = tile // 8
+        low_rows = down_ref[pl.ds(step * groups * chunks, groups * chunks)]
+        low_rows = low_rows.reshape(groups, chunks, 8, 128)
+        w_down = jnp.concatenate([low_rows[:, j].reshape(tile, 128) for j in range(chunks)], axis=1)
         branch_ref[...] += jnp.dot(hid, w_down, preferred_element_type=f32)
         g_hid = lax.dot_general(g_ref[...], w_down, across, preferred_element_type=f32)
         g_gate = (g_hid * up * sigma * (1.0 + gate * (1.0 - sigma))).astype(bf16)
@@ -558,8 +561,8 @@
         ) + lax.dot_general(g_up, w_up, across, preferred_element_type=f32)
 
     whole = pl.BlockSpec((rows, D), lambda t: (0, 0))
-    part = pl.BlockSpec((rows, 256), lambda t: (0, t))
-    line = pl.BlockSpec((1, 256), lambda t: (0, t))
+    part = pl.BlockSpec((rows, tile), lambda t: (0, t))
+    line = pl.BlockSpec((1, tile), lambda t: (0, t))
     return pl.pallas_call(
         body,
         grid=(steps,),
@@ -567,7 +570,7 @@
             whole,
             whole,
             line,
-            pl.BlockSpec((1, 256), lambda t: (0, steps + t)),
+            pl.BlockSpec((1, tile), lambda t: (0, steps + t)),
             pl.BlockSpec(memory_space=pl.ANY),
         ],
         out_specs=[part, part, part, whole, whole, line, line],
@@ -582,7 +585,7 @@
         cost_estimate=pl.CostEstimate(
             flops=12 * rows * D * FF, bytes_accessed=30_000_000, transcendentals=rows * FF
         ),
-        compiler_params=pltpu.CompilerParams(vmem_limit_bytes=46 << 20),
+        compiler_params=pltpu.CompilerParams(vmem_limit_bytes=56 << 20),
         name="mlp_both_ways",
     )(x, g, bias, bias, gathered)
 
@@ -638,7 +641,7 @@
 
     place = PLACE_B[1]
 
-    def body(place_ref, xo, xp, gog, gpg, gou, gpu, ho, hp, go, gp, *outs):
+    def body(place_ref, xo7, xo8, xp7, xp8, gog, gpg, gou, gpu, ho, hp, go, gp, *outs):
         step = pl.program_id(0)
 
         @pl.when(step == 0)
@@ -656,16 +659,17 @@
 
         @pl.when(step < mlp_steps)
         def _():
+            xo = jnp.concatenate([xo7[...], xo8[...]], axis=1)
+            xp = jnp.concatenate([xp7[...], xp8[...]], axis=1)
             for out_ref, g_own, g_par in ((outs[0], gog, gpg), (outs[1], gou, gpu)):
                 value = pair_product(xo, xp, g_own, g_par)
-                skip = value.shape[0] - mlp_groups * 8
                 for group in range(mlp_groups):
                     first = place[16 + group // 7] * half_tiles + group % 7 * (FF // 128)
                     store_tiles(
                         out_ref,
                         (),
                         first + step * 4,
-                        value[skip + 8 * group : skip + 8 * group + 8],
+                        value[8 * group : 8 * group + 8],
                     )
 
         @pl.when(step >= mlp_steps)
@@ -683,7 +687,7 @@
                 pl.when(part % 2 == 0)(lambda put=put: put(outs[0]))
                 pl.when(part % 2 == 1)(lambda put=put: put(outs[1]))
 
-    x_spec = pl.BlockSpec((rows, 384), lambda t: (0, 2))
+    x_specs = [pl.BlockSpec((rows, 128), lambda t: (0, 7)), pl.BlockSpec((rows, 128), lambda t: (0, 8))]
     g_spec = pl.BlockSpec((rows, 512), lambda t: (0, jnp.minimum(t, mlp_steps - 1)))
     h_spec = pl.BlockSpec((rows, wide), lambda t: (0, jnp.maximum(t - mlp_steps, 0)))
     b_spec = pl.BlockSpec((rows, D), lambda t: (0, 0))
@@ -693,7 +697,7 @@
         body,
         grid=(mlp_steps + down_steps,),
         in_specs=[pl.BlockSpec(memory_space=pltpu.SMEM)]
-        + [x_spec] * 2
+        + x_specs * 2
         + [g_spec] * 4
         + [h_spec] * 2
         + [b_spec] * 2,
@@ -701,7 +705,7 @@
         out_shape=[jax.ShapeDtypeStruct(shape, bf16)] * 2,
         compiler_params=pltpu.CompilerParams(vmem_limit_bytes=44 << 20),
         name="grads_b_core_1",
-    )(down_place, *in_b, *g_gate, *g_up, *hidden, *g_branch)
+    )(down_place, in_b[0], in_b[0], in_b[1], in_b[1], *g_gate, *g_up, *hidden, *g_branch)
     return [part.reshape(-1, 128) for part in out]
 
 
@@ -1030,9 +1034,9 @@
             jnp.zeros(packed_rows * 128 - cond_count - bias_count, bf16),
         ]
     ).reshape(packed_rows, 128)
-    pieces_a = cut_pieces(weight_flat, PLAN_A)
-    packed, pieces_a = lax.optimization_barrier((packed, pieces_a))
-    gathered = gathered_weights(pieces_a, cut_pieces(weight_flat, PLAN_B))
+    pieces = cut_pieces(weight_flat, PLAN_A), cut_pieces(weight_flat, PLAN_B)
+    packed, pieces = lax.optimization_barrier((packed, pieces))
+    gathered = gathered_weights(*pieces)
     packed_all = gather_columns(gather_column(packed)).reshape(DEVICES, -1)
     cond_all = packed_all[:, :cond_count].reshape(images, D).astype(f32)
     places = lax.broadcasted_iota(jnp.int32, (DEVICES, DEVICES), 0)
@@ -1053,6 +1057,15 @@
     cond_rows = lax.dynamic_slice_in_dim(
         jnp.pad(cond_act.T, ((ADA_ROWS, ADA_ROWS), (0, 0))), ada_start, ADA_ROWS, 0
     )
+    cond_ordered = jnp.dot(
+        chosen, cond_act.reshape(DEVICES, cond_count), preferred_element_type=f32
+    ).astype(bf16)
+    rows_ordered = lax.dynamic_slice_in_dim(
+        jnp.pad(cond_ordered.reshape(images, D).T, ((ADA_ROWS, ADA_ROWS), (0, 0))),
+        ada_start,
+        ADA_ROWS,
+        0,
+    )
     terms = jnp.einsum("km,kn->mn", cond_rows, ada_local, preferred_element_type=f32)
     modulation = sum_to_owners(terms.reshape(DEVICES, slots, 6 * D)) + b_ada
     w_qkv, w_out = split_a(gathered)
@@ -1079,6 +1092,7 @@
     normed_b, inv_b = norm_parts(middle)
     input_b = (normed_b * (1.0 + scale_b) + shift_b).astype(bf16).reshape(rows_all, D)
     early = [share(array) for array in (input_a, attended, input_b, g_branch_b)]
+    input_b = after(input_b, early[0], early[3])
     hidden, g_gate, g_up, branch_b, g_input_b, sum_gate, sum_up = mlp_both_ways(
         input_b, g_branch_b, b_mlp.reshape(1, 2 * FF), gathered
     )
@@ -1102,15 +1116,15 @@
     orders = (SWAP_Y, SWAP_X), (SWAP_X, SWAP_Y)
     sends_b = first_sends(grads_b, BLOCK_B)
     arrived = over_planes(sends_b, orders[0])
-    g_attended = jnp.einsum("re,de->rd", g_branch_a, w_out, preferred_element_type=f32)
-    g_attended = after(g_attended.astype(bf16), sends_b)
+    g_attended = jnp.einsum(
+        "re,de->rd", after(g_branch_a, sends_b), w_out, preferred_element_type=f32
+    )
+    g_attended = g_attended.astype(bf16)
     g_projected, proj_sums = attention_backward(
         projected, queries, keys, values, log_total, g_attended, cosines, sines
     )
     grad_b_qkv = jnp.sum(proj_sums, axis=(0, 1))
     shared_proj = share(g_projected)
-    kept_b, sends_b = second_sends(grads_b, after(arrived, g_projected), BLOCK_B)
-    g_projected, shared_proj = after((g_projected, shared_proj), sends_b)
     g_input_a = jnp.einsum("re,de->rd", g_projected, w_qkv, preferred_element_type=f32)
     g_input_a = lax.optimization_barrier(g_input_a).reshape(slots, length, D)
     g_shift_a = jnp.sum(g_input_a, axis=1)
@@ -1120,10 +1134,9 @@
     ).astype(bf16)
     bias_sums = [grad_b_qkv, grad_b_out, sum_gate.reshape(-1), sum_up.reshape(-1)]
     small = jnp.concatenate([g_modulation.reshape(-1)] + [b.astype(bf16) for b in bias_sums])
-    shared_proj = after(shared_proj, small)
-    small_all = lax.all_gather(small.reshape(-1, 128), axes, axis=0, tiled=False).reshape(
-        DEVICES, -1
-    )
+    kept_b, sends_b = second_sends(grads_b, after(arrived, small), BLOCK_B)
+    shared_proj = after(shared_proj, sends_b)
+    small_all = lax.all_gather(small.reshape(-1, 128), axes, axis=0, tiled=True)
     made_a = lax.cond(
         core == 0,
         lambda: grads_a(0, early[0], shared_proj, early[1], shared_branch_a),
@@ -1150,15 +1163,13 @@
     )
     planes_a = plane_sums(kept_a, after(over_planes(sends_a, orders[1]), sum_b))
     sends_a = line_sends(planes_a)
+    small_all = after(small_all, sends_a).reshape(DEVICES, -1)
+    g_mod_all = small_all[:, : slots * 6 * D].reshape(images, 6 * D)
+    g_cond_rows = jnp.einsum("mn,kn->mk", g_mod_all, ada_local, preferred_element_type=f32)
     back_b = send_back(after(sum_b, sends_a), PLAN_B, PLACE_B)
     sum_a = sum_line(sends_a[0], after(from_line(sends_a), back_b)).astype(bf16)
     sum_a = jnp.where(is_kind(PLACE_A, QKV_BLOCKS), from_tiles(sum_a, 9), from_tiles(sum_a, 27))
     back_a = send_back(sum_a, PLAN_A, PLACE_A)
-    g_mod_all = (
-        jnp.dot(chosen, small_all[:, : slots * 6 * D], preferred_element_type=f32)
-        .astype(bf16)
-        .reshape(images, 6 * D)
-    )
     grad_biases = jnp.concatenate(
         [
             jnp.sum(small_all[:, slots * 6 * D :].astype(f32), axis=0),
@@ -1166,15 +1177,10 @@
         ]
     )
     part_biases = lax.dynamic_slice_in_dim(grad_biases, me * bias_count, bias_count, 0)
-    grad_ada = jnp.einsum("km,mn->kn", cond_rows, g_mod_all, preferred_element_type=f32)
-    g_cond_rows = jnp.einsum("mn,kn->mk", g_mod_all, ada_local, preferred_element_type=f32)
-    rows_of_all = lax.all_gather(
-        jnp.pad(g_cond_rows, ((0, 0), (0, 128 - ADA_ROWS))), axes, axis=0, tiled=False
-    )
-    came = jnp.where(
-        (jnp.arange(DEVICES)[:, None] ^ me) == jnp.arange(DEVICES)[None, :], 1.0, 0.0
-    )[:, :, None, None] * rows_of_all[:, :, :ADA_ROWS].reshape(DEVICES, DEVICES, slots, ADA_ROWS)
-    came = jnp.sum(came, axis=1)
+    grad_ada = jnp.einsum("km,mn->kn", rows_ordered, g_mod_all, preferred_element_type=f32)
+    came = lax.all_to_all(
+        g_cond_rows.reshape(DEVICES, slots, ADA_ROWS), axes, split_axis=0, concat_axis=0, tiled=True
+    )
     first = FIRST_ADA * 128 // (6 * D)
     g_cond = came.transpose(1, 0, 2).reshape(slots, DEVICES * ADA_ROWS)[:, first : first + D]
     cond_f = conditions.astype(f32)

time: 741 us -> 723 us (0.976)
  waiting for transfers between devices: 297 us -> 273 us
  starting transfers between devices: 86.7 us -> 110 us
  Pallas kernels: 156 us -> 147 us
    ppermute x9, waiting for transfers between devices: 17.1 us -> 0.02 us  [share(): return (array, lax.ppermute(array, 'dp', SWAP_CORE))]
    ppermute x6, waiting for transfers between devices: 50.7 us -> 35.5 us  [from_line(): lax.ppermute(sends[k], 'dp', [(d, d ^ 2 * k) for d in range(8)])]
    unnamed x225 -> x172, local copies, waits for them, and re-layouts: 27.7 us -> 15 us
    pallas_call x1, Pallas kernels: 50.4 us -> 38.6 us  [mlp_both_ways(): pl.pallas_call(body, grid=(steps,), in_specs=[whole, whole, line, pl.Bloc...]
    ppermute x8, waiting for transfers between devices: 24.7 us -> 34.2 us  [over_planes(): lax.ppermute(send, 'fsdp', axis)]
    all_gather x2 -> x1, waiting for transfers between devices: 8.76 us -> 0.01 us  [on_device_32(): small_all = lax.all_gather(small.reshape(-1, 128), axes, axis=0, tiled=True)]
    all_to_all x0 -> x1, waiting for transfers between devices: none -> 8.5 us  [on_device_32(): lax.all_to_all(g_cond_rows.reshape(DEVICES, slots, ADA_ROWS), axes, split...]
    all_gather x1, waiting for transfers between devices: 116 us -> 108 us  [gathered_weights(): lax.all_gather(block, ('fsdp', 'dp'), axis=0, tiled=True)]
  transfers between devices with their start and end apart: 61 -> 61, of which waited for: 19 -> 19; matrix products, arithmetic and copies ran while one was open for 17% -> 19% of each run, Pallas kernels for 6% -> 14%
where the time goes in v4:
time: 723 us; the launch traced here: 713 us
  waiting for transfers between devices  273 us (38%)
  Pallas kernels  147 us (20%)
  starting transfers between devices  110 us (15%)
  local copies, waits for them, and re-layouts  74.8 us (10%)
  other arithmetic  62.6 us (9%)
  matrix products  29.7 us (4%)
  between operations  16 us (2%)
    all_gather x1, waiting for transfers between devices, gathered_weights(): lax.all_gather(block, ('fsdp', 'dp'), axis=0, tiled=True)  108 us
    ppermute x9, waiting for transfers between devices, spread(): got = lax.ppermute(piece, ('fsdp', 'dp'), pairs)  38.9 us
    pallas_call x1, Pallas kernels, mlp_both_ways(): pl.pallas_call(body, grid=(steps,), in_specs=[whole, whole, line, pl.Bloc...  38.6 us
    ppermute x6, waiting for transfers between devices, from_line(): lax.ppermute(sends[k], 'dp', [(d, d ^ 2 * k) for d in range(8)])  35.5 us
    ppermute x8, waiting for transfers between devices, over_planes(): lax.ppermute(send, 'fsdp', axis)  34.2 us
    pallas_call x1, Pallas kernels, grads_b_core_1(): pl.pallas_call(body, grid=(mlp_steps + down_steps,), in_specs=[pl.BlockSp...  33.7 us
    pallas_call x1, Pallas kernels, attention_backward(): pl.pallas_call(body, grid=(images,), in_specs=[pl.BlockSpec((length, 2 *...  26.7 us
    ppermute x9, starting transfers between devices, send_back(): lax.ppermute(block, ('fsdp', 'dp'), [(device, owner) for owner, device in...  26.7 us
  transfers between devices with their start and end apart: 61, of which 19 were waited for; matrix products, arithmetic and copies ran while one was open for 19% of the time, Pallas kernels for 14%

profile of v4, /device:TPU:9, one launch (start us, length us, event | category | flops | bytes accessed | tf_op | source)
XLA Modules:
  0.0 713.2 jit_solution(4562924175260305006)
XLA Ops:
  8.9 3.8 pad_dynamic-slice_fusion
  12.8 4.3 pad_dynamic-slice_fusion.12
  17.1 4.1 collective-permute-start.17
  21.2 3.0 collective-permute-start.18
  24.2 2.0 collective-permute-start.19
  28.2 2.0 collective-permute-start.21
  30.2 6.1 collective-permute-done.17
  37.8 15.1 %collective-permute-done.18 = bf16[1296,128]{1,0:T(8,128)(2,1)} collective-permute-done((bf16[1296,128]{1,0:T(8,128)(2,1)}, bf16[1296,128]{1,0:T(8,128)(2,1)}, u32[]{:S(2)}, u32[]{:S(2)}) %collective-permute-start.18) | collective-permute-done | bytes 331808 | tf_op jit(solution)/shard_map/ppermute | solution.py:331
  54.4 3.1 collective-permute-done.19
  63.0 14.5 %collective-permute-done.24 = bf16[2688,128]{1,0:T(8,128)(2,1)} collective-permute-done((bf16[2688,128]{1,0:T(8,128)(2,1)}, bf16[2688,128]{1,0:T(8,128)(2,1)}, u32[]{:S(2)}, u32[]{:S(2)}) %collective-permute-start.24) | collective-permute-done | bytes 688160 | tf_op jit(solution)/shard_map/ppermute | solution.py:331
  83.9 2.0 collective-permute-start.2
  85.9 7.5 %collective-permute-start.3 = (bf16[23,128]{1,0:T(8,128)(2,1)S(1)}, bf16[23,128]{1,0:T(8,128)(2,1)S(1)}, u32[]{:S(2)}, u32[]{:S(2)}) collective-permute-start(bf16[23,128]{1,0:T(8,128)(2,1)S(1)} %bitcast.323), channel_id=1, source_target_pairs={{0,4},{1,5},{2,6},{3,7},{4,0},{5,1},{6,2},{7,3},{8,12},{9,13},{10,... | collective-permute-start | bytes 17672 | tf_op jit(solution)/shard_map/ppermute | solution.py:468
  96.2 2.9 collective-permute-start.5
  104.9 7.8 %collective-permute-start.9 = (bf16[8,23,128]{2,1,0:T(8,128)(2,1)}, bf16[8,23,128]{2,1,0:T(8,128)(2,1)}, u32[]{:S(2)}, u32[]{:S(2)}) collective-permute-start(bf16[8,23,128]{2,1,0:T(8,128)(2,1)} %constant_dynamic-update-slice_fusion), channel_id=1, source_target_pairs={{0,24},{8,16},{16,8},{24,0},{1,25},{9,17},{17,9},{25,1},{2,26},{10... | collective-permute-start | bytes 141320 | tf_op jit(solution)/shard_map/ppermute | solution.py:475
  112.8 2.7 reshape.575
  133.4 14.5 %collective-permute-done.12 = f32[4,2,6912]{2,0,1:T(4,128)S(1)} collective-permute-done((f32[4,2,6912]{2,0,1:T(4,128)S(1)}, f32[4,2,6912]{2,0,1:T(4,128)S(1)}, u32[]{:S(2)}, u32[]{:S(2)}) %collective-permute-start.12) | collective-permute-done | bytes 221216 | tf_op jit(solution)/shard_map/ppermute | solution.py:486
  147.9 7.2 %collective-permute-done.13 = f32[4,2,6912]{2,0,1:T(4,128)S(1)} collective-permute-done((f32[4,2,6912]{2,0,1:T(4,128)S(1)}, f32[4,2,6912]{2,0,1:T(4,128)S(1)}, u32[]{:S(2)}, u32[]{:S(2)}) %collective-permute-start.13) | collective-permute-done | bytes 221216 | tf_op jit(solution)/shard_map/ppermute | solution.py:486
  157.6 1.9 collective-permute-start.15
  167.3 3.5 collective-permute-done.16
  172.4 2.3 fusion.9
  174.7 2.3 collective-permute-start.26
  177.0 2.1 fusion.10.g_ref
  179.1 108.2 %all-gather.3.cloned.1.call-done = bf16[127488,128]{1,0:T(8,128)(2,1)} async-done(((bf16[3984,128]{1,0:T(8,128)(2,1)}), bf16[127488,128]{1,0:T(8,128)(2,1)}) %all-gather.3.cloned.1.call-update) | async-done | bytes 32636944 | tf_op jit(solution)/shard_map/all_gather | solution.py:783
  287.3 4.3 split_a.1
  291.6 9.5 %convolution_add_fusion.proj_ref = f32[512,3456]{1,0:T(8,128)} fusion(bf16[512,1152]{1,0:T(8,128)(2,1)} %fusion.9, bf16[1152,3456]{1,0:T(8,128)(2,1)S(1)} %bitcast.279, f32[3456]{0:T(1024)S(1)} %slice-done.2), kind=kOutput, calls=%fused_computation | convolution fusion | flops 4078632960 | bytes 16233984 | tf_op jit(solution)/shard_map/dot_general | solution.py:1086
  301.1 23.1 %attention_forward.1 = (bf16[512,1152]{1,0:T(8,128)(2,1)S(1)}, bf16[512,1152]{1,0:T(8,128)(2,1)S(1)}, bf16[512,1152]{1,0:T(8,128)(2,1)S(1)}, bf16[512,1152]{1,0:T(8,128)(2,1)S(1)}, f32[512,16]{1,0:T(8,128)S(1)}) custom-call(f32[512,3456]{1,0:T(8,128)} %convolution_add_fusion.proj_ref, f32[256,1152]{1,0:T(8,128)S(1)} %copy.71.cos_ref, ...), custom_call_target="tpu_custom_call" | custom-call | flops 1207959552 | bytes 20000000 | tf_op jit(solution)/shard_map/attention_forward/pallas_call | solution.py:856
  324.3 3.3 fusion.74
  330.0 38.6 %mlp_both_ways.1 = (bf16[512,3072]{1,0:T(8,128)(2,1)}, bf16[512,3072]{1,0:T(8,128)(2,1)}, bf16[512,3072]{1,0:T(8,128)(2,1)}, f32[512,1152]{1,0:T(8,128)}, f32[51...) custom-call(bf16[512,1152]{1,0:T(8,128)(2,1)} %fusion.15.x_ref, bf16[512,1152]{1,0:T(8,128)(2,1)} %fusion.10.g_ref, ...), custom_call_target="tpu_custom_call" | custom-call | flops 21743271936 | bytes 30000000 | tf_op jit(solution)/shard_map/mlp_both_ways/pallas_call | solution.py:566
  372.1 5.6 fusion.19
  380.8 5.2 fusion.72
  392.4 34.4 %conditional.2 = (bf16[2,2,4,1344,128]{4,3,2,1,0:T(8,128)(2,1)}, bf16[2,2,4,1344,128]{4,3,2,1,0:T(8,128)(2,1)S(1)}) conditional(s32[]{:T(128)} %convert_element_type.267, (bf16[512,1152]{1,0:T(8,128)(2,1)}, bf16[512,1152]{1,0:T(8,128)(2,1)}, bf16[512,3072]{1,0:T(8,128)(2,1)}, bf16[512,3072]{1,0:T(8,128)(2,1)}, bf16[512,3072]{1,0:T(8,128)(2,1)}, ...), branch_computations={%region_6.7_spmd.clone, %region_7.8_spmd} | conditional | bytes 220 | solution.py:1111
  393.1 33.7 %grads_b_core_1.1 = (bf16[2688,8,128]{2,1,0:T(8,128)(2,1)}, bf16[2688,8,128]{2,1,0:T(8,128)(2,1)S(1)}) custom-call(s32[11]{0:T(128)S(1)} %copy-done.12, bf16[512,1152]{1,0:T(8,128)(2,1)} %get-tuple-element.215.xo7.xo8, bf16[512,1152]{1,0:T(8,128)(2,1)} %get-tuple-element.215.xo7.xo8, bf16[512,1152]{1,0:T(8,128)(2,1)} %get-tuple-element.216.xp7.xp8, ...), custom_call_target="tpu_custom_call" | custom-call | tf_op jit(solution)/shard_map/cond/branch_0_fun/grads_b_core_1/pallas_call | solution.py:696
  428.6 2.3 copy-done.35
  437.3 26.7 %attention_backward.1 = (bf16[512,3456]{1,0:T(8,128)(2,1)}, f32[2,1,3456]{2,1,0:T(1,128)S(1)}) custom-call(f32[512,3456]{1,0:T(8,128)} %convolution_add_fusion.proj_ref, bf16[512,1152]{1,0:T(8,128)(2,1)S(1)} %get-tuple-element.173.q_ref, bf16[512,1152]{1,0:T(8,128)(2,1)S(1)} %copy-done.3, bf16[512,1152]{1,0:T(8,128)(2,1)S(1)} %copy-done.5, ...), custom_call_target="tpu_custom_call" | custom-call | flops 1000 | bytes 1000 | tf_op jit(solution)/shard_map/attention_backward/pallas_call | solution.py:915
  464.2 7.0 fusion.79
  472.8 3.0 fusion.17
  478.6 3.3 fusion
  483.2 3.4 fusion.1
  488.6 4.6 collective-permute-start.40
  493.2 5.7 collective-permute-start.39
  499.0 2.7 reshape.576
  502.1 2.5 fusion.18
  504.7 14.8 %conditional.3 = (bf16[2,2,4,648,128]{4,3,2,1,0:T(8,128)(2,1)S(1)}, bf16[2,2,4,648,128]{4,3,2,1,0:T(8,128)(2,1)S(1)}) conditional(s32[]{:T(128)} %convert_element_type.267, (bf16[512,1152]{1,0:T(8,128)(2,1)}, bf16[512,1152]{1,0:T(8,128)(2,1)}, bf16[512,3456]{1,0:T(8,128)(2,1)}, bf16[512,3456]{1,0:T(8,128)(2,1)}, bf16[512,1152]{1,0:T(8,128)(2,1)}, ...), branch_computations={%region_18.19_spmd, %region_19.20_spmd} | conditional | bytes 16 | solution.py:1140
  504.8 14.6 %grads_a_core_1.1 = (bf16[16,81,8,128]{3,2,1,0:T(8,128)(2,1)S(1)}, bf16[16,81,8,128]{3,2,1,0:T(8,128)(2,1)S(1)}) custom-call(bf16[512,1152]{1,0:T(8,128)(2,1)} %get-tuple-element.88.xo, bf16[512,1152]{1,0:T(8,128)(2,1)} %get-tuple-element.89.xp, bf16[512,3456]{1,0:T(8,128)(2,1)} %get-tuple-element.90.go, bf16[512,3456]{1,0:T(8,128)(2,1)} %get-tuple-element.91.gp, ...), custom_call_target="tpu_custom_call" | custom-call | tf_op jit(solution)/shard_map/cond/branch_0_fun/grads_a_core_1/pallas_call | solution.py:760
  522.3 3.1 collective-permute-done.40
  525.3 5.7 collective-permute-done.39
  535.0 2.1 collective-permute-start.44
  537.4 24.1 %collective-permute-done.38 = bf16[2,4,648,128]{3,2,1,0:T(8,128)(2,1)S(1)} collective-permute-done((bf16[2,4,648,128]{3,2,1,0:T(8,128)(2,1)S(1)}, bf16[2,4,648,128]{3,2,1,0:T(8,128)(2,1)S(1)}, u32[]{:S(2)}, u32[]{:S(2)}) %collective-permute-start.38) | collective-permute-done | bytes 1327136 | tf_op jit(solution)/shard_map/ppermute | solution.py:428
  566.3 3.2 collective-permute-done.44
  569.4 31.7 %collective-permute-done.45 = bf16[2688,128]{1,0:T(8,128)(2,1)S(1)} collective-permute-done((bf16[2688,128]{1,0:T(8,128)(2,1)S(1)}, bf16[2688,128]{1,0:T(8,128)(2,1)S(1)}, u32[]{:S(2)}, u32[]{:S(2)}) %collective-permute-start.45) | collective-permute-done | bytes 688160 | tf_op jit(solution)/shard_map/ppermute | solution.py:455
  602.8 2.2 reshape.550
  611.2 2.2 multiply_add_fusion
  615.0 6.0 collective-permute-start.47
  622.6 3.4 collective-permute-start.51
  628.2 2.0 fusion.24
  630.9 6.9 all-to-all-start
  639.3 2.3 fusion.54
  643.8 2.6 reshape.559.refs_9_
  646.5 8.5 %all-to-all-done = f32[32,2,108]{2,1,0:T(2,128)S(1)} async-done(((f32[32,2,108]{2,1,0:T(2,128)}), f32[32,2,108]{2,1,0:T(2,128)S(1)}, u32[]{:S(2)}, u32[]{:S(2)}) %all-to-all-start) | async-done | bytes 27680 | tf_op jit(solution)/shard_map/all_to_all | solution.py:1181
  657.6 2.0 reshape.554
  665.4 10.8 %collective-permute-start.56 = (bf16[1296,128]{1,0:T(8,128)(2,1)S(1)}, bf16[1296,128]{1,0:T(8,128)(2,1)S(1)}, u32[]{:S(2)}, u32[]{:S(2)}) collective-permute-start(bf16[1296,128]{1,0:T(8,128)(2,1)S(1)} %broadcast_select_fusion), channel_id=1, source_target_pairs={{24,0},{26,1},{3,2},{22,3},{28,4},{13,5},{23,6}} | collective-permute-start | bytes 995336 | tf_op jit(solution)/shard_map/ppermute | solution.py:340
  678.2 3.8 collective-permute-done.53.refs_4_
  682.0 18.5 %collective-permute-done.54.refs_5_ = bf16[1296,128]{1,0:T(8,128)(2,1)S(1)} collective-permute-done((bf16[1296,128]{1,0:T(8,128)(2,1)S(1)}, bf16[1296,128]{1,0:T(8,128)(2,1)S(1)}, u32[]{:S(2)}, u32[]{:S(2)}) %collective-permute-start.54) | collective-permute-done | bytes 331808 | tf_op jit(solution)/shard_map/ppermute | solution.py:340
  700.5 5.7 owned_rows.1
  (382 shorter events, 127.9 us)
Async XLA Ops:
  7.2 280.1 %all-gather.3.cloned.1.call-start = ((), (), s32[]{:S(2)}) async-start(), calls=%async_computation.1 | async-start | bytes 33656832 | tf_op jit(solution)/shard_map/all_gather | solution.py:783
  17.1 19.2 %collective-permute-start.17 = (bf16[1296,128]{1,0:T(8,128)(2,1)}, bf16[1296,128]{1,0:T(8,128)(2,1)S(1)}, u32[]{:S(2)}, u32[]{:S(2)}) collective-permute-start(bf16[1296,128]{1,0:T(8,128)(2,1)} %get-tuple-element.158), channel_id=1, source_target_pairs={{0,0},{1,4},{2,9},{3,13},{4,18},{5,22},{6,27},{7,31}} | collective-permute-start | bytes 995336 | tf_op jit(solution)/shard_map/ppermute | solution.py:331
  21.2 31.7 %collective-permute-start.18 = (bf16[1296,128]{1,0:T(8,128)(2,1)}, bf16[1296,128]{1,0:T(8,128)(2,1)}, u32[]{:S(2)}, u32[]{:S(2)}) collective-permute-start(bf16[1296,128]{1,0:T(8,128)(2,1)} %get-tuple-element.159), channel_id=1, source_target_pairs={{0,1},{1,5},{2,10},{3,14},{4,19},{5,23},{6,28}} | collective-permute-start | bytes 995336 | tf_op jit(solution)/shard_map/ppermute | solution.py:331
  24.2 33.3 %collective-permute-start.19 = (bf16[1296,128]{1,0:T(8,128)(2,1)}, bf16[1296,128]{1,0:T(8,128)(2,1)}, u32[]{:S(2)}, u32[]{:S(2)}) collective-permute-start(bf16[1296,128]{1,0:T(8,128)(2,1)} %get-tuple-element.160), channel_id=1, source_target_pairs={{0,2},{1,6},{2,11},{3,15},{4,20},{5,24},{6,29}} | collective-permute-start | bytes 995336 | tf_op jit(solution)/shard_map/ppermute | solution.py:331
  26.2 32.6 %collective-permute-start.20 = (bf16[1296,128]{1,0:T(8,128)(2,1)S(1)}, bf16[1296,128]{1,0:T(8,128)(2,1)}, u32[]{:S(2)}, u32[]{:S(2)}) collective-permute-start(bf16[1296,128]{1,0:T(8,128)(2,1)S(1)} %get-tuple-element.161), channel_id=1, source_target_pairs={{0,3},{1,7},{2,12},{3,16},{4,21},{5,25},{6,30}} | collective-permute-start | bytes 995336 | tf_op jit(solution)/shard_map/ppermute | solution.py:331
  28.2 32.2 %collective-permute-start.21 = (bf16[1296,128]{1,0:T(8,128)(2,1)S(1)}, bf16[1296,128]{1,0:T(8,128)(2,1)}, u32[]{:S(2)}, u32[]{:S(2)}) collective-permute-start(bf16[1296,128]{1,0:T(8,128)(2,1)S(1)} %get-tuple-element.162), channel_id=1, source_target_pairs={{0,4},{1,8},{2,13},{3,17},{4,22},{5,26},{6,31}} | collective-permute-start | bytes 995336 | tf_op jit(solution)/shard_map/ppermute | solution.py:331
  36.3 26.8 %collective-permute-start.22 = (bf16[2688,128]{1,0:T(8,128)(2,1)}, bf16[2688,128]{1,0:T(8,128)(2,1)}, u32[]{:S(2)}, u32[]{:S(2)}) collective-permute-start(bf16[2688,128]{1,0:T(8,128)(2,1)} %get-tuple-element.163), channel_id=1, source_target_pairs={{8,1},{9,4},{10,6},{11,8},{12,10},{13,12},{14,14},{15,17},{16,19},... | collective-permute-start | bytes 2064392 | tf_op jit(solution)/shard_map/ppermute | solution.py:331
  52.9 10.2 %collective-permute-start.23 = (bf16[2688,128]{1,0:T(8,128)(2,1)}, bf16[2688,128]{1,0:T(8,128)(2,1)}, u32[]{:S(2)}, u32[]{:S(2)}) collective-permute-start(bf16[2688,128]{1,0:T(8,128)(2,1)} %get-tuple-element.164), channel_id=1, source_target_pairs={{7,0},{8,2},{9,5},{10,7},{11,9},{12,11},{13,13},{14,15},{15,18},{1... | collective-permute-start | bytes 2064392 | tf_op jit(solution)/shard_map/ppermute | solution.py:331
  57.5 20.1 %collective-permute-start.24 = (bf16[2688,128]{1,0:T(8,128)(2,1)}, bf16[2688,128]{1,0:T(8,128)(2,1)}, u32[]{:S(2)}, u32[]{:S(2)}) collective-permute-start(bf16[2688,128]{1,0:T(8,128)(2,1)} %get-tuple-element.165), channel_id=1, source_target_pairs={{7,1},{8,3},{9,6},{10,8},{11,10},{12,12},{13,14},{14,16},{15,19},{... | collective-permute-start | bytes 2064392 | tf_op jit(solution)/shard_map/ppermute | solution.py:331
  58.8 18.8 %collective-permute-start.25 = (bf16[2688,128]{1,0:T(8,128)(2,1)S(1)}, bf16[2688,128]{1,0:T(8,128)(2,1)}, u32[]{:S(2)}, u32[]{:S(2)}) collective-permute-start(bf16[2688,128]{1,0:T(8,128)(2,1)S(1)} %get-tuple-element.166), channel_id=1, source_target_pairs={{8,4},{14,17},{29,27}} | collective-permute-start | bytes 2064392 | tf_op jit(solution)/shard_map/ppermute | solution.py:331
  83.7 542.3 %all-gather.5.cloned.1.call-start = ((), (), s32[]{:S(2)}) async-start(), calls=%async_computation.2 | async-start | bytes 1622016 | tf_op jit(solution)/shard_map/all_gather | solution.py:1139
  83.7 12.5 %collective-permute-start = (bf16[23,128]{1,0:T(8,128)(2,1)S(1)}, bf16[23,128]{1,0:T(8,128)(2,1)S(1)}, u32[]{:S(2)}, u32[]{:S(2)}) collective-permute-start(bf16[23,128]{1,0:T(8,128)(2,1)S(1)} %bitcast.320), channel_id=1, source_target_pairs={{0,1},{1,0},{2,3},{3,2},{4,5},{5,4},{6,7},{7,6},{8,9},{9,8},{10,11... | collective-permute-start | bytes 17672 | tf_op jit(solution)/shard_map/ppermute | solution.py:468
  83.8 15.9 %collective-permute-start.1 = (bf16[23,128]{1,0:T(8,128)(2,1)S(1)}, bf16[23,128]{1,0:T(8,128)(2,1)S(1)}, u32[]{:S(2)}, u32[]{:S(2)}) collective-permute-start(bf16[23,128]{1,0:T(8,128)(2,1)S(1)} %bitcast.321), channel_id=1, source_target_pairs={{0,2},{1,3},{2,0},{3,1},{4,6},{5,7},{6,4},{7,5},{8,10},{9,11},{10,... | collective-permute-start | bytes 17672 | tf_op jit(solution)/shard_map/ppermute | solution.py:468
  83.9 16.4 %collective-permute-start.2 = (bf16[23,128]{1,0:T(8,128)(2,1)S(1)}, bf16[23,128]{1,0:T(8,128)(2,1)S(1)}, u32[]{:S(2)}, u32[]{:S(2)}) collective-permute-start(bf16[23,128]{1,0:T(8,128)(2,1)S(1)} %bitcast.322), channel_id=1, source_target_pairs={{0,3},{1,2},{2,1},{3,0},{4,7},{5,6},{6,5},{7,4},{8,11},{9,10},{10,... | collective-permute-start | bytes 17672 | tf_op jit(solution)/shard_map/ppermute | solution.py:468
  85.9 14.9 %collective-permute-start.3 = (bf16[23,128]{1,0:T(8,128)(2,1)S(1)}, bf16[23,128]{1,0:T(8,128)(2,1)S(1)}, u32[]{:S(2)}, u32[]{:S(2)}) collective-permute-start(bf16[23,128]{1,0:T(8,128)(2,1)S(1)} %bitcast.323), channel_id=1, source_target_pairs={{0,4},{1,5},{2,6},{3,7},{4,0},{5,1},{6,2},{7,3},{8,12},{9,13},{10,... | collective-permute-start | bytes 17672 | tf_op jit(solution)/shard_map/ppermute | solution.py:468
  93.4 8.0 %collective-permute-start.4 = (bf16[23,128]{1,0:T(8,128)(2,1)S(1)}, bf16[23,128]{1,0:T(8,128)(2,1)S(1)}, u32[]{:S(2)}, u32[]{:S(2)}) collective-permute-start(bf16[23,128]{1,0:T(8,128)(2,1)S(1)} %bitcast.324), channel_id=1, source_target_pairs={{0,5},{1,4},{2,7},{3,6},{4,1},{5,0},{6,3},{7,2},{8,13},{9,12},{10,... | collective-permute-start | bytes 17672 | tf_op jit(solution)/shard_map/ppermute | solution.py:468
  96.2 5.9 collective-permute-start.5
  99.7 3.5 collective-permute-start.6
  103.8 13.1 %collective-permute-start.7 = (bf16[8,23,128]{2,1,0:T(8,128)(2,1)}, bf16[8,23,128]{2,1,0:T(8,128)(2,1)}, u32[]{:S(2)}, u32[]{:S(2)}) collective-permute-start(bf16[8,23,128]{2,1,0:T(8,128)(2,1)} %constant_dynamic-update-slice_fusion), channel_id=1, source_target_pairs={{0,8},{8,0},{16,24},{24,16},{1,9},{9,1},{17,25},{25,17},{2,10},{10... | collective-permute-start | bytes 141320 | tf_op jit(solution)/shard_map/ppermute | solution.py:475
  103.8 13.1 %collective-permute-start.8 = (bf16[8,23,128]{2,1,0:T(8,128)(2,1)}, bf16[8,23,128]{2,1,0:T(8,128)(2,1)}, u32[]{:S(2)}, u32[]{:S(2)}) collective-permute-start(bf16[8,23,128]{2,1,0:T(8,128)(2,1)} %constant_dynamic-update-slice_fusion), channel_id=1, source_target_pairs={{0,16},{8,24},{16,0},{24,8},{1,17},{9,25},{17,1},{25,9},{2,18},{10... | collective-permute-start | bytes 141320 | tf_op jit(solution)/shard_map/ppermute | solution.py:475
  104.9 11.9 %collective-permute-start.9 = (bf16[8,23,128]{2,1,0:T(8,128)(2,1)}, bf16[8,23,128]{2,1,0:T(8,128)(2,1)}, u32[]{:S(2)}, u32[]{:S(2)}) collective-permute-start(bf16[8,23,128]{2,1,0:T(8,128)(2,1)} %constant_dynamic-update-slice_fusion), channel_id=1, source_target_pairs={{0,24},{8,16},{16,8},{24,0},{1,25},{9,17},{17,9},{25,1},{2,26},{10... | collective-permute-start | bytes 141320 | tf_op jit(solution)/shard_map/ppermute | solution.py:475
  112.8 47.8 %copy-start.71 = (s32[32]{0:T(128)}, s32[32]{0:T(128)S(1)}, u32[]{:S(2)}) copy-start(s32[32]{0:T(128)S(1)} %iota_xor_fusion) | copy-start | bytes 388
  121.0 6.9 collective-permute-start.10
  125.9 46.5 %copy-start.50 = (f32[512]{0:T(512)}, f32[512]{0:T(512)S(1)}, u32[]{:S(2)}) copy-start(f32[512]{0:T(512)S(1)} %broadcast_multiply_fusion.7) | copy-start | bytes 6148
  129.6 3.8 collective-permute-start.11
  130.3 17.7 %collective-permute-start.12 = (f32[4,2,6912]{2,0,1:T(4,128)S(1)}, f32[4,2,6912]{2,0,1:T(4,128)S(1)}, u32[]{:S(2)}, u32[]{:S(2)}) collective-permute-start(f32[4,2,6912]{2,0,1:T(4,128)S(1)} %get-tuple-element.272), channel_id=1, source_target_pairs={{16,0},{17,1},{18,2},{19,3},{20,4},{21,5},{22,6},{23,7},{24,8},{25... | collective-permute-start | bytes 663560 | tf_op jit(solution)/shard_map/ppermute | solution.py:486
  131.6 23.5 %collective-permute-start.13 = (f32[4,2,6912]{2,0,1:T(4,128)S(1)}, f32[4,2,6912]{2,0,1:T(4,128)S(1)}, u32[]{:S(2)}, u32[]{:S(2)}) collective-permute-start(f32[4,2,6912]{2,0,1:T(4,128)S(1)} %get-tuple-element.273), channel_id=1, source_target_pairs={{16,8},{17,9},{18,10},{19,11},{20,12},{21,13},{22,14},{23,15},{24,... | collective-permute-start | bytes 663560 | tf_op jit(solution)/shard_map/ppermute | solution.py:486
  156.6 10.7 %collective-permute-start.14 = (f32[2,6912]{1,0:T(2,128)}, f32[2,6912]{1,0:T(2,128)}, u32[]{:S(2)}, u32[]{:S(2)}) collective-permute-start(f32[2,6912]{1,0:T(2,128)} %bitcast.275), channel_id=1, source_target_pairs={{0,2},{1,3},{2,0},{3,1},{4,6},{5,7},{6,4},{7,5},{8,10},{9,11},{10,... | collective-permute-start | bytes 165896 | tf_op jit(solution)/shard_map/ppermute | solution.py:486
  157.6 9.7 %collective-permute-start.15 = (f32[2,6912]{1,0:T(2,128)}, f32[2,6912]{1,0:T(2,128)}, u32[]{:S(2)}, u32[]{:S(2)}) collective-permute-start(f32[2,6912]{1,0:T(2,128)} %bitcast.274), channel_id=1, source_target_pairs={{0,4},{1,5},{2,6},{3,7},{4,0},{5,1},{6,2},{7,3},{8,12},{9,13},{10,... | collective-permute-start | bytes 165896 | tf_op jit(solution)/shard_map/ppermute | solution.py:486
  160.2 10.7 %collective-permute-start.16 = (f32[2,6912]{1,0:T(2,128)}, f32[2,6912]{1,0:T(2,128)}, u32[]{:S(2)}, u32[]{:S(2)}) collective-permute-start(f32[2,6912]{1,0:T(2,128)} %bitcast.276), channel_id=1, source_target_pairs={{0,6},{1,7},{2,4},{3,5},{4,2},{5,3},{6,0},{7,1},{8,14},{9,15},{10,... | collective-permute-start | bytes 165896 | tf_op jit(solution)/shard_map/ppermute | solution.py:486
  174.7 155.2 %collective-permute-start.26 = (bf16[512,1152]{1,0:T(8,128)(2,1)}, bf16[512,1152]{1,0:T(8,128)(2,1)}, u32[]{:S(2)}, u32[]{:S(2)}) collective-permute-start(bf16[512,1152]{1,0:T(8,128)(2,1)} %fusion.9), channel_id=1, source_target_pairs={{0,1},{1,0},{2,3},{3,2},{4,5},{5,4},{6,7},{7,6},{8,9},{9,8},{10,11... | collective-permute-start | bytes 3538952 | tf_op jit(solution)/shard_map/ppermute | solution.py:1074
  179.1 150.9 %collective-permute-start.27 = (bf16[512,1152]{1,0:T(8,128)(2,1)}, bf16[512,1152]{1,0:T(8,128)(2,1)}, u32[]{:S(2)}, u32[]{:S(2)}) collective-permute-start(bf16[512,1152]{1,0:T(8,128)(2,1)} %fusion.10.g_ref), channel_id=1, source_target_pairs={{0,1},{1,0},{2,3},{3,2},{4,5},{5,4},{6,7},{7,6},{8,9},{9,8},{10,11... | collective-permute-start | bytes 3538952 | tf_op jit(solution)/shard_map/ppermute | solution.py:1074
  368.6 23.8 %collective-permute-start.29 = (bf16[512,3072]{1,0:T(8,128)(2,1)}, bf16[512,3072]{1,0:T(8,128)(2,1)}, u32[]{:S(2)}, u32[]{:S(2)}) collective-permute-start(bf16[512,3072]{1,0:T(8,128)(2,1)} %get-tuple-element.229), channel_id=1, source_target_pairs={{0,1},{1,0},{2,3},{3,2},{4,5},{5,4},{6,7},{7,6},{8,9},{9,8},{10,11... | collective-permute-start | bytes 9437192 | tf_op jit(solution)/shard_map/ppermute | solution.py:1074
  368.9 23.5 %collective-permute-start.30 = (bf16[512,3072]{1,0:T(8,128)(2,1)}, bf16[512,3072]{1,0:T(8,128)(2,1)}, u32[]{:S(2)}, u32[]{:S(2)}) collective-permute-start(bf16[512,3072]{1,0:T(8,128)(2,1)} %get-tuple-element.231), channel_id=1, source_target_pairs={{0,1},{1,0},{2,3},{3,2},{4,5},{5,4},{6,7},{7,6},{8,9},{9,8},{10,11... | collective-permute-start | bytes 9437192 | tf_op jit(solution)/shard_map/ppermute | solution.py:1074
  369.2 23.2 %collective-permute-start.31 = (bf16[512,3072]{1,0:T(8,128)(2,1)}, bf16[512,3072]{1,0:T(8,128)(2,1)}, u32[]{:S(2)}, u32[]{:S(2)}) collective-permute-start(bf16[512,3072]{1,0:T(8,128)(2,1)} %get-tuple-element.233), channel_id=1, source_target_pairs={{0,1},{1,0},{2,3},{3,2},{4,5},{5,4},{6,7},{7,6},{8,9},{9,8},{10,11... | collective-permute-start | bytes 9437192 | tf_op jit(solution)/shard_map/ppermute | solution.py:1074
  369.4 22.7 %collective-permute-start.28 = (bf16[512,1152]{1,0:T(8,128)(2,1)}, bf16[512,1152]{1,0:T(8,128)(2,1)}, u32[]{:S(2)}, u32[]{:S(2)}) collective-permute-start(bf16[512,1152]{1,0:T(8,128)(2,1)} %fusion.15.x_ref), channel_id=1, source_target_pairs={{0,1},{1,0},{2,3},{3,2},{4,5},{5,4},{6,7},{7,6},{8,9},{9,8},{10,11... | collective-permute-start | bytes 3538952 | tf_op jit(solution)/shard_map/ppermute | solution.py:1074
  389.2 115.5 %collective-permute-start.35 = (bf16[512,1152]{1,0:T(8,128)(2,1)}, bf16[512,1152]{1,0:T(8,128)(2,1)}, u32[]{:S(2)}, u32[]{:S(2)}) collective-permute-start(bf16[512,1152]{1,0:T(8,128)(2,1)} %copy-done.38), channel_id=1, source_target_pairs={{0,1},{1,0},{2,3},{3,2},{4,5},{5,4},{6,7},{7,6},{8,9},{9,8},{10,11... | collective-permute-start | bytes 3538952 | tf_op jit(solution)/shard_map/ppermute | solution.py:1074
  392.1 112.6 %collective-permute-start.36 = (bf16[512,1152]{1,0:T(8,128)(2,1)}, bf16[512,1152]{1,0:T(8,128)(2,1)}, u32[]{:S(2)}, u32[]{:S(2)}) collective-permute-start(bf16[512,1152]{1,0:T(8,128)(2,1)} %get-tuple-element.182), channel_id=1, source_target_pairs={{0,1},{1,0},{2,3},{3,2},{4,5},{5,4},{6,7},{7,6},{8,9},{9,8},{10,11... | collective-permute-start | bytes 3538952 | tf_op jit(solution)/shard_map/ppermute | solution.py:1074
  430.9 46.3 %collective-permute-start.34 = (bf16[2,4,1344,128]{3,2,1,0:T(8,128)(2,1)}, bf16[2,4,1344,128]{3,2,1,0:T(8,128)(2,1)}, u32[]{:S(2)}, u32[]{:S(2)}) collective-permute-start(bf16[2,4,1344,128]{3,2,1,0:T(8,128)(2,1)} %dynamic-slice_bitcast_fusion), channel_id=1, source_target_pairs={{0,8},{8,0},{16,24},{24,16},{1,9},{9,1},{17,25},{25,17},{2,10},{10... | collective-permute-start | bytes 8257544 | tf_op jit(solution)/shard_map/ppermute | solution.py:428
  434.0 44.6 %collective-permute-start.33 = (bf16[2,4,1344,128]{3,2,1,0:T(8,128)(2,1)}, bf16[2,4,1344,128]{3,2,1,0:T(8,128)(2,1)}, u32[]{:S(2)}, u32[]{:S(2)}) collective-permute-start(bf16[2,4,1344,128]{3,2,1,0:T(8,128)(2,1)} %dynamic-slice_bitcast_fusion.1), channel_id=1, source_target_pairs={{0,16},{16,0},{8,24},{24,8},{1,17},{17,1},{9,25},{25,9},{2,18},{18... | collective-permute-start | bytes 8257544 | tf_op jit(solution)/shard_map/ppermute | solution.py:428
  471.3 33.5 %collective-permute-start.32 = (bf16[512,3456]{1,0:T(8,128)(2,1)}, bf16[512,3456]{1,0:T(8,128)(2,1)}, u32[]{:S(2)}, u32[]{:S(2)}) collective-permute-start(bf16[512,3456]{1,0:T(8,128)(2,1)} %get-tuple-element.189), channel_id=1, source_target_pairs={{0,1},{1,0},{2,3},{3,2},{4,5},{5,4},{6,7},{7,6},{8,9},{9,8},{10,11... | collective-permute-start | bytes 10616840 | tf_op jit(solution)/shard_map/ppermute | solution.py:1074
  488.6 36.7 %collective-permute-start.40 = (bf16[4,1344,128]{2,1,0:T(8,128)(2,1)}, bf16[4,1344,128]{2,1,0:T(8,128)(2,1)}, u32[]{:S(2)}, u32[]{:S(2)}) collective-permute-start(bf16[4,1344,128]{2,1,0:T(8,128)(2,1)} %dynamic-slice_bitcast_fusion.2), channel_id=1, source_target_pairs={{0,16},{16,0},{8,24},{24,8},{1,17},{17,1},{9,25},{25,9},{2,18},{18... | collective-permute-start | bytes 4128776 | tf_op jit(solution)/shard_map/ppermute | solution.py:428
  493.2 37.8 %collective-permute-start.39 = (bf16[4,1344,128]{2,1,0:T(8,128)(2,1)}, bf16[4,1344,128]{2,1,0:T(8,128)(2,1)}, u32[]{:S(2)}, u32[]{:S(2)}) collective-permute-start(bf16[4,1344,128]{2,1,0:T(8,128)(2,1)} %dynamic-slice_bitcast_fusion.3), channel_id=1, source_target_pairs={{0,8},{8,0},{16,24},{24,16},{1,9},{9,1},{17,25},{25,17},{2,10},{10... | collective-permute-start | bytes 4128776 | tf_op jit(solution)/shard_map/ppermute | solution.py:428
  519.7 41.8 %collective-permute-start.38 = (bf16[2,4,648,128]{3,2,1,0:T(8,128)(2,1)S(1)}, bf16[2,4,648,128]{3,2,1,0:T(8,128)(2,1)S(1)}, u32[]{:S(2)}, u32[]{:S(2)}) collective-permute-start(bf16[2,4,648,128]{3,2,1,0:T(8,128)(2,1)S(1)} %dynamic-slice_bitcast_fusion.4), channel_id=1, source_target_pairs={{0,8},{8,0},{16,24},{24,16},{1,9},{9,1},{17,25},{25,17},{2,10},{10... | collective-permute-start | bytes 3981320 | tf_op jit(solution)/shard_map/ppermute | solution.py:428
  521.0 40.5 %collective-permute-start.37 = (bf16[2,4,648,128]{3,2,1,0:T(8,128)(2,1)S(1)}, bf16[2,4,648,128]{3,2,1,0:T(8,128)(2,1)S(1)}, u32[]{:S(2)}, u32[]{:S(2)}) collective-permute-start(bf16[2,4,648,128]{3,2,1,0:T(8,128)(2,1)S(1)} %dynamic-slice_bitcast_fusion.5), channel_id=1, source_target_pairs={{0,16},{16,0},{8,24},{24,8},{1,17},{17,1},{9,25},{25,9},{2,18},{18... | collective-permute-start | bytes 3981320 | tf_op jit(solution)/shard_map/ppermute | solution.py:428
  534.7 31.6 %collective-permute-start.43 = (bf16[2688,128]{1,0:T(8,128)(2,1)S(1)}, bf16[2688,128]{1,0:T(8,128)(2,1)S(1)}, u32[]{:S(2)}, u32[]{:S(2)}) collective-permute-start(bf16[2688,128]{1,0:T(8,128)(2,1)S(1)} %get-tuple-element.256), channel_id=1, source_target_pairs={{0,2},{1,3},{2,0},{3,1},{4,6},{5,7},{6,4},{7,5},{8,10},{9,11},{10,... | collective-permute-start | bytes 2064392 | tf_op jit(solution)/shard_map/ppermute | solution.py:455
  535.0 34.4 %collective-permute-start.44 = (bf16[2688,128]{1,0:T(8,128)(2,1)S(1)}, bf16[2688,128]{1,0:T(8,128)(2,1)S(1)}, u32[]{:S(2)}, u32[]{:S(2)}) collective-permute-start(bf16[2688,128]{1,0:T(8,128)(2,1)S(1)} %get-tuple-element.257), channel_id=1, source_target_pairs={{0,4},{1,5},{2,6},{3,7},{4,0},{5,1},{6,2},{7,3},{8,12},{9,13},{10,... | collective-permute-start | bytes 2064392 | tf_op jit(solution)/shard_map/ppermute | solution.py:455
  537.1 64.0 %collective-permute-start.45 = (bf16[2688,128]{1,0:T(8,128)(2,1)S(1)}, bf16[2688,128]{1,0:T(8,128)(2,1)S(1)}, u32[]{:S(2)}, u32[]{:S(2)}) collective-permute-start(bf16[2688,128]{1,0:T(8,128)(2,1)S(1)} %get-tuple-element.254), channel_id=1, source_target_pairs={{0,6},{1,7},{2,4},{3,5},{4,2},{5,3},{6,0},{7,1},{8,14},{9,15},{10,... | collective-permute-start | bytes 2064392 | tf_op jit(solution)/shard_map/ppermute | solution.py:455
  562.7 44.5 %collective-permute-start.42 = (bf16[4,648,128]{2,1,0:T(8,128)(2,1)}, bf16[4,648,128]{2,1,0:T(8,128)(2,1)}, u32[]{:S(2)}, u32[]{:S(2)}) collective-permute-start(bf16[4,648,128]{2,1,0:T(8,128)(2,1)} %dynamic-slice_bitcast_fusion.6), channel_id=1, source_target_pairs={{0,16},{16,0},{8,24},{24,8},{1,17},{17,1},{9,25},{25,9},{2,18},{18... | collective-permute-start | bytes 1990664 | tf_op jit(solution)/shard_map/ppermute | solution.py:428
  564.3 37.2 %copy-start.36 = (bf16[2,4,648,128]{3,2,1,0:T(8,128)(2,1)}, bf16[2,4,648,128]{3,2,1,0:T(8,128)(2,1)S(1)}, u32[]{:S(2)}) copy-start(bf16[2,4,648,128]{3,2,1,0:T(8,128)(2,1)S(1)} %fusion.5) | copy-start | bytes 3981316
  565.2 42.0 %collective-permute-start.41 = (bf16[4,648,128]{2,1,0:T(8,128)(2,1)}, bf16[4,648,128]{2,1,0:T(8,128)(2,1)}, u32[]{:S(2)}, u32[]{:S(2)}) collective-permute-start(bf16[4,648,128]{2,1,0:T(8,128)(2,1)} %dynamic-slice_bitcast_fusion.7), channel_id=1, source_target_pairs={{0,8},{8,0},{16,24},{24,16},{1,9},{9,1},{17,25},{25,17},{2,10},{10... | collective-permute-start | bytes 1990664 | tf_op jit(solution)/shard_map/ppermute | solution.py:428
  611.2 26.6 %collective-permute-start.50 = (bf16[1296,128]{1,0:T(8,128)(2,1)}, bf16[1296,128]{1,0:T(8,128)(2,1)}, u32[]{:S(2)}, u32[]{:S(2)}) collective-permute-start(bf16[1296,128]{1,0:T(8,128)(2,1)} %get-tuple-element.270), channel_id=1, source_target_pairs={{0,2},{1,3},{2,0},{3,1},{4,6},{5,7},{6,4},{7,5},{8,10},{9,11},{10,... | collective-permute-start | bytes 995336 | tf_op jit(solution)/shard_map/ppermute | solution.py:455
  613.4 41.7 %collective-permute-start.46 = (bf16[2688,128]{1,0:T(8,128)(2,1)}, bf16[2688,128]{1,0:T(8,128)(2,1)}, u32[]{:S(2)}, u32[]{:S(2)}) collective-permute-start(bf16[2688,128]{1,0:T(8,128)(2,1)} %bitcast_select_fusion.1), channel_id=1, source_target_pairs={{30,8},{16,9},{2,10},{18,11},{4,12},{20,13},{6,14},{17,15},{15,16}... | collective-permute-start | bytes 2064392 | tf_op jit(solution)/shard_map/ppermute | solution.py:340
  615.0 40.2 %collective-permute-start.47 = (bf16[2688,128]{1,0:T(8,128)(2,1)}, bf16[2688,128]{1,0:T(8,128)(2,1)}, u32[]{:S(2)}, u32[]{:S(2)}) collective-permute-start(bf16[2688,128]{1,0:T(8,128)(2,1)} %bitcast_select_fusion.1), channel_id=1, source_target_pairs={{14,7},{0,8},{24,9},{10,10},{26,11},{12,12},{28,13},{22,14},{25,15... | collective-permute-start | bytes 2064392 | tf_op jit(solution)/shard_map/ppermute | solution.py:340
  621.0 34.1 %collective-permute-start.48 = (bf16[2688,128]{1,0:T(8,128)(2,1)}, bf16[2688,128]{1,0:T(8,128)(2,1)}, u32[]{:S(2)}, u32[]{:S(2)}) collective-permute-start(bf16[2688,128]{1,0:T(8,128)(2,1)} %bitcast_select_fusion.1), channel_id=1, source_target_pairs={{30,7},{8,8},{2,9},{18,10},{4,11},{20,12},{6,13},{9,14},{15,15},{1... | collective-permute-start | bytes 2064392 | tf_op jit(solution)/shard_map/ppermute | solution.py:340
  622.6 19.1 %collective-permute-start.51 = (bf16[1296,128]{1,0:T(8,128)(2,1)}, bf16[1296,128]{1,0:T(8,128)(2,1)}, u32[]{:S(2)}, u32[]{:S(2)}) collective-permute-start(bf16[1296,128]{1,0:T(8,128)(2,1)} %get-tuple-element.271), channel_id=1, source_target_pairs={{0,4},{1,5},{2,6},{3,7},{4,0},{5,1},{6,2},{7,3},{8,12},{9,13},{10,... | collective-permute-start | bytes 995336 | tf_op jit(solution)/shard_map/ppermute | solution.py:455
  630.9 24.1 %all-to-all-start = ((f32[32,2,108]{2,1,0:T(2,128)}), f32[32,2,108]{2,1,0:T(2,128)S(1)}, u32[]{:S(2)}, u32[]{:S(2)}) async-start(f32[32,2,108]{2,1,0:T(2,128)} %copy.79), calls=%async_computation | async-start | bytes 65536 | tf_op jit(solution)/shard_map/all_to_all | solution.py:1181
  637.8 17.4 %collective-permute-start.49 = (bf16[2688,128]{1,0:T(8,128)(2,1)}, bf16[2688,128]{1,0:T(8,128)(2,1)}, u32[]{:S(2)}, u32[]{:S(2)}) collective-permute-start(bf16[2688,128]{1,0:T(8,128)(2,1)} %bitcast_select_fusion.1), channel_id=1, source_target_pairs={{16,8},{17,14},{21,29}} | collective-permute-start | bytes 2064392 | tf_op jit(solution)/shard_map/ppermute | solution.py:340
  641.6 13.5 %collective-permute-start.52 = (bf16[1296,128]{1,0:T(8,128)(2,1)}, bf16[1296,128]{1,0:T(8,128)(2,1)}, u32[]{:S(2)}, u32[]{:S(2)}) collective-permute-start(bf16[1296,128]{1,0:T(8,128)(2,1)} %get-tuple-element.268), channel_id=1, source_target_pairs={{0,6},{1,7},{2,4},{3,5},{4,2},{5,3},{6,0},{7,1},{8,14},{9,15},{10,... | collective-permute-start | bytes 995336 | tf_op jit(solution)/shard_map/ppermute | solution.py:455
  661.5 20.4 %collective-permute-start.53 = (bf16[1296,128]{1,0:T(8,128)(2,1)S(1)}, bf16[1296,128]{1,0:T(8,128)(2,1)S(1)}, u32[]{:S(2)}, u32[]{:S(2)}) collective-permute-start(bf16[1296,128]{1,0:T(8,128)(2,1)S(1)} %broadcast_select_fusion), channel_id=1, source_target_pairs={{0,0},{2,1},{9,2},{11,3},{4,4},{6,5},{29,6},{31,7}} | collective-permute-start | bytes 995336 | tf_op jit(solution)/shard_map/ppermute | solution.py:340
  662.8 37.6 %collective-permute-start.54 = (bf16[1296,128]{1,0:T(8,128)(2,1)S(1)}, bf16[1296,128]{1,0:T(8,128)(2,1)S(1)}, u32[]{:S(2)}, u32[]{:S(2)}) collective-permute-start(bf16[1296,128]{1,0:T(8,128)(2,1)S(1)} %broadcast_select_fusion), channel_id=1, source_target_pairs={{8,0},{10,1},{17,2},{19,3},{12,4},{14,5},{7,6}} | collective-permute-start | bytes 995336 | tf_op jit(solution)/shard_map/ppermute | solution.py:340
  664.1 36.3 %collective-permute-start.55 = (bf16[1296,128]{1,0:T(8,128)(2,1)S(1)}, bf16[1296,128]{1,0:T(8,128)(2,1)S(1)}, u32[]{:S(2)}, u32[]{:S(2)}) collective-permute-start(bf16[1296,128]{1,0:T(8,128)(2,1)S(1)} %broadcast_select_fusion), channel_id=1, source_target_pairs={{16,0},{18,1},{25,2},{27,3},{20,4},{5,5},{15,6}} | collective-permute-start | bytes 995336 | tf_op jit(solution)/shard_map/ppermute | solution.py:340
  665.4 35.0 %collective-permute-start.56 = (bf16[1296,128]{1,0:T(8,128)(2,1)S(1)}, bf16[1296,128]{1,0:T(8,128)(2,1)S(1)}, u32[]{:S(2)}, u32[]{:S(2)}) collective-permute-start(bf16[1296,128]{1,0:T(8,128)(2,1)S(1)} %broadcast_select_fusion), channel_id=1, source_target_pairs={{24,0},{26,1},{3,2},{22,3},{28,4},{13,5},{23,6}} | collective-permute-start | bytes 995336 | tf_op jit(solution)/shard_map/ppermute | solution.py:340
  676.3 24.2 %collective-permute-start.57 = (bf16[1296,128]{1,0:T(8,128)(2,1)S(1)}, bf16[1296,128]{1,0:T(8,128)(2,1)S(1)}, u32[]{:S(2)}, u32[]{:S(2)}) collective-permute-start(bf16[1296,128]{1,0:T(8,128)(2,1)S(1)} %broadcast_select_fusion), channel_id=1, source_target_pairs={{2,0},{1,1},{11,2},{30,3},{6,4},{21,5},{31,6}} | collective-permute-start | bytes 995336 | tf_op jit(solution)/shard_map/ppermute | solution.py:340
  (74 other events, 579.3 us)
Sparse Core Ops, SparseCore 0:
  83.8 203.4 all-gather.2
  504.8 88.2 all-gather.4

commit v5 on v4

--- a/solution.py
+++ b/solution.py
@@ -672,20 +672,18 @@
                         value[8 * group : 8 * group + 8],
                     )
 
-        @pl.when(step >= mlp_steps)
-        def _():
+        def down_step(phase):
             value = pair_product(ho, hp, go, gp)
             for group in range(wide // 8):
                 at = (step - mlp_steps) * (wide // 8) + group
-                part = at // half_groups
-                first = place_ref[part // 2] * half_tiles + (at % half_groups) * 9
-                piece = value[8 * group : 8 * group + 8]
-
-                def put(out_ref, first=first, piece=piece):
-                    store_tiles(out_ref, (), first, piece)
-
-                pl.when(part % 2 == 0)(lambda put=put: put(outs[0]))
-                pl.when(part % 2 == 1)(lambda put=put: put(outs[1]))
+                half = (phase * (wide // 8) + group) // half_groups % 2
+                first = place_ref[at // (2 * half_groups)] * half_tiles + (at % half_groups) * 9
+                store_tiles(outs[half], (), first, value[8 * group : 8 * group + 8])
+
+        for phase in range(3):
+            pl.when((step >= mlp_steps) & ((step - mlp_steps) % 3 == phase))(
+                lambda phase=phase: down_step(phase)
+            )
 
     x_specs = [pl.BlockSpec((rows, 128), lambda t: (0, 7)), pl.BlockSpec((rows, 128), lambda t: (0, 8))]
     g_spec = pl.BlockSpec((rows, 512), lambda t: (0, jnp.minimum(t, mlp_steps - 1)))

time: 723 us -> 723 us (level)
  Pallas kernels: 147 us -> 136 us
  waiting for transfers between devices: 273 us -> 284 us
    ppermute x8, waiting for transfers between devices: 34.2 us -> 44.4 us  [over_planes(): lax.ppermute(send, 'fsdp', axis)]
    pallas_call x1, Pallas kernels: 33.7 us -> 23.6 us  [grads_b_core_1(): pl.pallas_call(body, grid=(mlp_steps + down_steps,), in_specs=[pl.BlockSp...]
  transfers between devices with their start and end apart: 61 -> 61, of which waited for: 19 -> 20; matrix products, arithmetic and copies ran while one was open for 19% -> 19% of each run, Pallas kernels for 14% -> 13%
where the time goes in v5:
time: 723 us; the launch traced here: 713 us
  waiting for transfers between devices  284 us (39%)
  Pallas kernels  136 us (19%)
  starting transfers between devices  110 us (15%)
  local copies, waits for them, and re-layouts  74.8 us (10%)
  other arithmetic  62.6 us (9%)
  matrix products  29.7 us (4%)
  between operations  15.9 us (2%)
    all_gather x1, waiting for transfers between devices, gathered_weights(): lax.all_gather(block, ('fsdp', 'dp'), axis=0, tiled=True)  108 us
    ppermute x8, waiting for transfers between devices, over_planes(): lax.ppermute(send, 'fsdp', axis)  44.4 us
    ppermute x9, waiting for transfers between devices, spread(): got = lax.ppermute(piece, ('fsdp', 'dp'), pairs)  38.9 us
    pallas_call x1, Pallas kernels, mlp_both_ways(): pl.pallas_call(body, grid=(steps,), in_specs=[whole, whole, line, pl.Bloc...  38.6 us
    ppermute x6, waiting for transfers between devices, from_line(): lax.ppermute(sends[k], 'dp', [(d, d ^ 2 * k) for d in range(8)])  35.5 us
    pallas_call x1, Pallas kernels, attention_backward(): pl.pallas_call(body, grid=(images,), in_specs=[pl.BlockSpec((length, 2 *...  26.7 us
    ppermute x9, starting transfers between devices, send_back(): lax.ppermute(block, ('fsdp', 'dp'), [(device, owner) for owner, device in...  26.7 us
    ppermute x7, waiting for transfers between devices, send(): return lax.ppermute(array, ('fsdp', 'dp'), pairs)  25.2 us
  transfers between devices with their start and end apart: 61, of which 20 were waited for; matrix products, arithmetic and copies ran while one was open for 19% of the time, Pallas kernels for 13%

profile of v5, /device:TPU:9, one launch (start us, length us, event | category | flops | bytes accessed | tf_op | source)
XLA Modules:
  0.0 713.2 jit_solution(2024911678108067332)
XLA Ops:
  8.9 3.8 pad_dynamic-slice_fusion
  12.8 4.3 pad_dynamic-slice_fusion.12
  17.1 4.1 collective-permute-start.17
  21.2 3.0 collective-permute-start.18
  24.2 2.0 collective-permute-start.19
  28.2 2.0 collective-permute-start.21
  30.2 6.1 collective-permute-done.17
  37.8 15.1 %collective-permute-done.18 = bf16[1296,128]{1,0:T(8,128)(2,1)} collective-permute-done((bf16[1296,128]{1,0:T(8,128)(2,1)}, bf16[1296,128]{1,0:T(8,128)(2,1)}, u32[]{:S(2)}, u32[]{:S(2)}) %collective-permute-start.18) | collective-permute-done | bytes 331808 | tf_op jit(solution)/shard_map/ppermute | solution.py:331
  54.4 3.1 collective-permute-done.19
  63.0 14.5 %collective-permute-done.24 = bf16[2688,128]{1,0:T(8,128)(2,1)} collective-permute-done((bf16[2688,128]{1,0:T(8,128)(2,1)}, bf16[2688,128]{1,0:T(8,128)(2,1)}, u32[]{:S(2)}, u32[]{:S(2)}) %collective-permute-start.24) | collective-permute-done | bytes 688160 | tf_op jit(solution)/shard_map/ppermute | solution.py:331
  83.9 2.0 collective-permute-start.2
  85.9 7.5 %collective-permute-start.3 = (bf16[23,128]{1,0:T(8,128)(2,1)S(1)}, bf16[23,128]{1,0:T(8,128)(2,1)S(1)}, u32[]{:S(2)}, u32[]{:S(2)}) collective-permute-start(bf16[23,128]{1,0:T(8,128)(2,1)S(1)} %bitcast.323), channel_id=1, source_target_pairs={{0,4},{1,5},{2,6},{3,7},{4,0},{5,1},{6,2},{7,3},{8,12},{9,13},{10,... | collective-permute-start | bytes 17672 | tf_op jit(solution)/shard_map/ppermute | solution.py:468
  96.2 2.9 collective-permute-start.5
  104.9 7.8 %collective-permute-start.9 = (bf16[8,23,128]{2,1,0:T(8,128)(2,1)}, bf16[8,23,128]{2,1,0:T(8,128)(2,1)}, u32[]{:S(2)}, u32[]{:S(2)}) collective-permute-start(bf16[8,23,128]{2,1,0:T(8,128)(2,1)} %constant_dynamic-update-slice_fusion), channel_id=1, source_target_pairs={{0,24},{8,16},{16,8},{24,0},{1,25},{9,17},{17,9},{25,1},{2,26},{10... | collective-permute-start | bytes 141320 | tf_op jit(solution)/shard_map/ppermute | solution.py:475
  112.8 2.7 reshape.575
  133.4 14.5 %collective-permute-done.12 = f32[4,2,6912]{2,0,1:T(4,128)S(1)} collective-permute-done((f32[4,2,6912]{2,0,1:T(4,128)S(1)}, f32[4,2,6912]{2,0,1:T(4,128)S(1)}, u32[]{:S(2)}, u32[]{:S(2)}) %collective-permute-start.12) | collective-permute-done | bytes 221216 | tf_op jit(solution)/shard_map/ppermute | solution.py:486
  147.9 7.2 %collective-permute-done.13 = f32[4,2,6912]{2,0,1:T(4,128)S(1)} collective-permute-done((f32[4,2,6912]{2,0,1:T(4,128)S(1)}, f32[4,2,6912]{2,0,1:T(4,128)S(1)}, u32[]{:S(2)}, u32[]{:S(2)}) %collective-permute-start.13) | collective-permute-done | bytes 221216 | tf_op jit(solution)/shard_map/ppermute | solution.py:486
  167.3 3.5 collective-permute-done.16
  172.4 2.3 fusion.9
  174.7 2.3 collective-permute-start.26
  177.0 2.1 fusion.10.g_ref
  179.1 108.2 %all-gather.3.cloned.1.call-done = bf16[127488,128]{1,0:T(8,128)(2,1)} async-done(((bf16[3984,128]{1,0:T(8,128)(2,1)}), bf16[127488,128]{1,0:T(8,128)(2,1)}) %all-gather.3.cloned.1.call-update) | async-done | bytes 32636944 | tf_op jit(solution)/shard_map/all_gather | solution.py:781
  287.3 4.3 split_a.1
  291.6 9.5 %convolution_add_fusion.proj_ref = f32[512,3456]{1,0:T(8,128)} fusion(bf16[512,1152]{1,0:T(8,128)(2,1)} %fusion.9, bf16[1152,3456]{1,0:T(8,128)(2,1)S(1)} %bitcast.279, f32[3456]{0:T(1024)S(1)} %slice-done.2), kind=kOutput, calls=%fused_computation | convolution fusion | flops 4078632960 | bytes 16233984 | tf_op jit(solution)/shard_map/dot_general | solution.py:1084
  301.1 23.1 %attention_forward.1 = (bf16[512,1152]{1,0:T(8,128)(2,1)S(1)}, bf16[512,1152]{1,0:T(8,128)(2,1)S(1)}, bf16[512,1152]{1,0:T(8,128)(2,1)S(1)}, bf16[512,1152]{1,0:T(8,128)(2,1)S(1)}, f32[512,16]{1,0:T(8,128)S(1)}) custom-call(f32[512,3456]{1,0:T(8,128)} %convolution_add_fusion.proj_ref, f32[256,1152]{1,0:T(8,128)S(1)} %copy.71.cos_ref, ...), custom_call_target="tpu_custom_call" | custom-call | flops 1207959552 | bytes 20000000 | tf_op jit(solution)/shard_map/attention_forward/pallas_call | solution.py:854
  324.3 3.3 fusion.74
  330.0 38.6 %mlp_both_ways.1 = (bf16[512,3072]{1,0:T(8,128)(2,1)}, bf16[512,3072]{1,0:T(8,128)(2,1)}, bf16[512,3072]{1,0:T(8,128)(2,1)}, f32[512,1152]{1,0:T(8,128)}, f32[51...) custom-call(bf16[512,1152]{1,0:T(8,128)(2,1)} %fusion.15.x_ref, bf16[512,1152]{1,0:T(8,128)(2,1)} %fusion.10.g_ref, ...), custom_call_target="tpu_custom_call" | custom-call | flops 21743271936 | bytes 30000000 | tf_op jit(solution)/shard_map/mlp_both_ways/pallas_call | solution.py:566
  372.1 5.6 fusion.19
  380.8 5.2 fusion.72
  392.4 24.2 %conditional.2 = (bf16[2,2,4,1344,128]{4,3,2,1,0:T(8,128)(2,1)}, bf16[2,2,4,1344,128]{4,3,2,1,0:T(8,128)(2,1)S(1)}) conditional(s32[]{:T(128)} %convert_element_type.267, (bf16[512,1152]{1,0:T(8,128)(2,1)}, bf16[512,1152]{1,0:T(8,128)(2,1)}, bf16[512,3072]{1,0:T(8,128)(2,1)}, bf16[512,3072]{1,0:T(8,128)(2,1)}, bf16[512,3072]{1,0:T(8,128)(2,1)}, ...), branch_computations={%region_6.7_spmd.clone, %region_7.8_spmd} | conditional | bytes 220 | solution.py:1109
  393.1 23.6 %grads_b_core_1.1 = (bf16[2688,8,128]{2,1,0:T(8,128)(2,1)}, bf16[2688,8,128]{2,1,0:T(8,128)(2,1)S(1)}) custom-call(s32[11]{0:T(128)S(1)} %copy-done.12, bf16[512,1152]{1,0:T(8,128)(2,1)} %get-tuple-element.215.xo7.xo8, bf16[512,1152]{1,0:T(8,128)(2,1)} %get-tuple-element.215.xo7.xo8, bf16[512,1152]{1,0:T(8,128)(2,1)} %get-tuple-element.216.xp7.xp8, ...), custom_call_target="tpu_custom_call" | custom-call | tf_op jit(solution)/shard_map/cond/branch_0_fun/grads_b_core_1/pallas_call | solution.py:694
  418.4 2.3 copy-done.35
  427.1 26.7 %attention_backward.1 = (bf16[512,3456]{1,0:T(8,128)(2,1)}, f32[2,1,3456]{2,1,0:T(1,128)S(1)}) custom-call(f32[512,3456]{1,0:T(8,128)} %convolution_add_fusion.proj_ref, bf16[512,1152]{1,0:T(8,128)(2,1)S(1)} %get-tuple-element.173.q_ref, bf16[512,1152]{1,0:T(8,128)(2,1)S(1)} %copy-done.3, bf16[512,1152]{1,0:T(8,128)(2,1)S(1)} %copy-done.5, ...), custom_call_target="tpu_custom_call" | custom-call | flops 1000 | bytes 1000 | tf_op jit(solution)/shard_map/attention_backward/pallas_call | solution.py:913
  454.0 7.0 fusion.79
  462.6 3.0 fusion.17
  467.1 8.3 %collective-permute-done.34 = bf16[2,4,1344,128]{3,2,1,0:T(8,128)(2,1)} collective-permute-done((bf16[2,4,1344,128]{3,2,1,0:T(8,128)(2,1)}, bf16[2,4,1344,128]{3,2,1,0:T(8,128)(2,1)}, u32[]{:S(2)}, u32[]{:S(2)}) %collective-permute-start.34) | collective-permute-done | bytes 2752544 | tf_op jit(solution)/shard_map/ppermute | solution.py:428
  475.4 3.2 collective-permute-done.33
  478.6 3.3 fusion
  483.2 3.4 fusion.1
  488.6 4.6 collective-permute-start.40
  493.2 5.7 collective-permute-start.39
  499.0 2.7 reshape.576
  502.1 2.5 fusion.18
  504.7 14.8 %conditional.3 = (bf16[2,2,4,648,128]{4,3,2,1,0:T(8,128)(2,1)S(1)}, bf16[2,2,4,648,128]{4,3,2,1,0:T(8,128)(2,1)S(1)}) conditional(s32[]{:T(128)} %convert_element_type.267, (bf16[512,1152]{1,0:T(8,128)(2,1)}, bf16[512,1152]{1,0:T(8,128)(2,1)}, bf16[512,3456]{1,0:T(8,128)(2,1)}, bf16[512,3456]{1,0:T(8,128)(2,1)}, bf16[512,1152]{1,0:T(8,128)(2,1)}, ...), branch_computations={%region_18.19_spmd, %region_19.20_spmd} | conditional | bytes 16 | solution.py:1138
  504.8 14.6 %grads_a_core_1.1 = (bf16[16,81,8,128]{3,2,1,0:T(8,128)(2,1)S(1)}, bf16[16,81,8,128]{3,2,1,0:T(8,128)(2,1)S(1)}) custom-call(bf16[512,1152]{1,0:T(8,128)(2,1)} %get-tuple-element.88.xo, bf16[512,1152]{1,0:T(8,128)(2,1)} %get-tuple-element.89.xp, bf16[512,3456]{1,0:T(8,128)(2,1)} %get-tuple-element.90.go, bf16[512,3456]{1,0:T(8,128)(2,1)} %get-tuple-element.91.gp, ...), custom_call_target="tpu_custom_call" | custom-call | tf_op jit(solution)/shard_map/cond/branch_0_fun/grads_a_core_1/pallas_call | solution.py:758
  522.3 3.1 collective-permute-done.40
  525.3 5.7 collective-permute-done.39
  535.0 2.1 collective-permute-start.44
  537.4 24.1 %collective-permute-done.38 = bf16[2,4,648,128]{3,2,1,0:T(8,128)(2,1)S(1)} collective-permute-done((bf16[2,4,648,128]{3,2,1,0:T(8,128)(2,1)S(1)}, bf16[2,4,648,128]{3,2,1,0:T(8,128)(2,1)S(1)}, u32[]{:S(2)}, u32[]{:S(2)}) %collective-permute-start.38) | collective-permute-done | bytes 1327136 | tf_op jit(solution)/shard_map/ppermute | solution.py:428
  566.3 3.2 collective-permute-done.44
  569.4 31.7 %collective-permute-done.45 = bf16[2688,128]{1,0:T(8,128)(2,1)S(1)} collective-permute-done((bf16[2688,128]{1,0:T(8,128)(2,1)S(1)}, bf16[2688,128]{1,0:T(8,128)(2,1)S(1)}, u32[]{:S(2)}, u32[]{:S(2)}) %collective-permute-start.45) | collective-permute-done | bytes 688160 | tf_op jit(solution)/shard_map/ppermute | solution.py:455
  602.8 2.2 reshape.550
  611.2 2.2 multiply_add_fusion
  615.0 6.0 collective-permute-start.47
  622.6 3.4 collective-permute-start.51
  628.2 2.0 fusion.24
  630.9 6.9 all-to-all-start
  639.3 2.3 fusion.54
  643.8 2.6 reshape.559.refs_9_
  646.5 8.5 %all-to-all-done = f32[32,2,108]{2,1,0:T(2,128)S(1)} async-done(((f32[32,2,108]{2,1,0:T(2,128)}), f32[32,2,108]{2,1,0:T(2,128)S(1)}, u32[]{:S(2)}, u32[]{:S(2)}) %all-to-all-start) | async-done | bytes 27680 | tf_op jit(solution)/shard_map/all_to_all | solution.py:1179
  665.4 10.8 %collective-permute-start.56 = (bf16[1296,128]{1,0:T(8,128)(2,1)S(1)}, bf16[1296,128]{1,0:T(8,128)(2,1)S(1)}, u32[]{:S(2)}, u32[]{:S(2)}) collective-permute-start(bf16[1296,128]{1,0:T(8,128)(2,1)S(1)} %broadcast_select_fusion), channel_id=1, source_target_pairs={{24,0},{26,1},{3,2},{22,3},{28,4},{13,5},{23,6}} | collective-permute-start | bytes 995336 | tf_op jit(solution)/shard_map/ppermute | solution.py:340
  678.2 3.8 collective-permute-done.53.refs_4_
  682.0 18.5 %collective-permute-done.54.refs_5_ = bf16[1296,128]{1,0:T(8,128)(2,1)S(1)} collective-permute-done((bf16[1296,128]{1,0:T(8,128)(2,1)S(1)}, bf16[1296,128]{1,0:T(8,128)(2,1)S(1)}, u32[]{:S(2)}, u32[]{:S(2)}) %collective-permute-start.54) | collective-permute-done | bytes 331808 | tf_op jit(solution)/shard_map/ppermute | solution.py:340
  700.5 5.7 owned_rows.1
  (382 shorter events, 130.5 us)
Async XLA Ops:
  7.2 280.1 %all-gather.3.cloned.1.call-start = ((), (), s32[]{:S(2)}) async-start(), calls=%async_computation.1 | async-start | bytes 33656832 | tf_op jit(solution)/shard_map/all_gather | solution.py:781
  17.1 19.2 %collective-permute-start.17 = (bf16[1296,128]{1,0:T(8,128)(2,1)}, bf16[1296,128]{1,0:T(8,128)(2,1)S(1)}, u32[]{:S(2)}, u32[]{:S(2)}) collective-permute-start(bf16[1296,128]{1,0:T(8,128)(2,1)} %get-tuple-element.158), channel_id=1, source_target_pairs={{0,0},{1,4},{2,9},{3,13},{4,18},{5,22},{6,27},{7,31}} | collective-permute-start | bytes 995336 | tf_op jit(solution)/shard_map/ppermute | solution.py:331
  21.2 31.7 %collective-permute-start.18 = (bf16[1296,128]{1,0:T(8,128)(2,1)}, bf16[1296,128]{1,0:T(8,128)(2,1)}, u32[]{:S(2)}, u32[]{:S(2)}) collective-permute-start(bf16[1296,128]{1,0:T(8,128)(2,1)} %get-tuple-element.159), channel_id=1, source_target_pairs={{0,1},{1,5},{2,10},{3,14},{4,19},{5,23},{6,28}} | collective-permute-start | bytes 995336 | tf_op jit(solution)/shard_map/ppermute | solution.py:331
  24.2 33.3 %collective-permute-start.19 = (bf16[1296,128]{1,0:T(8,128)(2,1)}, bf16[1296,128]{1,0:T(8,128)(2,1)}, u32[]{:S(2)}, u32[]{:S(2)}) collective-permute-start(bf16[1296,128]{1,0:T(8,128)(2,1)} %get-tuple-element.160), channel_id=1, source_target_pairs={{0,2},{1,6},{2,11},{3,15},{4,20},{5,24},{6,29}} | collective-permute-start | bytes 995336 | tf_op jit(solution)/shard_map/ppermute | solution.py:331
  26.2 32.6 %collective-permute-start.20 = (bf16[1296,128]{1,0:T(8,128)(2,1)S(1)}, bf16[1296,128]{1,0:T(8,128)(2,1)}, u32[]{:S(2)}, u32[]{:S(2)}) collective-permute-start(bf16[1296,128]{1,0:T(8,128)(2,1)S(1)} %get-tuple-element.161), channel_id=1, source_target_pairs={{0,3},{1,7},{2,12},{3,16},{4,21},{5,25},{6,30}} | collective-permute-start | bytes 995336 | tf_op jit(solution)/shard_map/ppermute | solution.py:331
  28.2 32.2 %collective-permute-start.21 = (bf16[1296,128]{1,0:T(8,128)(2,1)S(1)}, bf16[1296,128]{1,0:T(8,128)(2,1)}, u32[]{:S(2)}, u32[]{:S(2)}) collective-permute-start(bf16[1296,128]{1,0:T(8,128)(2,1)S(1)} %get-tuple-element.162), channel_id=1, source_target_pairs={{0,4},{1,8},{2,13},{3,17},{4,22},{5,26},{6,31}} | collective-permute-start | bytes 995336 | tf_op jit(solution)/shard_map/ppermute | solution.py:331
  36.3 26.8 %collective-permute-start.22 = (bf16[2688,128]{1,0:T(8,128)(2,1)}, bf16[2688,128]{1,0:T(8,128)(2,1)}, u32[]{:S(2)}, u32[]{:S(2)}) collective-permute-start(bf16[2688,128]{1,0:T(8,128)(2,1)} %get-tuple-element.163), channel_id=1, source_target_pairs={{8,1},{9,4},{10,6},{11,8},{12,10},{13,12},{14,14},{15,17},{16,19},... | collective-permute-start | bytes 2064392 | tf_op jit(solution)/shard_map/ppermute | solution.py:331
  52.9 10.2 %collective-permute-start.23 = (bf16[2688,128]{1,0:T(8,128)(2,1)}, bf16[2688,128]{1,0:T(8,128)(2,1)}, u32[]{:S(2)}, u32[]{:S(2)}) collective-permute-start(bf16[2688,128]{1,0:T(8,128)(2,1)} %get-tuple-element.164), channel_id=1, source_target_pairs={{7,0},{8,2},{9,5},{10,7},{11,9},{12,11},{13,13},{14,15},{15,18},{1... | collective-permute-start | bytes 2064392 | tf_op jit(solution)/shard_map/ppermute | solution.py:331
  57.5 20.1 %collective-permute-start.24 = (bf16[2688,128]{1,0:T(8,128)(2,1)}, bf16[2688,128]{1,0:T(8,128)(2,1)}, u32[]{:S(2)}, u32[]{:S(2)}) collective-permute-start(bf16[2688,128]{1,0:T(8,128)(2,1)} %get-tuple-element.165), channel_id=1, source_target_pairs={{7,1},{8,3},{9,6},{10,8},{11,10},{12,12},{13,14},{14,16},{15,19},{... | collective-permute-start | bytes 2064392 | tf_op jit(solution)/shard_map/ppermute | solution.py:331
  58.8 18.8 %collective-permute-start.25 = (bf16[2688,128]{1,0:T(8,128)(2,1)S(1)}, bf16[2688,128]{1,0:T(8,128)(2,1)}, u32[]{:S(2)}, u32[]{:S(2)}) collective-permute-start(bf16[2688,128]{1,0:T(8,128)(2,1)S(1)} %get-tuple-element.166), channel_id=1, source_target_pairs={{8,4},{14,17},{29,27}} | collective-permute-start | bytes 2064392 | tf_op jit(solution)/shard_map/ppermute | solution.py:331
  83.7 542.3 %all-gather.5.cloned.1.call-start = ((), (), s32[]{:S(2)}) async-start(), calls=%async_computation.2 | async-start | bytes 1622016 | tf_op jit(solution)/shard_map/all_gather | solution.py:1137
  83.7 12.5 %collective-permute-start = (bf16[23,128]{1,0:T(8,128)(2,1)S(1)}, bf16[23,128]{1,0:T(8,128)(2,1)S(1)}, u32[]{:S(2)}, u32[]{:S(2)}) collective-permute-start(bf16[23,128]{1,0:T(8,128)(2,1)S(1)} %bitcast.320), channel_id=1, source_target_pairs={{0,1},{1,0},{2,3},{3,2},{4,5},{5,4},{6,7},{7,6},{8,9},{9,8},{10,11... | collective-permute-start | bytes 17672 | tf_op jit(solution)/shard_map/ppermute | solution.py:468
  83.8 15.9 %collective-permute-start.1 = (bf16[23,128]{1,0:T(8,128)(2,1)S(1)}, bf16[23,128]{1,0:T(8,128)(2,1)S(1)}, u32[]{:S(2)}, u32[]{:S(2)}) collective-permute-start(bf16[23,128]{1,0:T(8,128)(2,1)S(1)} %bitcast.321), channel_id=1, source_target_pairs={{0,2},{1,3},{2,0},{3,1},{4,6},{5,7},{6,4},{7,5},{8,10},{9,11},{10,... | collective-permute-start | bytes 17672 | tf_op jit(solution)/shard_map/ppermute | solution.py:468
  83.9 16.4 %collective-permute-start.2 = (bf16[23,128]{1,0:T(8,128)(2,1)S(1)}, bf16[23,128]{1,0:T(8,128)(2,1)S(1)}, u32[]{:S(2)}, u32[]{:S(2)}) collective-permute-start(bf16[23,128]{1,0:T(8,128)(2,1)S(1)} %bitcast.322), channel_id=1, source_target_pairs={{0,3},{1,2},{2,1},{3,0},{4,7},{5,6},{6,5},{7,4},{8,11},{9,10},{10,... | collective-permute-start | bytes 17672 | tf_op jit(solution)/shard_map/ppermute | solution.py:468
  85.9 14.9 %collective-permute-start.3 = (bf16[23,128]{1,0:T(8,128)(2,1)S(1)}, bf16[23,128]{1,0:T(8,128)(2,1)S(1)}, u32[]{:S(2)}, u32[]{:S(2)}) collective-permute-start(bf16[23,128]{1,0:T(8,128)(2,1)S(1)} %bitcast.323), channel_id=1, source_target_pairs={{0,4},{1,5},{2,6},{3,7},{4,0},{5,1},{6,2},{7,3},{8,12},{9,13},{10,... | collective-permute-start | bytes 17672 | tf_op jit(solution)/shard_map/ppermute | solution.py:468
  93.4 8.0 %collective-permute-start.4 = (bf16[23,128]{1,0:T(8,128)(2,1)S(1)}, bf16[23,128]{1,0:T(8,128)(2,1)S(1)}, u32[]{:S(2)}, u32[]{:S(2)}) collective-permute-start(bf16[23,128]{1,0:T(8,128)(2,1)S(1)} %bitcast.324), channel_id=1, source_target_pairs={{0,5},{1,4},{2,7},{3,6},{4,1},{5,0},{6,3},{7,2},{8,13},{9,12},{10,... | collective-permute-start | bytes 17672 | tf_op jit(solution)/shard_map/ppermute | solution.py:468
  96.2 5.9 collective-permute-start.5
  99.7 3.5 collective-permute-start.6
  103.8 13.1 %collective-permute-start.7 = (bf16[8,23,128]{2,1,0:T(8,128)(2,1)}, bf16[8,23,128]{2,1,0:T(8,128)(2,1)}, u32[]{:S(2)}, u32[]{:S(2)}) collective-permute-start(bf16[8,23,128]{2,1,0:T(8,128)(2,1)} %constant_dynamic-update-slice_fusion), channel_id=1, source_target_pairs={{0,8},{8,0},{16,24},{24,16},{1,9},{9,1},{17,25},{25,17},{2,10},{10... | collective-permute-start | bytes 141320 | tf_op jit(solution)/shard_map/ppermute | solution.py:475
  103.8 13.1 %collective-permute-start.8 = (bf16[8,23,128]{2,1,0:T(8,128)(2,1)}, bf16[8,23,128]{2,1,0:T(8,128)(2,1)}, u32[]{:S(2)}, u32[]{:S(2)}) collective-permute-start(bf16[8,23,128]{2,1,0:T(8,128)(2,1)} %constant_dynamic-update-slice_fusion), channel_id=1, source_target_pairs={{0,16},{8,24},{16,0},{24,8},{1,17},{9,25},{17,1},{25,9},{2,18},{10... | collective-permute-start | bytes 141320 | tf_op jit(solution)/shard_map/ppermute | solution.py:475
  104.9 11.9 %collective-permute-start.9 = (bf16[8,23,128]{2,1,0:T(8,128)(2,1)}, bf16[8,23,128]{2,1,0:T(8,128)(2,1)}, u32[]{:S(2)}, u32[]{:S(2)}) collective-permute-start(bf16[8,23,128]{2,1,0:T(8,128)(2,1)} %constant_dynamic-update-slice_fusion), channel_id=1, source_target_pairs={{0,24},{8,16},{16,8},{24,0},{1,25},{9,17},{17,9},{25,1},{2,26},{10... | collective-permute-start | bytes 141320 | tf_op jit(solution)/shard_map/ppermute | solution.py:475
  112.8 47.8 %copy-start.71 = (s32[32]{0:T(128)}, s32[32]{0:T(128)S(1)}, u32[]{:S(2)}) copy-start(s32[32]{0:T(128)S(1)} %iota_xor_fusion) | copy-start | bytes 388
  121.0 6.9 collective-permute-start.10
  125.9 46.5 %copy-start.50 = (f32[512]{0:T(512)}, f32[512]{0:T(512)S(1)}, u32[]{:S(2)}) copy-start(f32[512]{0:T(512)S(1)} %broadcast_multiply_fusion.7) | copy-start | bytes 6148
  129.6 3.8 collective-permute-start.11
  130.3 17.7 %collective-permute-start.12 = (f32[4,2,6912]{2,0,1:T(4,128)S(1)}, f32[4,2,6912]{2,0,1:T(4,128)S(1)}, u32[]{:S(2)}, u32[]{:S(2)}) collective-permute-start(f32[4,2,6912]{2,0,1:T(4,128)S(1)} %get-tuple-element.272), channel_id=1, source_target_pairs={{16,0},{17,1},{18,2},{19,3},{20,4},{21,5},{22,6},{23,7},{24,8},{25... | collective-permute-start | bytes 663560 | tf_op jit(solution)/shard_map/ppermute | solution.py:486
  131.6 23.5 %collective-permute-start.13 = (f32[4,2,6912]{2,0,1:T(4,128)S(1)}, f32[4,2,6912]{2,0,1:T(4,128)S(1)}, u32[]{:S(2)}, u32[]{:S(2)}) collective-permute-start(f32[4,2,6912]{2,0,1:T(4,128)S(1)} %get-tuple-element.273), channel_id=1, source_target_pairs={{16,8},{17,9},{18,10},{19,11},{20,12},{21,13},{22,14},{23,15},{24,... | collective-permute-start | bytes 663560 | tf_op jit(solution)/shard_map/ppermute | solution.py:486
  156.6 10.7 %collective-permute-start.14 = (f32[2,6912]{1,0:T(2,128)}, f32[2,6912]{1,0:T(2,128)}, u32[]{:S(2)}, u32[]{:S(2)}) collective-permute-start(f32[2,6912]{1,0:T(2,128)} %bitcast.275), channel_id=1, source_target_pairs={{0,2},{1,3},{2,0},{3,1},{4,6},{5,7},{6,4},{7,5},{8,10},{9,11},{10,... | collective-permute-start | bytes 165896 | tf_op jit(solution)/shard_map/ppermute | solution.py:486
  157.6 9.7 %collective-permute-start.15 = (f32[2,6912]{1,0:T(2,128)}, f32[2,6912]{1,0:T(2,128)}, u32[]{:S(2)}, u32[]{:S(2)}) collective-permute-start(f32[2,6912]{1,0:T(2,128)} %bitcast.274), channel_id=1, source_target_pairs={{0,4},{1,5},{2,6},{3,7},{4,0},{5,1},{6,2},{7,3},{8,12},{9,13},{10,... | collective-permute-start | bytes 165896 | tf_op jit(solution)/shard_map/ppermute | solution.py:486
  160.2 10.7 %collective-permute-start.16 = (f32[2,6912]{1,0:T(2,128)}, f32[2,6912]{1,0:T(2,128)}, u32[]{:S(2)}, u32[]{:S(2)}) collective-permute-start(f32[2,6912]{1,0:T(2,128)} %bitcast.276), channel_id=1, source_target_pairs={{0,6},{1,7},{2,4},{3,5},{4,2},{5,3},{6,0},{7,1},{8,14},{9,15},{10,... | collective-permute-start | bytes 165896 | tf_op jit(solution)/shard_map/ppermute | solution.py:486
  174.7 155.2 %collective-permute-start.26 = (bf16[512,1152]{1,0:T(8,128)(2,1)}, bf16[512,1152]{1,0:T(8,128)(2,1)}, u32[]{:S(2)}, u32[]{:S(2)}) collective-permute-start(bf16[512,1152]{1,0:T(8,128)(2,1)} %fusion.9), channel_id=1, source_target_pairs={{0,1},{1,0},{2,3},{3,2},{4,5},{5,4},{6,7},{7,6},{8,9},{9,8},{10,11... | collective-permute-start | bytes 3538952 | tf_op jit(solution)/shard_map/ppermute | solution.py:1072
  179.1 150.9 %collective-permute-start.27 = (bf16[512,1152]{1,0:T(8,128)(2,1)}, bf16[512,1152]{1,0:T(8,128)(2,1)}, u32[]{:S(2)}, u32[]{:S(2)}) collective-permute-start(bf16[512,1152]{1,0:T(8,128)(2,1)} %fusion.10.g_ref), channel_id=1, source_target_pairs={{0,1},{1,0},{2,3},{3,2},{4,5},{5,4},{6,7},{7,6},{8,9},{9,8},{10,11... | collective-permute-start | bytes 3538952 | tf_op jit(solution)/shard_map/ppermute | solution.py:1072
  368.6 23.8 %collective-permute-start.29 = (bf16[512,3072]{1,0:T(8,128)(2,1)}, bf16[512,3072]{1,0:T(8,128)(2,1)}, u32[]{:S(2)}, u32[]{:S(2)}) collective-permute-start(bf16[512,3072]{1,0:T(8,128)(2,1)} %get-tuple-element.229), channel_id=1, source_target_pairs={{0,1},{1,0},{2,3},{3,2},{4,5},{5,4},{6,7},{7,6},{8,9},{9,8},{10,11... | collective-permute-start | bytes 9437192 | tf_op jit(solution)/shard_map/ppermute | solution.py:1072
  368.9 23.5 %collective-permute-start.30 = (bf16[512,3072]{1,0:T(8,128)(2,1)}, bf16[512,3072]{1,0:T(8,128)(2,1)}, u32[]{:S(2)}, u32[]{:S(2)}) collective-permute-start(bf16[512,3072]{1,0:T(8,128)(2,1)} %get-tuple-element.231), channel_id=1, source_target_pairs={{0,1},{1,0},{2,3},{3,2},{4,5},{5,4},{6,7},{7,6},{8,9},{9,8},{10,11... | collective-permute-start | bytes 9437192 | tf_op jit(solution)/shard_map/ppermute | solution.py:1072
  369.2 23.2 %collective-permute-start.31 = (bf16[512,3072]{1,0:T(8,128)(2,1)}, bf16[512,3072]{1,0:T(8,128)(2,1)}, u32[]{:S(2)}, u32[]{:S(2)}) collective-permute-start(bf16[512,3072]{1,0:T(8,128)(2,1)} %get-tuple-element.233), channel_id=1, source_target_pairs={{0,1},{1,0},{2,3},{3,2},{4,5},{5,4},{6,7},{7,6},{8,9},{9,8},{10,11... | collective-permute-start | bytes 9437192 | tf_op jit(solution)/shard_map/ppermute | solution.py:1072
  369.4 22.7 %collective-permute-start.28 = (bf16[512,1152]{1,0:T(8,128)(2,1)}, bf16[512,1152]{1,0:T(8,128)(2,1)}, u32[]{:S(2)}, u32[]{:S(2)}) collective-permute-start(bf16[512,1152]{1,0:T(8,128)(2,1)} %fusion.15.x_ref), channel_id=1, source_target_pairs={{0,1},{1,0},{2,3},{3,2},{4,5},{5,4},{6,7},{7,6},{8,9},{9,8},{10,11... | collective-permute-start | bytes 3538952 | tf_op jit(solution)/shard_map/ppermute | solution.py:1072
  389.2 115.5 %collective-permute-start.35 = (bf16[512,1152]{1,0:T(8,128)(2,1)}, bf16[512,1152]{1,0:T(8,128)(2,1)}, u32[]{:S(2)}, u32[]{:S(2)}) collective-permute-start(bf16[512,1152]{1,0:T(8,128)(2,1)} %copy-done.38), channel_id=1, source_target_pairs={{0,1},{1,0},{2,3},{3,2},{4,5},{5,4},{6,7},{7,6},{8,9},{9,8},{10,11... | collective-permute-start | bytes 3538952 | tf_op jit(solution)/shard_map/ppermute | solution.py:1072
  392.1 112.6 %collective-permute-start.36 = (bf16[512,1152]{1,0:T(8,128)(2,1)}, bf16[512,1152]{1,0:T(8,128)(2,1)}, u32[]{:S(2)}, u32[]{:S(2)}) collective-permute-start(bf16[512,1152]{1,0:T(8,128)(2,1)} %get-tuple-element.182), channel_id=1, source_target_pairs={{0,1},{1,0},{2,3},{3,2},{4,5},{5,4},{6,7},{7,6},{8,9},{9,8},{10,11... | collective-permute-start | bytes 3538952 | tf_op jit(solution)/shard_map/ppermute | solution.py:1072
  420.7 54.6 %collective-permute-start.34 = (bf16[2,4,1344,128]{3,2,1,0:T(8,128)(2,1)}, bf16[2,4,1344,128]{3,2,1,0:T(8,128)(2,1)}, u32[]{:S(2)}, u32[]{:S(2)}) collective-permute-start(bf16[2,4,1344,128]{3,2,1,0:T(8,128)(2,1)} %dynamic-slice_bitcast_fusion), channel_id=1, source_target_pairs={{0,8},{8,0},{16,24},{24,16},{1,9},{9,1},{17,25},{25,17},{2,10},{10... | collective-permute-start | bytes 8257544 | tf_op jit(solution)/shard_map/ppermute | solution.py:428
  423.8 54.8 %collective-permute-start.33 = (bf16[2,4,1344,128]{3,2,1,0:T(8,128)(2,1)}, bf16[2,4,1344,128]{3,2,1,0:T(8,128)(2,1)}, u32[]{:S(2)}, u32[]{:S(2)}) collective-permute-start(bf16[2,4,1344,128]{3,2,1,0:T(8,128)(2,1)} %dynamic-slice_bitcast_fusion.1), channel_id=1, source_target_pairs={{0,16},{16,0},{8,24},{24,8},{1,17},{17,1},{9,25},{25,9},{2,18},{18... | collective-permute-start | bytes 8257544 | tf_op jit(solution)/shard_map/ppermute | solution.py:428
  461.1 43.6 %collective-permute-start.32 = (bf16[512,3456]{1,0:T(8,128)(2,1)}, bf16[512,3456]{1,0:T(8,128)(2,1)}, u32[]{:S(2)}, u32[]{:S(2)}) collective-permute-start(bf16[512,3456]{1,0:T(8,128)(2,1)} %get-tuple-element.189), channel_id=1, source_target_pairs={{0,1},{1,0},{2,3},{3,2},{4,5},{5,4},{6,7},{7,6},{8,9},{9,8},{10,11... | collective-permute-start | bytes 10616840 | tf_op jit(solution)/shard_map/ppermute | solution.py:1072
  488.6 36.7 %collective-permute-start.40 = (bf16[4,1344,128]{2,1,0:T(8,128)(2,1)}, bf16[4,1344,128]{2,1,0:T(8,128)(2,1)}, u32[]{:S(2)}, u32[]{:S(2)}) collective-permute-start(bf16[4,1344,128]{2,1,0:T(8,128)(2,1)} %dynamic-slice_bitcast_fusion.2), channel_id=1, source_target_pairs={{0,16},{16,0},{8,24},{24,8},{1,17},{17,1},{9,25},{25,9},{2,18},{18... | collective-permute-start | bytes 4128776 | tf_op jit(solution)/shard_map/ppermute | solution.py:428
  493.2 37.8 %collective-permute-start.39 = (bf16[4,1344,128]{2,1,0:T(8,128)(2,1)}, bf16[4,1344,128]{2,1,0:T(8,128)(2,1)}, u32[]{:S(2)}, u32[]{:S(2)}) collective-permute-start(bf16[4,1344,128]{2,1,0:T(8,128)(2,1)} %dynamic-slice_bitcast_fusion.3), channel_id=1, source_target_pairs={{0,8},{8,0},{16,24},{24,16},{1,9},{9,1},{17,25},{25,17},{2,10},{10... | collective-permute-start | bytes 4128776 | tf_op jit(solution)/shard_map/ppermute | solution.py:428
  519.7 41.8 %collective-permute-start.38 = (bf16[2,4,648,128]{3,2,1,0:T(8,128)(2,1)S(1)}, bf16[2,4,648,128]{3,2,1,0:T(8,128)(2,1)S(1)}, u32[]{:S(2)}, u32[]{:S(2)}) collective-permute-start(bf16[2,4,648,128]{3,2,1,0:T(8,128)(2,1)S(1)} %dynamic-slice_bitcast_fusion.4), channel_id=1, source_target_pairs={{0,8},{8,0},{16,24},{24,16},{1,9},{9,1},{17,25},{25,17},{2,10},{10... | collective-permute-start | bytes 3981320 | tf_op jit(solution)/shard_map/ppermute | solution.py:428
  521.0 40.5 %collective-permute-start.37 = (bf16[2,4,648,128]{3,2,1,0:T(8,128)(2,1)S(1)}, bf16[2,4,648,128]{3,2,1,0:T(8,128)(2,1)S(1)}, u32[]{:S(2)}, u32[]{:S(2)}) collective-permute-start(bf16[2,4,648,128]{3,2,1,0:T(8,128)(2,1)S(1)} %dynamic-slice_bitcast_fusion.5), channel_id=1, source_target_pairs={{0,16},{16,0},{8,24},{24,8},{1,17},{17,1},{9,25},{25,9},{2,18},{18... | collective-permute-start | bytes 3981320 | tf_op jit(solution)/shard_map/ppermute | solution.py:428
  534.7 31.6 %collective-permute-start.43 = (bf16[2688,128]{1,0:T(8,128)(2,1)S(1)}, bf16[2688,128]{1,0:T(8,128)(2,1)S(1)}, u32[]{:S(2)}, u32[]{:S(2)}) collective-permute-start(bf16[2688,128]{1,0:T(8,128)(2,1)S(1)} %get-tuple-element.256), channel_id=1, source_target_pairs={{0,2},{1,3},{2,0},{3,1},{4,6},{5,7},{6,4},{7,5},{8,10},{9,11},{10,... | collective-permute-start | bytes 2064392 | tf_op jit(solution)/shard_map/ppermute | solution.py:455
  535.0 34.4 %collective-permute-start.44 = (bf16[2688,128]{1,0:T(8,128)(2,1)S(1)}, bf16[2688,128]{1,0:T(8,128)(2,1)S(1)}, u32[]{:S(2)}, u32[]{:S(2)}) collective-permute-start(bf16[2688,128]{1,0:T(8,128)(2,1)S(1)} %get-tuple-element.257), channel_id=1, source_target_pairs={{0,4},{1,5},{2,6},{3,7},{4,0},{5,1},{6,2},{7,3},{8,12},{9,13},{10,... | collective-permute-start | bytes 2064392 | tf_op jit(solution)/shard_map/ppermute | solution.py:455
  537.1 64.0 %collective-permute-start.45 = (bf16[2688,128]{1,0:T(8,128)(2,1)S(1)}, bf16[2688,128]{1,0:T(8,128)(2,1)S(1)}, u32[]{:S(2)}, u32[]{:S(2)}) collective-permute-start(bf16[2688,128]{1,0:T(8,128)(2,1)S(1)} %get-tuple-element.254), channel_id=1, source_target_pairs={{0,6},{1,7},{2,4},{3,5},{4,2},{5,3},{6,0},{7,1},{8,14},{9,15},{10,... | collective-permute-start | bytes 2064392 | tf_op jit(solution)/shard_map/ppermute | solution.py:455
  562.7 44.5 %collective-permute-start.42 = (bf16[4,648,128]{2,1,0:T(8,128)(2,1)}, bf16[4,648,128]{2,1,0:T(8,128)(2,1)}, u32[]{:S(2)}, u32[]{:S(2)}) collective-permute-start(bf16[4,648,128]{2,1,0:T(8,128)(2,1)} %dynamic-slice_bitcast_fusion.6), channel_id=1, source_target_pairs={{0,16},{16,0},{8,24},{24,8},{1,17},{17,1},{9,25},{25,9},{2,18},{18... | collective-permute-start | bytes 1990664 | tf_op jit(solution)/shard_map/ppermute | solution.py:428
  564.3 37.2 %copy-start.36 = (bf16[2,4,648,128]{3,2,1,0:T(8,128)(2,1)}, bf16[2,4,648,128]{3,2,1,0:T(8,128)(2,1)S(1)}, u32[]{:S(2)}) copy-start(bf16[2,4,648,128]{3,2,1,0:T(8,128)(2,1)S(1)} %fusion.5) | copy-start | bytes 3981316
  565.2 42.0 %collective-permute-start.41 = (bf16[4,648,128]{2,1,0:T(8,128)(2,1)}, bf16[4,648,128]{2,1,0:T(8,128)(2,1)}, u32[]{:S(2)}, u32[]{:S(2)}) collective-permute-start(bf16[4,648,128]{2,1,0:T(8,128)(2,1)} %dynamic-slice_bitcast_fusion.7), channel_id=1, source_target_pairs={{0,8},{8,0},{16,24},{24,16},{1,9},{9,1},{17,25},{25,17},{2,10},{10... | collective-permute-start | bytes 1990664 | tf_op jit(solution)/shard_map/ppermute | solution.py:428
  611.2 26.6 %collective-permute-start.50 = (bf16[1296,128]{1,0:T(8,128)(2,1)}, bf16[1296,128]{1,0:T(8,128)(2,1)}, u32[]{:S(2)}, u32[]{:S(2)}) collective-permute-start(bf16[1296,128]{1,0:T(8,128)(2,1)} %get-tuple-element.270), channel_id=1, source_target_pairs={{0,2},{1,3},{2,0},{3,1},{4,6},{5,7},{6,4},{7,5},{8,10},{9,11},{10,... | collective-permute-start | bytes 995336 | tf_op jit(solution)/shard_map/ppermute | solution.py:455
  613.4 41.7 %collective-permute-start.46 = (bf16[2688,128]{1,0:T(8,128)(2,1)}, bf16[2688,128]{1,0:T(8,128)(2,1)}, u32[]{:S(2)}, u32[]{:S(2)}) collective-permute-start(bf16[2688,128]{1,0:T(8,128)(2,1)} %bitcast_select_fusion.1), channel_id=1, source_target_pairs={{30,8},{16,9},{2,10},{18,11},{4,12},{20,13},{6,14},{17,15},{15,16}... | collective-permute-start | bytes 2064392 | tf_op jit(solution)/shard_map/ppermute | solution.py:340
  615.0 40.2 %collective-permute-start.47 = (bf16[2688,128]{1,0:T(8,128)(2,1)}, bf16[2688,128]{1,0:T(8,128)(2,1)}, u32[]{:S(2)}, u32[]{:S(2)}) collective-permute-start(bf16[2688,128]{1,0:T(8,128)(2,1)} %bitcast_select_fusion.1), channel_id=1, source_target_pairs={{14,7},{0,8},{24,9},{10,10},{26,11},{12,12},{28,13},{22,14},{25,15... | collective-permute-start | bytes 2064392 | tf_op jit(solution)/shard_map/ppermute | solution.py:340
  621.0 34.1 %collective-permute-start.48 = (bf16[2688,128]{1,0:T(8,128)(2,1)}, bf16[2688,128]{1,0:T(8,128)(2,1)}, u32[]{:S(2)}, u32[]{:S(2)}) collective-permute-start(bf16[2688,128]{1,0:T(8,128)(2,1)} %bitcast_select_fusion.1), channel_id=1, source_target_pairs={{30,7},{8,8},{2,9},{18,10},{4,11},{20,12},{6,13},{9,14},{15,15},{1... | collective-permute-start | bytes 2064392 | tf_op jit(solution)/shard_map/ppermute | solution.py:340
  622.6 19.1 %collective-permute-start.51 = (bf16[1296,128]{1,0:T(8,128)(2,1)}, bf16[1296,128]{1,0:T(8,128)(2,1)}, u32[]{:S(2)}, u32[]{:S(2)}) collective-permute-start(bf16[1296,128]{1,0:T(8,128)(2,1)} %get-tuple-element.271), channel_id=1, source_target_pairs={{0,4},{1,5},{2,6},{3,7},{4,0},{5,1},{6,2},{7,3},{8,12},{9,13},{10,... | collective-permute-start | bytes 995336 | tf_op jit(solution)/shard_map/ppermute | solution.py:455
  630.9 24.1 %all-to-all-start = ((f32[32,2,108]{2,1,0:T(2,128)}), f32[32,2,108]{2,1,0:T(2,128)S(1)}, u32[]{:S(2)}, u32[]{:S(2)}) async-start(f32[32,2,108]{2,1,0:T(2,128)} %copy.79), calls=%async_computation | async-start | bytes 65536 | tf_op jit(solution)/shard_map/all_to_all | solution.py:1179
  637.8 17.4 %collective-permute-start.49 = (bf16[2688,128]{1,0:T(8,128)(2,1)}, bf16[2688,128]{1,0:T(8,128)(2,1)}, u32[]{:S(2)}, u32[]{:S(2)}) collective-permute-start(bf16[2688,128]{1,0:T(8,128)(2,1)} %bitcast_select_fusion.1), channel_id=1, source_target_pairs={{16,8},{17,14},{21,29}} | collective-permute-start | bytes 2064392 | tf_op jit(solution)/shard_map/ppermute | solution.py:340
  641.6 13.5 %collective-permute-start.52 = (bf16[1296,128]{1,0:T(8,128)(2,1)}, bf16[1296,128]{1,0:T(8,128)(2,1)}, u32[]{:S(2)}, u32[]{:S(2)}) collective-permute-start(bf16[1296,128]{1,0:T(8,128)(2,1)} %get-tuple-element.268), channel_id=1, source_target_pairs={{0,6},{1,7},{2,4},{3,5},{4,2},{5,3},{6,0},{7,1},{8,14},{9,15},{10,... | collective-permute-start | bytes 995336 | tf_op jit(solution)/shard_map/ppermute | solution.py:455
  661.5 20.4 %collective-permute-start.53 = (bf16[1296,128]{1,0:T(8,128)(2,1)S(1)}, bf16[1296,128]{1,0:T(8,128)(2,1)S(1)}, u32[]{:S(2)}, u32[]{:S(2)}) collective-permute-start(bf16[1296,128]{1,0:T(8,128)(2,1)S(1)} %broadcast_select_fusion), channel_id=1, source_target_pairs={{0,0},{2,1},{9,2},{11,3},{4,4},{6,5},{29,6},{31,7}} | collective-permute-start | bytes 995336 | tf_op jit(solution)/shard_map/ppermute | solution.py:340
  662.8 37.6 %collective-permute-start.54 = (bf16[1296,128]{1,0:T(8,128)(2,1)S(1)}, bf16[1296,128]{1,0:T(8,128)(2,1)S(1)}, u32[]{:S(2)}, u32[]{:S(2)}) collective-permute-start(bf16[1296,128]{1,0:T(8,128)(2,1)S(1)} %broadcast_select_fusion), channel_id=1, source_target_pairs={{8,0},{10,1},{17,2},{19,3},{12,4},{14,5},{7,6}} | collective-permute-start | bytes 995336 | tf_op jit(solution)/shard_map/ppermute | solution.py:340
  664.1 36.3 %collective-permute-start.55 = (bf16[1296,128]{1,0:T(8,128)(2,1)S(1)}, bf16[1296,128]{1,0:T(8,128)(2,1)S(1)}, u32[]{:S(2)}, u32[]{:S(2)}) collective-permute-start(bf16[1296,128]{1,0:T(8,128)(2,1)S(1)} %broadcast_select_fusion), channel_id=1, source_target_pairs={{16,0},{18,1},{25,2},{27,3},{20,4},{5,5},{15,6}} | collective-permute-start | bytes 995336 | tf_op jit(solution)/shard_map/ppermute | solution.py:340
  665.4 35.0 %collective-permute-start.56 = (bf16[1296,128]{1,0:T(8,128)(2,1)S(1)}, bf16[1296,128]{1,0:T(8,128)(2,1)S(1)}, u32[]{:S(2)}, u32[]{:S(2)}) collective-permute-start(bf16[1296,128]{1,0:T(8,128)(2,1)S(1)} %broadcast_select_fusion), channel_id=1, source_target_pairs={{24,0},{26,1},{3,2},{22,3},{28,4},{13,5},{23,6}} | collective-permute-start | bytes 995336 | tf_op jit(solution)/shard_map/ppermute | solution.py:340
  676.3 24.2 %collective-permute-start.57 = (bf16[1296,128]{1,0:T(8,128)(2,1)S(1)}, bf16[1296,128]{1,0:T(8,128)(2,1)S(1)}, u32[]{:S(2)}, u32[]{:S(2)}) collective-permute-start(bf16[1296,128]{1,0:T(8,128)(2,1)S(1)} %broadcast_select_fusion), channel_id=1, source_target_pairs={{2,0},{1,1},{11,2},{30,3},{6,4},{21,5},{31,6}} | collective-permute-start | bytes 995336 | tf_op jit(solution)/shard_map/ppermute | solution.py:340
  (74 other events, 589.5 us)
Sparse Core Ops, SparseCore 0:
  83.8 203.4 all-gather.2
  504.8 88.2 all-gather.4

commit v6 on v4

--- a/solution.py
+++ b/solution.py
@@ -507,9 +507,9 @@
         mix_ref, down_ref, sem = rest
         step = pl.program_id(0)
 
-        def each(act):
+        def each(act, blocks=range(DEVICES)):
             stride = (BLOCK_A + BLOCK_B) // 8
-            for i in range(DEVICES):
+            for i in blocks:
                 first = i * stride + BLOCK_A // 8
                 if i < MLP_BLOCKS:
                     piece = source.at[pl.ds(first, full)]
@@ -525,7 +525,7 @@
             each(lambda copy: copy.start())
             branch_ref[...] = jnp.zeros_like(branch_ref)
             gin_ref[...] = jnp.zeros_like(gin_ref)
-            each(lambda copy: copy.wait())
+            each(lambda copy: copy.wait(), range(MLP_BLOCKS))
 
         def columns(first):
             return jnp.concatenate(
@@ -544,6 +544,10 @@
         silu = gate * sigma
         hid = (silu * up).astype(bf16)
         hid_ref[...] = hid
+        @pl.when(step == 0)
+        def _():
+            each(lambda copy: copy.wait(), range(MLP_BLOCKS, DEVICES))
+
         groups = tile // 8
         low_rows = down_ref[pl.ds(step * groups * chunks, groups * chunks)]
         low_rows = low_rows.reshape(groups, chunks, 8, 128)
@@ -846,8 +850,10 @@
                 * scale
             )
             top = jnp.max(scores, axis=1, keepdims=True)
-            log_total = top + jnp.log(jnp.sum(jnp.exp(scores - top), axis=1, keepdims=True))
-            probs = jnp.exp(scores - log_total).astype(bf16)
+            raised = jnp.exp(scores - top)
+            total = jnp.sum(raised, axis=1, keepdims=True)
+            log_total = top + jnp.log(total)
+            probs = (raised * (1.0 / total)).astype(bf16)
             att_ref[:, at] = jnp.dot(probs, v_ref[:, at], preferred_element_type=f32).astype(bf16)
             log_ref[:, h : h + 1] = log_total
 

time: 723 us -> 729 us (level)
  Pallas kernels: 147 us -> 157 us
    pallas_call x1, Pallas kernels: 23.1 us -> 34 us  [attention_forward(): pl.pallas_call(body, grid=(rows // length,), in_specs=[pl.BlockSpec((leng...]
  transfers between devices with their start and end apart: 61 -> 61, of which waited for: 19 -> 19; matrix products, arithmetic and copies ran while one was open for 19% -> 19% of each run, Pallas kernels for 14% -> 16%
where the time goes in v6:
time: 729 us; the launch traced here: 724 us
  waiting for transfers between devices  273 us (37%)
  Pallas kernels  157 us (22%)
  starting transfers between devices  110 us (15%)
  local copies, waits for them, and re-layouts  74.8 us (10%)
  other arithmetic  62.6 us (9%)
  matrix products  29.4 us (4%)
  between operations  16 us (2%)
    all_gather x1, waiting for transfers between devices, gathered_weights(): lax.all_gather(block, ('fsdp', 'dp'), axis=0, tiled=True)  108 us
    ppermute x9, waiting for transfers between devices, spread(): got = lax.ppermute(piece, ('fsdp', 'dp'), pairs)  38.9 us
    pallas_call x1, Pallas kernels, mlp_both_ways(): pl.pallas_call(body, grid=(steps,), in_specs=[whole, whole, line, pl.Bloc...  38.3 us
    ppermute x6, waiting for transfers between devices, from_line(): lax.ppermute(sends[k], 'dp', [(d, d ^ 2 * k) for d in range(8)])  35.5 us
    ppermute x8, waiting for transfers between devices, over_planes(): lax.ppermute(send, 'fsdp', axis)  34.3 us
    pallas_call x1, Pallas kernels, attention_forward(): pl.pallas_call(body, grid=(rows // length,), in_specs=[pl.BlockSpec((leng...  34 us
    pallas_call x1, Pallas kernels, grads_b_core_1(): pl.pallas_call(body, grid=(mlp_steps + down_steps,), in_specs=[pl.BlockSp...  33.7 us
    pallas_call x1, Pallas kernels, attention_backward(): pl.pallas_call(body, grid=(images,), in_specs=[pl.BlockSpec((length, 2 *...  26.7 us
  transfers between devices with their start and end apart: 61, of which 19 were waited for; matrix products, arithmetic and copies ran while one was open for 19% of the time, Pallas kernels for 16%

profile of v6, /device:TPU:9, one launch (start us, length us, event | category | flops | bytes accessed | tf_op | source)
XLA Modules:
  0.0 723.8 jit_solution(9789141242301991966)
XLA Ops:
  8.9 3.8 pad_dynamic-slice_fusion
  12.8 4.3 pad_dynamic-slice_fusion.12
  17.1 4.1 collective-permute-start.17
  21.2 3.0 collective-permute-start.18
  24.2 2.0 collective-permute-start.19
  28.2 2.0 collective-permute-start.21
  30.2 6.1 collective-permute-done.17
  37.8 15.1 %collective-permute-done.18 = bf16[1296,128]{1,0:T(8,128)(2,1)} collective-permute-done((bf16[1296,128]{1,0:T(8,128)(2,1)}, bf16[1296,128]{1,0:T(8,128)(2,1)}, u32[]{:S(2)}, u32[]{:S(2)}) %collective-permute-start.18) | collective-permute-done | bytes 331808 | tf_op jit(solution)/shard_map/ppermute | solution.py:331
  54.4 3.1 collective-permute-done.19
  63.0 14.5 %collective-permute-done.24 = bf16[2688,128]{1,0:T(8,128)(2,1)} collective-permute-done((bf16[2688,128]{1,0:T(8,128)(2,1)}, bf16[2688,128]{1,0:T(8,128)(2,1)}, u32[]{:S(2)}, u32[]{:S(2)}) %collective-permute-start.24) | collective-permute-done | bytes 688160 | tf_op jit(solution)/shard_map/ppermute | solution.py:331
  83.9 2.0 collective-permute-start.2
  85.9 7.5 %collective-permute-start.3 = (bf16[23,128]{1,0:T(8,128)(2,1)S(1)}, bf16[23,128]{1,0:T(8,128)(2,1)S(1)}, u32[]{:S(2)}, u32[]{:S(2)}) collective-permute-start(bf16[23,128]{1,0:T(8,128)(2,1)S(1)} %bitcast.323), channel_id=1, source_target_pairs={{0,4},{1,5},{2,6},{3,7},{4,0},{5,1},{6,2},{7,3},{8,12},{9,13},{10,... | collective-permute-start | bytes 17672 | tf_op jit(solution)/shard_map/ppermute | solution.py:468
  96.2 2.9 collective-permute-start.5
  104.9 7.9 %collective-permute-start.9 = (bf16[8,23,128]{2,1,0:T(8,128)(2,1)}, bf16[8,23,128]{2,1,0:T(8,128)(2,1)}, u32[]{:S(2)}, u32[]{:S(2)}) collective-permute-start(bf16[8,23,128]{2,1,0:T(8,128)(2,1)} %constant_dynamic-update-slice_fusion), channel_id=1, source_target_pairs={{0,24},{8,16},{16,8},{24,0},{1,25},{9,17},{17,9},{25,1},{2,26},{10... | collective-permute-start | bytes 141320 | tf_op jit(solution)/shard_map/ppermute | solution.py:475
  112.8 2.7 reshape.575
  133.5 14.6 %collective-permute-done.12 = f32[4,2,6912]{2,0,1:T(4,128)S(1)} collective-permute-done((f32[4,2,6912]{2,0,1:T(4,128)S(1)}, f32[4,2,6912]{2,0,1:T(4,128)S(1)}, u32[]{:S(2)}, u32[]{:S(2)}) %collective-permute-start.12) | collective-permute-done | bytes 221216 | tf_op jit(solution)/shard_map/ppermute | solution.py:486
  148.0 7.2 collective-permute-done.13
  157.6 2.0 collective-permute-start.15
  167.4 3.4 collective-permute-done.16
  172.4 2.3 fusion.9
  174.7 2.7 collective-permute-start.26
  177.4 2.1 fusion.10.g_ref
  179.5 107.8 %all-gather.3.cloned.1.call-done = bf16[127488,128]{1,0:T(8,128)(2,1)} async-done(((bf16[3984,128]{1,0:T(8,128)(2,1)}), bf16[127488,128]{1,0:T(8,128)(2,1)}) %all-gather.3.cloned.1.call-update) | async-done | bytes 32636944 | tf_op jit(solution)/shard_map/all_gather | solution.py:787
  287.3 4.3 split_a.1
  291.6 9.3 %convolution_add_fusion.proj_ref = f32[512,3456]{1,0:T(8,128)} fusion(bf16[512,1152]{1,0:T(8,128)(2,1)} %fusion.9, bf16[1152,3456]{1,0:T(8,128)(2,1)S(1)} %bitcast.279, f32[3456]{0:T(1024)S(1)} %slice-done.2), kind=kOutput, calls=%fused_computation | convolution fusion | flops 4078632960 | bytes 16233984 | tf_op jit(solution)/shard_map/dot_general | solution.py:1092
  300.9 34.0 %attention_forward.1 = (bf16[512,1152]{1,0:T(8,128)(2,1)S(1)}, bf16[512,1152]{1,0:T(8,128)(2,1)S(1)}, bf16[512,1152]{1,0:T(8,128)(2,1)S(1)}, bf16[512,1152]{1,0:T(8,128)(2,1)S(1)}, f32[512,16]{1,0:T(8,128)S(1)}) custom-call(f32[512,3456]{1,0:T(8,128)} %convolution_add_fusion.proj_ref, f32[256,1152]{1,0:T(8,128)S(1)} %copy.71.cos_ref, ...), custom_call_target="tpu_custom_call" | custom-call | flops 1207959552 | bytes 20000000 | tf_op jit(solution)/shard_map/attention_forward/pallas_call | solution.py:862
  335.1 3.3 fusion.74
  340.8 38.3 %mlp_both_ways.1 = (bf16[512,3072]{1,0:T(8,128)(2,1)}, bf16[512,3072]{1,0:T(8,128)(2,1)}, bf16[512,3072]{1,0:T(8,128)(2,1)}, f32[512,1152]{1,0:T(8,128)}, f32[51...) custom-call(bf16[512,1152]{1,0:T(8,128)(2,1)} %fusion.15.x_ref, bf16[512,1152]{1,0:T(8,128)(2,1)} %fusion.10.g_ref, ...), custom_call_target="tpu_custom_call" | custom-call | flops 21743271936 | bytes 30000000 | tf_op jit(solution)/shard_map/mlp_both_ways/pallas_call | solution.py:570
  382.6 5.6 fusion.19
  391.4 5.2 fusion.72
  402.9 34.4 %conditional.2 = (bf16[2,2,4,1344,128]{4,3,2,1,0:T(8,128)(2,1)}, bf16[2,2,4,1344,128]{4,3,2,1,0:T(8,128)(2,1)S(1)}) conditional(s32[]{:T(128)} %convert_element_type.267, (bf16[512,1152]{1,0:T(8,128)(2,1)}, bf16[512,1152]{1,0:T(8,128)(2,1)}, bf16[512,3072]{1,0:T(8,128)(2,1)}, bf16[512,3072]{1,0:T(8,128)(2,1)}, bf16[512,3072]{1,0:T(8,128)(2,1)}, ...), branch_computations={%region_6.7_spmd.clone, %region_7.8_spmd} | conditional | bytes 220 | solution.py:1117
  403.6 33.7 %grads_b_core_1.1 = (bf16[2688,8,128]{2,1,0:T(8,128)(2,1)}, bf16[2688,8,128]{2,1,0:T(8,128)(2,1)S(1)}) custom-call(s32[11]{0:T(128)S(1)} %copy-done.12, bf16[512,1152]{1,0:T(8,128)(2,1)} %get-tuple-element.215.xo7.xo8, bf16[512,1152]{1,0:T(8,128)(2,1)} %get-tuple-element.215.xo7.xo8, bf16[512,1152]{1,0:T(8,128)(2,1)} %get-tuple-element.216.xp7.xp8, ...), custom_call_target="tpu_custom_call" | custom-call | tf_op jit(solution)/shard_map/cond/branch_0_fun/grads_b_core_1/pallas_call | solution.py:700
  439.1 2.3 copy-done.35
  447.8 26.7 %attention_backward.1 = (bf16[512,3456]{1,0:T(8,128)(2,1)}, f32[2,1,3456]{2,1,0:T(1,128)S(1)}) custom-call(f32[512,3456]{1,0:T(8,128)} %convolution_add_fusion.proj_ref, bf16[512,1152]{1,0:T(8,128)(2,1)S(1)} %get-tuple-element.173.q_ref, bf16[512,1152]{1,0:T(8,128)(2,1)S(1)} %copy-done.3, bf16[512,1152]{1,0:T(8,128)(2,1)S(1)} %copy-done.5, ...), custom_call_target="tpu_custom_call" | custom-call | flops 1000 | bytes 1000 | tf_op jit(solution)/shard_map/attention_backward/pallas_call | solution.py:921
  474.7 7.0 fusion.79
  483.3 3.0 fusion.17
  489.1 3.3 fusion
  493.8 3.4 fusion.1
  499.2 4.6 collective-permute-start.40
  503.8 5.7 collective-permute-start.39
  509.5 2.7 reshape.576
  512.7 2.5 fusion.18
  515.3 14.8 %conditional.3 = (bf16[2,2,4,648,128]{4,3,2,1,0:T(8,128)(2,1)S(1)}, bf16[2,2,4,648,128]{4,3,2,1,0:T(8,128)(2,1)S(1)}) conditional(s32[]{:T(128)} %convert_element_type.267, (bf16[512,1152]{1,0:T(8,128)(2,1)}, bf16[512,1152]{1,0:T(8,128)(2,1)}, bf16[512,3456]{1,0:T(8,128)(2,1)}, bf16[512,3456]{1,0:T(8,128)(2,1)}, bf16[512,1152]{1,0:T(8,128)(2,1)}, ...), branch_computations={%region_18.19_spmd, %region_19.20_spmd} | conditional | bytes 16 | solution.py:1146
  515.3 14.6 %grads_a_core_1.1 = (bf16[16,81,8,128]{3,2,1,0:T(8,128)(2,1)S(1)}, bf16[16,81,8,128]{3,2,1,0:T(8,128)(2,1)S(1)}) custom-call(bf16[512,1152]{1,0:T(8,128)(2,1)} %get-tuple-element.88.xo, bf16[512,1152]{1,0:T(8,128)(2,1)} %get-tuple-element.89.xp, bf16[512,3456]{1,0:T(8,128)(2,1)} %get-tuple-element.90.go, bf16[512,3456]{1,0:T(8,128)(2,1)} %get-tuple-element.91.gp, ...), custom_call_target="tpu_custom_call" | custom-call | tf_op jit(solution)/shard_map/cond/branch_0_fun/grads_a_core_1/pallas_call | solution.py:764
  532.8 3.1 collective-permute-done.40
  535.9 5.7 collective-permute-done.39
  545.6 2.1 collective-permute-start.44
  547.9 24.1 %collective-permute-done.38 = bf16[2,4,648,128]{3,2,1,0:T(8,128)(2,1)S(1)} collective-permute-done((bf16[2,4,648,128]{3,2,1,0:T(8,128)(2,1)S(1)}, bf16[2,4,648,128]{3,2,1,0:T(8,128)(2,1)S(1)}, u32[]{:S(2)}, u32[]{:S(2)}) %collective-permute-start.38) | collective-permute-done | bytes 1327136 | tf_op jit(solution)/shard_map/ppermute | solution.py:428
  576.8 3.1 collective-permute-done.44
  579.9 31.7 %collective-permute-done.45 = bf16[2688,128]{1,0:T(8,128)(2,1)S(1)} collective-permute-done((bf16[2688,128]{1,0:T(8,128)(2,1)S(1)}, bf16[2688,128]{1,0:T(8,128)(2,1)S(1)}, u32[]{:S(2)}, u32[]{:S(2)}) %collective-permute-start.45) | collective-permute-done | bytes 688160 | tf_op jit(solution)/shard_map/ppermute | solution.py:455
  613.4 2.2 reshape.550
  621.8 2.2 multiply_add_fusion
  625.5 6.0 collective-permute-start.47
  633.1 3.4 collective-permute-start.51
  638.7 2.0 fusion.24
  641.4 6.9 all-to-all-start
  649.9 2.3 fusion.54
  654.4 2.6 reshape.559.refs_9_
  657.0 8.5 %all-to-all-done = f32[32,2,108]{2,1,0:T(2,128)S(1)} async-done(((f32[32,2,108]{2,1,0:T(2,128)}), f32[32,2,108]{2,1,0:T(2,128)S(1)}, u32[]{:S(2)}, u32[]{:S(2)}) %all-to-all-start) | async-done | bytes 27680 | tf_op jit(solution)/shard_map/all_to_all | solution.py:1187
  668.1 2.0 reshape.554
  676.0 10.8 %collective-permute-start.56 = (bf16[1296,128]{1,0:T(8,128)(2,1)S(1)}, bf16[1296,128]{1,0:T(8,128)(2,1)S(1)}, u32[]{:S(2)}, u32[]{:S(2)}) collective-permute-start(bf16[1296,128]{1,0:T(8,128)(2,1)S(1)} %broadcast_select_fusion), channel_id=1, source_target_pairs={{24,0},{26,1},{3,2},{22,3},{28,4},{13,5},{23,6}} | collective-permute-start | bytes 995336 | tf_op jit(solution)/shard_map/ppermute | solution.py:340
  688.7 3.8 collective-permute-done.53.refs_4_
  692.5 18.5 %collective-permute-done.54.refs_5_ = bf16[1296,128]{1,0:T(8,128)(2,1)S(1)} collective-permute-done((bf16[1296,128]{1,0:T(8,128)(2,1)S(1)}, bf16[1296,128]{1,0:T(8,128)(2,1)S(1)}, u32[]{:S(2)}, u32[]{:S(2)}) %collective-permute-start.54) | collective-permute-done | bytes 331808 | tf_op jit(solution)/shard_map/ppermute | solution.py:340
  711.0 5.7 owned_rows.1
  (382 shorter events, 127.9 us)
Async XLA Ops:
  7.2 280.1 %all-gather.3.cloned.1.call-start = ((), (), s32[]{:S(2)}) async-start(), calls=%async_computation.1 | async-start | bytes 33656832 | tf_op jit(solution)/shard_map/all_gather | solution.py:787
  17.1 19.2 %collective-permute-start.17 = (bf16[1296,128]{1,0:T(8,128)(2,1)}, bf16[1296,128]{1,0:T(8,128)(2,1)S(1)}, u32[]{:S(2)}, u32[]{:S(2)}) collective-permute-start(bf16[1296,128]{1,0:T(8,128)(2,1)} %get-tuple-element.158), channel_id=1, source_target_pairs={{0,0},{1,4},{2,9},{3,13},{4,18},{5,22},{6,27},{7,31}} | collective-permute-start | bytes 995336 | tf_op jit(solution)/shard_map/ppermute | solution.py:331
  21.2 31.7 %collective-permute-start.18 = (bf16[1296,128]{1,0:T(8,128)(2,1)}, bf16[1296,128]{1,0:T(8,128)(2,1)}, u32[]{:S(2)}, u32[]{:S(2)}) collective-permute-start(bf16[1296,128]{1,0:T(8,128)(2,1)} %get-tuple-element.159), channel_id=1, source_target_pairs={{0,1},{1,5},{2,10},{3,14},{4,19},{5,23},{6,28}} | collective-permute-start | bytes 995336 | tf_op jit(solution)/shard_map/ppermute | solution.py:331
  24.2 33.3 %collective-permute-start.19 = (bf16[1296,128]{1,0:T(8,128)(2,1)}, bf16[1296,128]{1,0:T(8,128)(2,1)}, u32[]{:S(2)}, u32[]{:S(2)}) collective-permute-start(bf16[1296,128]{1,0:T(8,128)(2,1)} %get-tuple-element.160), channel_id=1, source_target_pairs={{0,2},{1,6},{2,11},{3,15},{4,20},{5,24},{6,29}} | collective-permute-start | bytes 995336 | tf_op jit(solution)/shard_map/ppermute | solution.py:331
  26.2 32.6 %collective-permute-start.20 = (bf16[1296,128]{1,0:T(8,128)(2,1)S(1)}, bf16[1296,128]{1,0:T(8,128)(2,1)}, u32[]{:S(2)}, u32[]{:S(2)}) collective-permute-start(bf16[1296,128]{1,0:T(8,128)(2,1)S(1)} %get-tuple-element.161), channel_id=1, source_target_pairs={{0,3},{1,7},{2,12},{3,16},{4,21},{5,25},{6,30}} | collective-permute-start | bytes 995336 | tf_op jit(solution)/shard_map/ppermute | solution.py:331
  28.2 32.2 %collective-permute-start.21 = (bf16[1296,128]{1,0:T(8,128)(2,1)S(1)}, bf16[1296,128]{1,0:T(8,128)(2,1)}, u32[]{:S(2)}, u32[]{:S(2)}) collective-permute-start(bf16[1296,128]{1,0:T(8,128)(2,1)S(1)} %get-tuple-element.162), channel_id=1, source_target_pairs={{0,4},{1,8},{2,13},{3,17},{4,22},{5,26},{6,31}} | collective-permute-start | bytes 995336 | tf_op jit(solution)/shard_map/ppermute | solution.py:331
  36.3 26.8 %collective-permute-start.22 = (bf16[2688,128]{1,0:T(8,128)(2,1)}, bf16[2688,128]{1,0:T(8,128)(2,1)}, u32[]{:S(2)}, u32[]{:S(2)}) collective-permute-start(bf16[2688,128]{1,0:T(8,128)(2,1)} %get-tuple-element.163), channel_id=1, source_target_pairs={{8,1},{9,4},{10,6},{11,8},{12,10},{13,12},{14,14},{15,17},{16,19},... | collective-permute-start | bytes 2064392 | tf_op jit(solution)/shard_map/ppermute | solution.py:331
  52.9 10.2 %collective-permute-start.23 = (bf16[2688,128]{1,0:T(8,128)(2,1)}, bf16[2688,128]{1,0:T(8,128)(2,1)}, u32[]{:S(2)}, u32[]{:S(2)}) collective-permute-start(bf16[2688,128]{1,0:T(8,128)(2,1)} %get-tuple-element.164), channel_id=1, source_target_pairs={{7,0},{8,2},{9,5},{10,7},{11,9},{12,11},{13,13},{14,15},{15,18},{1... | collective-permute-start | bytes 2064392 | tf_op jit(solution)/shard_map/ppermute | solution.py:331
  57.5 20.1 %collective-permute-start.24 = (bf16[2688,128]{1,0:T(8,128)(2,1)}, bf16[2688,128]{1,0:T(8,128)(2,1)}, u32[]{:S(2)}, u32[]{:S(2)}) collective-permute-start(bf16[2688,128]{1,0:T(8,128)(2,1)} %get-tuple-element.165), channel_id=1, source_target_pairs={{7,1},{8,3},{9,6},{10,8},{11,10},{12,12},{13,14},{14,16},{15,19},{... | collective-permute-start | bytes 2064392 | tf_op jit(solution)/shard_map/ppermute | solution.py:331
  58.8 18.8 %collective-permute-start.25 = (bf16[2688,128]{1,0:T(8,128)(2,1)S(1)}, bf16[2688,128]{1,0:T(8,128)(2,1)}, u32[]{:S(2)}, u32[]{:S(2)}) collective-permute-start(bf16[2688,128]{1,0:T(8,128)(2,1)S(1)} %get-tuple-element.166), channel_id=1, source_target_pairs={{8,4},{14,17},{29,27}} | collective-permute-start | bytes 2064392 | tf_op jit(solution)/shard_map/ppermute | solution.py:331
  83.7 552.8 %all-gather.5.cloned.1.call-start = ((), (), s32[]{:S(2)}) async-start(), calls=%async_computation.2 | async-start | bytes 1622016 | tf_op jit(solution)/shard_map/all_gather | solution.py:1145
  83.7 12.5 %collective-permute-start = (bf16[23,128]{1,0:T(8,128)(2,1)S(1)}, bf16[23,128]{1,0:T(8,128)(2,1)S(1)}, u32[]{:S(2)}, u32[]{:S(2)}) collective-permute-start(bf16[23,128]{1,0:T(8,128)(2,1)S(1)} %bitcast.320), channel_id=1, source_target_pairs={{0,1},{1,0},{2,3},{3,2},{4,5},{5,4},{6,7},{7,6},{8,9},{9,8},{10,11... | collective-permute-start | bytes 17672 | tf_op jit(solution)/shard_map/ppermute | solution.py:468
  83.8 15.9 %collective-permute-start.1 = (bf16[23,128]{1,0:T(8,128)(2,1)S(1)}, bf16[23,128]{1,0:T(8,128)(2,1)S(1)}, u32[]{:S(2)}, u32[]{:S(2)}) collective-permute-start(bf16[23,128]{1,0:T(8,128)(2,1)S(1)} %bitcast.321), channel_id=1, source_target_pairs={{0,2},{1,3},{2,0},{3,1},{4,6},{5,7},{6,4},{7,5},{8,10},{9,11},{10,... | collective-permute-start | bytes 17672 | tf_op jit(solution)/shard_map/ppermute | solution.py:468
  83.9 16.4 %collective-permute-start.2 = (bf16[23,128]{1,0:T(8,128)(2,1)S(1)}, bf16[23,128]{1,0:T(8,128)(2,1)S(1)}, u32[]{:S(2)}, u32[]{:S(2)}) collective-permute-start(bf16[23,128]{1,0:T(8,128)(2,1)S(1)} %bitcast.322), channel_id=1, source_target_pairs={{0,3},{1,2},{2,1},{3,0},{4,7},{5,6},{6,5},{7,4},{8,11},{9,10},{10,... | collective-permute-start | bytes 17672 | tf_op jit(solution)/shard_map/ppermute | solution.py:468
  85.9 14.9 %collective-permute-start.3 = (bf16[23,128]{1,0:T(8,128)(2,1)S(1)}, bf16[23,128]{1,0:T(8,128)(2,1)S(1)}, u32[]{:S(2)}, u32[]{:S(2)}) collective-permute-start(bf16[23,128]{1,0:T(8,128)(2,1)S(1)} %bitcast.323), channel_id=1, source_target_pairs={{0,4},{1,5},{2,6},{3,7},{4,0},{5,1},{6,2},{7,3},{8,12},{9,13},{10,... | collective-permute-start | bytes 17672 | tf_op jit(solution)/shard_map/ppermute | solution.py:468
  93.4 8.0 %collective-permute-start.4 = (bf16[23,128]{1,0:T(8,128)(2,1)S(1)}, bf16[23,128]{1,0:T(8,128)(2,1)S(1)}, u32[]{:S(2)}, u32[]{:S(2)}) collective-permute-start(bf16[23,128]{1,0:T(8,128)(2,1)S(1)} %bitcast.324), channel_id=1, source_target_pairs={{0,5},{1,4},{2,7},{3,6},{4,1},{5,0},{6,3},{7,2},{8,13},{9,12},{10,... | collective-permute-start | bytes 17672 | tf_op jit(solution)/shard_map/ppermute | solution.py:468
  96.2 5.9 collective-permute-start.5
  99.7 3.5 collective-permute-start.6
  103.8 13.1 %collective-permute-start.7 = (bf16[8,23,128]{2,1,0:T(8,128)(2,1)}, bf16[8,23,128]{2,1,0:T(8,128)(2,1)}, u32[]{:S(2)}, u32[]{:S(2)}) collective-permute-start(bf16[8,23,128]{2,1,0:T(8,128)(2,1)} %constant_dynamic-update-slice_fusion), channel_id=1, source_target_pairs={{0,8},{8,0},{16,24},{24,16},{1,9},{9,1},{17,25},{25,17},{2,10},{10... | collective-permute-start | bytes 141320 | tf_op jit(solution)/shard_map/ppermute | solution.py:475
  103.8 13.1 %collective-permute-start.8 = (bf16[8,23,128]{2,1,0:T(8,128)(2,1)}, bf16[8,23,128]{2,1,0:T(8,128)(2,1)}, u32[]{:S(2)}, u32[]{:S(2)}) collective-permute-start(bf16[8,23,128]{2,1,0:T(8,128)(2,1)} %constant_dynamic-update-slice_fusion), channel_id=1, source_target_pairs={{0,16},{8,24},{16,0},{24,8},{1,17},{9,25},{17,1},{25,9},{2,18},{10... | collective-permute-start | bytes 141320 | tf_op jit(solution)/shard_map/ppermute | solution.py:475
  104.9 12.0 %collective-permute-start.9 = (bf16[8,23,128]{2,1,0:T(8,128)(2,1)}, bf16[8,23,128]{2,1,0:T(8,128)(2,1)}, u32[]{:S(2)}, u32[]{:S(2)}) collective-permute-start(bf16[8,23,128]{2,1,0:T(8,128)(2,1)} %constant_dynamic-update-slice_fusion), channel_id=1, source_target_pairs={{0,24},{8,16},{16,8},{24,0},{1,25},{9,17},{17,9},{25,1},{2,26},{10... | collective-permute-start | bytes 141320 | tf_op jit(solution)/shard_map/ppermute | solution.py:475
  112.8 47.8 %copy-start.71 = (s32[32]{0:T(128)}, s32[32]{0:T(128)S(1)}, u32[]{:S(2)}) copy-start(s32[32]{0:T(128)S(1)} %iota_xor_fusion) | copy-start | bytes 388
  121.1 6.9 collective-permute-start.10
  126.0 46.4 %copy-start.50 = (f32[512]{0:T(512)}, f32[512]{0:T(512)S(1)}, u32[]{:S(2)}) copy-start(f32[512]{0:T(512)S(1)} %broadcast_multiply_fusion.7) | copy-start | bytes 6148
  129.6 3.8 collective-permute-start.11
  130.3 17.7 %collective-permute-start.12 = (f32[4,2,6912]{2,0,1:T(4,128)S(1)}, f32[4,2,6912]{2,0,1:T(4,128)S(1)}, u32[]{:S(2)}, u32[]{:S(2)}) collective-permute-start(f32[4,2,6912]{2,0,1:T(4,128)S(1)} %get-tuple-element.272), channel_id=1, source_target_pairs={{16,0},{17,1},{18,2},{19,3},{20,4},{21,5},{22,6},{23,7},{24,8},{25... | collective-permute-start | bytes 663560 | tf_op jit(solution)/shard_map/ppermute | solution.py:486
  131.6 23.6 %collective-permute-start.13 = (f32[4,2,6912]{2,0,1:T(4,128)S(1)}, f32[4,2,6912]{2,0,1:T(4,128)S(1)}, u32[]{:S(2)}, u32[]{:S(2)}) collective-permute-start(f32[4,2,6912]{2,0,1:T(4,128)S(1)} %get-tuple-element.273), channel_id=1, source_target_pairs={{16,8},{17,9},{18,10},{19,11},{20,12},{21,13},{22,14},{23,15},{24,... | collective-permute-start | bytes 663560 | tf_op jit(solution)/shard_map/ppermute | solution.py:486
  156.7 10.7 %collective-permute-start.14 = (f32[2,6912]{1,0:T(2,128)}, f32[2,6912]{1,0:T(2,128)}, u32[]{:S(2)}, u32[]{:S(2)}) collective-permute-start(f32[2,6912]{1,0:T(2,128)} %bitcast.275), channel_id=1, source_target_pairs={{0,2},{1,3},{2,0},{3,1},{4,6},{5,7},{6,4},{7,5},{8,10},{9,11},{10,... | collective-permute-start | bytes 165896 | tf_op jit(solution)/shard_map/ppermute | solution.py:486
  157.6 9.7 %collective-permute-start.15 = (f32[2,6912]{1,0:T(2,128)}, f32[2,6912]{1,0:T(2,128)}, u32[]{:S(2)}, u32[]{:S(2)}) collective-permute-start(f32[2,6912]{1,0:T(2,128)} %bitcast.274), channel_id=1, source_target_pairs={{0,4},{1,5},{2,6},{3,7},{4,0},{5,1},{6,2},{7,3},{8,12},{9,13},{10,... | collective-permute-start | bytes 165896 | tf_op jit(solution)/shard_map/ppermute | solution.py:486
  160.2 10.6 %collective-permute-start.16 = (f32[2,6912]{1,0:T(2,128)}, f32[2,6912]{1,0:T(2,128)}, u32[]{:S(2)}, u32[]{:S(2)}) collective-permute-start(f32[2,6912]{1,0:T(2,128)} %bitcast.276), channel_id=1, source_target_pairs={{0,6},{1,7},{2,4},{3,5},{4,2},{5,3},{6,0},{7,1},{8,14},{9,15},{10,... | collective-permute-start | bytes 165896 | tf_op jit(solution)/shard_map/ppermute | solution.py:486
  174.7 166.0 %collective-permute-start.26 = (bf16[512,1152]{1,0:T(8,128)(2,1)}, bf16[512,1152]{1,0:T(8,128)(2,1)}, u32[]{:S(2)}, u32[]{:S(2)}) collective-permute-start(bf16[512,1152]{1,0:T(8,128)(2,1)} %fusion.9), channel_id=1, source_target_pairs={{0,1},{1,0},{2,3},{3,2},{4,5},{5,4},{6,7},{7,6},{8,9},{9,8},{10,11... | collective-permute-start | bytes 3538952 | tf_op jit(solution)/shard_map/ppermute | solution.py:1080
  179.5 161.3 %collective-permute-start.27 = (bf16[512,1152]{1,0:T(8,128)(2,1)}, bf16[512,1152]{1,0:T(8,128)(2,1)}, u32[]{:S(2)}, u32[]{:S(2)}) collective-permute-start(bf16[512,1152]{1,0:T(8,128)(2,1)} %fusion.10.g_ref), channel_id=1, source_target_pairs={{0,1},{1,0},{2,3},{3,2},{4,5},{5,4},{6,7},{7,6},{8,9},{9,8},{10,11... | collective-permute-start | bytes 3538952 | tf_op jit(solution)/shard_map/ppermute | solution.py:1080
  291.6 43.4 %copy-start = (bf16[1296,8,128]{2,1,0:T(8,128)(2,1)}, bf16[1296,8,128]{2,1,0:T(8,128)(2,1)S(1)}, u32[]{:S(2)}) copy-start(bf16[1296,8,128]{2,1,0:T(8,128)(2,1)S(1)} %get-tuple-element.169) | copy-start | bytes 7962628
  379.1 23.8 %collective-permute-start.29 = (bf16[512,3072]{1,0:T(8,128)(2,1)}, bf16[512,3072]{1,0:T(8,128)(2,1)}, u32[]{:S(2)}, u32[]{:S(2)}) collective-permute-start(bf16[512,3072]{1,0:T(8,128)(2,1)} %get-tuple-element.229), channel_id=1, source_target_pairs={{0,1},{1,0},{2,3},{3,2},{4,5},{5,4},{6,7},{7,6},{8,9},{9,8},{10,11... | collective-permute-start | bytes 9437192 | tf_op jit(solution)/shard_map/ppermute | solution.py:1080
  379.4 23.5 %collective-permute-start.30 = (bf16[512,3072]{1,0:T(8,128)(2,1)}, bf16[512,3072]{1,0:T(8,128)(2,1)}, u32[]{:S(2)}, u32[]{:S(2)}) collective-permute-start(bf16[512,3072]{1,0:T(8,128)(2,1)} %get-tuple-element.231), channel_id=1, source_target_pairs={{0,1},{1,0},{2,3},{3,2},{4,5},{5,4},{6,7},{7,6},{8,9},{9,8},{10,11... | collective-permute-start | bytes 9437192 | tf_op jit(solution)/shard_map/ppermute | solution.py:1080
  379.7 23.2 %collective-permute-start.31 = (bf16[512,3072]{1,0:T(8,128)(2,1)}, bf16[512,3072]{1,0:T(8,128)(2,1)}, u32[]{:S(2)}, u32[]{:S(2)}) collective-permute-start(bf16[512,3072]{1,0:T(8,128)(2,1)} %get-tuple-element.233), channel_id=1, source_target_pairs={{0,1},{1,0},{2,3},{3,2},{4,5},{5,4},{6,7},{7,6},{8,9},{9,8},{10,11... | collective-permute-start | bytes 9437192 | tf_op jit(solution)/shard_map/ppermute | solution.py:1080
  379.9 22.7 %collective-permute-start.28 = (bf16[512,1152]{1,0:T(8,128)(2,1)}, bf16[512,1152]{1,0:T(8,128)(2,1)}, u32[]{:S(2)}, u32[]{:S(2)}) collective-permute-start(bf16[512,1152]{1,0:T(8,128)(2,1)} %fusion.15.x_ref), channel_id=1, source_target_pairs={{0,1},{1,0},{2,3},{3,2},{4,5},{5,4},{6,7},{7,6},{8,9},{9,8},{10,11... | collective-permute-start | bytes 3538952 | tf_op jit(solution)/shard_map/ppermute | solution.py:1080
  399.7 115.5 %collective-permute-start.35 = (bf16[512,1152]{1,0:T(8,128)(2,1)}, bf16[512,1152]{1,0:T(8,128)(2,1)}, u32[]{:S(2)}, u32[]{:S(2)}) collective-permute-start(bf16[512,1152]{1,0:T(8,128)(2,1)} %copy-done.38), channel_id=1, source_target_pairs={{0,1},{1,0},{2,3},{3,2},{4,5},{5,4},{6,7},{7,6},{8,9},{9,8},{10,11... | collective-permute-start | bytes 3538952 | tf_op jit(solution)/shard_map/ppermute | solution.py:1080
  402.7 112.6 %collective-permute-start.36 = (bf16[512,1152]{1,0:T(8,128)(2,1)}, bf16[512,1152]{1,0:T(8,128)(2,1)}, u32[]{:S(2)}, u32[]{:S(2)}) collective-permute-start(bf16[512,1152]{1,0:T(8,128)(2,1)} %get-tuple-element.182), channel_id=1, source_target_pairs={{0,1},{1,0},{2,3},{3,2},{4,5},{5,4},{6,7},{7,6},{8,9},{9,8},{10,11... | collective-permute-start | bytes 3538952 | tf_op jit(solution)/shard_map/ppermute | solution.py:1080
  441.4 46.3 %collective-permute-start.34 = (bf16[2,4,1344,128]{3,2,1,0:T(8,128)(2,1)}, bf16[2,4,1344,128]{3,2,1,0:T(8,128)(2,1)}, u32[]{:S(2)}, u32[]{:S(2)}) collective-permute-start(bf16[2,4,1344,128]{3,2,1,0:T(8,128)(2,1)} %dynamic-slice_bitcast_fusion), channel_id=1, source_target_pairs={{0,8},{8,0},{16,24},{24,16},{1,9},{9,1},{17,25},{25,17},{2,10},{10... | collective-permute-start | bytes 8257544 | tf_op jit(solution)/shard_map/ppermute | solution.py:428
  444.5 44.6 %collective-permute-start.33 = (bf16[2,4,1344,128]{3,2,1,0:T(8,128)(2,1)}, bf16[2,4,1344,128]{3,2,1,0:T(8,128)(2,1)}, u32[]{:S(2)}, u32[]{:S(2)}) collective-permute-start(bf16[2,4,1344,128]{3,2,1,0:T(8,128)(2,1)} %dynamic-slice_bitcast_fusion.1), channel_id=1, source_target_pairs={{0,16},{16,0},{8,24},{24,8},{1,17},{17,1},{9,25},{25,9},{2,18},{18... | collective-permute-start | bytes 8257544 | tf_op jit(solution)/shard_map/ppermute | solution.py:428
  481.8 33.5 %collective-permute-start.32 = (bf16[512,3456]{1,0:T(8,128)(2,1)}, bf16[512,3456]{1,0:T(8,128)(2,1)}, u32[]{:S(2)}, u32[]{:S(2)}) collective-permute-start(bf16[512,3456]{1,0:T(8,128)(2,1)} %get-tuple-element.189), channel_id=1, source_target_pairs={{0,1},{1,0},{2,3},{3,2},{4,5},{5,4},{6,7},{7,6},{8,9},{9,8},{10,11... | collective-permute-start | bytes 10616840 | tf_op jit(solution)/shard_map/ppermute | solution.py:1080
  499.2 36.7 %collective-permute-start.40 = (bf16[4,1344,128]{2,1,0:T(8,128)(2,1)}, bf16[4,1344,128]{2,1,0:T(8,128)(2,1)}, u32[]{:S(2)}, u32[]{:S(2)}) collective-permute-start(bf16[4,1344,128]{2,1,0:T(8,128)(2,1)} %dynamic-slice_bitcast_fusion.2), channel_id=1, source_target_pairs={{0,16},{16,0},{8,24},{24,8},{1,17},{17,1},{9,25},{25,9},{2,18},{18... | collective-permute-start | bytes 4128776 | tf_op jit(solution)/shard_map/ppermute | solution.py:428
  503.8 37.8 %collective-permute-start.39 = (bf16[4,1344,128]{2,1,0:T(8,128)(2,1)}, bf16[4,1344,128]{2,1,0:T(8,128)(2,1)}, u32[]{:S(2)}, u32[]{:S(2)}) collective-permute-start(bf16[4,1344,128]{2,1,0:T(8,128)(2,1)} %dynamic-slice_bitcast_fusion.3), channel_id=1, source_target_pairs={{0,8},{8,0},{16,24},{24,16},{1,9},{9,1},{17,25},{25,17},{2,10},{10... | collective-permute-start | bytes 4128776 | tf_op jit(solution)/shard_map/ppermute | solution.py:428
  530.2 41.9 %collective-permute-start.38 = (bf16[2,4,648,128]{3,2,1,0:T(8,128)(2,1)S(1)}, bf16[2,4,648,128]{3,2,1,0:T(8,128)(2,1)S(1)}, u32[]{:S(2)}, u32[]{:S(2)}) collective-permute-start(bf16[2,4,648,128]{3,2,1,0:T(8,128)(2,1)S(1)} %dynamic-slice_bitcast_fusion.4), channel_id=1, source_target_pairs={{0,8},{8,0},{16,24},{24,16},{1,9},{9,1},{17,25},{25,17},{2,10},{10... | collective-permute-start | bytes 3981320 | tf_op jit(solution)/shard_map/ppermute | solution.py:428
  531.5 40.5 %collective-permute-start.37 = (bf16[2,4,648,128]{3,2,1,0:T(8,128)(2,1)S(1)}, bf16[2,4,648,128]{3,2,1,0:T(8,128)(2,1)S(1)}, u32[]{:S(2)}, u32[]{:S(2)}) collective-permute-start(bf16[2,4,648,128]{3,2,1,0:T(8,128)(2,1)S(1)} %dynamic-slice_bitcast_fusion.5), channel_id=1, source_target_pairs={{0,16},{16,0},{8,24},{24,8},{1,17},{17,1},{9,25},{25,9},{2,18},{18... | collective-permute-start | bytes 3981320 | tf_op jit(solution)/shard_map/ppermute | solution.py:428
  545.2 31.6 %collective-permute-start.43 = (bf16[2688,128]{1,0:T(8,128)(2,1)S(1)}, bf16[2688,128]{1,0:T(8,128)(2,1)S(1)}, u32[]{:S(2)}, u32[]{:S(2)}) collective-permute-start(bf16[2688,128]{1,0:T(8,128)(2,1)S(1)} %get-tuple-element.256), channel_id=1, source_target_pairs={{0,2},{1,3},{2,0},{3,1},{4,6},{5,7},{6,4},{7,5},{8,10},{9,11},{10,... | collective-permute-start | bytes 2064392 | tf_op jit(solution)/shard_map/ppermute | solution.py:455
  545.6 34.4 %collective-permute-start.44 = (bf16[2688,128]{1,0:T(8,128)(2,1)S(1)}, bf16[2688,128]{1,0:T(8,128)(2,1)S(1)}, u32[]{:S(2)}, u32[]{:S(2)}) collective-permute-start(bf16[2688,128]{1,0:T(8,128)(2,1)S(1)} %get-tuple-element.257), channel_id=1, source_target_pairs={{0,4},{1,5},{2,6},{3,7},{4,0},{5,1},{6,2},{7,3},{8,12},{9,13},{10,... | collective-permute-start | bytes 2064392 | tf_op jit(solution)/shard_map/ppermute | solution.py:455
  547.6 64.0 %collective-permute-start.45 = (bf16[2688,128]{1,0:T(8,128)(2,1)S(1)}, bf16[2688,128]{1,0:T(8,128)(2,1)S(1)}, u32[]{:S(2)}, u32[]{:S(2)}) collective-permute-start(bf16[2688,128]{1,0:T(8,128)(2,1)S(1)} %get-tuple-element.254), channel_id=1, source_target_pairs={{0,6},{1,7},{2,4},{3,5},{4,2},{5,3},{6,0},{7,1},{8,14},{9,15},{10,... | collective-permute-start | bytes 2064392 | tf_op jit(solution)/shard_map/ppermute | solution.py:455
  573.3 44.5 %collective-permute-start.42 = (bf16[4,648,128]{2,1,0:T(8,128)(2,1)}, bf16[4,648,128]{2,1,0:T(8,128)(2,1)}, u32[]{:S(2)}, u32[]{:S(2)}) collective-permute-start(bf16[4,648,128]{2,1,0:T(8,128)(2,1)} %dynamic-slice_bitcast_fusion.6), channel_id=1, source_target_pairs={{0,16},{16,0},{8,24},{24,8},{1,17},{17,1},{9,25},{25,9},{2,18},{18... | collective-permute-start | bytes 1990664 | tf_op jit(solution)/shard_map/ppermute | solution.py:428
  575.8 42.0 %collective-permute-start.41 = (bf16[4,648,128]{2,1,0:T(8,128)(2,1)}, bf16[4,648,128]{2,1,0:T(8,128)(2,1)}, u32[]{:S(2)}, u32[]{:S(2)}) collective-permute-start(bf16[4,648,128]{2,1,0:T(8,128)(2,1)} %dynamic-slice_bitcast_fusion.7), channel_id=1, source_target_pairs={{0,8},{8,0},{16,24},{24,16},{1,9},{9,1},{17,25},{25,17},{2,10},{10... | collective-permute-start | bytes 1990664 | tf_op jit(solution)/shard_map/ppermute | solution.py:428
  621.7 26.6 %collective-permute-start.50 = (bf16[1296,128]{1,0:T(8,128)(2,1)}, bf16[1296,128]{1,0:T(8,128)(2,1)}, u32[]{:S(2)}, u32[]{:S(2)}) collective-permute-start(bf16[1296,128]{1,0:T(8,128)(2,1)} %get-tuple-element.270), channel_id=1, source_target_pairs={{0,2},{1,3},{2,0},{3,1},{4,6},{5,7},{6,4},{7,5},{8,10},{9,11},{10,... | collective-permute-start | bytes 995336 | tf_op jit(solution)/shard_map/ppermute | solution.py:455
  623.9 41.7 %collective-permute-start.46 = (bf16[2688,128]{1,0:T(8,128)(2,1)}, bf16[2688,128]{1,0:T(8,128)(2,1)}, u32[]{:S(2)}, u32[]{:S(2)}) collective-permute-start(bf16[2688,128]{1,0:T(8,128)(2,1)} %bitcast_select_fusion.1), channel_id=1, source_target_pairs={{30,8},{16,9},{2,10},{18,11},{4,12},{20,13},{6,14},{17,15},{15,16}... | collective-permute-start | bytes 2064392 | tf_op jit(solution)/shard_map/ppermute | solution.py:340
  625.5 40.2 %collective-permute-start.47 = (bf16[2688,128]{1,0:T(8,128)(2,1)}, bf16[2688,128]{1,0:T(8,128)(2,1)}, u32[]{:S(2)}, u32[]{:S(2)}) collective-permute-start(bf16[2688,128]{1,0:T(8,128)(2,1)} %bitcast_select_fusion.1), channel_id=1, source_target_pairs={{14,7},{0,8},{24,9},{10,10},{26,11},{12,12},{28,13},{22,14},{25,15... | collective-permute-start | bytes 2064392 | tf_op jit(solution)/shard_map/ppermute | solution.py:340
  631.6 34.1 %collective-permute-start.48 = (bf16[2688,128]{1,0:T(8,128)(2,1)}, bf16[2688,128]{1,0:T(8,128)(2,1)}, u32[]{:S(2)}, u32[]{:S(2)}) collective-permute-start(bf16[2688,128]{1,0:T(8,128)(2,1)} %bitcast_select_fusion.1), channel_id=1, source_target_pairs={{30,7},{8,8},{2,9},{18,10},{4,11},{20,12},{6,13},{9,14},{15,15},{1... | collective-permute-start | bytes 2064392 | tf_op jit(solution)/shard_map/ppermute | solution.py:340
  633.1 19.1 %collective-permute-start.51 = (bf16[1296,128]{1,0:T(8,128)(2,1)}, bf16[1296,128]{1,0:T(8,128)(2,1)}, u32[]{:S(2)}, u32[]{:S(2)}) collective-permute-start(bf16[1296,128]{1,0:T(8,128)(2,1)} %get-tuple-element.271), channel_id=1, source_target_pairs={{0,4},{1,5},{2,6},{3,7},{4,0},{5,1},{6,2},{7,3},{8,12},{9,13},{10,... | collective-permute-start | bytes 995336 | tf_op jit(solution)/shard_map/ppermute | solution.py:455
  641.4 24.1 %all-to-all-start = ((f32[32,2,108]{2,1,0:T(2,128)}), f32[32,2,108]{2,1,0:T(2,128)S(1)}, u32[]{:S(2)}, u32[]{:S(2)}) async-start(f32[32,2,108]{2,1,0:T(2,128)} %copy.79), calls=%async_computation | async-start | bytes 65536 | tf_op jit(solution)/shard_map/all_to_all | solution.py:1187
  648.3 17.4 %collective-permute-start.49 = (bf16[2688,128]{1,0:T(8,128)(2,1)}, bf16[2688,128]{1,0:T(8,128)(2,1)}, u32[]{:S(2)}, u32[]{:S(2)}) collective-permute-start(bf16[2688,128]{1,0:T(8,128)(2,1)} %bitcast_select_fusion.1), channel_id=1, source_target_pairs={{16,8},{17,14},{21,29}} | collective-permute-start | bytes 2064392 | tf_op jit(solution)/shard_map/ppermute | solution.py:340
  652.2 13.5 %collective-permute-start.52 = (bf16[1296,128]{1,0:T(8,128)(2,1)}, bf16[1296,128]{1,0:T(8,128)(2,1)}, u32[]{:S(2)}, u32[]{:S(2)}) collective-permute-start(bf16[1296,128]{1,0:T(8,128)(2,1)} %get-tuple-element.268), channel_id=1, source_target_pairs={{0,6},{1,7},{2,4},{3,5},{4,2},{5,3},{6,0},{7,1},{8,14},{9,15},{10,... | collective-permute-start | bytes 995336 | tf_op jit(solution)/shard_map/ppermute | solution.py:455
  672.1 20.4 %collective-permute-start.53 = (bf16[1296,128]{1,0:T(8,128)(2,1)S(1)}, bf16[1296,128]{1,0:T(8,128)(2,1)S(1)}, u32[]{:S(2)}, u32[]{:S(2)}) collective-permute-start(bf16[1296,128]{1,0:T(8,128)(2,1)S(1)} %broadcast_select_fusion), channel_id=1, source_target_pairs={{0,0},{2,1},{9,2},{11,3},{4,4},{6,5},{29,6},{31,7}} | collective-permute-start | bytes 995336 | tf_op jit(solution)/shard_map/ppermute | solution.py:340
  673.4 37.6 %collective-permute-start.54 = (bf16[1296,128]{1,0:T(8,128)(2,1)S(1)}, bf16[1296,128]{1,0:T(8,128)(2,1)S(1)}, u32[]{:S(2)}, u32[]{:S(2)}) collective-permute-start(bf16[1296,128]{1,0:T(8,128)(2,1)S(1)} %broadcast_select_fusion), channel_id=1, source_target_pairs={{8,0},{10,1},{17,2},{19,3},{12,4},{14,5},{7,6}} | collective-permute-start | bytes 995336 | tf_op jit(solution)/shard_map/ppermute | solution.py:340
  674.7 36.3 %collective-permute-start.55 = (bf16[1296,128]{1,0:T(8,128)(2,1)S(1)}, bf16[1296,128]{1,0:T(8,128)(2,1)S(1)}, u32[]{:S(2)}, u32[]{:S(2)}) collective-permute-start(bf16[1296,128]{1,0:T(8,128)(2,1)S(1)} %broadcast_select_fusion), channel_id=1, source_target_pairs={{16,0},{18,1},{25,2},{27,3},{20,4},{5,5},{15,6}} | collective-permute-start | bytes 995336 | tf_op jit(solution)/shard_map/ppermute | solution.py:340
  676.0 35.0 %collective-permute-start.56 = (bf16[1296,128]{1,0:T(8,128)(2,1)S(1)}, bf16[1296,128]{1,0:T(8,128)(2,1)S(1)}, u32[]{:S(2)}, u32[]{:S(2)}) collective-permute-start(bf16[1296,128]{1,0:T(8,128)(2,1)S(1)} %broadcast_select_fusion), channel_id=1, source_target_pairs={{24,0},{26,1},{3,2},{22,3},{28,4},{13,5},{23,6}} | collective-permute-start | bytes 995336 | tf_op jit(solution)/shard_map/ppermute | solution.py:340
  686.8 24.2 %collective-permute-start.57 = (bf16[1296,128]{1,0:T(8,128)(2,1)S(1)}, bf16[1296,128]{1,0:T(8,128)(2,1)S(1)}, u32[]{:S(2)}, u32[]{:S(2)}) collective-permute-start(bf16[1296,128]{1,0:T(8,128)(2,1)S(1)} %broadcast_select_fusion), channel_id=1, source_target_pairs={{2,0},{1,1},{11,2},{30,3},{6,4},{21,5},{31,6}} | collective-permute-start | bytes 995336 | tf_op jit(solution)/shard_map/ppermute | solution.py:340
  (74 other events, 617.3 us)
Sparse Core Ops, SparseCore 0:
  83.8 203.4 all-gather.2
  515.3 88.2 all-gather.4
